TPU v7x, 32 devices: a whole 2x2x4 slice. The times are simulated.
32 devices in a mesh: head: 4 (over x, core), blk: 8 (over z, y).
Axes of the slice: x: 2, y: 2, z: 4, core: 2. Of those that a mesh axis runs over, the one named last changes fastest.
Arguments:
- inputs: bfloat16 [2, 2048, 768], P(None, ('blk', 'head')), may hold values from -6 to 6
- time_embed: float32 [2, 128], replicated, may hold values from -6 to 6
- segments: int32 [2, 2048], P(None, ('blk', 'head')), may hold values from 0 to 15, never falling along the last dimension, each value on 1 to 1280 neighbouring positions
- valid_mask: int32 [2, 2048], P(None, ('blk', 'head')), may hold values from 0 to 1
- teacher: bfloat16 [2, 2048, 768], P(None, ('blk', 'head')), may hold values from -6 to 6
- ada_weight: bfloat16 [128, 4608], P(None, ('head', 'blk')), may hold values from -0.25 to 0.25
- ada_bias: bfloat16 [4608], P(('head', 'blk')), may hold values from -3 to 3
- gain_attn: bfloat16 [768], P(('head', 'blk')), may hold values from 0.5 to 1.5
- qkv_weight: bfloat16 [768, 2304], P(('head', 'blk')), may hold values from -0.21875 to 0.21875
- out_weight: bfloat16 [768, 768], P(('head', 'blk')), may hold values from -3 to 3
- gain_mlp: bfloat16 [768], P(('head', 'blk')), may hold values from 0.5 to 1.5
- up_weight: bfloat16 [768, 3072], P(('head', 'blk')), may hold values from -0.21875 to 0.21875
- up_bias: bfloat16 [3072], P(('head', 'blk')), may hold values from -3 to 3
- down_weight: bfloat16 [3072, 768], P(('head', 'blk')), may hold values from -0.109375 to 0.109375
- down_bias: bfloat16 [768], P(('head', 'blk')), may hold values from -3 to 3
Outputs:
- output: bfloat16 [2, 2048, 768], P(None, ('blk', 'head'))
- loss_value: float32 [], replicated
- grad_input: float32 [2, 2048, 768], P(None, ('blk', 'head'))
- grad_ada_weight: float32 [128, 4608], P(None, ('head', 'blk'))
- grad_ada_bias: float32 [4608], P(('head', 'blk'))
- grad_gain_attn: float32 [768], P(('head', 'blk'))
- grad_qkv_weight: float32 [768, 2304], P(('head', 'blk'))
- grad_out_weight: float32 [768, 768], P(('head', 'blk'))
- grad_gain_mlp: float32 [768], P(('head', 'blk'))
- grad_up_weight: float32 [768, 3072], P(('head', 'blk'))
- grad_up_bias: float32 [3072], P(('head', 'blk'))
- grad_down_weight: float32 [3072, 768], P(('head', 'blk'))
- grad_down_bias: float32 [768], P(('head', 'blk'))
Inputs may be any that keep to these rules, and one draw needn't show every extreme that they name: `segments`: documents are numbered from 0 along each sequence, never falling; a document has 1 to 1280 tokens, and one has exactly that many.
All inputs are finite; a program needn't handle non-finite values.
Results may differ from a plain program's by a relative error of at most 0.019.
Values may be sent and summed in bfloat16 or wider, within the bound.
No kernel may reach another device: no remote copies, remote signals or barrier semaphores. Data moves between devices by JAX's collectives and lax.ppermute only.
A program may use at most 576 MiB of HBM per device.

v0:
```python
from functools import partial

import jax
import jax.numpy as jnp
from jax import lax
from jax.sharding import PartitionSpec as P

HEADS = 12
HEAD_DIM = 64


precise = lax.Precision.HIGHEST


def normalize(hidden):
    average = jnp.mean(hidden, axis=-1, keepdims=True)
    centred = hidden - average
    variance = jnp.mean(centred * centred, axis=-1, keepdims=True)
    inverse = lax.rsqrt(variance + 1e-05)
    return (centred * inverse, inverse)


def norm_back(upstream, normed, inverse):
    first_mean = jnp.mean(upstream, axis=-1, keepdims=True)
    second_mean = jnp.mean(upstream * normed, axis=-1, keepdims=True)
    return inverse * (upstream - first_mean - normed * second_mean)


def split_three(value):
    high_part = value.astype(jnp.bfloat16)
    rest = value - high_part.astype(jnp.float32)
    middle_part = rest.astype(jnp.bfloat16)
    last_part = (rest - middle_part.astype(jnp.float32)).astype(jnp.bfloat16)
    return jnp.stack([high_part, middle_part, last_part], axis=2)


def on_device(
    inputs,
    time_embed,
    segments,
    valid_mask,
    teacher,
    ada_weight,
    ada_bias,
    gain_attn,
    qkv_weight,
    out_weight,
    gain_mlp,
    up_weight,
    up_bias,
    down_weight,
    down_bias,
):
    seq_count, tokens, model_width = inputs.shape
    n_head = lax.axis_size("head")
    n_blk = lax.axis_size("blk")
    length = tokens * n_head * n_blk
    queries = tokens * n_head
    heads_here = HEADS // n_head
    local_width = heads_here * HEAD_DIM
    scale_factor = HEAD_DIM ** (-0.5)
    bf16 = jnp.bfloat16
    f32 = jnp.float32
    blk_here = lax.axis_index("blk")
    all_docs = lax.all_gather(segments, ("head", "blk"), axis=1, tiled=True)
    key_docs = (
        all_docs.reshape(seq_count, n_head, n_blk, tokens)
        .transpose(0, 2, 1, 3)
        .reshape(seq_count, length)
    )
    query_docs = lax.dynamic_slice_in_dim(key_docs, blk_here * queries, queries, 1)
    mask_float = valid_mask.astype(f32)
    count_here = jnp.sum(mask_float)
    gathered = (
        lax.all_gather(qkv_weight, ("head", "blk"), axis=0, tiled=True),
        lax.all_gather(out_weight, ("head", "blk"), axis=0, tiled=True),
        lax.all_gather(up_weight, ("head", "blk"), axis=0, tiled=True),
        lax.all_gather(down_weight, ("head", "blk"), axis=0, tiled=True),
        lax.all_gather(ada_weight, ("head", "blk"), axis=1, tiled=True),
        lax.all_gather(ada_bias, ("head", "blk"), axis=0, tiled=True),
        lax.all_gather(gain_attn, ("head", "blk"), axis=0, tiled=True),
        lax.all_gather(gain_mlp, ("head", "blk"), axis=0, tiled=True),
        lax.all_gather(up_bias, ("head", "blk"), axis=0, tiled=True),
        lax.all_gather(down_bias, ("head", "blk"), axis=0, tiled=True),
    )
    (
        full_qkv,
        full_out,
        full_up,
        full_down,
        full_ada,
        full_ada_bias,
        full_gain_attn,
        full_gain_mlp,
        full_up_bias,
        full_down_bias,
    ) = gathered
    gain_one = full_gain_attn.astype(f32)
    gain_two = full_gain_mlp.astype(f32)
    modulation = jnp.dot(
        time_embed, full_ada.astype(f32), precision=precise
    ) + full_ada_bias.astype(f32)
    pieces = modulation.reshape(seq_count, 6, 1, model_width)
    shift_attn = pieces[:, 0]
    scale_attn = pieces[:, 1]
    gate_attn = pieces[:, 2]
    shift_mlp = pieces[:, 3]
    scale_mlp = pieces[:, 4]
    gate_mlp = pieces[:, 5]
    residual = inputs.astype(f32)
    normed_one, inverse_one = normalize(residual)
    scaled_one = normed_one * gain_one
    entered = (scaled_one * (1.0 + scale_attn) + shift_attn).astype(bf16)
    triple = jnp.einsum("std,df->stf", entered, full_qkv, preferred_element_type=f32).astype(bf16)
    triple = triple.reshape(seq_count, tokens, 3, model_width)
    grouped = lax.all_to_all(triple, "head", split_axis=3, concat_axis=1, tiled=True)
    query_send = grouped[:, :, 0]
    query_heads = query_send.reshape(seq_count, queries, heads_here, HEAD_DIM).transpose(0, 2, 1, 3)
    key_rows = grouped[:, :, 1]
    value_rows = grouped[:, :, 2]

    def heads_first(part):
        part_rows = part.shape[1]
        return part.reshape(seq_count, part_rows, heads_here, HEAD_DIM).transpose(0, 2, 1, 3)

    def forward_step(running, arrived, first_row, live=True):
        row_max, denominator, numerator = running
        key_part, value_part = arrived
        part_rows = key_part.shape[1]
        key_four = heads_first(key_part)
        value_four = heads_first(value_part)
        allowed = jnp.logical_and(query_docs[:, :, None] == key_docs[:, None, :], live)[:, None]
        scores = (
            jnp.einsum("shqe,shke->shqk", query_heads, key_four, preferred_element_type=f32)
            * scale_factor
        )
        masked = jnp.where(allowed, scores, -1e30)
        new_max = jnp.maximum(row_max, jnp.max(masked, axis=-1))
        exponent = jnp.where(allowed, jnp.exp(scores - new_max[..., None]), 0.0)
        denominator = jnp.sum(exponent, axis=-1)
        numerator = jnp.einsum(
            "shqk,shke->shqe", exponent.astype(bf16), value_four, preferred_element_type=f32
        )
        return (new_max, denominator, numerator)

    start_state = (
        jnp.full((seq_count, heads_here, queries), -1e30, f32),
        jnp.zeros((seq_count, heads_here, queries), f32),
        jnp.zeros((seq_count, heads_here, queries, HEAD_DIM), f32),
    )
    row_max, denominator, numerator = forward_step(
        start_state,
        (
            lax.all_gather(key_rows, "blk", axis=1, tiled=True),
            lax.all_gather(value_rows, "blk", axis=1, tiled=True),
        ),
        jnp.int32(0),
    )
    attention = numerator / denominator[..., None]
    log_total = row_max + jnp.log(denominator)
    attn_send = (
        attention.astype(bf16).transpose(0, 2, 1, 3).reshape(seq_count, queries, local_width)
    )
    mixed = lax.all_to_all(attn_send, "head", split_axis=1, concat_axis=2, tiled=True)
    branch = jnp.einsum("std,de->ste", mixed, full_out, preferred_element_type=f32)
    hidden = residual + gate_attn * branch
    normed_two, inverse_two = normalize(hidden)
    scaled_two = normed_two * gain_two
    moved = (scaled_two * (1.0 + scale_mlp) + shift_mlp).astype(bf16)
    upper_in = jnp.einsum(
        "std,df->stf", moved, full_up, preferred_element_type=f32
    ) + full_up_bias.astype(f32)
    active = jax.nn.gelu(upper_in, approximate=True).astype(bf16)
    lower_out = jnp.einsum(
        "stf,fd->std", active, full_down, preferred_element_type=f32
    ) + full_down_bias.astype(f32)
    final_state = hidden + gate_mlp * lower_out
    mismatch = final_state - teacher.astype(f32)
    error_here = jnp.sum(mask_float[:, :, None] * mismatch * mismatch)
    error_all, count_all = lax.psum((error_here, count_here), ("head", "blk"))
    loss_value = error_all / (count_all * model_width)
    grad_final = seq_count * length / count_all * mask_float[:, :, None] * mismatch
    grad_lower = (gate_mlp * grad_final).astype(bf16)
    grad_gate_mlp = jnp.sum(grad_final * lower_out, axis=1)
    grad_down_weight = jnp.einsum("stf,std->fd", active, grad_lower, preferred_element_type=f32)
    grad_down_bias = jnp.sum(grad_lower.astype(f32), axis=(0, 1))
    grad_active = jnp.einsum("std,fd->stf", grad_lower, full_down, preferred_element_type=f32)
    unused_value, gelu_back = jax.vjp(partial(jax.nn.gelu, approximate=True), upper_in)
    grad_upper = gelu_back(grad_active)[0].astype(bf16)
    grad_up_weight = jnp.einsum("std,stf->df", moved, grad_upper, preferred_element_type=f32)
    grad_up_bias = jnp.sum(grad_upper.astype(f32), axis=(0, 1))
    grad_moved = jnp.einsum("stf,df->std", grad_upper, full_up, preferred_element_type=f32)
    grad_shift_mlp = jnp.sum(grad_moved, axis=1)
    grad_scale_mlp = jnp.sum(grad_moved * scaled_two, axis=1)
    grad_scaled_two = grad_moved * (1.0 + scale_mlp)
    grad_gain_mlp = jnp.sum(grad_scaled_two * normed_two, axis=(0, 1))
    grad_hidden = grad_final + norm_back(grad_scaled_two * gain_two, normed_two, inverse_two)
    grad_branch = (gate_attn * grad_hidden).astype(bf16)
    grad_gate_attn = jnp.sum(grad_hidden * branch, axis=1)
    grad_out_weight = jnp.einsum("ste,std->ed", mixed, grad_branch, preferred_element_type=f32)
    grad_mixed = jnp.einsum(
        "std,ed->ste", grad_branch, full_out, preferred_element_type=f32
    ).astype(bf16)
    grad_heads = lax.all_to_all(grad_mixed, "head", split_axis=2, concat_axis=1, tiled=True)
    grad_four = heads_first(grad_heads)
    row_delta = jnp.sum(grad_four.astype(f32) * attention, axis=-1)

    def query_step(running, arrived, first_row, live=True):
        key_part, value_part = arrived
        part_rows = key_part.shape[1]
        key_four = heads_first(key_part)
        value_four = heads_first(value_part)
        allowed = jnp.logical_and(query_docs[:, :, None] == key_docs[:, None, :], live)[:, None]
        scores = (
            jnp.einsum("shqe,shke->shqk", query_heads, key_four, preferred_element_type=f32)
            * scale_factor
        )
        probabilities = jnp.where(allowed, jnp.exp(scores - log_total[..., None]), 0.0)
        grad_probs = jnp.einsum(
            "shqe,shke->shqk", grad_four, value_four, preferred_element_type=f32
        )
        grad_scores = (probabilities * (grad_probs - row_delta[..., None])).astype(bf16)
        return (
            jnp.einsum("shqk,shke->shqe", grad_scores, key_four, preferred_element_type=f32)
            * scale_factor
        )

    key_local = heads_first(key_rows)
    value_local = heads_first(value_rows)

    def key_step(running, arrived, first_row, live=True):
        query_part, grad_part, stat_part = arrived
        part_rows = query_part.shape[1]
        query_low = heads_first(query_part)
        grad_low = heads_first(grad_part)
        stats = jnp.sum(
            stat_part.astype(f32).reshape(seq_count, part_rows, 2, 3, heads_here), axis=3
        )
        total_part = stats[:, :, 0].transpose(0, 2, 1)
        delta_part = stats[:, :, 1].transpose(0, 2, 1)
        allowed = jnp.logical_and(key_docs[:, :, None] == query_docs[:, None, :], live)[:, None]
        scores = (
            jnp.einsum("shqe,shke->shqk", query_low, key_local, preferred_element_type=f32)
            * scale_factor
        )
        probabilities = jnp.where(allowed, jnp.exp(scores - total_part[..., None]), 0.0)
        grad_probs = jnp.einsum(
            "shqe,shke->shqk", grad_low, value_local, preferred_element_type=f32
        )
        grad_scores = (probabilities * (grad_probs - delta_part[..., None])).astype(bf16)
        grad_value = jnp.einsum(
            "shqk,shqe->shke", probabilities.astype(bf16), grad_low, preferred_element_type=f32
        )
        grad_key = (
            jnp.einsum("shqk,shqe->shke", grad_scores, query_low, preferred_element_type=f32)
            * scale_factor
        )
        return (grad_key, grad_value)

    total_rows = log_total.transpose(0, 2, 1)
    delta_rows = row_delta.transpose(0, 2, 1)
    stat_send = jnp.stack([split_three(total_rows), split_three(delta_rows)], axis=2).reshape(
        seq_count, queries, 6 * heads_here
    )
    empty_grad = jnp.zeros((seq_count, heads_here, queries, HEAD_DIM), f32)
    grad_query = query_step(
        empty_grad,
        (
            lax.all_gather(key_rows, "blk", axis=1, tiled=True),
            lax.all_gather(value_rows, "blk", axis=1, tiled=True),
        ),
        jnp.int32(0),
    )
    grad_key, grad_value = key_step(
        (empty_grad, empty_grad),
        (
            lax.all_gather(query_send, "blk", axis=1, tiled=True),
            lax.all_gather(grad_heads, "blk", axis=1, tiled=True),
            lax.all_gather(stat_send, "blk", axis=1, tiled=True),
        ),
        jnp.int32(0),
    )

    def rows_first(value):
        return value.transpose(0, 2, 1, 3).reshape(seq_count, queries, local_width)

    grad_triple = jnp.stack(
        [rows_first(grad_query), rows_first(grad_key), rows_first(grad_value)], axis=2
    ).astype(bf16)
    grad_tokens = lax.all_to_all(grad_triple, "head", split_axis=1, concat_axis=3, tiled=True)
    grad_flat = grad_tokens.reshape(seq_count, tokens, 3 * model_width)
    grad_qkv_weight = jnp.einsum("std,stf->df", entered, grad_flat, preferred_element_type=f32)
    grad_entered = jnp.einsum("stf,df->std", grad_flat, full_qkv, preferred_element_type=f32)
    grad_shift_attn = jnp.sum(grad_entered, axis=1)
    grad_scale_attn = jnp.sum(grad_entered * scaled_one, axis=1)
    grad_scaled_one = grad_entered * (1.0 + scale_attn)
    grad_gain_attn = jnp.sum(grad_scaled_one * normed_one, axis=(0, 1))
    grad_input = grad_hidden + norm_back(grad_scaled_one * gain_one, normed_one, inverse_one)
    grad_modulation = jnp.stack(
        [
            grad_shift_attn,
            grad_scale_attn,
            grad_gate_attn,
            grad_shift_mlp,
            grad_scale_mlp,
            grad_gate_mlp,
        ],
        axis=1,
    ).reshape(seq_count, 6 * model_width)
    grad_ada_weight = jnp.dot(time_embed.T, grad_modulation, precision=precise)
    grad_ada_bias = jnp.sum(grad_modulation, axis=0)
    later_owned = (
        lax.psum_scatter(grad_out_weight, ("head", "blk"), scatter_dimension=0, tiled=True),
        lax.psum_scatter(grad_up_weight, ("head", "blk"), scatter_dimension=0, tiled=True),
        lax.psum_scatter(grad_down_weight, ("head", "blk"), scatter_dimension=0, tiled=True),
        lax.psum_scatter(grad_gain_mlp, ("head", "blk"), scatter_dimension=0, tiled=True),
        lax.psum_scatter(grad_up_bias, ("head", "blk"), scatter_dimension=0, tiled=True),
        lax.psum_scatter(grad_down_bias, ("head", "blk"), scatter_dimension=0, tiled=True),
    )
    shard_out, shard_up, shard_down, shard_gain_mlp, shard_up_bias, shard_down_bias = later_owned
    first_owned = (
        lax.psum_scatter(grad_qkv_weight, ("head", "blk"), scatter_dimension=0, tiled=True),
        lax.psum_scatter(grad_ada_weight, ("head", "blk"), scatter_dimension=1, tiled=True),
        lax.psum_scatter(grad_ada_bias, ("head", "blk"), scatter_dimension=0, tiled=True),
        lax.psum_scatter(grad_gain_attn, ("head", "blk"), scatter_dimension=0, tiled=True),
    )
    shard_qkv, shard_ada, shard_ada_bias, shard_gain_attn = first_owned
    return (
        final_state.astype(bf16),
        loss_value,
        grad_input,
        shard_ada,
        shard_ada_bias,
        shard_gain_attn,
        shard_qkv,
        shard_out,
        shard_gain_mlp,
        shard_up,
        shard_up_bias,
        shard_down,
        shard_down_bias,
    )


def solution(mesh):
    return jax.shard_map(
        on_device,
        mesh=mesh,
        in_specs=(
            P(None, ("blk", "head"), None),
            P(),
            P(None, ("blk", "head")),
            P(None, ("blk", "head")),
            P(None, ("blk", "head"), None),
            P(None, ("head", "blk")),
            P(("head", "blk")),
            P(("head", "blk")),
            P(("head", "blk"), None),
            P(("head", "blk"), None),
            P(("head", "blk")),
            P(("head", "blk"), None),
            P(("head", "blk")),
            P(("head", "blk"), None),
            P(("head", "blk")),
        ),
        out_specs=(
            P(None, ("blk", "head"), None),
            P(),
            P(None, ("blk", "head"), None),
            P(None, ("head", "blk")),
            P(("head", "blk")),
            P(("head", "blk")),
            P(("head", "blk"), None),
            P(("head", "blk"), None),
            P(("head", "blk")),
            P(("head", "blk"), None),
            P(("head", "blk")),
            P(("head", "blk"), None),
            P(("head", "blk")),
        ),
        check_vma=False,
    )
```

profile of v0, /device:TPU:0, one launch (start us, length us, event | category | flops | bytes accessed | tf_op | source)
XLA Modules:
  0.0 1162.8 jit_solution(6677036301440943555)
XLA Ops:
  13.0 42.4 %all-reduce.11 = (bf16[4608]{0:T(1024)(128)(2,1)S(1)}, bf16[768]{0:T(1024)(128)(2,1)S(1)}, bf16[768]{0:T(1024)(128)(2,1)S(1)}, bf16[3072]{0:T(1024)(128)(2,1)S(1)}, bf16[768]{0:T(1024)(128)(2,1)S(1)}) all-reduce(bf16[4608]{0:T(1024)(128)(2,1)S(1)} %dynamic-update-slice, ...), channel_id=1, replica_groups=mesh['head'=4,'blk'=8] {'head','blk'}, use_global_device_ids=true, to_apply=%add | all-reduce | flops 9984 | bytes 39936
  57.6 10.2 all-gather.14.cloned.1.call-done
  70.2 59.7 %all-gather.16.cloned.1.call-done = bf16[768,2304]{1,0:T(8,128)(2,1)} async-done(((bf16[24,2304]{1,0:T(8,128)(2,1)}), bf16[768,2304]{1,0:T(8,128)(2,1)}) %all-gather.16.cloned.1.call-update) | async-done | bytes 3538960 | tf_op jit(solution)/shard_map/all_gather | solution.py:75
  135.3 12.0 %all_to_all.69 = bf16[4,2,36864]{2,1,0:T(2,128)(2,1)S(1)} all-to-all(bf16[4,2,36864]{2,1,0:T(2,128)(2,1)S(1)} %reshape.208), channel_id=1, replica_groups=mesh['head'=4,'blk'=8] {'head'}, dimensions={0} | all-to-all | bytes 1179648 | tf_op jit(solution)/shard_map/all_to_all | solution.py:116
  154.6 39.7 %psum.15 = f32[]{:T(128)} all-reduce(f32[]{:T(128)} %convert_reduce_fusion.4), channel_id=1, replica_groups=mesh['head'=4,'blk'=8] {'head','blk'}, use_global_device_ids=true, to_apply=%region_9.10 | all-reduce | flops 1 | bytes 8 | tf_op jit(solution)/shard_map/psum | solution.py:180
  194.3 66.4 %all-gather.3 = s32[32,64,2]{1,2,0:T(2,128)S(1)} all-gather(s32[1,64,2]{1,2,0:T(2,128)S(1)} %bitcast.271), channel_id=1, replica_groups=mesh['head'=4,'blk'=8] {'head','blk'}, dimensions={0}, use_global_device_ids=true | all-gather | bytes 16896 | tf_op jit(solution)/shard_map/all_gather | solution.py:65
  265.5 4.4 copy.137
  269.9 5.9 select_reduce_fusion
  275.9 7.0 fusion
  282.9 7.0 fusion.75
  295.4 4.7 all-to-all-done.1
  300.6 5.3 all-gather.18.cloned.1.call-done
  308.5 62.9 %all-gather.20.cloned.1.call-done = bf16[768,3072]{1,0:T(8,128)(2,1)} async-done(((bf16[24,3072]{1,0:T(8,128)(2,1)}), bf16[768,3072]{1,0:T(8,128)(2,1)}) %all-gather.20.cloned.1.call-update) | async-done | bytes 4718608 | tf_op jit(solution)/shard_map/all_gather | solution.py:77
  374.6 62.2 %all-gather.22.cloned.1.call-done = bf16[3072,768]{1,0:T(8,128)(2,1)} async-done(((bf16[96,768]{1,0:T(8,128)(2,1)}), bf16[3072,768]{1,0:T(8,128)(2,1)}) %all-gather.22.cloned.1.call-update) | async-done | bytes 4718608 | tf_op jit(solution)/shard_map/all_gather | solution.py:78
  436.8 4.9 convert_reduce_fusion.2
  452.3 9.4 all_to_all.70
  470.3 17.1 %all-gather.30.cloned.1.call-done = bf16[2,2048,1,192]{3,1,2,0:T(8,128)(2,1)} async-done(((bf16[2,256,1,192]{3,1,2,0:T(8,128)(2,1)}), bf16[2,2048,1,192]{3,1,2,0:T(8,128)(2,1)}) %all-gather.30.cloned.1.call-update) | async-done | bytes 1572880 | tf_op jit(solution)/shard_map/all_gather | solution.py:277
  491.3 7.8 fusion.101
  504.7 12.0 %fusion.52 = bf16[2,3,256,64]{2,3,1,0:T(8,128)(2,1)} fusion(bf16[2,3,2048,64]{2,3,1,0:T(8,128)(2,1)} %bitcast.231, f32[2,3,256,2048]{3,2,1,0:T(8,128)} %get-tuple-element.63, f32[2,3,256]{2,1,0:T(4,128)S(1)} %multiply_reduce_fusion.4, f32[2,3,256]{2,1,0:T(4,128)S(1)} %log_add_fusion, pred[2,256,2048]{2,1,0:T(8,128)(4,1)S(1)} %broadcast_compare_fusion.1, ...), kind=kOutput, calls=%fused_computation.58 | convolution fusion | flops 824377344 | bytes 17182720 | tf_op jit(solution)/shard_map/shqk,shke->shqe/dot_general | solution.py:224
  517.9 20.3 %all_gather.64 = bf16[2,2048,18]{1,0,2:T(2,128)(2,1)S(1)} all-gather(bf16[2,256,18]{1,0,2:T(2,128)(2,1)S(1)} %bitcast.268), channel_id=1, replica_groups=mesh['head'=4,'blk'=8] {'blk'}, dimensions={1}, use_global_device_ids=true | all-gather | bytes 165888 | tf_op jit(solution)/shard_map/all_gather | solution.py:279
  543.7 11.6 fusion.53
  557.0 7.4 fusion.54
  567.8 14.5 %all_to_all.71 = bf16[2,256,3,192]{3,0,2,1:T(2,128)(2,1)S(1)} all-to-all(bf16[2,256,3,192]{3,0,2,1:T(2,128)(2,1)S(1)} %pad_maximum_fusion), channel_id=1, replica_groups=mesh['head'=4,'blk'=8] {'head'}, dimensions={1} | all-to-all | bytes 1179648 | tf_op jit(solution)/shard_map/all_to_all | solution.py:290
  583.8 4.7 fusion.72
  589.2 5.2 convolution_bitcast_fusion
  594.5 5.9 convolution_bitcast_fusion.2
  601.3 5.2 convolution_bitcast_fusion.1
  612.3 39.6 %all-reduce.10 = (f32[]{:T(128)}, f32[4608]{0:T(1024)S(1)}, f32[768]{0:T(1024)S(1)}, f32[768]{0:T(1024)S(1)}, f32[3072]{0:T(1024)S(1)}, /*index=5*/f32[768]{0:T(1024)S(1)}) all-reduce(f32[]{:T(128)} %get-tuple-element.47, f32[4608]{0:T(1024)S(1)} %reduce_sum.238, ...), channel_id=1, replica_groups=mesh['head'=4,'blk'=8] {'head','blk'}, use_global_device_ids=true, to_apply=%region_7.8 | all-reduce | flops 9985 | bytes 79880 | tf_op jit(solution)/shard_map/psum | solution.py:180
  656.5 91.2 %reduce-scatter.6.cloned.1.call-done = f32[128,144]{0,1:T(8,128)} async-done(((f32[128,4608]{0,1:T(8,128)}), f32[128,144]{0,1:T(8,128)}) %reduce-scatter.6.cloned.1.call-update) | async-done | bytes 73744 | tf_op jit(solution)/shard_map/reduce_scatter | solution.py:323
  747.8 141.0 %reduce-scatter.12.cloned.1.call-done = f32[24,3072]{1,0:T(8,128)} async-done(((f32[768,3072]{1,0:T(8,128)}), f32[24,3072]{1,0:T(8,128)}) %reduce-scatter.12.cloned.1.call-update) | async-done | bytes 294928 | tf_op jit(solution)/shard_map/reduce_scatter | solution.py:314
  888.7 142.1 %reduce-scatter.14.cloned.1.call-done = f32[96,768]{1,0:T(8,128)} async-done(((f32[3072,768]{1,0:T(8,128)}), f32[96,768]{1,0:T(8,128)}) %reduce-scatter.14.cloned.1.call-update) | async-done | bytes 294928 | tf_op jit(solution)/shard_map/reduce_scatter | solution.py:315
  1030.8 124.0 %reduce-scatter.8.cloned.1.call-done = f32[24,2304]{1,0:T(8,128)} async-done(((f32[768,2304]{1,0:T(8,128)}), f32[24,2304]{1,0:T(8,128)}) %reduce-scatter.8.cloned.1.call-update) | async-done | bytes 221200 | tf_op jit(solution)/shard_map/reduce_scatter | solution.py:322
  (250 shorter events, 90.7 us)
Async XLA Ops:
  7.2 60.6 %copy-start = (f32[2,128]{1,0:T(2,128)S(1)}, f32[2,128]{1,0:T(2,128)}, u32[]{:S(2)}) copy-start(f32[2,128]{1,0:T(2,128)} %param.16) | copy-start | bytes 3076
  7.2 122.7 %copy-start.1 = (bf16[2,64,768]{2,1,0:T(8,128)(2,1)S(1)}, bf16[2,64,768]{2,1,0:T(8,128)(2,1)}, u32[]{:S(2)}) copy-start(bf16[2,64,768]{2,1,0:T(8,128)(2,1)} %param.15) | copy-start | bytes 589828
  7.2 60.6 %all-gather.14.cloned.1.call-start = ((), (), s32[]{:S(2)}) async-start(), calls=%async_computation.9 | async-start | bytes 1216512 | tf_op jit(solution)/shard_map/all_gather | solution.py:79
  7.9 122.0 %all-gather.16.cloned.1.call-start = ((), (), s32[]{:S(2)}) async-start(), calls=%async_computation.10 | async-start | bytes 3649536 | tf_op jit(solution)/shard_map/all_gather | solution.py:75
  8.7 253.9 %all-gather.26.cloned.1.call-start = ((), (), s32[]{:S(2)}) async-start(), calls=%async_computation.20 | async-start | bytes 2359296 | tf_op jit(solution)/shard_map/all_gather | solution.py:154
  56.4 76.2 %copy-start.31 = (f32[2,64]{1,0:T(2,128)}, f32[2,64]{1,0:T(2,128)S(1)}, u32[]{:S(2)}) copy-start(f32[2,64]{1,0:T(2,128)S(1)} %broadcast_multiply_fusion.6) | copy-start | bytes 1540
  57.6 75.1 %copy-start.33 = (f32[2,64]{1,0:T(2,128)}, f32[2,64]{1,0:T(2,128)S(1)}, u32[]{:S(2)}) copy-start(f32[2,64]{1,0:T(2,128)S(1)} %add_rsqrt_fusion.1) | copy-start | bytes 1540
  70.2 62.4 %copy-start.24 = (f32[2,1,1,768]{3,0,1,2:T(2,128)}, f32[2,1,1,768]{3,0,1,2:T(2,128)S(1)}, u32[]{:S(2)}) copy-start(f32[2,1,1,768]{3,0,1,2:T(2,128)S(1)} %copy.171) | copy-start | bytes 18436
  70.2 62.4 %copy-start.26 = (f32[2,1,1,768]{3,0,1,2:T(2,128)}, f32[2,1,1,768]{3,0,1,2:T(2,128)S(1)}, u32[]{:S(2)}) copy-start(f32[2,1,1,768]{3,0,1,2:T(2,128)S(1)} %copy.170) | copy-start | bytes 18436
  150.4 43.8 %copy-start.46 = (s32[2,64]{1,0:T(2,128)S(1)}, s32[2,64]{1,0:T(2,128)}, u32[]{:S(2)}) copy-start(s32[2,64]{1,0:T(2,128)} %param.17) | copy-start | bytes 1540
  151.4 114.0 %copy-start.11 = (bf16[2,256,1,192]{3,1,2,0:T(8,128)(2,1)}, bf16[2,256,1,192]{3,1,2,0:T(8,128)(2,1)S(1)}, u32[]{:S(2)}) copy-start(bf16[2,256,1,192]{3,1,2,0:T(8,128)(2,1)S(1)} %get-tuple-element.46) | copy-start | bytes 589828
  151.5 114.0 %all-gather.28.cloned.1.call-start = ((), (), s32[]{:S(2)}) async-start(), calls=%async_computation.21 | async-start | bytes 2359296 | tf_op jit(solution)/shard_map/all_gather | solution.py:155
  152.0 153.9 %all-gather.18.cloned.1.call-start = ((), (), s32[]{:S(2)}) async-start(), calls=%async_computation.11 | async-start | bytes 1216512 | tf_op jit(solution)/shard_map/all_gather | solution.py:76
  152.6 218.8 %all-gather.20.cloned.1.call-start = ((), (), s32[]{:S(2)}) async-start(), calls=%async_computation.12 | async-start | bytes 4866048 | tf_op jit(solution)/shard_map/all_gather | solution.py:77
  153.2 283.6 %all-gather.22.cloned.1.call-start = ((), (), s32[]{:S(2)}) async-start(), calls=%async_computation.13 | async-start | bytes 4866048 | tf_op jit(solution)/shard_map/all_gather | solution.py:78
  290.7 9.4 all-to-all-start.1
  294.1 193.3 %all-gather.30.cloned.1.call-start = ((), (), s32[]{:S(2)}) async-start(), calls=%async_computation.22 | async-start | bytes 2359296 | tf_op jit(solution)/shard_map/all_gather | solution.py:277
  294.2 77.2 %copy-start.28 = (f32[2,768]{1,0:T(2,128)}, f32[2,768]{1,0:T(2,128)S(1)}, u32[]{:S(2)}) copy-start(f32[2,768]{1,0:T(2,128)S(1)} %get-tuple-element.72) | copy-start | bytes 18436
  294.2 152.6 %copy-start.19 = (f32[2,768]{1,0:T(2,128)}, f32[2,768]{1,0:T(2,128)S(1)}, u32[]{:S(2)}) copy-start(f32[2,768]{1,0:T(2,128)S(1)} %get-tuple-element.73) | copy-start | bytes 18436
  294.8 244.9 %all-gather.24.cloned.1.call-start = ((), (), s32[]{:S(2)}) async-start(), calls=%async_computation.14 | async-start | bytes 2359296 | tf_op jit(solution)/shard_map/all_gather | solution.py:278
  300.6 70.8 %copy-start.12 = (bf16[2,64,768]{2,1,0:T(8,128)(2,1)}, bf16[2,64,768]{2,1,0:T(8,128)(2,1)S(1)}, u32[]{:S(2)}) copy-start(bf16[2,64,768]{2,1,0:T(8,128)(2,1)S(1)} %all_to_all.57) | copy-start | bytes 589828
  308.5 138.3 %copy-start.29 = (f32[2,64]{1,0:T(2,128)}, f32[2,64]{1,0:T(2,128)S(1)}, u32[]{:S(2)}) copy-start(f32[2,64]{1,0:T(2,128)S(1)} %add_rsqrt_fusion) | copy-start | bytes 1540
  465.5 191.0 %reduce-scatter.10.cloned.1.call-start = ((), (), s32[]{:S(2)}) async-start(), calls=%async_computation.17 | async-start | bytes 2433024 | tf_op jit(solution)/shard_map/reduce_scatter | solution.py:313
  470.3 21.0 %copy-start.17 = (bf16[2,256,1,192]{1,3,0,2:T(8,128)(2,1)S(1)}, bf16[2,256,1,192]{1,3,0,2:T(8,128)(2,1)}, u32[]{:S(2)}) copy-start(bf16[2,256,1,192]{1,3,0,2:T(8,128)(2,1)} %copy.145) | copy-start | bytes 589828
  501.1 246.7 %reduce-scatter.6.cloned.1.call-start = ((), (), s32[]{:S(2)}) async-start(), calls=%async_computation.15 | async-start | bytes 2433024 | tf_op jit(solution)/shard_map/reduce_scatter | solution.py:323
  594.4 294.3 %reduce-scatter.12.cloned.1.call-start = ((), (), s32[]{:S(2)}) async-start(), calls=%async_computation.18 | async-start | bytes 9732096 | tf_op jit(solution)/shard_map/reduce_scatter | solution.py:314
  600.4 430.4 %reduce-scatter.14.cloned.1.call-start = ((), (), s32[]{:S(2)}) async-start(), calls=%async_computation.19 | async-start | bytes 9732096 | tf_op jit(solution)/shard_map/reduce_scatter | solution.py:315
  606.6 548.3 %reduce-scatter.8.cloned.1.call-start = ((), (), s32[]{:S(2)}) async-start(), calls=%async_computation.16 | async-start | bytes 7299072 | tf_op jit(solution)/shard_map/reduce_scatter | solution.py:322
  611.4 44.1 %copy-start.48 = (f32[2,64]{1,0:T(2,128)S(1)}, f32[2,64]{1,0:T(2,128)}, u32[]{:S(2)}) copy-start(f32[2,64]{1,0:T(2,128)} %get-tuple-element.17) | copy-start | bytes 1540
  611.4 44.1 %copy-start.47 = (f32[2,64]{1,0:T(2,128)S(1)}, f32[2,64]{1,0:T(2,128)}, u32[]{:S(2)}) copy-start(f32[2,64]{1,0:T(2,128)} %get-tuple-element.19) | copy-start | bytes 1540
  611.4 44.1 %copy-start.5 = (f32[2,64,768]{2,1,0:T(8,128)S(1)}, f32[2,64,768]{2,1,0:T(8,128)}, u32[]{:S(2)}) copy-start(f32[2,64,768]{2,1,0:T(8,128)} %copy-done.3) | copy-start | bytes 1179652
  611.4 44.1 %copy-start.18 = (f32[2,64,768]{2,1,0:T(8,128)S(1)}, f32[2,64,768]{2,1,0:T(8,128)}, u32[]{:S(2)}) copy-start(f32[2,64,768]{2,1,0:T(8,128)} %get-tuple-element.69) | copy-start | bytes 1179652
  (35 other events, 146.2 us)
Sparse Core Ops, SparseCore 0:
  11.0 56.8 all-gather.13
  70.7 59.1 all-gather.15
  151.6 47.5 all-gather.25
  201.8 48.6 all-gather.27
  253.3 52.6 all-gather.17
  308.7 62.6 all-gather.19
  374.3 62.4 all-gather.21
  439.0 48.3 all-gather.29
  489.5 49.2 all-gather.23
  544.5 98.4 reduce-scatter.9
  649.7 97.9 reduce-scatter.5
  754.1 134.6 reduce-scatter.11
  896.2 134.5 reduce-scatter.13
  1036.9 117.8 reduce-scatter.7
where the time goes:
time: 1170 us; the launch traced here: 1160 us
  waiting for transfers between devices  725 us (62%)
  blocking collectives  244 us (21%)
  matrix products  99.7 us (9%)
  local copies, waits for them, and re-layouts  52.4 us (4%)
  other arithmetic  18.4 us (2%)
  between operations  18.3 us (2%)
    reduce_scatter x1, waiting for transfers between devices, on_device(): lax.psum_scatter(grad_down_weight, ('head', 'blk'), scatter_dimension=0,...  142 us
    reduce_scatter x1, waiting for transfers between devices, on_device(): lax.psum_scatter(grad_up_weight, ('head', 'blk'), scatter_dimension=0, ti...  141 us
    reduce_scatter x1, waiting for transfers between devices, on_device(): lax.psum_scatter(grad_qkv_weight, ('head', 'blk'), scatter_dimension=0, t...  124 us
    reduce_scatter x1, waiting for transfers between devices, on_device(): lax.psum_scatter(grad_ada_weight, ('head', 'blk'), scatter_dimension=1, t...  91.2 us
    psum x2, blocking collectives, on_device(): error_all, count_all = lax.psum((error_here, count_here), ('head', 'blk'))  79.3 us
    all_gather x1, blocking collectives, on_device(): all_docs = lax.all_gather(segments, ('head', 'blk'), axis=1, tiled=True)  66.4 us
    all_gather x1, waiting for transfers between devices, on_device(): lax.all_gather(up_weight, ('head', 'blk'), axis=0, tiled=True)  62.9 us
    all_gather x1, waiting for transfers between devices, on_device(): lax.all_gather(down_weight, ('head', 'blk'), axis=0, tiled=True)  62.2 us
  transfers between devices with their start and end apart: 15, of which 11 were waited for; matrix products, arithmetic and copies ran while one was open for 14% of the time, Pallas kernels for 0%

commit v1 on v0

v1 whole, which is shorter than its diff:
```python
from functools import partial

import jax
import jax.numpy as jnp
from jax import lax
from jax.experimental import pallas as pl
from jax.experimental.pallas import tpu as pltpu
from jax.sharding import Mesh, PartitionSpec as P

HEADS = 12
HEAD_DIM = 64
GROUPS = 4
WIDTH = HEADS // GROUPS * HEAD_DIM
EVERY = ("hx", "hc", "rb", "sz", "sy")
SPOT = ("sz", "sy")
bf16 = jnp.bfloat16
f32 = jnp.float32
precise = lax.Precision.HIGHEST


def normalize(hidden):
    average = jnp.mean(hidden, axis=-1, keepdims=True)
    centred = hidden - average
    variance = jnp.mean(centred * centred, axis=-1, keepdims=True)
    inverse = lax.rsqrt(variance + 1e-05)
    return (centred * inverse, inverse)


def norm_back(upstream, normed, inverse):
    first_mean = jnp.mean(upstream, axis=-1, keepdims=True)
    second_mean = jnp.mean(upstream * normed, axis=-1, keepdims=True)
    return inverse * (upstream - first_mean - normed * second_mean)


def swap(value, axis):
    return lax.ppermute(value, axis, [(0, 1), (1, 0)])


def turn(value, axis, step):
    size = lax.axis_size(axis)
    return lax.ppermute(value, axis, [(i, (i - step) % size) for i in range(size)])


def place():
    return jnp.stack([lax.axis_index(name) for name in ("hx", "hc", "sz", "sy")]).astype(jnp.int32)


def piece_copies(place_ref, halves, whole, sems, inward):
    hx, hc, sz, sy = (place_ref[i] for i in range(4))
    rows, half = halves[0].shape[-2:]
    copies = []
    for side in range(2):
        for core in range(2):
            for second in range(2):
                for first in range(2):
                    for deep in range(4):
                        across, down = (first, second) if side == 0 else (second, first)
                        spot = (((hx ^ across) * 2 + (hc ^ core)) * 4 + lax.rem(sz + deep, 4)) * 2 + (sy ^ down)
                        near = halves[side].at[core, second, first, deep]
                        far = whole.at[spot, :, pl.ds(side * half, half)]
                        source, target = (near, far) if inward else (far, near)
                        copies.append(pltpu.make_async_copy(source, target, sems.at[len(copies)]))
    for copy in copies:
        copy.start()
    for copy in copies:
        copy.wait()


def join_kernel(place_ref, left, right, whole, sems):
    piece_copies(place_ref, (left, right), whole, sems, True)


def part_kernel(place_ref, whole, left, right, sems):
    piece_copies(place_ref, (left, right), whole, sems, False)


ANY = pl.BlockSpec(memory_space=pl.ANY)
SMEM = pl.BlockSpec(memory_space=pltpu.SMEM)


def join(here, left, right):
    rows, half = left.shape[-2:]
    return pl.pallas_call(
        join_kernel,
        out_shape=jax.ShapeDtypeStruct((32, rows, half * 2), left.dtype),
        in_specs=[SMEM, ANY, ANY],
        out_specs=ANY,
        scratch_shapes=[pltpu.SemaphoreType.DMA((64,))],
    )(here, left, right).reshape(rows * 32, half * 2)


def part(here, whole):
    rows, half = whole.shape[0] // 32, whole.shape[1] // 2
    side = jax.ShapeDtypeStruct((2, 2, 2, 4, rows, half), whole.dtype)
    return pl.pallas_call(
        part_kernel,
        out_shape=(side, side),
        in_specs=[SMEM, ANY],
        out_specs=(ANY, ANY),
        scratch_shapes=[pltpu.SemaphoreType.DMA((64,))],
    )(here, whole.reshape(32, rows, half * 2))


def gather_rows(here, shard):
    if lax.axis_size("rb") > 1:
        return lax.all_gather(shard, EVERY, axis=0, tiled=True)
    half = shard.shape[1] // 2
    sides = []
    for side, order in ((0, ("hx", "sy")), (1, ("sy", "hx"))):
        mine = shard[:, side * half : (side + 1) * half]
        level = jnp.stack([mine] + [turn(mine, "sz", k) for k in (1, 2, 3)])
        for axis in order + ("hc",):
            level = jnp.stack([level, swap(level, axis)])
        sides.append(level)
    return join(here, *sides)


def scatter_rows(here, whole):
    if lax.axis_size("rb") > 1:
        return lax.psum_scatter(whole, EVERY, scatter_dimension=0, tiled=True)
    sides = part(here, whole.astype(bf16))
    out = []
    for side, order in ((0, ("hx", "sy")), (1, ("sy", "hx"))):
        level = sides[side]
        for axis in ("hc",) + order[::-1]:
            total = level[0].astype(f32) + swap(level[1].astype(bf16), axis).astype(f32)
            level = total
        total = level[0]
        for k in (1, 2, 3):
            total = total + turn(level[k].astype(bf16), "sz", -k).astype(f32)
        out.append(total)
    return jnp.concatenate(out, axis=1)


def on_device(
    inputs,
    time_embed,
    segments,
    valid_mask,
    teacher,
    ada_weight,
    ada_bias,
    gain_attn,
    qkv_weight,
    out_weight,
    gain_mlp,
    up_weight,
    up_bias,
    down_weight,
    down_bias,
):
    seqs, tokens, width = inputs.shape
    hidden_units = up_weight.shape[1]
    parts = lax.axis_size("rb")
    devices = 32 * parts
    length = tokens * devices
    queries = 8 * tokens
    heads_here = HEADS // GROUPS
    scale_factor = HEAD_DIM ** (-0.5)
    here = place()
    hx, hc, rb = lax.axis_index("hx"), lax.axis_index("hc"), lax.axis_index("rb")
    spot = lax.axis_index("sz") * 2 + lax.axis_index("sy")
    own_seq = spot // GROUPS

    own_modulation = jnp.dot(
        time_embed, ada_weight.astype(f32), precision=precise
    ) + ada_bias.astype(f32)
    mask_float = valid_mask.astype(f32)
    fields = [
        own_modulation.reshape(-1),
        gain_attn.astype(f32),
        gain_mlp.astype(f32),
        up_bias.astype(f32),
        down_bias.astype(f32),
        segments.astype(f32).reshape(-1),
        jnp.sum(mask_float).reshape(1),
    ]
    sizes = [field.shape[0] for field in fields]
    packed = jnp.concatenate(fields)
    everyone = lax.all_to_all(
        jnp.broadcast_to(packed, (devices, packed.shape[0])), EVERY, 0, 0, tiled=True
    )
    columns = []
    begin = 0
    for size in sizes:
        columns.append(everyone[:, begin : begin + size])
        begin += size
    modulation = columns[0].reshape(devices, seqs, -1).transpose(1, 0, 2).reshape(seqs, -1)
    gain_one, gain_two, full_up_bias, full_down_bias = (c.reshape(-1) for c in columns[1:5])
    docs = columns[5].reshape(2, 2, parts, 8, seqs, tokens)
    count_all = jnp.sum(columns[6])
    pieces = modulation.reshape(seqs, 6, 1, width)
    shift_attn, scale_attn, gate_attn, shift_mlp, scale_mlp, gate_mlp = (
        pieces[:, i] for i in range(6)
    )

    full_qkv = gather_rows(here, qkv_weight)
    full_out = gather_rows(here, out_weight)
    full_up = gather_rows(here, up_weight)
    full_down = gather_rows(here, down_weight)

    residual = inputs.astype(f32)
    normed_one, inverse_one = normalize(residual)
    scaled_one = normed_one * gain_one
    entered = (scaled_one * (1.0 + scale_attn) + shift_attn).astype(bf16)
    triple = jnp.einsum("std,df->stf", entered, full_qkv, preferred_element_type=f32).astype(bf16)
    leave = (
        triple.reshape(seqs, tokens, 3, GROUPS, WIDTH)
        .transpose(0, 3, 2, 1, 4)
        .reshape(8, 3, tokens, WIDTH)
    )
    came = lax.all_to_all(leave, SPOT, 0, 0, tiled=True)
    came = came.transpose(1, 0, 2, 3).reshape(3, queries, WIDTH)
    query_rows = came[0]
    pair = came[1:]
    if parts > 1:
        pair = lax.all_gather(pair, "rb", axis=1, tiled=True)
    for axis in ("hx", "hc"):
        pair = jnp.stack([pair, swap(pair, axis)], axis=1)

    def heads_first(value):
        return value.reshape(-1, heads_here, HEAD_DIM).transpose(1, 0, 2)

    query_three = heads_first(query_rows)
    key_three = heads_first(pair[0])
    value_three = heads_first(pair[1])
    docs_here = lax.dynamic_index_in_dim(docs, own_seq, 4, keepdims=False)
    docs_here = jnp.where(hx == 1, docs_here[::-1], docs_here)
    docs_here = jnp.where(hc == 1, docs_here[:, ::-1], docs_here)
    key_docs = docs_here.transpose(1, 0, 2, 3, 4).reshape(-1)
    query_docs = lax.dynamic_index_in_dim(docs_here[0, 0], rb, 0, keepdims=False).reshape(-1)
    allowed = (query_docs[:, None] == key_docs[None, :])[None]
    scores = (
        jnp.einsum("hqe,hke->hqk", query_three, key_three, preferred_element_type=f32)
        * scale_factor
    )
    masked = jnp.where(allowed, scores, -1e30)
    row_max = jnp.max(masked, axis=-1)
    exponent = jnp.where(allowed, jnp.exp(scores - row_max[..., None]), 0.0)
    denominator = jnp.sum(exponent, axis=-1)
    numerator = jnp.einsum(
        "hqk,hke->hqe", exponent.astype(bf16), value_three, preferred_element_type=f32
    )
    attention = numerator / denominator[..., None]
    log_total = row_max + jnp.log(denominator)

    def rows_first(value):
        return value.astype(bf16).transpose(1, 0, 2).reshape(-1, WIDTH)

    def to_owner(rows):
        back = lax.all_to_all(rows.reshape(8, tokens, WIDTH), SPOT, 0, 0, tiled=True)
        return (
            back.reshape(seqs, GROUPS, tokens, WIDTH)
            .transpose(0, 2, 1, 3)
            .reshape(seqs, tokens, width)
        )

    mixed = to_owner(rows_first(attention))
    branch = jnp.einsum("std,de->ste", mixed, full_out, preferred_element_type=f32)
    hidden = residual + gate_attn * branch
    normed_two, inverse_two = normalize(hidden)
    scaled_two = normed_two * gain_two
    moved = (scaled_two * (1.0 + scale_mlp) + shift_mlp).astype(bf16)
    upper_in = jnp.einsum("std,df->stf", moved, full_up, preferred_element_type=f32) + full_up_bias
    active = jax.nn.gelu(upper_in, approximate=True).astype(bf16)
    lower_out = (
        jnp.einsum("stf,fd->std", active, full_down, preferred_element_type=f32) + full_down_bias
    )
    final_state = hidden + gate_mlp * lower_out
    mismatch = final_state - teacher.astype(f32)
    error_here = jnp.sum(mask_float[:, :, None] * mismatch * mismatch)
    grad_final = seqs * length / count_all * mask_float[:, :, None] * mismatch
    grad_lower = (gate_mlp * grad_final).astype(bf16)
    grad_gate_mlp = jnp.sum(grad_final * lower_out, axis=1)
    grad_down_weight = jnp.einsum("stf,std->fd", active, grad_lower, preferred_element_type=f32)
    grad_down_bias = jnp.sum(grad_lower.astype(f32), axis=(0, 1))
    grad_active = jnp.einsum("std,fd->stf", grad_lower, full_down, preferred_element_type=f32)
    unused_value, gelu_back = jax.vjp(partial(jax.nn.gelu, approximate=True), upper_in)
    grad_upper = gelu_back(grad_active)[0].astype(bf16)
    grad_up_weight = jnp.einsum("std,stf->df", moved, grad_upper, preferred_element_type=f32)
    grad_up_bias = jnp.sum(grad_upper.astype(f32), axis=(0, 1))
    grad_moved = jnp.einsum("stf,df->std", grad_upper, full_up, preferred_element_type=f32)
    grad_shift_mlp = jnp.sum(grad_moved, axis=1)
    grad_scale_mlp = jnp.sum(grad_moved * scaled_two, axis=1)
    grad_scaled_two = grad_moved * (1.0 + scale_mlp)
    grad_gain_mlp = jnp.sum(grad_scaled_two * normed_two, axis=(0, 1))
    grad_hidden = grad_final + norm_back(grad_scaled_two * gain_two, normed_two, inverse_two)
    grad_branch = (gate_attn * grad_hidden).astype(bf16)
    grad_gate_attn = jnp.sum(grad_hidden * branch, axis=1)
    grad_out_weight = jnp.einsum("ste,std->ed", mixed, grad_branch, preferred_element_type=f32)
    grad_mixed = jnp.einsum(
        "std,ed->ste", grad_branch, full_out, preferred_element_type=f32
    ).astype(bf16)
    grad_leave = (
        grad_mixed.reshape(seqs, tokens, GROUPS, WIDTH)
        .transpose(0, 2, 1, 3)
        .reshape(8, tokens, WIDTH)
    )
    grad_rows = lax.all_to_all(grad_leave, SPOT, 0, 0, tiled=True).reshape(queries, WIDTH)
    grad_three = heads_first(grad_rows)
    row_delta = jnp.sum(grad_three.astype(f32) * attention, axis=-1)

    shard_out = scatter_rows(here, grad_out_weight)
    shard_up = scatter_rows(here, grad_up_weight)
    shard_down = scatter_rows(here, grad_down_weight)

    probabilities = jnp.where(allowed, jnp.exp(scores - log_total[..., None]), 0.0)
    grad_probs = jnp.einsum("hqe,hke->hqk", grad_three, value_three, preferred_element_type=f32)
    grad_scores = (probabilities * (grad_probs - row_delta[..., None])).astype(bf16)
    grad_query = (
        jnp.einsum("hqk,hke->hqe", grad_scores, key_three, preferred_element_type=f32)
        * scale_factor
    )
    grad_value = jnp.einsum(
        "hqk,hqe->hke", probabilities.astype(bf16), grad_three, preferred_element_type=f32
    )
    grad_key = (
        jnp.einsum("hqk,hqe->hke", grad_scores, query_three, preferred_element_type=f32)
        * scale_factor
    )
    grad_pair = jnp.stack([rows_first(grad_key), rows_first(grad_value)]).reshape(
        2, 2, 2, parts * queries, WIDTH
    )
    for axis in ("hc", "hx"):
        grad_pair = (
            grad_pair[:, 0].astype(f32) + swap(grad_pair[:, 1].astype(bf16), axis).astype(f32)
        )
    if parts > 1:
        grad_pair = lax.psum_scatter(grad_pair, "rb", scatter_dimension=1, tiled=True)
    home = jnp.concatenate([rows_first(grad_query)[None], grad_pair.astype(bf16)])
    home = home.reshape(3, 8, tokens, WIDTH).transpose(1, 0, 2, 3)
    home = lax.all_to_all(home, SPOT, 0, 0, tiled=True)
    grad_flat = (
        home.reshape(seqs, GROUPS, 3, tokens, WIDTH)
        .transpose(0, 3, 2, 1, 4)
        .reshape(seqs, tokens, 3 * width)
    )
    grad_qkv_weight = jnp.einsum("std,stf->df", entered, grad_flat, preferred_element_type=f32)
    shard_qkv = scatter_rows(here, grad_qkv_weight)
    grad_entered = jnp.einsum("stf,df->std", grad_flat, full_qkv, preferred_element_type=f32)
    grad_shift_attn = jnp.sum(grad_entered, axis=1)
    grad_scale_attn = jnp.sum(grad_entered * scaled_one, axis=1)
    grad_scaled_one = grad_entered * (1.0 + scale_attn)
    grad_gain_attn = jnp.sum(grad_scaled_one * normed_one, axis=(0, 1))
    grad_input = grad_hidden + norm_back(grad_scaled_one * gain_one, normed_one, inverse_one)
    grad_modulation = jnp.stack(
        [
            grad_shift_attn,
            grad_scale_attn,
            grad_gate_attn,
            grad_shift_mlp,
            grad_scale_mlp,
            grad_gate_mlp,
        ],
        axis=1,
    ).reshape(seqs, devices, -1)
    sums = [
        grad_modulation.transpose(1, 0, 2).reshape(devices, -1),
        grad_gain_attn.reshape(devices, -1),
        grad_gain_mlp.reshape(devices, -1),
        grad_up_bias.reshape(devices, -1),
        grad_down_bias.reshape(devices, -1),
        jnp.broadcast_to(error_here, (devices, 1)),
    ]
    sizes = [value.shape[1] for value in sums]
    added = jnp.sum(
        lax.all_to_all(jnp.concatenate(sums, axis=1), EVERY, 0, 0, tiled=True), axis=0
    )
    owned = []
    begin = 0
    for size in sizes:
        owned.append(added[begin : begin + size])
        begin += size
    own_grad = owned[0].reshape(seqs, -1)
    grad_ada_weight = jnp.sum(time_embed[:, :, None] * own_grad[:, None, :], axis=0)
    loss_value = owned[5][0] / (count_all * width)
    return (
        final_state.astype(bf16),
        loss_value,
        grad_input,
        grad_ada_weight,
        jnp.sum(own_grad, axis=0),
        owned[1],
        shard_qkv,
        shard_out,
        owned[2],
        shard_up,
        owned[3],
        shard_down,
        owned[4],
    )


def solution(mesh):
    blocks = mesh.shape["blk"]
    fine = Mesh(mesh.devices.reshape(2, 2, blocks // 8, 4, 2), EVERY)
    tokens = ("rb", "sz", "sy", "hx", "hc")
    return jax.shard_map(
        on_device,
        mesh=fine,
        in_specs=(
            P(None, tokens, None),
            P(),
            P(None, tokens),
            P(None, tokens),
            P(None, tokens, None),
            P(None, EVERY),
            P(EVERY),
            P(EVERY),
            P(EVERY, None),
            P(EVERY, None),
            P(EVERY),
            P(EVERY, None),
            P(EVERY),
            P(EVERY, None),
            P(EVERY),
        ),
        out_specs=(
            P(None, tokens, None),
            P(),
            P(None, tokens, None),
            P(None, EVERY),
            P(EVERY),
            P(EVERY),
            P(EVERY, None),
            P(EVERY, None),
            P(EVERY),
            P(EVERY, None),
            P(EVERY),
            P(EVERY, None),
            P(EVERY),
        ),
        check_vma=False,
    )
```

time: 1170 us -> 1340 us (1.15)
  Pallas kernels: 0 us -> 877 us
  waiting for transfers between devices: 725 us -> 103 us
  blocking collectives: 244 us -> 0 us
  starting transfers between devices: 4.66 us -> 133 us
  other arithmetic: 18.4 us -> 87.6 us
  matrix products: 99.7 us -> 60.3 us
  local copies, waits for them, and re-layouts: 52.4 us -> 68.1 us
    pallas_call x0 -> x8, Pallas kernels: none -> 877 us  [the longest x4 439 us: join(): pl.pallas_call(join_kernel, out_shape=jax.ShapeDtypeStruct((32, rows, hal...]
    reduce_scatter x5 -> x0, waiting for transfers between devices: 498 us -> none  [the longest x1 142 us: on_device(): lax.psum_scatter(grad_down_weight, ('head', 'blk'), scatter_dimension=0,...]
    all_gather x9 -> x0, waiting for transfers between devices: 217 us -> none  [the longest x1 62.9 us: on_device(): lax.all_gather(up_weight, ('head', 'blk'), axis=0, tiled=True)]
    ppermute x0 -> x100, waiting for transfers between devices: none -> 103 us  [the longest x52 65.1 us: swap(): return lax.ppermute(value, axis, [(0, 1), (1, 0)])]
    ppermute x0 -> x100, starting transfers between devices: none -> 101 us  [the longest x48 64.8 us: turn(): lax.ppermute(value, axis, [(i, (i - step) % size) for i in range(size)])]
    all_gather x2 -> x0, blocking collectives: 86.8 us -> none  [the longest x1 66.4 us: on_device(): all_docs = lax.all_gather(segments, ('head', 'blk'), axis=1, tiled=True)]
    psum x2 -> x0, blocking collectives: 79.3 us -> none  [on_device(): error_all, count_all = lax.psum((error_here, count_here), ('head', 'blk'))]
    another operation x8 -> x43, other arithmetic: 2.33 us -> 48.6 us  [the longest x32 43.5 us: gather_rows(): level = jnp.stack([level, swap(level, axis)])]
  transfers between devices with their start and end apart: 15 -> 106, of which waited for: 11 -> 27; matrix products, arithmetic and copies ran while one was open for 14% -> 13% of each run, Pallas kernels for 0% -> 66%
where the time goes in v1:
time: 1340 us; the launch traced here: 1330 us
  Pallas kernels  877 us (65%)
  starting transfers between devices  133 us (10%)
  waiting for transfers between devices  103 us (8%)
  other arithmetic  87.6 us (7%)
  local copies, waits for them, and re-layouts  68.1 us (5%)
  matrix products  60.3 us (4%)
    pallas_call x4, Pallas kernels, join(): pl.pallas_call(join_kernel, out_shape=jax.ShapeDtypeStruct((32, rows, hal...  439 us
    pallas_call x4, Pallas kernels, part(): pl.pallas_call(part_kernel, out_shape=(side, side), in_specs=[SMEM, ANY],...  438 us
    ppermute x52, waiting for transfers between devices, swap(): return lax.ppermute(value, axis, [(0, 1), (1, 0)])  65.1 us
    ppermute x48, starting transfers between devices, turn(): lax.ppermute(value, axis, [(i, (i - step) % size) for i in range(size)])  64.8 us
    another operation x32, other arithmetic, gather_rows(): level = jnp.stack([level, swap(level, axis)])  43.5 us
    ppermute x48, waiting for transfers between devices, turn(): lax.ppermute(value, axis, [(i, (i - step) % size) for i in range(size)])  37.5 us
    ppermute x52, starting transfers between devices, swap(): return lax.ppermute(value, axis, [(0, 1), (1, 0)])  36 us
  transfers between devices with their start and end apart: 106, of which 27 were waited for; matrix products, arithmetic and copies ran while one was open for 13% of the time, Pallas kernels for 66%

profile of v1, /device:TPU:0, one launch (start us, length us, event | category | flops | bytes accessed | tf_op | source)
XLA Modules:
  0.0 1334.3 jit_solution(2258503478030873461)
XLA Ops:
  1.4 4.1 collective-permute-start.21
  18.3 5.4 all-to-all-start
  50.2 5.2 collective-permute-done.27
  64.8 3.9 collective-permute-done.39
  86.6 7.1 collective-permute-done.10
  114.4 109.7 %shard_map.246 = bf16[32,24,2304]{2,1,0:T(8,128)(2,1)} custom-call(s32[4]{0:T(128)} %pad_add_fusion.place_ref, bf16[2,2,2,4,24,1152]{5,4,3,2,1,0:T(8,128)(2,1)} %pad_maximum_fusion.4.left, bf16[2,2,2,4,24,1152]{5,4,3,2,1,0:T(8,128)(2,1)} %pad_maximum_fusion.5.right), custom_call_target="tpu_custom_call" | custom-call | tf_op jit(solution)/shard_map/pallas_call | solution.py:83
  228.7 6.0 all-to-all-start.1
  244.8 13.7 %collective-permute-done.30 = bf16[2,4,24,1536]{3,2,1,0:T(8,128)(2,1)S(1)} collective-permute-done((bf16[2,4,24,1536]{3,2,1,0:T(8,128)(2,1)}, bf16[2,4,24,1536]{3,2,1,0:T(8,128)(2,1)S(1)}, u32[]{:S(2)}, u32[]{:S(2)}) %collective-permute-start.30) | collective-permute-done | bytes 589856 | tf_op jit(solution)/shard_map/ppermute | solution.py:36
  270.1 38.1 %shard_map.247 = bf16[32,24,768]{2,1,0:T(8,128)(2,1)} custom-call(s32[4]{0:T(128)} %pad_add_fusion.place_ref, bf16[2,2,2,4,24,384]{5,4,3,2,1,0:T(8,128)(2,1)} %pad_maximum_fusion.14.left, bf16[2,2,2,4,24,384]{5,4,3,2,1,0:T(8,128)(2,1)} %pad_maximum_fusion.15.right), custom_call_target="tpu_custom_call" | custom-call | tf_op jit(solution)/shard_map/pallas_call | solution.py:83
  322.4 145.4 %shard_map.248 = bf16[32,24,3072]{2,1,0:T(8,128)(2,1)} custom-call(s32[4]{0:T(128)} %pad_add_fusion.place_ref, bf16[2,2,2,4,24,1536]{5,4,3,2,1,0:T(8,128)(2,1)} %pad_maximum_fusion.left, bf16[2,2,2,4,24,1536]{5,4,3,2,1,0:T(8,128)(2,1)} %pad_maximum_fusion.1.right), custom_call_target="tpu_custom_call" | custom-call | tf_op jit(solution)/shard_map/pallas_call | solution.py:83
  480.6 5.9 select_reduce_fusion
  486.5 6.8 fusion
  495.9 6.9 fusion.71
  504.0 5.9 all-to-all-start.2
  512.8 145.4 %shard_map.249 = bf16[32,96,768]{2,1,0:T(8,128)(2,1)} custom-call(s32[4]{0:T(128)} %pad_add_fusion.place_ref, bf16[2,2,2,4,96,384]{5,4,3,2,1,0:T(8,128)(2,1)} %pad_maximum_fusion.2.left, bf16[2,2,2,4,96,384]{5,4,3,2,1,0:T(8,128)(2,1)} %pad_maximum_fusion.3.right), custom_call_target="tpu_custom_call" | custom-call | tf_op jit(solution)/shard_map/pallas_call | solution.py:83
  685.2 6.2 all-to-all-start.3
  691.4 38.1 %shard_map.251 = (bf16[2,2,2,4,24,384]{5,4,3,2,1,0:T(8,128)(2,1)}, bf16[2,2,2,4,24,384]{5,4,3,2,1,0:T(8,128)(2,1)}) custom-call(s32[4]{0:T(128)} %pad_add_fusion.place_ref, bf16[32,24,768]{2,1,0:T(8,128)(2,1)} %bitcast.557), custom_call_target="tpu_custom_call" | custom-call | tf_op jit(solution)/shard_map/pallas_call | solution.py:95
  732.1 145.3 %shard_map.253 = (bf16[2,2,2,4,96,384]{5,4,3,2,1,0:T(8,128)(2,1)}, bf16[2,2,2,4,96,384]{5,4,3,2,1,0:T(8,128)(2,1)}) custom-call(s32[4]{0:T(128)} %pad_add_fusion.place_ref, bf16[32,96,768]{2,1,0:T(8,128)(2,1)} %bitcast.554), custom_call_target="tpu_custom_call" | custom-call | tf_op jit(solution)/shard_map/pallas_call | solution.py:95
  879.9 145.3 %shard_map.252 = (bf16[2,2,2,4,24,1536]{5,4,3,2,1,0:T(8,128)(2,1)}, bf16[2,2,2,4,24,1536]{5,4,3,2,1,0:T(8,128)(2,1)}) custom-call(s32[4]{0:T(128)} %pad_add_fusion.place_ref, bf16[32,24,3072]{2,1,0:T(8,128)(2,1)} %bitcast.548), custom_call_target="tpu_custom_call" | custom-call | tf_op jit(solution)/shard_map/pallas_call | solution.py:95
  1037.9 7.2 fusion.14
  1045.1 7.5 multiply_convert_fusion
  1073.0 3.9 collective-permute-start.69
  1099.3 4.2 all-to-all-start.4
  1110.6 9.3 collective-permute-done.83
  1126.5 5.8 collective-permute-done.96
  1132.4 3.8 collective-permute-start.99
  1137.6 3.8 collective-permute-start.87
  1144.7 5.1 collective-permute-done.86
  1174.2 4.2 all-to-all-start.5
  1178.3 109.6 %shard_map.250 = (bf16[2,2,2,4,24,1152]{5,4,3,2,1,0:T(8,128)(2,1)}, bf16[2,2,2,4,24,1152]{5,4,3,2,1,0:T(8,128)(2,1)}) custom-call(s32[4]{0:T(128)} %pad_add_fusion.place_ref, bf16[32,24,2304]{2,1,0:T(8,128)(2,1)} %bitcast.551), custom_call_target="tpu_custom_call" | custom-call | tf_op jit(solution)/shard_map/pallas_call | solution.py:95
  1303.1 7.6 collective-permute-done.59
  1314.3 4.1 collective-permute-done.60
  (569 shorter events, 307.6 us)
Async XLA Ops:
  1.4 34.1 %collective-permute-start.21 = (bf16[24,384]{1,0:T(8,128)(2,1)S(1)}, bf16[24,384]{1,0:T(8,128)(2,1)S(1)}, u32[]{:S(2)}, u32[]{:S(2)}) collective-permute-start(bf16[24,384]{1,0:T(8,128)(2,1)S(1)} %get-tuple-element.170), channel_id=1, source_target_pairs={{0,4},{2,6},{4,0},{6,2},{1,5},{3,7},{5,1},{7,3},{8,12},{10,14},{12... | collective-permute-start | bytes 55304 | tf_op jit(solution)/shard_map/ppermute | solution.py:41
  5.5 30.3 %collective-permute-start.20 = (bf16[24,384]{1,0:T(8,128)(2,1)S(1)}, bf16[24,384]{1,0:T(8,128)(2,1)S(1)}, u32[]{:S(2)}, u32[]{:S(2)}) collective-permute-start(bf16[24,384]{1,0:T(8,128)(2,1)S(1)} %get-tuple-element.170), channel_id=1, source_target_pairs={{0,6},{2,0},{4,2},{6,4},{1,7},{3,1},{5,3},{7,5},{8,14},{10,8},{12,... | collective-permute-start | bytes 55304 | tf_op jit(solution)/shard_map/ppermute | solution.py:41
  9.9 24.2 %collective-permute-start.16 = (bf16[24,384]{1,0:T(8,128)(2,1)S(1)}, bf16[24,384]{1,0:T(8,128)(2,1)S(1)}, u32[]{:S(2)}, u32[]{:S(2)}) collective-permute-start(bf16[24,384]{1,0:T(8,128)(2,1)S(1)} %get-tuple-element.171), channel_id=1, source_target_pairs={{0,2},{2,4},{4,6},{6,0},{1,3},{3,5},{5,7},{7,1},{8,10},{10,12},{12... | collective-permute-start | bytes 55304 | tf_op jit(solution)/shard_map/ppermute | solution.py:41
  18.3 61.8 %all-to-all-start = ((f32[32,1,585]{2,1,0:T(1,128)}), f32[32,1,585]{2,1,0:T(1,128)S(1)}, u32[]{:S(2)}, u32[]{:S(2)}) async-start(f32[32,1,585]{2,1,0:T(1,128)} %broadcast_in_dim.26), calls=%async_computation | async-start | bytes 163840 | tf_op jit(solution)/shard_map/all_to_all | solution.py:180
  75.0 32.8 %collective-permute-start.35 = (bf16[4,24,1536]{2,1,0:T(8,128)(2,1)}, bf16[4,24,1536]{2,1,0:T(8,128)(2,1)}, u32[]{:S(2)}, u32[]{:S(2)}) collective-permute-start(bf16[4,24,1536]{2,1,0:T(8,128)(2,1)} %get-tuple-element.108), channel_id=1, source_target_pairs={{0,1},{1,0},{2,3},{3,2},{4,5},{5,4},{6,7},{7,6},{8,9},{9,8},{10,11... | collective-permute-start | bytes 884744 | tf_op jit(solution)/shard_map/ppermute | solution.py:36
  76.6 28.1 %collective-permute-start.29 = (bf16[4,24,1536]{2,1,0:T(8,128)(2,1)}, bf16[4,24,1536]{2,1,0:T(8,128)(2,1)}, u32[]{:S(2)}, u32[]{:S(2)}) collective-permute-start(bf16[4,24,1536]{2,1,0:T(8,128)(2,1)} %get-tuple-element.110), channel_id=1, source_target_pairs={{0,16},{16,0},{1,17},{17,1},{2,18},{18,2},{3,19},{19,3},{4,20},{20... | collective-permute-start | bytes 884744 | tf_op jit(solution)/shard_map/ppermute | solution.py:36
  78.8 159.8 %collective-permute-start.47 = (bf16[4,96,384]{2,1,0:T(8,128)(2,1)}, bf16[4,96,384]{2,1,0:T(8,128)(2,1)}, u32[]{:S(2)}, u32[]{:S(2)}) collective-permute-start(bf16[4,96,384]{2,1,0:T(8,128)(2,1)} %get-tuple-element.112), channel_id=1, source_target_pairs={{0,1},{1,0},{2,3},{3,2},{4,5},{5,4},{6,7},{7,6},{8,9},{9,8},{10,11... | collective-permute-start | bytes 884744 | tf_op jit(solution)/shard_map/ppermute | solution.py:36
  104.6 137.9 %collective-permute-start.41 = (bf16[4,96,384]{2,1,0:T(8,128)(2,1)}, bf16[4,96,384]{2,1,0:T(8,128)(2,1)}, u32[]{:S(2)}, u32[]{:S(2)}) collective-permute-start(bf16[4,96,384]{2,1,0:T(8,128)(2,1)} %get-tuple-element.114), channel_id=1, source_target_pairs={{0,16},{16,0},{1,17},{17,1},{2,18},{18,2},{3,19},{19,3},{4,20},{20... | collective-permute-start | bytes 884744 | tf_op jit(solution)/shard_map/ppermute | solution.py:36
  107.8 126.9 %collective-permute-start.18 = (bf16[2,4,24,384]{3,2,1,0:T(8,128)(2,1)}, bf16[2,4,24,384]{3,2,1,0:T(8,128)(2,1)}, u32[]{:S(2)}, u32[]{:S(2)}) collective-permute-start(bf16[2,4,24,384]{3,2,1,0:T(8,128)(2,1)} %get-tuple-element.144), channel_id=1, source_target_pairs={{0,1},{1,0},{2,3},{3,2},{4,5},{5,4},{6,7},{7,6},{8,9},{9,8},{10,11... | collective-permute-start | bytes 442376 | tf_op jit(solution)/shard_map/ppermute | solution.py:36
  111.0 151.5 %collective-permute-start.25 = (bf16[2,2,4,24,384]{4,3,2,1,0:T(8,128)(2,1)}, bf16[2,2,4,24,384]{4,3,2,1,0:T(8,128)(2,1)}, u32[]{:S(2)}, u32[]{:S(2)}) collective-permute-start(bf16[2,2,4,24,384]{4,3,2,1,0:T(8,128)(2,1)} %get-tuple-element.116), channel_id=1, source_target_pairs={{0,8},{8,0},{1,9},{9,1},{2,10},{10,2},{3,11},{11,3},{4,12},{12,4},... | collective-permute-start | bytes 884744 | tf_op jit(solution)/shard_map/ppermute | solution.py:36
  112.4 127.3 %collective-permute-start.36 = (bf16[2,4,24,1536]{3,2,1,0:T(8,128)(2,1)}, bf16[2,4,24,1536]{3,2,1,0:T(8,128)(2,1)}, u32[]{:S(2)}, u32[]{:S(2)}) collective-permute-start(bf16[2,4,24,1536]{3,2,1,0:T(8,128)(2,1)} %get-tuple-element.82), channel_id=1, source_target_pairs={{0,16},{16,0},{1,17},{17,1},{2,18},{18,2},{3,19},{19,3},{4,20},{20... | collective-permute-start | bytes 1769480 | tf_op jit(solution)/shard_map/ppermute | solution.py:36
  228.7 32.9 %all-to-all-start.1 = ((bf16[8,3,64,192]{3,2,1,0:T(8,128)(2,1)}), bf16[8,3,64,192]{3,2,1,0:T(8,128)(2,1)S(1)}, u32[]{:S(2)}, u32[]{:S(2)}) async-start(bf16[8,3,64,192]{3,2,1,0:T(8,128)(2,1)} %bitcast.31), calls=%async_computation.1 | async-start | bytes 1572864 | tf_op jit(solution)/shard_map/all_to_all | solution.py:212
  238.6 24.4 %collective-permute-start.19 = (bf16[2,2,4,24,384]{4,3,2,1,0:T(8,128)(2,1)}, bf16[2,2,4,24,384]{4,3,2,1,0:T(8,128)(2,1)}, u32[]{:S(2)}, u32[]{:S(2)}) collective-permute-start(bf16[2,2,4,24,384]{4,3,2,1,0:T(8,128)(2,1)} %get-tuple-element.118), channel_id=1, source_target_pairs={{0,8},{8,0},{1,9},{9,1},{2,10},{10,2},{3,11},{11,3},{4,12},{12,4},... | collective-permute-start | bytes 884744 | tf_op jit(solution)/shard_map/ppermute | solution.py:36
  242.5 74.0 %collective-permute-start.37 = (bf16[2,2,4,24,1536]{4,3,2,1,0:T(8,128)(2,1)}, bf16[2,2,4,24,1536]{4,3,2,1,0:T(8,128)(2,1)}, u32[]{:S(2)}, u32[]{:S(2)}) collective-permute-start(bf16[2,2,4,24,1536]{4,3,2,1,0:T(8,128)(2,1)} %get-tuple-element.67), channel_id=1, source_target_pairs={{0,8},{8,0},{1,9},{9,1},{2,10},{10,2},{3,11},{11,3},{4,12},{12,4},... | collective-permute-start | bytes 3538952 | tf_op jit(solution)/shard_map/ppermute | solution.py:36
  258.5 54.7 %collective-permute-start.42 = (bf16[2,4,96,384]{3,2,1,0:T(8,128)(2,1)}, bf16[2,4,96,384]{3,2,1,0:T(8,128)(2,1)}, u32[]{:S(2)}, u32[]{:S(2)}) collective-permute-start(bf16[2,4,96,384]{3,2,1,0:T(8,128)(2,1)} %get-tuple-element.88), channel_id=1, source_target_pairs={{0,1},{1,0},{2,3},{3,2},{4,5},{5,4},{6,7},{7,6},{8,9},{9,8},{10,11... | collective-permute-start | bytes 1769480 | tf_op jit(solution)/shard_map/ppermute | solution.py:36
  260.0 59.5 %collective-permute-start.31 = (bf16[2,2,4,24,1536]{4,3,2,1,0:T(8,128)(2,1)}, bf16[2,2,4,24,1536]{4,3,2,1,0:T(8,128)(2,1)}, u32[]{:S(2)}, u32[]{:S(2)}) collective-permute-start(bf16[2,2,4,24,1536]{4,3,2,1,0:T(8,128)(2,1)} %get-tuple-element.69), channel_id=1, source_target_pairs={{0,8},{8,0},{1,9},{9,1},{2,10},{10,2},{3,11},{11,3},{4,12},{12,4},... | collective-permute-start | bytes 3538952 | tf_op jit(solution)/shard_map/ppermute | solution.py:36
  262.5 205.3 %collective-permute-start.49 = (bf16[2,2,4,96,384]{4,3,2,1,0:T(8,128)(2,1)}, bf16[2,2,4,96,384]{4,3,2,1,0:T(8,128)(2,1)}, u32[]{:S(2)}, u32[]{:S(2)}) collective-permute-start(bf16[2,2,4,96,384]{4,3,2,1,0:T(8,128)(2,1)} %get-tuple-element.71), channel_id=1, source_target_pairs={{0,8},{8,0},{1,9},{9,1},{2,10},{10,2},{3,11},{11,3},{4,12},{12,4},... | collective-permute-start | bytes 3538952 | tf_op jit(solution)/shard_map/ppermute | solution.py:36
  263.0 45.2 %collective-permute-start.12 = (bf16[2,512,192]{2,1,0:T(8,128)(2,1)}, bf16[2,512,192]{2,1,0:T(8,128)(2,1)}, u32[]{:S(2)}, u32[]{:S(2)}) collective-permute-start(bf16[2,512,192]{2,1,0:T(8,128)(2,1)} %bitcast.35), channel_id=1, source_target_pairs={{0,16},{16,0},{1,17},{17,1},{2,18},{18,2},{3,19},{19,3},{4,20},{20... | collective-permute-start | bytes 1179656 | tf_op jit(solution)/shard_map/ppermute | solution.py:36
  313.2 158.3 %collective-permute-start.13 = (bf16[2,2,512,192]{2,3,1,0:T(8,128)(2,1)}, bf16[2,2,512,192]{2,3,1,0:T(8,128)(2,1)}, u32[]{:S(2)}, u32[]{:S(2)}) collective-permute-start(bf16[2,2,512,192]{2,3,1,0:T(8,128)(2,1)} %copy.83), channel_id=1, source_target_pairs={{0,8},{8,0},{1,9},{9,1},{2,10},{10,2},{3,11},{11,3},{4,12},{12,4},... | collective-permute-start | bytes 2359304 | tf_op jit(solution)/shard_map/ppermute | solution.py:36
  316.0 193.8 %collective-permute-start.43 = (bf16[2,2,4,96,384]{4,3,2,1,0:T(8,128)(2,1)}, bf16[2,2,4,96,384]{4,3,2,1,0:T(8,128)(2,1)}, u32[]{:S(2)}, u32[]{:S(2)}) collective-permute-start(bf16[2,2,4,96,384]{4,3,2,1,0:T(8,128)(2,1)} %get-tuple-element.73), channel_id=1, source_target_pairs={{0,8},{8,0},{1,9},{9,1},{2,10},{10,2},{3,11},{11,3},{4,12},{12,4},... | collective-permute-start | bytes 3538952 | tf_op jit(solution)/shard_map/ppermute | solution.py:36
  504.0 154.9 %all-to-all-start.2 = ((bf16[8,64,192]{2,1,0:T(8,128)(2,1)}), bf16[8,64,192]{2,1,0:T(8,128)(2,1)S(1)}, u32[]{:S(2)}, u32[]{:S(2)}) async-start(bf16[8,64,192]{2,1,0:T(8,128)(2,1)} %copy.87), calls=%async_computation.2 | async-start | bytes 524288 | tf_op jit(solution)/shard_map/all_to_all | solution.py:251
  685.2 351.1 %all-to-all-start.3 = ((bf16[8,64,192]{2,1,0:T(8,128)(2,1)}), bf16[8,64,192]{2,1,0:T(8,128)(2,1)S(1)}, u32[]{:S(2)}, u32[]{:S(2)}) async-start(bf16[8,64,192]{2,1,0:T(8,128)(2,1)} %bitcast.114), calls=%async_computation.3 | async-start | bytes 524288 | tf_op jit(solution)/shard_map/all_to_all | solution.py:299
  731.5 299.6 %collective-permute-start.70 = (bf16[2,2,4,24,384]{4,3,2,1,0:T(8,128)(2,1)S(1)}, bf16[2,2,4,24,384]{4,3,2,1,0:T(8,128)(2,1)S(1)}, u32[]{:S(2)}, u32[]{:S(2)}) collective-permute-start(bf16[2,2,4,24,384]{4,3,2,1,0:T(8,128)(2,1)S(1)} %slice_bitcast_fusion.23), channel_id=1, source_target_pairs={{0,8},{8,0},{1,9},{9,1},{2,10},{10,2},{3,11},{11,3},{4,12},{12,4},... | collective-permute-start | bytes 884744 | tf_op jit(solution)/shard_map/ppermute | solution.py:36
  731.6 301.8 %collective-permute-start.64 = (bf16[2,2,4,24,384]{4,3,2,1,0:T(8,128)(2,1)S(1)}, bf16[2,2,4,24,384]{4,3,2,1,0:T(8,128)(2,1)S(1)}, u32[]{:S(2)}, u32[]{:S(2)}) collective-permute-start(bf16[2,2,4,24,384]{4,3,2,1,0:T(8,128)(2,1)S(1)} %slice_bitcast_fusion.24), channel_id=1, source_target_pairs={{0,8},{8,0},{1,9},{9,1},{2,10},{10,2},{3,11},{11,3},{4,12},{12,4},... | collective-permute-start | bytes 884744 | tf_op jit(solution)/shard_map/ppermute | solution.py:36
  879.8 203.2 %collective-permute-start.94 = (bf16[2,2,4,96,384]{4,3,2,1,0:T(8,128)(2,1)}, bf16[2,2,4,96,384]{4,3,2,1,0:T(8,128)(2,1)}, u32[]{:S(2)}, u32[]{:S(2)}) collective-permute-start(bf16[2,2,4,96,384]{4,3,2,1,0:T(8,128)(2,1)} %slice_bitcast_fusion.4), channel_id=1, source_target_pairs={{0,8},{8,0},{1,9},{9,1},{2,10},{10,2},{3,11},{11,3},{4,12},{12,4},... | collective-permute-start | bytes 3538952 | tf_op jit(solution)/shard_map/ppermute | solution.py:36
  1031.8 29.1 %collective-permute-start.71 = (bf16[2,4,24,384]{3,2,1,0:T(8,128)(2,1)}, bf16[2,4,24,384]{3,2,1,0:T(8,128)(2,1)}, u32[]{:S(2)}, u32[]{:S(2)}) collective-permute-start(bf16[2,4,24,384]{3,2,1,0:T(8,128)(2,1)} %fusion.87), channel_id=1, source_target_pairs={{0,16},{16,0},{1,17},{17,1},{2,18},{18,2},{3,19},{19,3},{4,20},{20... | collective-permute-start | bytes 442376 | tf_op jit(solution)/shard_map/ppermute | solution.py:36
  1034.2 28.1 %collective-permute-start.65 = (bf16[2,4,24,384]{3,2,1,0:T(8,128)(2,1)}, bf16[2,4,24,384]{3,2,1,0:T(8,128)(2,1)}, u32[]{:S(2)}, u32[]{:S(2)}) collective-permute-start(bf16[2,4,24,384]{3,2,1,0:T(8,128)(2,1)} %fusion.86), channel_id=1, source_target_pairs={{0,1},{1,0},{2,3},{3,2},{4,5},{5,4},{6,7},{7,6},{8,9},{9,8},{10,11... | collective-permute-start | bytes 442376 | tf_op jit(solution)/shard_map/ppermute | solution.py:36
  1090.0 29.9 %collective-permute-start.83 = (bf16[2,4,24,1536]{3,2,1,0:T(8,128)(2,1)}, bf16[2,4,24,1536]{3,2,1,0:T(8,128)(2,1)}, u32[]{:S(2)}, u32[]{:S(2)}) collective-permute-start(bf16[2,4,24,1536]{3,2,1,0:T(8,128)(2,1)} %fusion.41), channel_id=1, source_target_pairs={{0,16},{16,0},{1,17},{17,1},{2,18},{18,2},{3,19},{19,3},{4,20},{20... | collective-permute-start | bytes 1769480 | tf_op jit(solution)/shard_map/ppermute | solution.py:36
  1093.3 30.6 %collective-permute-start.77 = (bf16[2,4,24,1536]{3,2,1,0:T(8,128)(2,1)}, bf16[2,4,24,1536]{3,2,1,0:T(8,128)(2,1)}, u32[]{:S(2)}, u32[]{:S(2)}) collective-permute-start(bf16[2,4,24,1536]{3,2,1,0:T(8,128)(2,1)} %fusion.40), channel_id=1, source_target_pairs={{0,1},{1,0},{2,3},{3,2},{4,5},{5,4},{6,7},{7,6},{8,9},{9,8},{10,11... | collective-permute-start | bytes 1769480 | tf_op jit(solution)/shard_map/ppermute | solution.py:36
  1099.3 63.8 %all-to-all-start.4 = ((bf16[8,3,64,192]{3,2,1,0:T(8,128)(2,1)}), bf16[8,3,64,192]{3,2,1,0:T(8,128)(2,1)}, u32[]{:S(2)}, u32[]{:S(2)}) async-start(bf16[8,3,64,192]{3,2,1,0:T(8,128)(2,1)} %copy.94), calls=%async_computation.4 | async-start | bytes 1572864 | tf_op jit(solution)/shard_map/all_to_all | solution.py:332
  1110.1 31.5 %collective-permute-start.90 = (bf16[4,96,384]{2,1,0:T(8,128)(2,1)S(1)}, bf16[4,96,384]{2,1,0:T(8,128)(2,1)S(1)}, u32[]{:S(2)}, u32[]{:S(2)}) collective-permute-start(bf16[4,96,384]{2,1,0:T(8,128)(2,1)S(1)} %fusion.76), channel_id=1, source_target_pairs={{0,16},{16,0},{1,17},{17,1},{2,18},{18,2},{3,19},{19,3},{4,20},{20... | collective-permute-start | bytes 884744 | tf_op jit(solution)/shard_map/ppermute | solution.py:36
  1174.2 118.5 %all-to-all-start.5 = ((f32[32,1,457]{2,1,0:T(1,128)}), f32[32,1,457]{2,1,0:T(1,128)S(1)}, u32[]{:S(2)}, u32[]{:S(2)}) async-start(f32[32,1,457]{2,1,0:T(1,128)} %copy.97), calls=%async_computation.5 | async-start | bytes 131072 | tf_op jit(solution)/shard_map/all_to_all | solution.py:367
  (145 other events, 2539.5 us)

commit v2 on v1

--- a/solution.py
+++ b/solution.py
@@ -76,6 +76,7 @@
 
 ANY = pl.BlockSpec(memory_space=pl.ANY)
 SMEM = pl.BlockSpec(memory_space=pltpu.SMEM)
+VMEM = pl.BlockSpec(memory_space=pltpu.VMEM)
 
 
 def join(here, left, right):
@@ -84,8 +85,9 @@
         join_kernel,
         out_shape=jax.ShapeDtypeStruct((32, rows, half * 2), left.dtype),
         in_specs=[SMEM, ANY, ANY],
-        out_specs=ANY,
+        out_specs=VMEM,
         scratch_shapes=[pltpu.SemaphoreType.DMA((64,))],
+        compiler_params=pltpu.CompilerParams(vmem_limit_bytes=40 << 20),
     )(here, left, right).reshape(rows * 32, half * 2)
 
 
@@ -95,9 +97,10 @@
     return pl.pallas_call(
         part_kernel,
         out_shape=(side, side),
-        in_specs=[SMEM, ANY],
+        in_specs=[SMEM, VMEM],
         out_specs=(ANY, ANY),
         scratch_shapes=[pltpu.SemaphoreType.DMA((64,))],
+        compiler_params=pltpu.CompilerParams(vmem_limit_bytes=40 << 20),
     )(here, whole.reshape(32, rows, half * 2))
 
 

time: 1340 us -> 502 us (0.37)
  Pallas kernels: 877 us -> 21.8 us
  waiting for transfers between devices: 103 us -> 118 us
    pallas_call x4, Pallas kernels: 439 us -> 10.9 us  [join(): pl.pallas_call(join_kernel, out_shape=jax.ShapeDtypeStruct((32, rows, hal...]
    pallas_call x4, Pallas kernels: 438 us -> 10.9 us  [part(): pl.pallas_call(part_kernel, out_shape=(side, side), in_specs=[SMEM, VMEM]...]
  transfers between devices with their start and end apart: 106 -> 106, of which waited for: 27 -> 29; matrix products, arithmetic and copies ran while one was open for 13% -> 34% of each run, Pallas kernels for 66% -> 4%
where the time goes in v2:
time: 502 us; the launch traced here: 492 us
  starting transfers between devices  130 us (26%)
  waiting for transfers between devices  118 us (24%)
  other arithmetic  79.4 us (16%)
  local copies, waits for them, and re-layouts  76.2 us (15%)
  matrix products  61.8 us (12%)
  Pallas kernels  21.8 us (4%)
  between operations  5.97 us (1%)
    ppermute x52, waiting for transfers between devices, swap(): return lax.ppermute(value, axis, [(0, 1), (1, 0)])  77.1 us
    ppermute x48, starting transfers between devices, turn(): lax.ppermute(value, axis, [(i, (i - step) % size) for i in range(size)])  64.1 us
    ppermute x48, waiting for transfers between devices, turn(): lax.ppermute(value, axis, [(i, (i - step) % size) for i in range(size)])  38.3 us
    ppermute x52, starting transfers between devices, swap(): return lax.ppermute(value, axis, [(0, 1), (1, 0)])  37.1 us
    another operation x32, other arithmetic, gather_rows(): level = jnp.stack([level, swap(level, axis)])  36.4 us
    unnamed x141, local copies, waits for them, and re-layouts  14.1 us
    add x16, other arithmetic, scatter_rows(): total = level[0].astype(f32) + swap(level[1].astype(bf16), axis).astype(f32)  13.1 us
    pallas_call x4, Pallas kernels, join(): pl.pallas_call(join_kernel, out_shape=jax.ShapeDtypeStruct((32, rows, hal...  10.9 us
  transfers between devices with their start and end apart: 106, of which 29 were waited for; matrix products, arithmetic and copies ran while one was open for 34% of the time, Pallas kernels for 4%

profile of v2, /device:TPU:0, one launch (start us, length us, event | category | flops | bytes accessed | tf_op | source)
XLA Modules:
  0.0 492.5 jit_solution(2468453863294499583)
XLA Ops:
  1.4 4.1 collective-permute-start.21
  18.3 5.4 %all-to-all-start = ((f32[32,1,585]{2,1,0:T(1,128)}), f32[32,1,585]{2,1,0:T(1,128)S(1)}, u32[]{:S(2)}, u32[]{:S(2)}) async-start(f32[32,1,585]{2,1,0:T(1,128)} %broadcast_in_dim.26), calls=%async_computation | async-start | bytes 163840 | tf_op jit(solution)/shard_map/all_to_all | solution.py:183
  41.0 3.5 collective-permute-start.33
  49.1 5.2 %collective-permute-done.27 = bf16[24,1536]{1,0:T(8,128)(2,1)S(1)} collective-permute-done((bf16[24,1536]{1,0:T(8,128)(2,1)S(1)}, bf16[24,1536]{1,0:T(8,128)(2,1)S(1)}, u32[]{:S(2)}, u32[]{:S(2)}) %collective-permute-start.27) | collective-permute-done | bytes 73760 | tf_op jit(solution)/shard_map/ppermute | solution.py:41
  63.8 3.9 collective-permute-done.39
  85.0 7.6 %collective-permute-done.10 = bf16[2,4,24,1152]{3,2,1,0:T(8,128)(2,1)S(1)} collective-permute-done((bf16[2,4,24,1152]{3,2,1,0:T(8,128)(2,1)S(1)}, bf16[2,4,24,1152]{3,2,1,0:T(8,128)(2,1)S(1)}, u32[]{:S(2)}, u32[]{:S(2)}) %collective-permute-start.10) | collective-permute-done | bytes 442400 | tf_op jit(solution)/shard_map/ppermute | solution.py:36
  119.0 5.8 %all-to-all-start.1 = ((bf16[8,3,64,192]{3,2,1,0:T(8,128)(2,1)}), bf16[8,3,64,192]{3,2,1,0:T(8,128)(2,1)S(1)}, u32[]{:S(2)}, u32[]{:S(2)}) async-start(bf16[8,3,64,192]{3,2,1,0:T(8,128)(2,1)} %bitcast.31), calls=%async_computation.1 | async-start | bytes 1572864 | tf_op jit(solution)/shard_map/all_to_all | solution.py:215
  134.0 14.5 %collective-permute-done.30 = bf16[2,4,24,1536]{3,2,1,0:T(8,128)(2,1)S(1)} collective-permute-done((bf16[2,4,24,1536]{3,2,1,0:T(8,128)(2,1)}, bf16[2,4,24,1536]{3,2,1,0:T(8,128)(2,1)S(1)}, u32[]{:S(2)}, u32[]{:S(2)}) %collective-permute-start.30) | collective-permute-done | bytes 589856 | tf_op jit(solution)/shard_map/ppermute | solution.py:36
  158.9 8.8 %collective-permute-done.12 = bf16[2,512,192]{2,1,0:T(8,128)(2,1)} collective-permute-done((bf16[2,512,192]{2,1,0:T(8,128)(2,1)}, bf16[2,512,192]{2,1,0:T(8,128)(2,1)}, u32[]{:S(2)}, u32[]{:S(2)}) %collective-permute-start.12) | collective-permute-done | bytes 393248 | tf_op jit(solution)/shard_map/ppermute | solution.py:36
  179.3 3.8 shard_map.248
  183.2 3.9 pad_maximum_fusion.3.right
  195.1 3.7 copy.85
  201.4 7.1 %select_reduce_fusion = (f32[3,512]{1,0:T(4,128)S(1)}, f32[3,512,2048]{2,1,0:T(8,128)}) fusion(pred[512,2048]{1,0:T(8,128)(4,1)S(1)} %copy-done.31, bf16[2048,3,64]{0,2,1:T(8,128)(2,1)S(1)} %reshape_squeeze.10, bf16[512,3,64]{0,2,1:T(8,128)(2,1)} %reshape_squeeze.9), kind=kOutput, calls=%fused_computation.3 | convolution fusion | flops 412088832 | bytes 14620672 | tf_op jit(solution)/shard_map/hqe,hke->hqk/dot_general | solution.py:237
  208.5 6.9 %fusion = f32[3,512]{1,0:T(4,128)S(1)} fusion(f32[3,512,2048]{2,1,0:T(8,128)} %get-tuple-element.176, f32[3,512]{1,0:T(4,128)S(1)} %get-tuple-element.175, pred[512,2048]{1,0:T(8,128)(4,1)S(1)} %copy-done.32), kind=kLoop, calls=%fused_computation.4 | loop fusion | flops 12581376 | bytes 13643776 | tf_op jit(solution)/shard_map/reduce_sum | solution.py:243
  217.9 7.6 %fusion.71 = (bf16[512,3,64]{0,2,1:T(8,128)(2,1)S(1)}, f32[3,512,64]{1,2,0:T(8,128)}) fusion(f32[512,3]{0,1:T(4,128)S(1)} %bitcast.595, bf16[2048,3,64]{0,2,1:T(8,128)(2,1)S(1)} %reshape_squeeze.11, f32[3,512,2048]{2,1,0:T(8,128)} %get-tuple-element.176, f32[3,512]{1,0:T(4,128)S(1)} %get-tuple-element.175, pred[512,2048]{1,0:T(8,128)(4,1)} %broadcast_compare_fusion), kind=kOutput, calls=%fused_computation.160 | convolution fusion | flops 415432704 | bytes 15020032 | tf_op jit(solution)/shard_map/hqk,hke->hqe/dot_general | solution.py:244
  226.7 5.7 %all-to-all-start.2 = ((bf16[8,64,192]{2,1,0:T(8,128)(2,1)}), bf16[8,64,192]{2,1,0:T(8,128)(2,1)S(1)}, u32[]{:S(2)}, u32[]{:S(2)}) async-start(bf16[8,64,192]{2,1,0:T(8,128)(2,1)} %copy.87), calls=%async_computation.2 | async-start | bytes 524288 | tf_op jit(solution)/shard_map/all_to_all | solution.py:254
  254.1 3.8 bitcast_convert_fusion
  257.9 3.6 bitcast_convert_fusion.1
  265.6 4.2 all-to-all-start.3
  278.2 3.8 shard_map.252
  292.6 8.8 %fusion.14 = bf16[2048,3,64]{0,2,1:T(8,128)(2,1)} fusion(f32[3,512,2048]{2,1,0:T(8,128)} %get-tuple-element.176, f32[3,512]{1,0:T(4,128)} %log_add_fusion, pred[512,2048]{1,0:T(8,128)(4,1)} %broadcast_compare_fusion, bf16[512,3,64]{0,2,1:T(8,128)(2,1)} %reshape_reshape.11), kind=kOutput, calls=%fused_computation.20 | convolution fusion | flops 415629312 | bytes 14620672 | tf_op jit(solution)/shard_map/hqk,hqe->hke/dot_general | solution.py:317
  301.4 7.6 %multiply_convert_fusion = bf16[3,512,2048]{2,1,0:T(8,128)(2,1)S(1)} fusion(f32[3,512,2048]{2,1,0:T(8,128)} %get-tuple-element.176, f32[3,512]{1,0:T(4,128)S(1)} %multiply_reduce_fusion.4, f32[3,512]{1,0:T(4,128)S(1)} %copy-done.60, pred[512,2048]{1,0:T(8,128)(4,1)S(1)} %copy-done.33, bf16[2048,3,64]{0,2,1:T(8,128)(2,1)S(1)} %copy-done.51, ...), kind=kOutput, calls=%fused_computation | convolution fusion | flops 421527552 | bytes 20918272 | tf_op jit(solution)/shard_map/hqe,hke->hqk/dot_general | solution.py:311
  313.9 3.5 stack.520
  360.3 4.4 all-to-all-start.4
  364.6 6.1 %collective-permute-done.95 = bf16[2,4,96,384]{3,2,1,0:T(8,128)(2,1)} collective-permute-done((bf16[2,4,96,384]{3,2,1,0:T(8,128)(2,1)}, bf16[2,4,96,384]{3,2,1,0:T(8,128)(2,1)}, u32[]{:S(2)}, u32[]{:S(2)}) %collective-permute-start.95) | collective-permute-done | bytes 589856 | tf_op jit(solution)/shard_map/ppermute | solution.py:36
  375.1 8.3 %collective-permute-done.83 = bf16[2,4,24,1536]{3,2,1,0:T(8,128)(2,1)} collective-permute-done((bf16[2,4,24,1536]{3,2,1,0:T(8,128)(2,1)}, bf16[2,4,24,1536]{3,2,1,0:T(8,128)(2,1)}, u32[]{:S(2)}, u32[]{:S(2)}) %collective-permute-start.83) | collective-permute-done | bytes 589856 | tf_op jit(solution)/shard_map/ppermute | solution.py:36
  390.2 6.2 %collective-permute-done.96 = bf16[4,96,384]{2,1,0:T(8,128)(2,1)S(1)} collective-permute-done((bf16[4,96,384]{2,1,0:T(8,128)(2,1)S(1)}, bf16[4,96,384]{2,1,0:T(8,128)(2,1)S(1)}, u32[]{:S(2)}, u32[]{:S(2)}) %collective-permute-start.96) | collective-permute-done | bytes 294944 | tf_op jit(solution)/shard_map/ppermute | solution.py:36
  396.6 3.8 collective-permute-start.99
  402.3 3.8 collective-permute-start.87
  409.4 5.5 %collective-permute-done.86 = bf16[24,1536]{1,0:T(8,128)(2,1)S(1)} collective-permute-done((bf16[24,1536]{1,0:T(8,128)(2,1)S(1)}, bf16[24,1536]{1,0:T(8,128)(2,1)S(1)}, u32[]{:S(2)}, u32[]{:S(2)}) %collective-permute-start.86) | collective-permute-done | bytes 73760 | tf_op jit(solution)/shard_map/ppermute | solution.py:41
  461.2 7.6 %collective-permute-done.59 = bf16[2,4,24,1152]{3,2,1,0:T(8,128)(2,1)S(1)} collective-permute-done((bf16[2,4,24,1152]{3,2,1,0:T(8,128)(2,1)S(1)}, bf16[2,4,24,1152]{3,2,1,0:T(8,128)(2,1)S(1)}, u32[]{:S(2)}, u32[]{:S(2)}) %collective-permute-start.59) | collective-permute-done | bytes 442400 | tf_op jit(solution)/shard_map/ppermute | solution.py:36
  472.6 3.9 collective-permute-done.60
  (563 shorter events, 304.0 us)
Async XLA Ops:
  1.4 33.0 %collective-permute-start.21 = (bf16[24,384]{1,0:T(8,128)(2,1)S(1)}, bf16[24,384]{1,0:T(8,128)(2,1)S(1)}, u32[]{:S(2)}, u32[]{:S(2)}) collective-permute-start(bf16[24,384]{1,0:T(8,128)(2,1)S(1)} %get-tuple-element.170), channel_id=1, source_target_pairs={{0,4},{2,6},{4,0},{6,2},{1,5},{3,7},{5,1},{7,3},{8,12},{10,14},{12... | collective-permute-start | bytes 55304 | tf_op jit(solution)/shard_map/ppermute | solution.py:41
  5.5 29.3 %collective-permute-start.20 = (bf16[24,384]{1,0:T(8,128)(2,1)S(1)}, bf16[24,384]{1,0:T(8,128)(2,1)S(1)}, u32[]{:S(2)}, u32[]{:S(2)}) collective-permute-start(bf16[24,384]{1,0:T(8,128)(2,1)S(1)} %get-tuple-element.170), channel_id=1, source_target_pairs={{0,6},{2,0},{4,2},{6,4},{1,7},{3,1},{5,3},{7,5},{8,14},{10,8},{12,... | collective-permute-start | bytes 55304 | tf_op jit(solution)/shard_map/ppermute | solution.py:41
  6.9 21.9 %collective-permute-start.15 = (bf16[24,384]{1,0:T(8,128)(2,1)S(1)}, bf16[24,384]{1,0:T(8,128)(2,1)S(1)}, u32[]{:S(2)}, u32[]{:S(2)}) collective-permute-start(bf16[24,384]{1,0:T(8,128)(2,1)S(1)} %get-tuple-element.171), channel_id=1, source_target_pairs={{0,4},{2,6},{4,0},{6,2},{1,5},{3,7},{5,1},{7,3},{8,12},{10,14},{12... | collective-permute-start | bytes 55304 | tf_op jit(solution)/shard_map/ppermute | solution.py:41
  8.6 22.1 %collective-permute-start.14 = (bf16[24,384]{1,0:T(8,128)(2,1)S(1)}, bf16[24,384]{1,0:T(8,128)(2,1)S(1)}, u32[]{:S(2)}, u32[]{:S(2)}) collective-permute-start(bf16[24,384]{1,0:T(8,128)(2,1)S(1)} %get-tuple-element.171), channel_id=1, source_target_pairs={{0,6},{2,0},{4,2},{6,4},{1,7},{3,1},{5,3},{7,5},{8,14},{10,8},{12,... | collective-permute-start | bytes 55304 | tf_op jit(solution)/shard_map/ppermute | solution.py:41
  9.9 23.1 %collective-permute-start.16 = (bf16[24,384]{1,0:T(8,128)(2,1)S(1)}, bf16[24,384]{1,0:T(8,128)(2,1)S(1)}, u32[]{:S(2)}, u32[]{:S(2)}) collective-permute-start(bf16[24,384]{1,0:T(8,128)(2,1)S(1)} %get-tuple-element.171), channel_id=1, source_target_pairs={{0,2},{2,4},{4,6},{6,0},{1,3},{3,5},{5,7},{7,1},{8,10},{10,12},{12... | collective-permute-start | bytes 55304 | tf_op jit(solution)/shard_map/ppermute | solution.py:41
  18.3 61.3 %all-to-all-start = ((f32[32,1,585]{2,1,0:T(1,128)}), f32[32,1,585]{2,1,0:T(1,128)S(1)}, u32[]{:S(2)}, u32[]{:S(2)}) async-start(f32[32,1,585]{2,1,0:T(1,128)} %broadcast_in_dim.26), calls=%async_computation | async-start | bytes 163840 | tf_op jit(solution)/shard_map/all_to_all | solution.py:183
  73.9 32.9 %collective-permute-start.35 = (bf16[4,24,1536]{2,1,0:T(8,128)(2,1)}, bf16[4,24,1536]{2,1,0:T(8,128)(2,1)}, u32[]{:S(2)}, u32[]{:S(2)}) collective-permute-start(bf16[4,24,1536]{2,1,0:T(8,128)(2,1)} %get-tuple-element.108), channel_id=1, source_target_pairs={{0,1},{1,0},{2,3},{3,2},{4,5},{5,4},{6,7},{7,6},{8,9},{9,8},{10,11... | collective-permute-start | bytes 884744 | tf_op jit(solution)/shard_map/ppermute | solution.py:36
  75.5 28.4 %collective-permute-start.29 = (bf16[4,24,1536]{2,1,0:T(8,128)(2,1)}, bf16[4,24,1536]{2,1,0:T(8,128)(2,1)}, u32[]{:S(2)}, u32[]{:S(2)}) collective-permute-start(bf16[4,24,1536]{2,1,0:T(8,128)(2,1)} %get-tuple-element.110), channel_id=1, source_target_pairs={{0,16},{16,0},{1,17},{17,1},{2,18},{18,2},{3,19},{19,3},{4,20},{20... | collective-permute-start | bytes 884744 | tf_op jit(solution)/shard_map/ppermute | solution.py:36
  77.7 50.1 %collective-permute-start.47 = (bf16[4,96,384]{2,1,0:T(8,128)(2,1)}, bf16[4,96,384]{2,1,0:T(8,128)(2,1)}, u32[]{:S(2)}, u32[]{:S(2)}) collective-permute-start(bf16[4,96,384]{2,1,0:T(8,128)(2,1)} %get-tuple-element.112), channel_id=1, source_target_pairs={{0,1},{1,0},{2,3},{3,2},{4,5},{5,4},{6,7},{7,6},{8,9},{9,8},{10,11... | collective-permute-start | bytes 884744 | tf_op jit(solution)/shard_map/ppermute | solution.py:36
  103.8 27.9 %collective-permute-start.41 = (bf16[4,96,384]{2,1,0:T(8,128)(2,1)}, bf16[4,96,384]{2,1,0:T(8,128)(2,1)}, u32[]{:S(2)}, u32[]{:S(2)}) collective-permute-start(bf16[4,96,384]{2,1,0:T(8,128)(2,1)} %get-tuple-element.114), channel_id=1, source_target_pairs={{0,16},{16,0},{1,17},{17,1},{2,18},{18,2},{3,19},{19,3},{4,20},{20... | collective-permute-start | bytes 884744 | tf_op jit(solution)/shard_map/ppermute | solution.py:36
  110.3 42.7 %collective-permute-start.25 = (bf16[2,2,4,24,384]{4,3,2,1,0:T(8,128)(2,1)}, bf16[2,2,4,24,384]{4,3,2,1,0:T(8,128)(2,1)}, u32[]{:S(2)}, u32[]{:S(2)}) collective-permute-start(bf16[2,2,4,24,384]{4,3,2,1,0:T(8,128)(2,1)} %get-tuple-element.116), channel_id=1, source_target_pairs={{0,8},{8,0},{1,9},{9,1},{2,10},{10,2},{3,11},{11,3},{4,12},{12,4},... | collective-permute-start | bytes 884744 | tf_op jit(solution)/shard_map/ppermute | solution.py:36
  119.0 33.2 %all-to-all-start.1 = ((bf16[8,3,64,192]{3,2,1,0:T(8,128)(2,1)}), bf16[8,3,64,192]{3,2,1,0:T(8,128)(2,1)S(1)}, u32[]{:S(2)}, u32[]{:S(2)}) async-start(bf16[8,3,64,192]{3,2,1,0:T(8,128)(2,1)} %bitcast.31), calls=%async_computation.1 | async-start | bytes 1572864 | tf_op jit(solution)/shard_map/all_to_all | solution.py:215
  124.8 23.7 %collective-permute-start.30 = (bf16[2,4,24,1536]{3,2,1,0:T(8,128)(2,1)}, bf16[2,4,24,1536]{3,2,1,0:T(8,128)(2,1)S(1)}, u32[]{:S(2)}, u32[]{:S(2)}) collective-permute-start(bf16[2,4,24,1536]{3,2,1,0:T(8,128)(2,1)} %get-tuple-element.84), channel_id=1, source_target_pairs={{0,1},{1,0},{2,3},{3,2},{4,5},{5,4},{6,7},{7,6},{8,9},{9,8},{10,11... | collective-permute-start | bytes 1769480 | tf_op jit(solution)/shard_map/ppermute | solution.py:36
  127.8 25.8 %collective-permute-start.19 = (bf16[2,2,4,24,384]{4,3,2,1,0:T(8,128)(2,1)}, bf16[2,2,4,24,384]{4,3,2,1,0:T(8,128)(2,1)}, u32[]{:S(2)}, u32[]{:S(2)}) collective-permute-start(bf16[2,2,4,24,384]{4,3,2,1,0:T(8,128)(2,1)} %get-tuple-element.118), channel_id=1, source_target_pairs={{0,8},{8,0},{1,9},{9,1},{2,10},{10,2},{3,11},{11,3},{4,12},{12,4},... | collective-permute-start | bytes 884744 | tf_op jit(solution)/shard_map/ppermute | solution.py:36
  128.9 21.6 %collective-permute-start.48 = (bf16[2,4,96,384]{3,2,1,0:T(8,128)(2,1)S(1)}, bf16[2,4,96,384]{3,2,1,0:T(8,128)(2,1)S(1)}, u32[]{:S(2)}, u32[]{:S(2)}) collective-permute-start(bf16[2,4,96,384]{3,2,1,0:T(8,128)(2,1)S(1)} %get-tuple-element.86), channel_id=1, source_target_pairs={{0,16},{16,0},{1,17},{17,1},{2,18},{18,2},{3,19},{19,3},{4,20},{20... | collective-permute-start | bytes 1769480 | tf_op jit(solution)/shard_map/ppermute | solution.py:36
  131.7 44.5 %collective-permute-start.37 = (bf16[2,2,4,24,1536]{4,3,2,1,0:T(8,128)(2,1)}, bf16[2,2,4,24,1536]{4,3,2,1,0:T(8,128)(2,1)}, u32[]{:S(2)}, u32[]{:S(2)}) collective-permute-start(bf16[2,2,4,24,1536]{4,3,2,1,0:T(8,128)(2,1)} %get-tuple-element.67), channel_id=1, source_target_pairs={{0,8},{8,0},{1,9},{9,1},{2,10},{10,2},{3,11},{11,3},{4,12},{12,4},... | collective-permute-start | bytes 3538952 | tf_op jit(solution)/shard_map/ppermute | solution.py:36
  148.6 24.2 %collective-permute-start.42 = (bf16[2,4,96,384]{3,2,1,0:T(8,128)(2,1)}, bf16[2,4,96,384]{3,2,1,0:T(8,128)(2,1)}, u32[]{:S(2)}, u32[]{:S(2)}) collective-permute-start(bf16[2,4,96,384]{3,2,1,0:T(8,128)(2,1)} %get-tuple-element.88), channel_id=1, source_target_pairs={{0,1},{1,0},{2,3},{3,2},{4,5},{5,4},{6,7},{7,6},{8,9},{9,8},{10,11... | collective-permute-start | bytes 1769480 | tf_op jit(solution)/shard_map/ppermute | solution.py:36
  150.5 27.3 %collective-permute-start.31 = (bf16[2,2,4,24,1536]{4,3,2,1,0:T(8,128)(2,1)}, bf16[2,2,4,24,1536]{4,3,2,1,0:T(8,128)(2,1)}, u32[]{:S(2)}, u32[]{:S(2)}) collective-permute-start(bf16[2,2,4,24,1536]{4,3,2,1,0:T(8,128)(2,1)} %get-tuple-element.69), channel_id=1, source_target_pairs={{0,8},{8,0},{1,9},{9,1},{2,10},{10,2},{3,11},{11,3},{4,12},{12,4},... | collective-permute-start | bytes 3538952 | tf_op jit(solution)/shard_map/ppermute | solution.py:36
  153.0 30.1 %collective-permute-start.49 = (bf16[2,2,4,96,384]{4,3,2,1,0:T(8,128)(2,1)}, bf16[2,2,4,96,384]{4,3,2,1,0:T(8,128)(2,1)}, u32[]{:S(2)}, u32[]{:S(2)}) collective-permute-start(bf16[2,2,4,96,384]{4,3,2,1,0:T(8,128)(2,1)} %get-tuple-element.71), channel_id=1, source_target_pairs={{0,8},{8,0},{1,9},{9,1},{2,10},{10,2},{3,11},{11,3},{4,12},{12,4},... | collective-permute-start | bytes 3538952 | tf_op jit(solution)/shard_map/ppermute | solution.py:36
  175.7 56.7 %collective-permute-start.43 = (bf16[2,2,4,96,384]{4,3,2,1,0:T(8,128)(2,1)}, bf16[2,2,4,96,384]{4,3,2,1,0:T(8,128)(2,1)}, u32[]{:S(2)}, u32[]{:S(2)}) collective-permute-start(bf16[2,2,4,96,384]{4,3,2,1,0:T(8,128)(2,1)} %get-tuple-element.73), channel_id=1, source_target_pairs={{0,8},{8,0},{1,9},{9,1},{2,10},{10,2},{3,11},{11,3},{4,12},{12,4},... | collective-permute-start | bytes 3538952 | tf_op jit(solution)/shard_map/ppermute | solution.py:36
  265.6 23.7 %all-to-all-start.3 = ((bf16[8,64,192]{2,1,0:T(8,128)(2,1)}), bf16[8,64,192]{2,1,0:T(8,128)(2,1)}, u32[]{:S(2)}, u32[]{:S(2)}) async-start(bf16[8,64,192]{2,1,0:T(8,128)(2,1)} %bitcast.114), calls=%async_computation.3 | async-start | bytes 524288 | tf_op jit(solution)/shard_map/all_to_all | solution.py:302
  278.1 69.5 %collective-permute-start.94 = (bf16[2,2,4,96,384]{4,3,2,1,0:T(8,128)(2,1)}, bf16[2,2,4,96,384]{4,3,2,1,0:T(8,128)(2,1)}, u32[]{:S(2)}, u32[]{:S(2)}) collective-permute-start(bf16[2,2,4,96,384]{4,3,2,1,0:T(8,128)(2,1)} %slice_bitcast_fusion.4), channel_id=1, source_target_pairs={{0,8},{8,0},{1,9},{9,1},{2,10},{10,2},{3,11},{11,3},{4,12},{12,4},... | collective-permute-start | bytes 3538952 | tf_op jit(solution)/shard_map/ppermute | solution.py:36
  285.7 38.9 %collective-permute-start.71 = (bf16[2,4,24,384]{3,2,1,0:T(8,128)(2,1)S(1)}, bf16[2,4,24,384]{3,2,1,0:T(8,128)(2,1)}, u32[]{:S(2)}, u32[]{:S(2)}) collective-permute-start(bf16[2,4,24,384]{3,2,1,0:T(8,128)(2,1)S(1)} %fusion.87), channel_id=1, source_target_pairs={{0,16},{16,0},{1,17},{17,1},{2,18},{18,2},{3,19},{19,3},{4,20},{20... | collective-permute-start | bytes 442376 | tf_op jit(solution)/shard_map/ppermute | solution.py:36
  287.4 39.3 %collective-permute-start.65 = (bf16[2,4,24,384]{3,2,1,0:T(8,128)(2,1)}, bf16[2,4,24,384]{3,2,1,0:T(8,128)(2,1)}, u32[]{:S(2)}, u32[]{:S(2)}) collective-permute-start(bf16[2,4,24,384]{3,2,1,0:T(8,128)(2,1)} %fusion.86), channel_id=1, source_target_pairs={{0,1},{1,0},{2,3},{3,2},{4,5},{5,4},{6,7},{7,6},{8,9},{9,8},{10,11... | collective-permute-start | bytes 442376 | tf_op jit(solution)/shard_map/ppermute | solution.py:36
  324.4 21.4 %collective-permute-start.50 = (bf16[2,2,512,192]{2,3,0,1:T(8,128)(2,1)S(1)}, bf16[2,2,512,192]{2,3,0,1:T(8,128)(2,1)S(1)}, u32[]{:S(2)}, u32[]{:S(2)}) collective-permute-start(bf16[2,2,512,192]{2,3,0,1:T(8,128)(2,1)S(1)} %slice_bitcast_fusion.13), channel_id=1, source_target_pairs={{0,8},{8,0},{1,9},{9,1},{2,10},{10,2},{3,11},{11,3},{4,12},{12,4},... | collective-permute-start | bytes 2359304 | tf_op jit(solution)/shard_map/ppermute | solution.py:36
  350.1 20.7 %collective-permute-start.95 = (bf16[2,4,96,384]{3,2,1,0:T(8,128)(2,1)}, bf16[2,4,96,384]{3,2,1,0:T(8,128)(2,1)}, u32[]{:S(2)}, u32[]{:S(2)}) collective-permute-start(bf16[2,4,96,384]{3,2,1,0:T(8,128)(2,1)} %fusion.43), channel_id=1, source_target_pairs={{0,16},{16,0},{1,17},{17,1},{2,18},{18,2},{3,19},{19,3},{4,20},{20... | collective-permute-start | bytes 1769480 | tf_op jit(solution)/shard_map/ppermute | solution.py:36
  354.3 29.1 %collective-permute-start.83 = (bf16[2,4,24,1536]{3,2,1,0:T(8,128)(2,1)}, bf16[2,4,24,1536]{3,2,1,0:T(8,128)(2,1)}, u32[]{:S(2)}, u32[]{:S(2)}) collective-permute-start(bf16[2,4,24,1536]{3,2,1,0:T(8,128)(2,1)} %fusion.41), channel_id=1, source_target_pairs={{0,16},{16,0},{1,17},{17,1},{2,18},{18,2},{3,19},{19,3},{4,20},{20... | collective-permute-start | bytes 1769480 | tf_op jit(solution)/shard_map/ppermute | solution.py:36
  357.1 31.1 %collective-permute-start.77 = (bf16[2,4,24,1536]{3,2,1,0:T(8,128)(2,1)}, bf16[2,4,24,1536]{3,2,1,0:T(8,128)(2,1)}, u32[]{:S(2)}, u32[]{:S(2)}) collective-permute-start(bf16[2,4,24,1536]{3,2,1,0:T(8,128)(2,1)} %fusion.40), channel_id=1, source_target_pairs={{0,1},{1,0},{2,3},{3,2},{4,5},{5,4},{6,7},{7,6},{8,9},{9,8},{10,11... | collective-permute-start | bytes 1769480 | tf_op jit(solution)/shard_map/ppermute | solution.py:36
  360.3 67.9 %all-to-all-start.4 = ((bf16[8,3,64,192]{3,2,1,0:T(8,128)(2,1)}), bf16[8,3,64,192]{3,2,1,0:T(8,128)(2,1)}, u32[]{:S(2)}, u32[]{:S(2)}) async-start(bf16[8,3,64,192]{3,2,1,0:T(8,128)(2,1)} %copy.94), calls=%async_computation.4 | async-start | bytes 1572864 | tf_op jit(solution)/shard_map/all_to_all | solution.py:335
  372.0 24.4 %collective-permute-start.96 = (bf16[4,96,384]{2,1,0:T(8,128)(2,1)S(1)}, bf16[4,96,384]{2,1,0:T(8,128)(2,1)S(1)}, u32[]{:S(2)}, u32[]{:S(2)}) collective-permute-start(bf16[4,96,384]{2,1,0:T(8,128)(2,1)S(1)} %fusion.77), channel_id=1, source_target_pairs={{0,1},{1,0},{2,3},{3,2},{4,5},{5,4},{6,7},{7,6},{8,9},{9,8},{10,11... | collective-permute-start | bytes 884744 | tf_op jit(solution)/shard_map/ppermute | solution.py:36
  374.0 32.2 %collective-permute-start.90 = (bf16[4,96,384]{2,1,0:T(8,128)(2,1)S(1)}, bf16[4,96,384]{2,1,0:T(8,128)(2,1)S(1)}, u32[]{:S(2)}, u32[]{:S(2)}) collective-permute-start(bf16[4,96,384]{2,1,0:T(8,128)(2,1)S(1)} %fusion.76), channel_id=1, source_target_pairs={{0,16},{16,0},{1,17},{17,1},{2,18},{18,2},{3,19},{19,3},{4,20},{20... | collective-permute-start | bytes 884744 | tf_op jit(solution)/shard_map/ppermute | solution.py:36
  396.6 20.0 %collective-permute-start.99 = (bf16[96,384]{1,0:T(8,128)(2,1)S(1)}, bf16[96,384]{1,0:T(8,128)(2,1)S(1)}, u32[]{:S(2)}, u32[]{:S(2)}) collective-permute-start(bf16[96,384]{1,0:T(8,128)(2,1)S(1)} %get-tuple-element.99), channel_id=1, source_target_pairs={{0,6},{2,0},{4,2},{6,4},{1,7},{3,1},{5,3},{7,5},{8,14},{10,8},{12,... | collective-permute-start | bytes 221192 | tf_op jit(solution)/shard_map/ppermute | solution.py:41
  (142 other events, 1143.5 us)

commit v3 on v2

v3 whole, which is shorter than its diff:
```python
from functools import partial

import jax
import jax.numpy as jnp
from jax import lax
from jax.experimental import pallas as pl
from jax.experimental.pallas import tpu as pltpu
from jax.sharding import Mesh, PartitionSpec as P

HEADS = 12
HEAD_DIM = 64
GROUPS = 4
WIDTH = HEADS // GROUPS * HEAD_DIM
EVERY = ("hx", "hc", "rb", "sz", "sy")
SPOT = ("sz", "sy")
bf16 = jnp.bfloat16
f32 = jnp.float32
precise = lax.Precision.HIGHEST


def normalize(hidden):
    average = jnp.mean(hidden, axis=-1, keepdims=True)
    centred = hidden - average
    variance = jnp.mean(centred * centred, axis=-1, keepdims=True)
    inverse = lax.rsqrt(variance + 1e-05)
    return (centred * inverse, inverse)


def dot(left, right):
    return jnp.dot(left, right, preferred_element_type=f32)


def dot_nt(left, right):
    return lax.dot_general(left, right, (((1,), (1,)), ((), ())), preferred_element_type=f32)


def norm_back(upstream, normed, inverse):
    first_mean = jnp.mean(upstream, axis=-1, keepdims=True)
    second_mean = jnp.mean(upstream * normed, axis=-1, keepdims=True)
    return inverse * (upstream - first_mean - normed * second_mean)


def swap(value, axis):
    return lax.ppermute(value, axis, [(0, 1), (1, 0)])


def turn(value, axis, step):
    size = lax.axis_size(axis)
    return lax.ppermute(value, axis, [(i, (i - step) % size) for i in range(size)])


def place():
    return jnp.stack([lax.axis_index(name) for name in ("hx", "hc", "sz", "sy")]).astype(jnp.int32)


ANY = pl.BlockSpec(memory_space=pl.ANY)
SMEM = pl.BlockSpec(memory_space=pltpu.SMEM)
VMEM = pl.BlockSpec(memory_space=pltpu.VMEM)


def run_all(copies):
    for copy in copies:
        copy.start()
    for copy in copies:
        copy.wait()


def join_kernel(place_ref, left, right, whole, sems):
    hx, hc, sz, sy = (place_ref[i] for i in range(4))
    half = left.shape[-1]
    copies = []
    for side, pieces in enumerate((left, right)):
        for core in range(2):
            for second in range(2):
                for first in range(2):
                    for deep in range(4):
                        across, down = (first, second) if side == 0 else (second, first)
                        block = (hx ^ across) * 2 + (hc ^ core)
                        spot = (block * 4 + lax.rem(sz + deep, 4)) * 2 + (sy ^ down)
                        copies.append(
                            pltpu.make_async_copy(
                                pieces.at[core, second, first, deep],
                                whole.at[spot, :, pl.ds(side * half, half)],
                                sems.at[len(copies)],
                            )
                        )
    run_all(copies)


def join(here, left, right):
    rows, half = left.shape[-2:]
    return pl.pallas_call(
        join_kernel,
        out_shape=jax.ShapeDtypeStruct((32, rows, half * 2), left.dtype),
        in_specs=[SMEM, ANY, ANY],
        out_specs=VMEM,
        scratch_shapes=[pltpu.SemaphoreType.DMA((64,))],
        compiler_params=pltpu.CompilerParams(vmem_limit_bytes=40 << 20),
    )(here, left, right).reshape(rows * 32, half * 2)


def gather_rows(here, shard):
    if lax.axis_size("rb") > 1:
        return lax.all_gather(shard, EVERY, axis=0, tiled=True)
    half = shard.shape[1] // 2
    sides = []
    deep = jnp.stack([shard] + [turn(shard, "sz", k) for k in (1, 2, 3)])
    for side, order in ((0, ("hx", "sy")), (1, ("sy", "hx"))):
        level = deep[:, :, side * half : (side + 1) * half]
        for axis in order + ("hc",):
            level = jnp.stack([level, swap(level, axis)])
        sides.append(level)
    return join(here, *sides)


def piece_copies(place_ref, blocks, keep, send, sems, side, columns=None):
    hx, sz, sy = place_ref[0], place_ref[2], place_ref[3]
    copies = []
    for second in range(2):
        for first in range(2):
            for deep in range(4):
                across, down = (first, second) if side == 0 else (second, first)
                spot = ((hx ^ across) * 4 + lax.rem(sz + deep, 4)) * 2 + (sy ^ down)
                source = blocks.at[spot] if columns is None else blocks.at[spot, :, columns]
                target = (keep, send)[second].at[first, deep]
                copies.append(pltpu.make_async_copy(source, target, sems.at[side, len(copies)]))
    for copy in copies:
        copy.start()
    return copies


ORDERS = (("sy", "hx"), ("hx", "sy"))


def collect(keep, send, order):
    total = keep.astype(f32) + swap(send, order[0]).astype(f32)
    total = total[0] + swap(total[1].astype(bf16), order[1]).astype(f32)
    result = total[0]
    for k in (1, 2, 3):
        result = result + turn(total[k].astype(bf16), "sz", -k).astype(f32)
    return result


def put_rows(leave_ref, slot, which, rows):
    tokens = rows.shape[0]
    if which == 0:
        leave_ref[slot, pl.ds(tokens, tokens // 2), pl.ds(0, WIDTH)] = rows[: tokens // 2]
        leave_ref[slot, pl.ds(tokens, tokens // 2), pl.ds(WIDTH, WIDTH)] = rows[tokens // 2 :]
    else:
        leave_ref[slot, pl.ds(0, tokens), pl.ds((which - 1) * WIDTH, WIDTH)] = rows


def enter_kernel(x_ref, mod_ref, gain_ref, weight_ref, entered_ref, leave_ref):
    seqs, tokens, width = x_ref.shape
    for s in range(seqs):
        normed = normalize(x_ref[s].astype(f32))[0]
        value = normed * gain_ref[...] * (1.0 + mod_ref[s, 1:2]) + mod_ref[s, 0:1]
        entered_ref[pl.ds(s * tokens, tokens), :] = value.astype(bf16)
    entered = entered_ref[...]
    for which in range(3):
        triple = dot(entered, weight_ref[:, pl.ds(which * width, width)]).astype(bf16)
        for s in range(seqs):
            for g in range(GROUPS):
                rows = triple[s * tokens : (s + 1) * tokens, g * WIDTH : (g + 1) * WIDTH]
                put_rows(leave_ref, s * GROUPS + g, which, rows)


def enter(inputs, pieces, gain, weight):
    seqs, tokens, width = inputs.shape
    return pl.pallas_call(
        enter_kernel,
        out_shape=(
            jax.ShapeDtypeStruct((seqs * tokens, width), bf16),
            jax.ShapeDtypeStruct((8, tokens + tokens // 2, 2 * WIDTH), bf16),
        ),
        in_specs=[VMEM] * 4,
        out_specs=(VMEM, VMEM),
        compiler_params=pltpu.CompilerParams(vmem_limit_bytes=40 << 20),
    )(inputs, pieces, gain, weight)


def head_lanes(rows, head):
    lane = lax.broadcasted_iota(jnp.int32, (rows, WIDTH), 1)
    return (lane >= head * HEAD_DIM) & (lane < (head + 1) * HEAD_DIM)


def load_pairs(pair_ref, slot, first_row, half):
    value = pair_ref[slot, pl.ds(first_row, half), :]
    return value[:, :WIDTH], value[:, WIDTH:]


def spread_heads(pair_ref, first_row, half, target, factor):
    heads = target.shape[0]
    zero = jnp.zeros((half, WIDTH), bf16)
    for slot in range(8):
        for part, rows in enumerate(load_pairs(pair_ref, slot, first_row, half)):
            rows = (rows.astype(f32) * factor).astype(bf16)
            for h in range(heads):
                target[h, pl.ds((slot * 2 + part) * half, half), :] = jnp.where(
                    head_lanes(half, h), rows, zero
                )


def fetch(step, pair_refs, starts, pair_sc):
    for ref, (begin, end) in zip(pair_refs, starts):
        @pl.when((step >= begin) & (step < end))
        def take(ref=ref):
            pair_sc[...] = ref[...]


def forward_kernel(
    starts, came_ref, first_ref, second_ref, third_ref, key_docs_ref, query_docs_ref,
    out_ref, turned_ref, total_ref, query_sc, pair_sc, top_sc, sum_sc, acc_sc,
):
    step = pl.program_id(0)
    heads, queries = query_sc.shape[:2]
    half = out_ref.shape[1]

    @pl.when(step == 0)
    def start():
        spread_heads(came_ref, 2 * half, half, query_sc, HEAD_DIM ** (-0.5))
        top_sc[...] = jnp.full(top_sc.shape, -1e30, f32)
        sum_sc[...] = jnp.zeros(sum_sc.shape, f32)
        acc_sc[...] = jnp.zeros(acc_sc.shape, f32)

    fetch(step, (first_ref, second_ref, third_ref), starts, pair_sc)
    key_part = pair_sc[:, :WIDTH]
    value_turned = pair_sc[:, WIDTH:].T
    allowed = key_docs_ref[...] == query_docs_ref[...]
    for h in range(heads):
        rows = pl.ds(h * HEAD_DIM, HEAD_DIM)
        scores = jnp.where(allowed, dot_nt(key_part, query_sc[h]), -1e30)
        old = top_sc[h : h + 1]
        new = jnp.maximum(old, jnp.max(scores, axis=0, keepdims=True))
        exponent = jnp.exp(scores - new)
        fade = jnp.exp(old - new)
        top_sc[h : h + 1] = new
        sum_sc[h : h + 1] = sum_sc[h : h + 1] * fade + jnp.sum(exponent, axis=0, keepdims=True)
        acc_sc[rows] = acc_sc[rows] * fade + dot(
            value_turned[h * HEAD_DIM : (h + 1) * HEAD_DIM], exponent.astype(bf16)
        )

    @pl.when(step == pl.num_programs(0) - 1)
    def finish():
        total_ref[...] = jnp.zeros(total_ref.shape, f32)
        for h in range(heads):
            rows = pl.ds(h * HEAD_DIM, HEAD_DIM)
            turned_ref[rows] = acc_sc[rows] / sum_sc[h : h + 1]
            total_ref[h : h + 1] = top_sc[h : h + 1] + jnp.log(sum_sc[h : h + 1])
        whole = turned_ref[...].T.astype(bf16)
        for slot in range(8):
            for part in range(2):
                begin = (slot * 2 + part) * half
                out_ref[slot, :, pl.ds(part * WIDTH, WIDTH)] = whole[begin : begin + half]


def pair_specs(pairs, chunk):
    specs, starts, begin = [], [], 0
    for pair in pairs:
        count = pair.shape[0] // chunk
        specs.append(
            pl.BlockSpec(
                (chunk, 2 * WIDTH),
                lambda i, begin=begin, count=count: (jnp.clip(i - begin, 0, count - 1), 0),
            )
        )
        starts.append((begin, begin + count))
        begin += count
    return specs, starts, begin


def whole_spec(shape):
    return pl.BlockSpec(shape, lambda i: (0,) * len(shape))


def attend(came, pairs, key_docs, query_docs):
    slots, rows, columns = came.shape
    half = rows // 3
    queries = slots * 2 * half
    heads = WIDTH // HEAD_DIM
    chunk = 512
    specs, starts, steps = pair_specs(pairs, chunk)
    outs = (
        jax.ShapeDtypeStruct((slots, half, columns), bf16),
        jax.ShapeDtypeStruct((WIDTH, queries), f32),
        jax.ShapeDtypeStruct((8, queries), f32),
    )
    return pl.pallas_call(
        partial(forward_kernel, starts),
        grid=(steps,),
        out_shape=outs,
        in_specs=[
            whole_spec(came.shape),
            *specs,
            pl.BlockSpec((chunk, 1), lambda i: (i, 0)),
            whole_spec(query_docs.shape),
        ],
        out_specs=tuple(whole_spec(o.shape) for o in outs),
        scratch_shapes=[
            pltpu.VMEM((heads, queries, WIDTH), bf16),
            pltpu.VMEM((chunk, 2 * WIDTH), bf16),
            pltpu.VMEM((8, queries), f32),
            pltpu.VMEM((8, queries), f32),
            pltpu.VMEM((WIDTH, queries), f32),
        ],
        compiler_params=pltpu.CompilerParams(vmem_limit_bytes=48 << 20),
    )(came, *pairs, key_docs, query_docs)


def backward_kernel(
    starts, came_ref, grad_ref, first_ref, second_ref, third_ref, key_docs_ref, query_docs_ref,
    turned_ref, total_ref, query_out, keep_ref, send_ref,
    query_sc, grad_sc, pair_sc, delta_sc, acc_sc,
):
    step = pl.program_id(0)
    heads, queries = query_sc.shape[:2]
    half = query_out.shape[1]

    @pl.when(step == 0)
    def start():
        spread_heads(came_ref, 2 * half, half, query_sc, HEAD_DIM ** (-0.5))
        spread_heads(grad_ref, 0, half, grad_sc, 1.0)
        acc_sc[...] = jnp.zeros(acc_sc.shape, f32)
        for h in range(heads):
            rows = slice(h * HEAD_DIM, (h + 1) * HEAD_DIM)
            turned = grad_sc[h].astype(f32).T
            delta_sc[h : h + 1] = jnp.sum(turned[rows] * turned_ref[rows], axis=0, keepdims=True)

    fetch(step, (first_ref, second_ref, third_ref), starts, pair_sc)
    key_part = pair_sc[:, :WIDTH]
    value_part = pair_sc[:, WIDTH:]
    key_turned = key_part.T
    allowed = key_docs_ref[...] == query_docs_ref[...]
    grad_key = grad_value = None
    for h in range(heads):
        rows = pl.ds(h * HEAD_DIM, HEAD_DIM)
        query, grad = query_sc[h], grad_sc[h]
        scores = jnp.where(allowed, dot_nt(key_part, query), -1e30)
        probabilities = jnp.exp(scores - total_ref[h : h + 1])
        slope = dot_nt(value_part, grad) - delta_sc[h : h + 1]
        grad_scores = (probabilities * slope).astype(bf16)
        value_term = dot(probabilities.astype(bf16), grad)
        key_term = dot(grad_scores, query)
        grad_value = value_term if grad_value is None else grad_value + value_term
        grad_key = key_term if grad_key is None else grad_key + key_term
        acc_sc[rows] = acc_sc[rows] + dot(
            key_turned[h * HEAD_DIM : (h + 1) * HEAD_DIM], grad_scores
        )
    middle = pl.num_programs(0) // 2

    @pl.when(step < middle)
    def mine():
        keep_ref[:, pl.ds(0, WIDTH)] = grad_key
        keep_ref[:, pl.ds(WIDTH, WIDTH)] = grad_value

    @pl.when(step >= middle)
    def theirs():
        send_ref[:, pl.ds(0, WIDTH)] = grad_key.astype(bf16)
        send_ref[:, pl.ds(WIDTH, WIDTH)] = grad_value.astype(bf16)

    @pl.when(step == pl.num_programs(0) - 1)
    def finish():
        whole = (acc_sc[...] * HEAD_DIM ** (-0.5)).T.astype(bf16)
        for slot in range(8):
            for part in range(2):
                begin = (slot * 2 + part) * half
                query_out[slot, :, pl.ds(part * WIDTH, WIDTH)] = whole[begin : begin + half]


def attend_back(came, grad, pairs, key_docs, query_docs, turned, total):
    slots, rows, columns = came.shape
    half = rows // 3
    queries = slots * 2 * half
    heads = WIDTH // HEAD_DIM
    chunk = 512
    specs, starts, steps = pair_specs(pairs, chunk)
    middle = steps // 2
    return pl.pallas_call(
        partial(backward_kernel, starts),
        grid=(steps,),
        out_shape=(
            jax.ShapeDtypeStruct((slots, half, columns), bf16),
            jax.ShapeDtypeStruct((middle * chunk, columns), f32),
            jax.ShapeDtypeStruct((middle * chunk, columns), bf16),
        ),
        in_specs=[
            whole_spec(came.shape),
            whole_spec(grad.shape),
            *specs,
            pl.BlockSpec((chunk, 1), lambda i: (i, 0)),
            whole_spec(query_docs.shape),
            whole_spec(turned.shape),
            whole_spec(total.shape),
        ],
        out_specs=(
            whole_spec((slots, half, columns)),
            pl.BlockSpec((chunk, columns), lambda i: (jnp.minimum(i, middle - 1), 0)),
            pl.BlockSpec((chunk, columns), lambda i: (jnp.maximum(i - middle, 0), 0)),
        ),
        scratch_shapes=[
            pltpu.VMEM((heads, queries, WIDTH), bf16),
            pltpu.VMEM((heads, queries, WIDTH), bf16),
            pltpu.VMEM((chunk, 2 * WIDTH), bf16),
            pltpu.VMEM((8, queries), f32),
            pltpu.VMEM((WIDTH, queries), f32),
        ],
        compiler_params=pltpu.CompilerParams(vmem_limit_bytes=48 << 20),
    )(came, grad, *pairs, key_docs, query_docs, turned, total)


def middle_kernel(
    came_ref, x_ref, teacher_ref, mask_ref, weight_ref, mod_ref, gain_ref, up_bias_ref,
    down_bias_ref, out_ref, up_hbm, down_hbm,
    final_ref, hidden_ref, leave_ref, pack_ref, sums_ref, up_sc, down_sc, slope_sc, sems,
):
    seqs, tokens, width = x_ref.shape
    units = up_sc.shape[1]
    rows = seqs * tokens
    half = tokens // 2
    up_copy = pltpu.make_async_copy(up_hbm, up_sc, sems.at[0])
    down_copy = pltpu.make_async_copy(down_hbm, down_sc, sems.at[1])
    up_copy.start()
    down_copy.start()

    def wide(index):
        return jnp.concatenate(
            [jnp.broadcast_to(mod_ref[s, index : index + 1], (tokens, width)) for s in range(seqs)]
        )

    def add_rows(first, value):
        for s in range(seqs):
            sums_ref[first + s : first + s + 1] = jnp.sum(
                value[s * tokens : (s + 1) * tokens], axis=0, keepdims=True
            )

    for s in range(seqs):
        for g in range(GROUPS):
            left, right = load_pairs(came_ref, s * GROUPS + g, 0, half)
            columns = pl.ds(g * WIDTH, WIDTH)
            pack_ref[pl.ds(s * tokens, half), columns] = left
            pack_ref[pl.ds(s * tokens + half, half), columns] = right
    mixed = pack_ref[:, pl.ds(0, width)]
    residual = jnp.concatenate([x_ref[s].astype(f32) for s in range(seqs)])
    branch = dot(mixed, out_ref[...])
    hidden = residual + wide(2) * branch
    normed, inverse = normalize(hidden)
    scaled = normed * gain_ref[...]
    moved = (scaled * (1.0 + wide(4)) + wide(3)).astype(bf16)
    pack_ref[:, pl.ds(width, width)] = moved
    up_copy.wait()
    lower = None
    for f in range(units // width):
        columns = pl.ds(f * width, width)
        u = dot(moved, up_sc[:, columns]) + up_bias_ref[:, columns]
        square = u * u
        t = jnp.tanh(0.7978845608028654 * (u + 0.044715 * u * square))
        active = (0.5 * u * (1.0 + t)).astype(bf16)
        slope_sc[:, columns] = 0.5 * (1.0 + t) + 0.5 * u * (1.0 - t * t) * 0.7978845608028654 * (
            1.0 + 0.134145 * square
        )
        pack_ref[:, pl.ds(2 * width + f * width, width)] = active
        if f == 0:
            down_copy.wait()
        term = dot(active, down_sc[columns, :])
        lower = term if lower is None else lower + term
    lower = lower + down_bias_ref[...]
    gate = wide(5)
    final = hidden + gate * lower
    for s in range(seqs):
        final_ref[s] = final[s * tokens : (s + 1) * tokens].astype(bf16)
    teacher = jnp.concatenate([teacher_ref[s].astype(f32) for s in range(seqs)])
    mismatch = final - teacher
    sums_ref[14:15] = jnp.sum(mask_ref[...] * mismatch * mismatch, axis=0, keepdims=True)
    sums_ref[15:16] = jnp.zeros((1, width), f32)
    grad_final = weight_ref[...] * mismatch
    add_rows(6, grad_final * lower)
    grad_lower = (gate * grad_final).astype(bf16)
    base = 2 * width + units
    pack_ref[:, pl.ds(base + width + units, width)] = grad_lower
    sums_ref[9:10] = jnp.sum(grad_lower.astype(f32), axis=0, keepdims=True)
    grad_moved = None
    for f in range(units // width):
        columns = pl.ds(f * width, width)
        grad_active = dot_nt(grad_lower, down_sc[columns, :])
        grad_upper = (grad_active * slope_sc[:, columns]).astype(bf16)
        pack_ref[:, pl.ds(base + width + f * width, width)] = grad_upper
        sums_ref[10 + f : 11 + f] = jnp.sum(grad_upper.astype(f32), axis=0, keepdims=True)
        term = dot_nt(grad_upper, up_sc[:, columns])
        grad_moved = term if grad_moved is None else grad_moved + term
    add_rows(2, grad_moved)
    add_rows(4, grad_moved * scaled)
    grad_scaled = grad_moved * (1.0 + wide(4))
    sums_ref[8:9] = jnp.sum(grad_scaled * normed, axis=0, keepdims=True)
    grad_hidden = grad_final + norm_back(grad_scaled * gain_ref[...], normed, inverse)
    hidden_ref[...] = grad_hidden
    add_rows(0, grad_hidden * branch)
    grad_branch = (wide(2) * grad_hidden).astype(bf16)
    pack_ref[:, pl.ds(base, width)] = grad_branch
    grad_mixed = dot_nt(grad_branch, out_ref[...]).astype(bf16)
    for s in range(seqs):
        for g in range(GROUPS):
            piece = grad_mixed[s * tokens : (s + 1) * tokens, g * WIDTH : (g + 1) * WIDTH]
            leave_ref[s * GROUPS + g, :, pl.ds(0, WIDTH)] = piece[:half]
            leave_ref[s * GROUPS + g, :, pl.ds(WIDTH, WIDTH)] = piece[half:]


def middle(came, inputs, teacher, mask, weight, pieces, gain, up_bias, down_bias, out, up, down):
    seqs, tokens, width = inputs.shape
    units = up.shape[1]
    rows = seqs * tokens
    return pl.pallas_call(
        middle_kernel,
        out_shape=(
            jax.ShapeDtypeStruct((seqs, tokens, width), bf16),
            jax.ShapeDtypeStruct((rows, width), f32),
            jax.ShapeDtypeStruct(came.shape, bf16),
            jax.ShapeDtypeStruct((rows, 4 * width + 2 * units), bf16),
            jax.ShapeDtypeStruct((16, width), f32),
        ),
        in_specs=[VMEM] * 10 + [ANY] * 2,
        out_specs=(VMEM,) * 5,
        scratch_shapes=[
            pltpu.VMEM((width, units), bf16),
            pltpu.VMEM((units, width), bf16),
            pltpu.VMEM((rows, units), f32),
            pltpu.SemaphoreType.DMA((2,)),
        ],
        compiler_params=pltpu.CompilerParams(vmem_limit_bytes=56 << 20),
    )(came, inputs, teacher, mask, weight, pieces, gain, up_bias, down_bias, out, up, down)


def weights_kernel(
    place_ref, own_ref, other_ref, keep_a, send_a, keep_b, send_b, left_sc, right_sc, a_sc, b_sc, sems
):
    rows, width = own_ref.shape[0], a_sc.shape[-1]
    units = 4 * width
    hc = place_ref[1]
    base = 2 * width + units
    for which, ref in enumerate((own_ref, other_ref)):
        left_sc[:, pl.ds(which * rows, rows)] = ref[:, pl.ds(0, base)].T
        right_sc[pl.ds(which * rows, rows), :] = ref[:, pl.ds(base, base)]
    for hx in range(2):
        begin = pl.multiple_of(hx * 384 + hc * 192, 64)
        for j in range(5):
            offset = 0 if j == 0 else width
            value = dot(left_sc[pl.ds(begin + offset, 192), :], right_sc[:, pl.ds(j * width, width)])
            for i in range(8):
                a_sc[hx * 8 + i, j] = value[i * 24 : (i + 1) * 24].astype(bf16)
    copies = piece_copies(place_ref, a_sc, keep_a, send_a, sems, 0)
    for hx in range(2):
        begin = pl.multiple_of(2 * width + hx * 1536 + hc * 768, 256)
        value = dot(left_sc[pl.ds(begin, 768), :], right_sc[:, pl.ds(width + units, width)])
        for i in range(8):
            for j in range(4):
                first = i * 96 + j * 24
                b_sc[hx * 8 + i, j] = value[first : first + 24].astype(bf16)
    copies += piece_copies(place_ref, b_sc, keep_b, send_b, sems, 1)
    for copy in copies:
        copy.wait()


def weight_terms(here, own, other, width):
    rows, total = own.shape
    a = jax.ShapeDtypeStruct((2, 4, 5, 24, width), bf16)
    b = jax.ShapeDtypeStruct((2, 4, 4, 24, width), bf16)
    return pl.pallas_call(
        weights_kernel,
        out_shape=(a, a, b, b),
        in_specs=[SMEM, VMEM, VMEM],
        out_specs=(ANY,) * 4,
        scratch_shapes=[
            pltpu.VMEM((total // 2, 2 * rows), bf16),
            pltpu.VMEM((2 * rows, total // 2), bf16),
            pltpu.VMEM((16, 5, 24, width), bf16),
            pltpu.VMEM((16, 4, 24, width), bf16),
            pltpu.SemaphoreType.DMA((2, 16)),
        ],
        compiler_params=pltpu.CompilerParams(vmem_limit_bytes=56 << 20),
    )(here, own, other)


def flat_rows(came_ref, target, first_row, seqs, tokens, width):
    half = tokens // 2
    for s in range(seqs):
        for g in range(GROUPS):
            slot = s * GROUPS + g
            row = first_row + s * tokens
            left, right = load_pairs(came_ref, slot, tokens, half)
            target[pl.ds(row, half), pl.ds(g * WIDTH, WIDTH)] = left
            target[pl.ds(row + half, half), pl.ds(g * WIDTH, WIDTH)] = right
            left, right = load_pairs(came_ref, slot, 0, tokens)
            target[pl.ds(row, tokens), pl.ds(width + g * WIDTH, WIDTH)] = left
            target[pl.ds(row, tokens), pl.ds(2 * width + g * WIDTH, WIDTH)] = right


def qkv_kernel(
    seqs, place_ref, entered_ref, entered_other, own_ref, other_ref,
    keep_a, send_a, keep_b, send_b, left_sc, right_sc, block_sc, sems,
):
    rows, width = entered_ref.shape
    hc = place_ref[1]
    for which, (left, right) in enumerate(((entered_ref, own_ref), (entered_other, other_ref))):
        left_sc[:, pl.ds(which * rows, rows)] = left[...].T
        flat_rows(right, right_sc, which * rows, seqs, rows // seqs, width)
    for hx in range(2):
        begin = pl.multiple_of(hx * 384 + hc * 192, 64)
        for j in range(3):
            value = dot(left_sc[pl.ds(begin, 192), :], right_sc[:, pl.ds(j * width, width)])
            for i in range(8):
                block_sc[hx * 8 + i, :, pl.ds(j * width, width)] = value[
                    i * 24 : (i + 1) * 24
                ].astype(bf16)
    half = 3 * width // 2
    copies = piece_copies(place_ref, block_sc, keep_a, send_a, sems, 0, pl.ds(0, half))
    copies += piece_copies(place_ref, block_sc, keep_b, send_b, sems, 1, pl.ds(half, half))
    for copy in copies:
        copy.wait()


def qkv_terms(here, seqs, entered, entered_other, own, other):
    rows, width = entered.shape
    side = jax.ShapeDtypeStruct((2, 4, 24, 3 * width // 2), bf16)
    return pl.pallas_call(
        partial(qkv_kernel, seqs),
        out_shape=(side,) * 4,
        in_specs=[SMEM] + [VMEM] * 4,
        out_specs=(ANY,) * 4,
        scratch_shapes=[
            pltpu.VMEM((width, 2 * rows), bf16),
            pltpu.VMEM((2 * rows, 3 * width), bf16),
            pltpu.VMEM((16, 24, 3 * width), bf16),
            pltpu.SemaphoreType.DMA((2, 16)),
        ],
        compiler_params=pltpu.CompilerParams(vmem_limit_bytes=40 << 20),
    )(here, entered, entered_other, own, other)


def leave_kernel(
    came_ref, x_ref, hidden_ref, mod_ref, gain_ref, weight_ref, grad_ref, sums_ref, flat_ref
):
    seqs, tokens, width = x_ref.shape
    flat_rows(came_ref, flat_ref, 0, seqs, tokens, width)
    grad_entered = None
    for which in range(3):
        columns = pl.ds(which * width, width)
        term = dot_nt(flat_ref[:, columns], weight_ref[:, columns])
        grad_entered = term if grad_entered is None else grad_entered + term
    sums_ref[...] = jnp.zeros(sums_ref.shape, f32)
    gain_sum = None
    for s in range(seqs):
        normed, inverse = normalize(x_ref[s].astype(f32))
        rows = slice(s * tokens, (s + 1) * tokens)
        grad = grad_entered[rows]
        sums_ref[s : s + 1] = jnp.sum(grad, axis=0, keepdims=True)
        sums_ref[2 + s : 3 + s] = jnp.sum(grad * (normed * gain_ref[...]), axis=0, keepdims=True)
        grad_scaled = grad * (1.0 + mod_ref[s, 1:2])
        term = jnp.sum(grad_scaled * normed, axis=0, keepdims=True)
        gain_sum = term if gain_sum is None else gain_sum + term
        grad_ref[s] = hidden_ref[rows] + norm_back(grad_scaled * gain_ref[...], normed, inverse)
    sums_ref[4:5] = gain_sum


def leave(came, inputs, grad_hidden, pieces, gain, weight):
    seqs, tokens, width = inputs.shape
    return pl.pallas_call(
        leave_kernel,
        out_shape=(
            jax.ShapeDtypeStruct((seqs, tokens, width), f32),
            jax.ShapeDtypeStruct((8, width), f32),
            jax.ShapeDtypeStruct((seqs * tokens, 3 * width), bf16),
        ),
        in_specs=[VMEM] * 6,
        out_specs=(VMEM,) * 3,
        compiler_params=pltpu.CompilerParams(vmem_limit_bytes=40 << 20),
    )(came, inputs, grad_hidden, pieces, gain, weight)


def exchange(rows):
    return lax.all_to_all(rows, SPOT, 0, 0, tiled=True)


def on_device(
    inputs,
    time_embed,
    segments,
    valid_mask,
    teacher,
    ada_weight,
    ada_bias,
    gain_attn,
    qkv_weight,
    out_weight,
    gain_mlp,
    up_weight,
    up_bias,
    down_weight,
    down_bias,
):
    seqs, tokens, width = inputs.shape
    units = up_weight.shape[1]
    parts = lax.axis_size("rb")
    devices = 32 * parts
    length = tokens * devices
    queries = 8 * tokens
    here = place()
    hx, hc, rb = lax.axis_index("hx"), lax.axis_index("hc"), lax.axis_index("rb")
    own_seq = (lax.axis_index("sz") * 2 + lax.axis_index("sy")) // GROUPS

    own_modulation = jnp.dot(
        time_embed, ada_weight.astype(f32), precision=precise
    ) + ada_bias.astype(f32)
    mask_float = valid_mask.astype(f32)
    fields = [
        own_modulation.reshape(-1),
        gain_attn.astype(f32),
        gain_mlp.astype(f32),
        up_bias.astype(f32),
        down_bias.astype(f32),
        segments.astype(f32).reshape(-1),
        jnp.sum(mask_float).reshape(1),
    ]
    sizes = [field.shape[0] for field in fields]
    packed = jnp.concatenate(fields)
    everyone = lax.all_to_all(
        jnp.broadcast_to(packed, (devices, packed.shape[0])), EVERY, 0, 0, tiled=True
    )
    columns = []
    begin = 0
    for size in sizes:
        columns.append(everyone[:, begin : begin + size])
        begin += size
    modulation = columns[0].reshape(devices, seqs, -1).transpose(1, 0, 2)
    pieces = modulation.reshape(seqs, 6, width)
    gain_one, gain_two, full_up_bias, full_down_bias = (c.reshape(1, -1) for c in columns[1:5])
    docs = columns[5].reshape(2, 2, parts, 8, seqs, tokens)
    count_all = jnp.sum(columns[6])

    full_qkv = gather_rows(here, qkv_weight)
    if parts > 1:
        full_out, full_up, full_down = (
            lax.all_gather(w, EVERY, axis=0, tiled=True)
            for w in (out_weight, up_weight, down_weight)
        )
    else:
        later = jnp.concatenate(
            [out_weight[None]]
            + [up_weight[None, :, j * width : (j + 1) * width] for j in range(4)]
            + [down_weight.reshape(4, 24, width)]
        )
        later = lax.all_gather(later, EVERY, axis=0, tiled=False)
        full_out = later[:, 0].reshape(width, width)
        full_up = later[:, 1:5].transpose(0, 2, 1, 3).reshape(width, units)
        full_down = later[:, 5:].reshape(units, width)

    entered, leaving = enter(inputs, pieces, gain_one, full_qkv)
    came = exchange(leaving)
    pair = came[:, :tokens].reshape(queries, 2 * WIDTH)
    if parts > 1:
        pair = lax.all_gather(pair, "rb", axis=0, tiled=True)
    pair_x = swap(pair, "hx")
    pair_c = jnp.concatenate([swap(pair, "hc"), swap(pair_x, "hc")])
    pairs = (pair, pair_x, pair_c)

    docs_here = lax.dynamic_index_in_dim(docs, own_seq, 4, keepdims=False)
    docs_here = jnp.where(hx == 1, docs_here[::-1], docs_here)
    docs_here = jnp.where(hc == 1, docs_here[:, ::-1], docs_here)
    key_docs = docs_here.transpose(1, 0, 2, 3, 4).reshape(-1, 1)
    query_docs = lax.dynamic_index_in_dim(docs_here[0, 0], rb, 0, keepdims=False).reshape(1, -1)
    attended, turned, total = attend(came, pairs, key_docs, query_docs)

    mask_column = mask_float.reshape(-1, 1)
    final, grad_hidden, grad_leaving, pack, sums = middle(
        exchange(attended),
        inputs,
        teacher,
        mask_column,
        mask_column * (seqs * length / count_all),
        pieces,
        gain_two,
        full_up_bias,
        full_down_bias,
        full_out,
        full_up,
        full_down,
    )
    grad_came = exchange(grad_leaving)
    if parts == 1:
        terms = weight_terms(here, pack, swap(pack, "hc"), width)
        side_a = collect(terms[0], terms[1], ORDERS[0])
        side_b = collect(terms[2], terms[3], ORDERS[1])
        shard_out = side_a[0]
        shard_up = side_a[1:].transpose(1, 0, 2).reshape(24, units)
        shard_down = side_b.reshape(96, width)
    else:
        base = 2 * width + units
        ends = (base + width, base + width + units)
        shard_out, shard_up, shard_down = (
            lax.psum_scatter(
                jnp.einsum("tk,tn->kn", left, right, preferred_element_type=f32),
                EVERY,
                scatter_dimension=0,
                tiled=True,
            )
            for left, right in (
                (pack[:, :width], pack[:, base : ends[0]]),
                (pack[:, width : 2 * width], pack[:, ends[0] : ends[1]]),
                (pack[:, 2 * width : base], pack[:, ends[1] :]),
            )
        )

    grad_query, keep, send = attend_back(
        came, grad_came, pairs, key_docs, query_docs, turned, total
    )
    grad_pair = keep + swap(send, "hc").astype(f32)
    middle_row = grad_pair.shape[0] // 2
    grad_pair = grad_pair[:middle_row] + swap(grad_pair[middle_row:].astype(bf16), "hx").astype(f32)
    if parts > 1:
        grad_pair = lax.psum_scatter(grad_pair, "rb", scatter_dimension=0, tiled=True)
    home = exchange(
        jnp.concatenate(
            [grad_pair.astype(bf16).reshape(8, tokens, 2 * WIDTH), grad_query], axis=1
        )
    )
    grad_input, sums_one, flat = leave(home, inputs, grad_hidden, pieces, gain_one, full_qkv)
    if parts == 1:
        terms = qkv_terms(here, seqs, entered, swap(entered, "hc"), home, swap(home, "hc"))
        shard_qkv = jnp.concatenate(
            [collect(terms[0], terms[1], ORDERS[0]), collect(terms[2], terms[3], ORDERS[1])],
            axis=1,
        )
    else:
        shard_qkv = lax.psum_scatter(
            jnp.einsum("tk,tn->kn", entered, flat, preferred_element_type=f32),
            EVERY,
            scatter_dimension=0,
            tiled=True,
        )
    grad_modulation = jnp.stack(
        [
            jnp.stack([sums_one[s], sums_one[2 + s], sums[s], sums[2 + s], sums[4 + s], sums[6 + s]])
            for s in range(seqs)
        ]
    ).reshape(seqs, devices, -1)
    fields = [
        grad_modulation.transpose(1, 0, 2).reshape(devices, -1),
        sums_one[4].reshape(devices, -1),
        sums[8].reshape(devices, -1),
        sums[10:14].reshape(devices, -1),
        sums[9].reshape(devices, -1),
        jnp.broadcast_to(jnp.sum(sums[14]), (devices, 1)),
    ]
    sizes = [value.shape[1] for value in fields]
    added = jnp.sum(
        lax.all_to_all(jnp.concatenate(fields, axis=1), EVERY, 0, 0, tiled=True), axis=0
    )
    owned = []
    begin = 0
    for size in sizes:
        owned.append(added[begin : begin + size])
        begin += size
    own_grad = owned[0].reshape(seqs, -1)
    grad_ada_weight = jnp.sum(time_embed[:, :, None] * own_grad[:, None, :], axis=0)
    loss_value = owned[5][0] / (count_all * width)
    return (
        final,
        loss_value,
        grad_input,
        grad_ada_weight,
        jnp.sum(own_grad, axis=0),
        owned[1],
        shard_qkv,
        shard_out,
        owned[2],
        shard_up,
        owned[3],
        shard_down,
        owned[4],
    )


def solution(mesh):
    blocks = mesh.shape["blk"]
    fine = Mesh(mesh.devices.reshape(2, 2, blocks // 8, 4, 2), EVERY)
    tokens = ("rb", "sz", "sy", "hx", "hc")
    return jax.shard_map(
        on_device,
        mesh=fine,
        in_specs=(
            P(None, tokens, None),
            P(),
            P(None, tokens),
            P(None, tokens),
            P(None, tokens, None),
            P(None, EVERY),
            P(EVERY),
            P(EVERY),
            P(EVERY, None),
            P(EVERY, None),
            P(EVERY),
            P(EVERY, None),
            P(EVERY),
            P(EVERY, None),
            P(EVERY),
        ),
        out_specs=(
            P(None, tokens, None),
            P(),
            P(None, tokens, None),
            P(None, EVERY),
            P(EVERY),
            P(EVERY),
            P(EVERY, None),
            P(EVERY, None),
            P(EVERY),
            P(EVERY, None),
            P(EVERY),
            P(EVERY, None),
            P(EVERY),
        ),
        check_vma=False,
    )
```

time: 502 us -> 382 us (0.76); the launches traced: 492 us -> 380 us
  starting transfers between devices: 130 us -> 65.7 us
  matrix products: 61.8 us -> 0.12 us
  other arithmetic: 79.4 us -> 22.4 us
  Pallas kernels: 21.8 us -> 52.6 us
  waiting for transfers between devices: 118 us -> 148 us
  local copies, waits for them, and re-layouts: 76.2 us -> 59 us
  blocking collectives: 0 us -> 14.1 us
  between operations: 5.97 us -> 18 us
    dot_general x18 -> x0, matrix products: 61 us -> none  [the longest x1 8.78 us: on_device(): jnp.einsum('hqk,hqe->hke', probabilities.astype(bf16), grad_three, prefer...]
    ppermute x48 -> x15, starting transfers between devices: 64.1 us -> 22.6 us  [turn(): lax.ppermute(value, axis, [(i, (i - step) % size) for i in range(size)])]
    pallas_call x4 -> x7, Pallas kernels: 10.9 us -> 49.5 us  [the longest x1 13.3 us: attend_back(): pl.pallas_call(partial(backward_kernel, starts), grid=(steps,), out_shape...]
    another operation x32 -> x6, other arithmetic: 36.4 us -> 4.02 us  [gather_rows(): level = jnp.stack([level, swap(level, axis)])]
    all_to_all x5 -> x4, waiting for transfers between devices: 2.26 us -> 33.4 us  [the longest x3 28.7 us: exchange(): return lax.all_to_all(rows, SPOT, 0, 0, tiled=True)]
    ppermute x52 -> x22, starting transfers between devices: 37.1 us -> 19.8 us  [swap(): return lax.ppermute(value, axis, [(0, 1), (1, 0)])]
    another operation x23 -> x8, local copies, waits for them, and re-layouts: 20.3 us -> 4.58 us  [the longest x2 1.45 us: on_device(): jnp.stack([sums_one[s], sums_one[2 + s], sums[s], sums[2 + s], sums[4 + s...]
    ppermute x48 -> x15, waiting for transfers between devices: 38.3 us -> 24.2 us  [turn(): lax.ppermute(value, axis, [(i, (i - step) % size) for i in range(size)])]
  transfers between devices with their start and end apart: 106 -> 43, of which waited for: 29 -> 21; matrix products, arithmetic and copies ran while one was open for 34% -> 18% of each run, Pallas kernels for 4% -> 7%
where the time goes in v3:
time: 382 us; the launch traced here: 380 us
  waiting for transfers between devices  148 us (39%)
  starting transfers between devices  65.7 us (17%)
  local copies, waits for them, and re-layouts  59 us (15%)
  Pallas kernels  52.6 us (14%)
  other arithmetic  22.4 us (6%)
  between operations  18 us (5%)
  blocking collectives  14.1 us (4%)
    ppermute x22, waiting for transfers between devices, swap(): return lax.ppermute(value, axis, [(0, 1), (1, 0)])  82.8 us
    all_to_all x3, waiting for transfers between devices, exchange(): return lax.all_to_all(rows, SPOT, 0, 0, tiled=True)  28.7 us
    ppermute x15, waiting for transfers between devices, turn(): lax.ppermute(value, axis, [(i, (i - step) % size) for i in range(size)])  24.2 us
    ppermute x15, starting transfers between devices, turn(): lax.ppermute(value, axis, [(i, (i - step) % size) for i in range(size)])  22.6 us
    ppermute x22, starting transfers between devices, swap(): return lax.ppermute(value, axis, [(0, 1), (1, 0)])  19.8 us
    unnamed x79, local copies, waits for them, and re-layouts  16.2 us
    all_to_all x1, blocking collectives, exchange(): return lax.all_to_all(rows, SPOT, 0, 0, tiled=True)  14.1 us
    pallas_call x1, Pallas kernels, attend_back(): pl.pallas_call(partial(backward_kernel, starts), grid=(steps,), out_shape...  13.3 us
  transfers between devices with their start and end apart: 43, of which 21 were waited for; matrix products, arithmetic and copies ran while one was open for 18% of the time, Pallas kernels for 7%

profile of v3, /device:TPU:0, one launch (start us, length us, event | category | flops | bytes accessed | tf_op | source)
XLA Modules:
  0.0 379.7 jit_solution(2046924280433890004)
XLA Ops:
  12.8 3.1 collective-permute-start.2
  22.1 3.9 %collective-permute-done.1 = bf16[24,2304]{1,0:T(8,128)(2,1)S(1)} collective-permute-done((bf16[24,2304]{1,0:T(8,128)(2,1)}, bf16[24,2304]{1,0:T(8,128)(2,1)S(1)}, u32[]{:S(2)}, u32[]{:S(2)}) %collective-permute-start.1) | collective-permute-done | bytes 110624 | tf_op jit(solution)/shard_map/ppermute | solution.py:49
  30.2 4.2 %collective-permute-done.3 = bf16[4,24,1152]{2,1,0:T(8,128)(2,1)S(1)} collective-permute-done((bf16[4,24,1152]{2,1,0:T(8,128)(2,1)S(1)}, bf16[4,24,1152]{2,1,0:T(8,128)(2,1)S(1)}, u32[]{:S(2)}, u32[]{:S(2)}) %collective-permute-start.3) | collective-permute-done | bytes 221216 | tf_op jit(solution)/shard_map/ppermute | solution.py:44
  37.7 10.7 %collective-permute-done.4 = bf16[2,4,24,1152]{3,2,1,0:T(8,128)(2,1)S(1)} collective-permute-done((bf16[2,4,24,1152]{3,2,1,0:T(8,128)(2,1)S(1)}, bf16[2,4,24,1152]{3,2,1,0:T(8,128)(2,1)S(1)}, u32[]{:S(2)}, u32[]{:S(2)}) %collective-permute-start.4) | collective-permute-done | bytes 442400 | tf_op jit(solution)/shard_map/ppermute | solution.py:44
  54.8 6.8 %all-to-all-start = ((f32[32,1,585]{2,1,0:T(1,128)}), f32[32,1,585]{2,1,0:T(1,128)S(1)}, u32[]{:S(2)}, u32[]{:S(2)}) async-start(f32[32,1,585]{2,1,0:T(1,128)} %broadcast_in_dim.23), calls=%async_computation | async-start | bytes 163840 | tf_op jit(solution)/shard_map/all_to_all | solution.py:724
  61.7 7.3 %all-to-all-done = f32[32,1,585]{2,1,0:T(1,128)S(1)} async-done(((f32[32,1,585]{2,1,0:T(1,128)}), f32[32,1,585]{2,1,0:T(1,128)S(1)}, u32[]{:S(2)}, u32[]{:S(2)}) %all-to-all-start) | async-done | bytes 74912 | tf_op jit(solution)/shard_map/all_to_all | solution.py:724
  72.6 3.1 shard_map.246
  78.1 4.2 %all-to-all-start.1 = ((bf16[8,96,384]{2,1,0:T(8,128)(2,1)}), bf16[8,96,384]{2,1,0:T(8,128)(2,1)}, u32[]{:S(2)}, u32[]{:S(2)}) async-start(bf16[8,96,384]{2,1,0:T(8,128)(2,1)} %copy-done.10), calls=%async_computation.1 | async-start | bytes 1179648 | tf_op jit(solution)/shard_map/all_to_all | solution.py:679
  87.4 26.5 %all-to-all-done.1.came_ref = bf16[8,96,384]{2,1,0:T(8,128)(2,1)} async-done(((bf16[8,96,384]{2,1,0:T(8,128)(2,1)}), bf16[8,96,384]{2,1,0:T(8,128)(2,1)}, u32[]{:S(2)}, u32[]{:S(2)}) %all-to-all-start.1) | async-done | bytes 589856 | tf_op jit(solution)/shard_map/all_to_all | solution.py:679
  119.3 7.0 %collective-permute-done.9.second_ref = bf16[512,384]{1,0:T(8,128)(2,1)} collective-permute-done((bf16[512,384]{1,0:T(8,128)(2,1)}, bf16[512,384]{1,0:T(8,128)(2,1)}, u32[]{:S(2)}, u32[]{:S(2)}) %collective-permute-start.9) | collective-permute-done | bytes 393248 | tf_op jit(solution)/shard_map/ppermute | solution.py:44
  141.2 9.8 %shard_map.248 = (bf16[8,32,384]{2,1,0:T(8,128)(2,1)S(1)}, f32[192,512]{1,0:T(8,128)S(1)}, f32[8,512]{1,0:T(8,128)S(1)}) custom-call(bf16[8,96,384]{2,1,0:T(8,128)(2,1)} %all-to-all-done.1.came_ref, bf16[512,384]{1,0:T(8,128)(2,1)} %bitcast.23.first_ref, bf16[512,384]{1,0:T(8,128)(2,1)} %collective-permute-done.9.second_ref, ...), custom_call_target="tpu_custom_call" | custom-call | tf_op jit(solution)/shard_map/pallas_call | solution.py:288
  153.1 4.2 %all-to-all-start.2 = ((bf16[8,32,384]{2,1,0:T(8,128)(2,1)}), bf16[8,32,384]{2,1,0:T(8,128)(2,1)}, u32[]{:S(2)}, u32[]{:S(2)}) async-start(bf16[8,32,384]{2,1,0:T(8,128)(2,1)} %copy-done.14), calls=%async_computation.2 | async-start | bytes 393216 | tf_op jit(solution)/shard_map/all_to_all | solution.py:679
  159.7 6.5 %fusion.33 = (bf16[32,4,24,768]{3,2,1,0:T(8,128)(2,1)}, bf16[32,24,4,768]{3,1,2,0:T(8,128)(2,1)S(1)}) fusion(bf16[32,9,24,768]{3,2,1,0:T(8,128)(2,1)} %bitcast.172), kind=kLoop, calls=%fused_computation.99 | loop fusion | bytes 18874368 | tf_op jit(solution)/shard_map/slice | solution.py:753
  168.5 3.2 copy.79
  171.8 11.9 %shard_map.249 = (bf16[2,64,768]{2,1,0:T(8,128)(2,1)}, f32[128,768]{1,0:T(8,128)}, bf16[8,32,384]{2,1,0:T(8,128)(2,1)}, bf16[128,9216]{1,0:T(8,128)(2,1)}, f32[16,768]{1,0:T(8,128)}) custom-call(bf16[8,32,384]{2,1,0:T(8,128)(2,1)} %all-to-all-done.2.came_ref, bf16[2,64,768]{2,1,0:T(8,128)(2,1)} %x_ref.5, bf16[2,64,768]{2,1,0:T(8,128)(2,1)} %teacher_ref.1, ...), custom_call_target="tpu_custom_call" | custom-call | tf_op jit(solution)/shard_map/pallas_call | solution.py:511
  183.7 14.1 %all_to_all.38.grad_ref = bf16[8,32,384]{2,1,0:T(8,128)(2,1)S(1)} all-to-all(bf16[8,32,384]{2,1,0:T(8,128)(2,1)} %get-tuple-element.39), channel_id=1, replica_groups=mesh['hx'=2,'hc'=2,'rb'=1,'sz'=4,'sy'=2] {'sz','sy'}, dimensions={0} | all-to-all | bytes 393216 | tf_op jit(solution)/shard_map/all_to_all | solution.py:679
  197.7 13.3 %shard_map.250 = (bf16[8,32,384]{2,1,0:T(8,128)(2,1)S(1)}, f32[1024,384]{1,0:T(8,128)}, bf16[1024,384]{1,0:T(8,128)(2,1)S(1)}) custom-call(bf16[8,96,384]{2,1,0:T(8,128)(2,1)} %all-to-all-done.1.came_ref, bf16[8,32,384]{2,1,0:T(8,128)(2,1)S(1)} %all_to_all.38.grad_ref, bf16[512,384]{1,0:T(8,128)(2,1)} %bitcast.23.first_ref, ...), custom_call_target="tpu_custom_call" | custom-call | tf_op jit(solution)/shard_map/pallas_call | solution.py:378
  211.6 2.9 collective-permute-done.12
  217.7 9.5 %collective-permute-done.13 = bf16[512,384]{1,0:T(8,128)(2,1)S(1)} collective-permute-done((bf16[512,384]{1,0:T(8,128)(2,1)S(1)}, bf16[512,384]{1,0:T(8,128)(2,1)S(1)}, u32[]{:S(2)}, u32[]{:S(2)}) %collective-permute-start.13) | collective-permute-done | bytes 393248 | tf_op jit(solution)/shard_map/ppermute | solution.py:44
  228.2 4.2 %all-to-all-start.4 = ((bf16[8,96,384]{2,1,0:T(8,128)(2,1)}), bf16[8,96,384]{2,1,0:T(8,128)(2,1)}, u32[]{:S(2)}, u32[]{:S(2)}) async-start(bf16[8,96,384]{2,1,0:T(8,128)(2,1)} %pad_maximum_fusion.4), calls=%async_computation.4 | async-start | bytes 1179648 | tf_op jit(solution)/shard_map/all_to_all | solution.py:679
  232.4 7.0 %shard_map.253 = (bf16[2,4,5,24,768]{4,3,2,1,0:T(8,128)(2,1)}, bf16[2,4,5,24,768]{4,3,2,1,0:T(8,128)(2,1)}, bf16[2,4,4,24,768]{4,3,2,1,0:T(8,128)(2,1)}, bf16[2,4,4,24,768]{4,3,2,1,0:T(8,128)(2,1)}) custom-call(s32[4]{0:T(128)} %copy-done.19, bf16[128,9216]{1,0:T(8,128)(2,1)} %get-tuple-element.54.own_ref, bf16[128,9216]{1,0:T(8,128)(2,1)} %collective-permute-done.26.other_ref), custom_call_target="tpu_custom_call" | custom-call | tf_op jit(solution)/shard_map/pallas_call | solution.py:566
  250.8 3.3 shard_map.251
  258.3 3.9 %all-to-all-start.5 = ((f32[32,1,457]{2,1,0:T(1,128)}), f32[32,1,457]{2,1,0:T(1,128)S(1)}, u32[]{:S(2)}, u32[]{:S(2)}) async-start(f32[32,1,457]{2,1,0:T(1,128)} %copy.75), calls=%async_computation.5 | async-start | bytes 131072 | tf_op jit(solution)/shard_map/all_to_all | solution.py:854
  264.9 4.7 %all-to-all-done.5 = f32[32,1,457]{2,1,0:T(1,128)S(1)} async-done(((f32[32,1,457]{2,1,0:T(1,128)}), f32[32,1,457]{2,1,0:T(1,128)S(1)}, u32[]{:S(2)}, u32[]{:S(2)}) %all-to-all-start.5) | async-done | bytes 58528 | tf_op jit(solution)/shard_map/all_to_all | solution.py:854
  275.1 3.4 shard_map.252
  283.2 7.4 %collective-permute-done.21 = bf16[2,4,24,1152]{3,2,1,0:T(8,128)(2,1)S(1)} collective-permute-done((bf16[2,4,24,1152]{3,2,1,0:T(8,128)(2,1)S(1)}, bf16[2,4,24,1152]{3,2,1,0:T(8,128)(2,1)S(1)}, u32[]{:S(2)}, u32[]{:S(2)}) %collective-permute-start.21) | collective-permute-done | bytes 442400 | tf_op jit(solution)/shard_map/ppermute | solution.py:44
  291.6 16.8 %collective-permute-done.16 = bf16[2,4,24,1152]{3,2,1,0:T(8,128)(2,1)S(1)} collective-permute-done((bf16[2,4,24,1152]{3,2,1,0:T(8,128)(2,1)S(1)}, bf16[2,4,24,1152]{3,2,1,0:T(8,128)(2,1)S(1)}, u32[]{:S(2)}, u32[]{:S(2)}) %collective-permute-start.16) | collective-permute-done | bytes 442400 | tf_op jit(solution)/shard_map/ppermute | solution.py:44
  310.2 15.1 %collective-permute-done.22 = bf16[4,24,1152]{2,1,0:T(8,128)(2,1)S(1)} collective-permute-done((bf16[4,24,1152]{2,1,0:T(8,128)(2,1)S(1)}, bf16[4,24,1152]{2,1,0:T(8,128)(2,1)S(1)}, u32[]{:S(2)}, u32[]{:S(2)}) %collective-permute-start.22) | collective-permute-done | bytes 221216 | tf_op jit(solution)/shard_map/ppermute | solution.py:44
  325.3 3.3 collective-permute-start.25
  344.4 7.4 %collective-permute-done.28 = bf16[4,5,24,768]{3,2,1,0:T(8,128)(2,1)S(1)} collective-permute-done((bf16[4,5,24,768]{3,2,1,0:T(8,128)(2,1)S(1)}, bf16[4,5,24,768]{3,2,1,0:T(8,128)(2,1)S(1)}, u32[]{:S(2)}, u32[]{:S(2)}) %collective-permute-start.28) | collective-permute-done | bytes 737312 | tf_op jit(solution)/shard_map/ppermute | solution.py:44
  352.0 3.6 collective-permute-start.31
  360.5 9.7 %collective-permute-done.30 = bf16[5,24,768]{2,1,0:T(8,128)(2,1)S(1)} collective-permute-done((bf16[5,24,768]{2,1,0:T(8,128)(2,1)S(1)}, bf16[5,24,768]{2,1,0:T(8,128)(2,1)S(1)}, u32[]{:S(2)}, u32[]{:S(2)}) %collective-permute-start.30) | collective-permute-done | bytes 184352 | tf_op jit(solution)/shard_map/ppermute | solution.py:49
  (240 shorter events, 119.8 us)
Async XLA Ops:
  7.2 150.1 %all-gather.3.cloned.1.call-start = ((), (), s32[]{:S(2)}) async-start(), calls=%async_computation.6 | async-start | bytes 10948608 | tf_op jit(solution)/shard_map/all_gather | solution.py:750
  12.8 9.3 %collective-permute-start.2 = (bf16[24,2304]{1,0:T(8,128)(2,1)}, bf16[24,2304]{1,0:T(8,128)(2,1)S(1)}, u32[]{:S(2)}, u32[]{:S(2)}) collective-permute-start(bf16[24,2304]{1,0:T(8,128)(2,1)} %param.23), channel_id=1, source_target_pairs={{0,2},{2,4},{4,6},{6,0},{1,3},{3,5},{5,7},{7,1},{8,10},{10,12},{12... | collective-permute-start | bytes 331784 | tf_op jit(solution)/shard_map/ppermute | solution.py:49
  15.9 10.1 %collective-permute-start.1 = (bf16[24,2304]{1,0:T(8,128)(2,1)}, bf16[24,2304]{1,0:T(8,128)(2,1)S(1)}, u32[]{:S(2)}, u32[]{:S(2)}) collective-permute-start(bf16[24,2304]{1,0:T(8,128)(2,1)} %param.23), channel_id=1, source_target_pairs={{0,4},{2,6},{4,0},{6,2},{1,5},{3,7},{5,1},{7,3},{8,12},{10,14},{12... | collective-permute-start | bytes 331784 | tf_op jit(solution)/shard_map/ppermute | solution.py:49
  34.4 13.9 %collective-permute-start.4 = (bf16[2,4,24,1152]{3,2,1,0:T(8,128)(2,1)S(1)}, bf16[2,4,24,1152]{3,2,1,0:T(8,128)(2,1)S(1)}, u32[]{:S(2)}, u32[]{:S(2)}) collective-permute-start(bf16[2,4,24,1152]{3,2,1,0:T(8,128)(2,1)S(1)} %get-tuple-element.89), channel_id=1, source_target_pairs={{0,1},{1,0},{2,3},{3,2},{4,5},{5,4},{6,7},{7,6},{8,9},{9,8},{10,11... | collective-permute-start | bytes 1327112 | tf_op jit(solution)/shard_map/ppermute | solution.py:44
  36.1 15.2 %collective-permute-start.7 = (bf16[2,4,24,1152]{3,2,1,0:T(8,128)(2,1)S(1)}, bf16[2,4,24,1152]{3,2,1,0:T(8,128)(2,1)S(1)}, u32[]{:S(2)}, u32[]{:S(2)}) collective-permute-start(bf16[2,4,24,1152]{3,2,1,0:T(8,128)(2,1)S(1)} %get-tuple-element.83), channel_id=1, source_target_pairs={{0,16},{16,0},{1,17},{17,1},{2,18},{18,2},{3,19},{19,3},{4,20},{20... | collective-permute-start | bytes 1327112 | tf_op jit(solution)/shard_map/ppermute | solution.py:44
  49.5 21.2 %collective-permute-start.5 = (bf16[2,2,4,24,1152]{4,3,2,1,0:T(8,128)(2,1)}, bf16[2,2,4,24,1152]{4,3,2,1,0:T(8,128)(2,1)S(1)}, u32[]{:S(2)}, u32[]{:S(2)}) collective-permute-start(bf16[2,2,4,24,1152]{4,3,2,1,0:T(8,128)(2,1)} %get-tuple-element.75), channel_id=1, source_target_pairs={{0,8},{8,0},{1,9},{9,1},{2,10},{10,2},{3,11},{11,3},{4,12},{12,4},... | collective-permute-start | bytes 2654216 | tf_op jit(solution)/shard_map/ppermute | solution.py:44
  52.4 18.5 %collective-permute-start.8 = (bf16[2,2,4,24,1152]{4,3,2,1,0:T(8,128)(2,1)}, bf16[2,2,4,24,1152]{4,3,2,1,0:T(8,128)(2,1)}, u32[]{:S(2)}, u32[]{:S(2)}) collective-permute-start(bf16[2,2,4,24,1152]{4,3,2,1,0:T(8,128)(2,1)} %get-tuple-element.73), channel_id=1, source_target_pairs={{0,8},{8,0},{1,9},{9,1},{2,10},{10,2},{3,11},{11,3},{4,12},{12,4},... | collective-permute-start | bytes 2654216 | tf_op jit(solution)/shard_map/ppermute | solution.py:44
  54.8 14.3 %all-to-all-start = ((f32[32,1,585]{2,1,0:T(1,128)}), f32[32,1,585]{2,1,0:T(1,128)S(1)}, u32[]{:S(2)}, u32[]{:S(2)}) async-start(f32[32,1,585]{2,1,0:T(1,128)} %broadcast_in_dim.23), calls=%async_computation | async-start | bytes 163840 | tf_op jit(solution)/shard_map/all_to_all | solution.py:724
  78.1 35.7 %all-to-all-start.1 = ((bf16[8,96,384]{2,1,0:T(8,128)(2,1)}), bf16[8,96,384]{2,1,0:T(8,128)(2,1)}, u32[]{:S(2)}, u32[]{:S(2)}) async-start(bf16[8,96,384]{2,1,0:T(8,128)(2,1)} %copy-done.10), calls=%async_computation.1 | async-start | bytes 1179648 | tf_op jit(solution)/shard_map/all_to_all | solution.py:679
  115.6 10.7 %collective-permute-start.9 = (bf16[512,384]{1,0:T(8,128)(2,1)}, bf16[512,384]{1,0:T(8,128)(2,1)}, u32[]{:S(2)}, u32[]{:S(2)}) collective-permute-start(bf16[512,384]{1,0:T(8,128)(2,1)} %bitcast.23.first_ref), channel_id=1, source_target_pairs={{0,16},{16,0},{1,17},{17,1},{2,18},{18,2},{3,19},{19,3},{4,20},{20... | collective-permute-start | bytes 1179656 | tf_op jit(solution)/shard_map/ppermute | solution.py:44
  118.0 21.1 %collective-permute-start.10 = (bf16[512,384]{1,0:T(8,128)(2,1)}, bf16[512,384]{1,0:T(8,128)(2,1)}, u32[]{:S(2)}, u32[]{:S(2)}) collective-permute-start(bf16[512,384]{1,0:T(8,128)(2,1)} %bitcast.23.first_ref), channel_id=1, source_target_pairs={{0,8},{8,0},{1,9},{9,1},{2,10},{10,2},{3,11},{11,3},{4,12},{12,4},... | collective-permute-start | bytes 1179656 | tf_op jit(solution)/shard_map/ppermute | solution.py:44
  126.3 13.8 %collective-permute-start.11 = (bf16[512,384]{1,0:T(8,128)(2,1)}, bf16[512,384]{1,0:T(8,128)(2,1)}, u32[]{:S(2)}, u32[]{:S(2)}) collective-permute-start(bf16[512,384]{1,0:T(8,128)(2,1)} %collective-permute-done.9.second_ref), channel_id=1, source_target_pairs={{0,8},{8,0},{1,9},{9,1},{2,10},{10,2},{3,11},{11,3},{4,12},{12,4},... | collective-permute-start | bytes 1179656 | tf_op jit(solution)/shard_map/ppermute | solution.py:44
  153.1 18.7 %all-to-all-start.2 = ((bf16[8,32,384]{2,1,0:T(8,128)(2,1)}), bf16[8,32,384]{2,1,0:T(8,128)(2,1)}, u32[]{:S(2)}, u32[]{:S(2)}) async-start(bf16[8,32,384]{2,1,0:T(8,128)(2,1)} %copy-done.14), calls=%async_computation.2 | async-start | bytes 393216 | tf_op jit(solution)/shard_map/all_to_all | solution.py:679
  211.1 21.4 %collective-permute-start.26 = (bf16[128,9216]{1,0:T(8,128)(2,1)}, bf16[128,9216]{1,0:T(8,128)(2,1)}, u32[]{:S(2)}, u32[]{:S(2)}) collective-permute-start(bf16[128,9216]{1,0:T(8,128)(2,1)} %get-tuple-element.54.own_ref), channel_id=1, source_target_pairs={{0,8},{8,0},{1,9},{9,1},{2,10},{10,2},{3,11},{11,3},{4,12},{12,4},... | collective-permute-start | bytes 7077896 | tf_op jit(solution)/shard_map/ppermute | solution.py:44
  216.0 11.2 %collective-permute-start.13 = (bf16[512,384]{1,0:T(8,128)(2,1)S(1)}, bf16[512,384]{1,0:T(8,128)(2,1)S(1)}, u32[]{:S(2)}, u32[]{:S(2)}) collective-permute-start(bf16[512,384]{1,0:T(8,128)(2,1)S(1)} %slice.417), channel_id=1, source_target_pairs={{0,16},{16,0},{1,17},{17,1},{2,18},{18,2},{3,19},{19,3},{4,20},{20... | collective-permute-start | bytes 1179656 | tf_op jit(solution)/shard_map/ppermute | solution.py:44
  228.2 19.9 %all-to-all-start.4 = ((bf16[8,96,384]{2,1,0:T(8,128)(2,1)}), bf16[8,96,384]{2,1,0:T(8,128)(2,1)}, u32[]{:S(2)}, u32[]{:S(2)}) async-start(bf16[8,96,384]{2,1,0:T(8,128)(2,1)} %pad_maximum_fusion.4), calls=%async_computation.4 | async-start | bytes 1179648 | tf_op jit(solution)/shard_map/all_to_all | solution.py:679
  239.4 40.5 %collective-permute-start.32 = (bf16[2,4,4,24,768]{4,3,2,1,0:T(8,128)(2,1)}, bf16[2,4,4,24,768]{4,3,2,1,0:T(8,128)(2,1)}, u32[]{:S(2)}, u32[]{:S(2)}) collective-permute-start(bf16[2,4,4,24,768]{4,3,2,1,0:T(8,128)(2,1)} %get-tuple-element.58), channel_id=1, source_target_pairs={{0,16},{16,0},{1,17},{17,1},{2,18},{18,2},{3,19},{19,3},{4,20},{20... | collective-permute-start | bytes 3538952 | tf_op jit(solution)/shard_map/ppermute | solution.py:44
  248.1 26.1 %collective-permute-start.15 = (bf16[8,96,384]{2,1,0:T(8,128)(2,1)}, bf16[8,96,384]{2,1,0:T(8,128)(2,1)}, u32[]{:S(2)}, u32[]{:S(2)}) collective-permute-start(bf16[8,96,384]{2,1,0:T(8,128)(2,1)} %all-to-all-done.4.came_ref.own_ref), channel_id=1, source_target_pairs={{0,8},{8,0},{1,9},{9,1},{2,10},{10,2},{3,11},{11,3},{4,12},{12,4},... | collective-permute-start | bytes 1769480 | tf_op jit(solution)/shard_map/ppermute | solution.py:44
  258.3 11.3 %all-to-all-start.5 = ((f32[32,1,457]{2,1,0:T(1,128)}), f32[32,1,457]{2,1,0:T(1,128)S(1)}, u32[]{:S(2)}, u32[]{:S(2)}) async-start(f32[32,1,457]{2,1,0:T(1,128)} %copy.75), calls=%async_computation.5 | async-start | bytes 131072 | tf_op jit(solution)/shard_map/all_to_all | solution.py:854
  262.9 11.3 %collective-permute-start.14 = (bf16[128,768]{1,0:T(8,128)(2,1)}, bf16[128,768]{1,0:T(8,128)(2,1)S(1)}, u32[]{:S(2)}, u32[]{:S(2)}) collective-permute-start(bf16[128,768]{1,0:T(8,128)(2,1)} %copy-done.15), channel_id=1, source_target_pairs={{0,8},{8,0},{1,9},{9,1},{2,10},{10,2},{3,11},{11,3},{4,12},{12,4},... | collective-permute-start | bytes 589832 | tf_op jit(solution)/shard_map/ppermute | solution.py:44
  263.2 66.7 %collective-permute-start.27 = (bf16[2,4,5,24,768]{4,3,2,1,0:T(8,128)(2,1)}, bf16[2,4,5,24,768]{4,3,2,1,0:T(8,128)(2,1)S(1)}, u32[]{:S(2)}, u32[]{:S(2)}) collective-permute-start(bf16[2,4,5,24,768]{4,3,2,1,0:T(8,128)(2,1)} %get-tuple-element.56), channel_id=1, source_target_pairs={{0,1},{1,0},{2,3},{3,2},{4,5},{5,4},{6,7},{7,6},{8,9},{9,8},{10,11... | collective-permute-start | bytes 4423688 | tf_op jit(solution)/shard_map/ppermute | solution.py:44
  278.5 12.2 %collective-permute-start.21 = (bf16[2,4,24,1152]{3,2,1,0:T(8,128)(2,1)S(1)}, bf16[2,4,24,1152]{3,2,1,0:T(8,128)(2,1)S(1)}, u32[]{:S(2)}, u32[]{:S(2)}) collective-permute-start(bf16[2,4,24,1152]{3,2,1,0:T(8,128)(2,1)S(1)} %get-tuple-element.53), channel_id=1, source_target_pairs={{0,16},{16,0},{1,17},{17,1},{2,18},{18,2},{3,19},{19,3},{4,20},{20... | collective-permute-start | bytes 1327112 | tf_op jit(solution)/shard_map/ppermute | solution.py:44
  279.2 29.3 %collective-permute-start.16 = (bf16[2,4,24,1152]{3,2,1,0:T(8,128)(2,1)S(1)}, bf16[2,4,24,1152]{3,2,1,0:T(8,128)(2,1)S(1)}, u32[]{:S(2)}, u32[]{:S(2)}) collective-permute-start(bf16[2,4,24,1152]{3,2,1,0:T(8,128)(2,1)S(1)} %get-tuple-element.51), channel_id=1, source_target_pairs={{0,1},{1,0},{2,3},{3,2},{4,5},{5,4},{6,7},{7,6},{8,9},{9,8},{10,11... | collective-permute-start | bytes 1327112 | tf_op jit(solution)/shard_map/ppermute | solution.py:44
  281.9 60.2 %collective-permute-start.33 = (bf16[4,4,24,768]{3,2,1,0:T(8,128)(2,1)S(1)}, bf16[4,4,24,768]{3,2,1,0:T(8,128)(2,1)S(1)}, u32[]{:S(2)}, u32[]{:S(2)}) collective-permute-start(bf16[4,4,24,768]{3,2,1,0:T(8,128)(2,1)S(1)} %fusion.4), channel_id=1, source_target_pairs={{0,1},{1,0},{2,3},{3,2},{4,5},{5,4},{6,7},{7,6},{8,9},{9,8},{10,11... | collective-permute-start | bytes 1769480 | tf_op jit(solution)/shard_map/ppermute | solution.py:44
  290.8 34.5 %collective-permute-start.22 = (bf16[4,24,1152]{2,1,0:T(8,128)(2,1)S(1)}, bf16[4,24,1152]{2,1,0:T(8,128)(2,1)S(1)}, u32[]{:S(2)}, u32[]{:S(2)}) collective-permute-start(bf16[4,24,1152]{2,1,0:T(8,128)(2,1)S(1)} %fusion.14), channel_id=1, source_target_pairs={{0,1},{1,0},{2,3},{3,2},{4,5},{5,4},{6,7},{7,6},{8,9},{9,8},{10,11... | collective-permute-start | bytes 663560 | tf_op jit(solution)/shard_map/ppermute | solution.py:44
  308.6 20.0 %collective-permute-start.17 = (bf16[4,24,1152]{2,1,0:T(8,128)(2,1)S(1)}, bf16[4,24,1152]{2,1,0:T(8,128)(2,1)S(1)}, u32[]{:S(2)}, u32[]{:S(2)}) collective-permute-start(bf16[4,24,1152]{2,1,0:T(8,128)(2,1)S(1)} %fusion.13), channel_id=1, source_target_pairs={{0,16},{16,0},{1,17},{17,1},{2,18},{18,2},{3,19},{19,3},{4,20},{20... | collective-permute-start | bytes 663560 | tf_op jit(solution)/shard_map/ppermute | solution.py:44
  335.6 16.2 %collective-permute-start.28 = (bf16[4,5,24,768]{3,2,1,0:T(8,128)(2,1)S(1)}, bf16[4,5,24,768]{3,2,1,0:T(8,128)(2,1)S(1)}, u32[]{:S(2)}, u32[]{:S(2)}) collective-permute-start(bf16[4,5,24,768]{3,2,1,0:T(8,128)(2,1)S(1)} %fusion.3), channel_id=1, source_target_pairs={{0,16},{16,0},{1,17},{17,1},{2,18},{18,2},{3,19},{19,3},{4,20},{20... | collective-permute-start | bytes 2211848 | tf_op jit(solution)/shard_map/ppermute | solution.py:44
  342.3 13.3 %collective-permute-start.36 = (bf16[4,24,768]{2,1,0:T(8,128)(2,1)S(1)}, bf16[4,24,768]{2,1,0:T(8,128)(2,1)S(1)}, u32[]{:S(2)}, u32[]{:S(2)}) collective-permute-start(bf16[4,24,768]{2,1,0:T(8,128)(2,1)S(1)} %get-tuple-element.80), channel_id=1, source_target_pairs={{0,6},{2,0},{4,2},{6,4},{1,7},{3,1},{5,3},{7,5},{8,14},{10,8},{12,... | collective-permute-start | bytes 442376 | tf_op jit(solution)/shard_map/ppermute | solution.py:49
  342.4 14.6 %collective-permute-start.35 = (bf16[4,24,768]{2,1,0:T(8,128)(2,1)S(1)}, bf16[4,24,768]{2,1,0:T(8,128)(2,1)S(1)}, u32[]{:S(2)}, u32[]{:S(2)}) collective-permute-start(bf16[4,24,768]{2,1,0:T(8,128)(2,1)S(1)} %get-tuple-element.81), channel_id=1, source_target_pairs={{0,4},{2,6},{4,0},{6,2},{1,5},{3,7},{5,1},{7,3},{8,12},{10,14},{12... | collective-permute-start | bytes 442376 | tf_op jit(solution)/shard_map/ppermute | solution.py:49
  342.4 14.5 %collective-permute-start.34 = (bf16[4,24,768]{2,1,0:T(8,128)(2,1)S(1)}, bf16[4,24,768]{2,1,0:T(8,128)(2,1)S(1)}, u32[]{:S(2)}, u32[]{:S(2)}) collective-permute-start(bf16[4,24,768]{2,1,0:T(8,128)(2,1)S(1)} %get-tuple-element.79), channel_id=1, source_target_pairs={{0,2},{2,4},{4,6},{6,0},{1,3},{3,5},{5,7},{7,1},{8,10},{10,12},{12... | collective-permute-start | bytes 442376 | tf_op jit(solution)/shard_map/ppermute | solution.py:49
  355.6 14.6 %collective-permute-start.30 = (bf16[5,24,768]{2,1,0:T(8,128)(2,1)S(1)}, bf16[5,24,768]{2,1,0:T(8,128)(2,1)S(1)}, u32[]{:S(2)}, u32[]{:S(2)}) collective-permute-start(bf16[5,24,768]{2,1,0:T(8,128)(2,1)S(1)} %get-tuple-element.78), channel_id=1, source_target_pairs={{0,4},{2,6},{4,0},{6,2},{1,5},{3,7},{5,1},{7,3},{8,12},{10,14},{12... | collective-permute-start | bytes 552968 | tf_op jit(solution)/shard_map/ppermute | solution.py:49
  355.6 14.6 %collective-permute-start.29 = (bf16[5,24,768]{2,1,0:T(8,128)(2,1)S(1)}, bf16[5,24,768]{2,1,0:T(8,128)(2,1)S(1)}, u32[]{:S(2)}, u32[]{:S(2)}) collective-permute-start(bf16[5,24,768]{2,1,0:T(8,128)(2,1)S(1)} %get-tuple-element.76), channel_id=1, source_target_pairs={{0,2},{2,4},{4,6},{6,0},{1,3},{3,5},{5,7},{7,1},{8,10},{10,12},{12... | collective-permute-start | bytes 552968 | tf_op jit(solution)/shard_map/ppermute | solution.py:49
  (46 other events, 379.1 us)
Sparse Core Ops, SparseCore 0:
  12.9 104.5 all-gather.2

commit v4 on v3

--- a/solution.py
+++ b/solution.py
@@ -50,7 +50,9 @@
 
 
 def place():
-    return jnp.stack([lax.axis_index(name) for name in ("hx", "hc", "sz", "sy")]).astype(jnp.int32)
+    return jnp.stack([lax.axis_index(name) for name in ("hx", "hc", "sz", "sy", "rb")]).astype(
+        jnp.int32
+    )
 
 
 ANY = pl.BlockSpec(memory_space=pl.ANY)
@@ -65,12 +67,12 @@
         copy.wait()
 
 
-def join_kernel(place_ref, left, right, whole, sems):
+def join_kernel(place_ref, left, left_other, right, right_other, whole, sems):
     hx, hc, sz, sy = (place_ref[i] for i in range(4))
     half = left.shape[-1]
     copies = []
-    for side, pieces in enumerate((left, right)):
-        for core in range(2):
+    for side, cores in enumerate(((left, left_other), (right, right_other))):
+        for core, pieces in enumerate(cores):
             for second in range(2):
                 for first in range(2):
                     for deep in range(4):
@@ -79,7 +81,7 @@
                         spot = (block * 4 + lax.rem(sz + deep, 4)) * 2 + (sy ^ down)
                         copies.append(
                             pltpu.make_async_copy(
-                                pieces.at[core, second, first, deep],
+                                pieces.at[second, first, deep],
                                 whole.at[spot, :, pl.ds(side * half, half)],
                                 sems.at[len(copies)],
                             )
@@ -87,30 +89,29 @@
     run_all(copies)
 
 
-def join(here, left, right):
-    rows, half = left.shape[-2:]
+def join(here, *sides):
+    rows, half = sides[0].shape[-2:]
     return pl.pallas_call(
         join_kernel,
-        out_shape=jax.ShapeDtypeStruct((32, rows, half * 2), left.dtype),
-        in_specs=[SMEM, ANY, ANY],
+        out_shape=jax.ShapeDtypeStruct((32, rows, half * 2), bf16),
+        in_specs=[SMEM] + [ANY] * 4,
         out_specs=VMEM,
         scratch_shapes=[pltpu.SemaphoreType.DMA((64,))],
         compiler_params=pltpu.CompilerParams(vmem_limit_bytes=40 << 20),
-    )(here, left, right).reshape(rows * 32, half * 2)
-
-
-def gather_rows(here, shard):
-    if lax.axis_size("rb") > 1:
-        return lax.all_gather(shard, EVERY, axis=0, tiled=True)
+    )(here, *sides).reshape(rows * 32, half * 2)
+
+
+def gather_rows(here, shard, first):
     half = shard.shape[1] // 2
     sides = []
     deep = jnp.stack([shard] + [turn(shard, "sz", k) for k in (1, 2, 3)])
+    deep, first = lax.optimization_barrier((deep, first))
     for side, order in ((0, ("hx", "sy")), (1, ("sy", "hx"))):
         level = deep[:, :, side * half : (side + 1) * half]
-        for axis in order + ("hc",):
+        for axis in order:
             level = jnp.stack([level, swap(level, axis)])
-        sides.append(level)
-    return join(here, *sides)
+        sides += [level, swap(level, "hc")]
+    return join(here, *sides), first
 
 
 def piece_copies(place_ref, blocks, keep, send, sems, side, columns=None):
@@ -132,51 +133,56 @@
 ORDERS = (("sy", "hx"), ("hx", "sy"))
 
 
-def collect(keep, send, order):
-    total = keep.astype(f32) + swap(send, order[0]).astype(f32)
-    total = total[0] + swap(total[1].astype(bf16), order[1]).astype(f32)
+def reduce_first(keep, send, order):
+    return keep.astype(f32) + swap(send, order[0]).astype(f32)
+
+
+def reduce_second(total, order):
+    return total[0] + swap(total[1].astype(bf16), order[1]).astype(f32)
+
+
+def reduce_third(total):
     result = total[0]
     for k in (1, 2, 3):
         result = result + turn(total[k].astype(bf16), "sz", -k).astype(f32)
     return result
 
 
-def put_rows(leave_ref, slot, which, rows):
-    tokens = rows.shape[0]
-    if which == 0:
-        leave_ref[slot, pl.ds(tokens, tokens // 2), pl.ds(0, WIDTH)] = rows[: tokens // 2]
-        leave_ref[slot, pl.ds(tokens, tokens // 2), pl.ds(WIDTH, WIDTH)] = rows[tokens // 2 :]
-    else:
-        leave_ref[slot, pl.ds(0, tokens), pl.ds((which - 1) * WIDTH, WIDTH)] = rows
-
-
-def enter_kernel(x_ref, mod_ref, gain_ref, weight_ref, entered_ref, leave_ref):
+def enter_kernel(x_ref, mod_ref, gains_ref, weight_ref, entered_ref, pair_ref, query_ref):
     seqs, tokens, width = x_ref.shape
+    half = tokens // 2
     for s in range(seqs):
         normed = normalize(x_ref[s].astype(f32))[0]
-        value = normed * gain_ref[...] * (1.0 + mod_ref[s, 1:2]) + mod_ref[s, 0:1]
+        shift, scale = (mod_ref[s : s + 1, pl.ds(i * width, width)] for i in (0, 1))
+        value = normed * gains_ref[0:1] * (1.0 + scale) + shift
         entered_ref[pl.ds(s * tokens, tokens), :] = value.astype(bf16)
     entered = entered_ref[...]
-    for which in range(3):
+    for which in (1, 2, 0):
         triple = dot(entered, weight_ref[:, pl.ds(which * width, width)]).astype(bf16)
         for s in range(seqs):
             for g in range(GROUPS):
                 rows = triple[s * tokens : (s + 1) * tokens, g * WIDTH : (g + 1) * WIDTH]
-                put_rows(leave_ref, s * GROUPS + g, which, rows)
-
-
-def enter(inputs, pieces, gain, weight):
+                slot = s * GROUPS + g
+                if which == 0:
+                    query_ref[slot, :, pl.ds(0, WIDTH)] = rows[:half]
+                    query_ref[slot, :, pl.ds(WIDTH, WIDTH)] = rows[half:]
+                else:
+                    pair_ref[slot, :, pl.ds((which - 1) * WIDTH, WIDTH)] = rows
+
+
+def enter(inputs, modulation, gains, weight):
     seqs, tokens, width = inputs.shape
     return pl.pallas_call(
         enter_kernel,
         out_shape=(
             jax.ShapeDtypeStruct((seqs * tokens, width), bf16),
-            jax.ShapeDtypeStruct((8, tokens + tokens // 2, 2 * WIDTH), bf16),
+            jax.ShapeDtypeStruct((8, tokens, 2 * WIDTH), bf16),
+            jax.ShapeDtypeStruct((8, tokens // 2, 2 * WIDTH), bf16),
         ),
         in_specs=[VMEM] * 4,
-        out_specs=(VMEM, VMEM),
+        out_specs=(VMEM,) * 3,
         compiler_params=pltpu.CompilerParams(vmem_limit_bytes=40 << 20),
-    )(inputs, pieces, gain, weight)
+    )(inputs, modulation, gains, weight)
 
 
 def head_lanes(rows, head):
@@ -209,7 +215,7 @@
 
 
 def forward_kernel(
-    starts, came_ref, first_ref, second_ref, third_ref, key_docs_ref, query_docs_ref,
+    starts, came_ref, first_ref, second_ref, third_ref, fourth_ref, key_docs_ref, query_docs_ref,
     out_ref, turned_ref, total_ref, query_sc, pair_sc, top_sc, sum_sc, acc_sc,
 ):
     step = pl.program_id(0)
@@ -218,12 +224,12 @@
 
     @pl.when(step == 0)
     def start():
-        spread_heads(came_ref, 2 * half, half, query_sc, HEAD_DIM ** (-0.5))
+        spread_heads(came_ref, 0, half, query_sc, HEAD_DIM ** (-0.5))
         top_sc[...] = jnp.full(top_sc.shape, -1e30, f32)
         sum_sc[...] = jnp.zeros(sum_sc.shape, f32)
         acc_sc[...] = jnp.zeros(acc_sc.shape, f32)
 
-    fetch(step, (first_ref, second_ref, third_ref), starts, pair_sc)
+    fetch(step, (first_ref, second_ref, third_ref, fourth_ref), starts, pair_sc)
     key_part = pair_sc[:, :WIDTH]
     value_turned = pair_sc[:, WIDTH:].T
     allowed = key_docs_ref[...] == query_docs_ref[...]
@@ -274,8 +280,7 @@
 
 
 def attend(came, pairs, key_docs, query_docs):
-    slots, rows, columns = came.shape
-    half = rows // 3
+    slots, half, columns = came.shape
     queries = slots * 2 * half
     heads = WIDTH // HEAD_DIM
     chunk = 512
@@ -308,7 +313,7 @@
 
 
 def backward_kernel(
-    starts, came_ref, grad_ref, first_ref, second_ref, third_ref, key_docs_ref, query_docs_ref,
+    starts, came_ref, grad_ref, first_ref, second_ref, third_ref, fourth_ref, key_docs_ref, query_docs_ref,
     turned_ref, total_ref, query_out, keep_ref, send_ref,
     query_sc, grad_sc, pair_sc, delta_sc, acc_sc,
 ):
@@ -318,7 +323,7 @@
 
     @pl.when(step == 0)
     def start():
-        spread_heads(came_ref, 2 * half, half, query_sc, HEAD_DIM ** (-0.5))
+        spread_heads(came_ref, 0, half, query_sc, HEAD_DIM ** (-0.5))
         spread_heads(grad_ref, 0, half, grad_sc, 1.0)
         acc_sc[...] = jnp.zeros(acc_sc.shape, f32)
         for h in range(heads):
@@ -326,7 +331,7 @@
             turned = grad_sc[h].astype(f32).T
             delta_sc[h : h + 1] = jnp.sum(turned[rows] * turned_ref[rows], axis=0, keepdims=True)
 
-    fetch(step, (first_ref, second_ref, third_ref), starts, pair_sc)
+    fetch(step, (first_ref, second_ref, third_ref, fourth_ref), starts, pair_sc)
     key_part = pair_sc[:, :WIDTH]
     value_part = pair_sc[:, WIDTH:]
     key_turned = key_part.T
@@ -368,8 +373,7 @@
 
 
 def attend_back(came, grad, pairs, key_docs, query_docs, turned, total):
-    slots, rows, columns = came.shape
-    half = rows // 3
+    slots, half, columns = came.shape
     queries = slots * 2 * half
     heads = WIDTH // HEAD_DIM
     chunk = 512
@@ -409,22 +413,60 @@
 
 
 def middle_kernel(
-    came_ref, x_ref, teacher_ref, mask_ref, weight_ref, mod_ref, gain_ref, up_bias_ref,
-    down_bias_ref, out_ref, up_hbm, down_hbm,
-    final_ref, hidden_ref, leave_ref, pack_ref, sums_ref, up_sc, down_sc, slope_sc, sems,
+    gathered, came_ref, x_ref, teacher_ref, mask_ref, mod_ref, gains_ref, up_bias_ref, *refs
 ):
+    if gathered:
+        later_hbm, *refs = refs
+    else:
+        out_hbm, up_hbm, down_hbm, *refs = refs
+    final_ref, hidden_ref, leave_ref, pack_ref, sums_ref, *refs = refs
+    out_sc, up_sc, down_sc, slope_sc, *refs = refs
+    if gathered:
+        block_sc, sems = refs
+    else:
+        (sems,) = refs
+
     seqs, tokens, width = x_ref.shape
     units = up_sc.shape[1]
     rows = seqs * tokens
     half = tokens // 2
-    up_copy = pltpu.make_async_copy(up_hbm, up_sc, sems.at[0])
-    down_copy = pltpu.make_async_copy(down_hbm, down_sc, sems.at[1])
-    up_copy.start()
-    down_copy.start()
+    if gathered:
+        copies = [
+            pltpu.make_async_copy(later_hbm.at[:, j], block_sc.at[j], sems.at[j]) for j in range(9)
+        ]
+    else:
+        copies = [
+            pltpu.make_async_copy(source, target, sems.at[i])
+            for i, (source, target) in enumerate(
+                ((out_hbm, out_sc), (up_hbm, up_sc), (down_hbm, down_sc))
+            )
+        ]
+    for copy in copies:
+        copy.start()
+
+    def settle(j):
+        if not gathered:
+            if j < 2 or j == 5:
+                copies[(0, 1, None, None, None, 2)[j]].wait()
+            return
+        copies[j].wait()
+        for i in range(32):
+            value = block_sc[j, i]
+            if j == 0:
+                out_sc[pl.ds(i * 24, 24), :] = value
+            elif j < 5:
+                up_sc[pl.ds(i * 24, 24), pl.ds((j - 1) * width, width)] = value
+            else:
+                down_sc[pl.ds(i * 96 + (j - 5) * 24, 24), :] = value
 
     def wide(index):
         return jnp.concatenate(
-            [jnp.broadcast_to(mod_ref[s, index : index + 1], (tokens, width)) for s in range(seqs)]
+            [
+                jnp.broadcast_to(
+                    mod_ref[s : s + 1, pl.ds(index * width, width)], (tokens, width)
+                )
+                for s in range(seqs)
+            ]
         )
 
     def add_rows(first, value):
@@ -441,17 +483,19 @@
             pack_ref[pl.ds(s * tokens + half, half), columns] = right
     mixed = pack_ref[:, pl.ds(0, width)]
     residual = jnp.concatenate([x_ref[s].astype(f32) for s in range(seqs)])
-    branch = dot(mixed, out_ref[...])
+    settle(0)
+    branch = dot(mixed, out_sc[...])
     hidden = residual + wide(2) * branch
     normed, inverse = normalize(hidden)
-    scaled = normed * gain_ref[...]
+    scaled = normed * gains_ref[1:2]
     moved = (scaled * (1.0 + wide(4)) + wide(3)).astype(bf16)
     pack_ref[:, pl.ds(width, width)] = moved
-    up_copy.wait()
+    for j in range(1, 9):
+        settle(j)
     lower = None
     for f in range(units // width):
         columns = pl.ds(f * width, width)
-        u = dot(moved, up_sc[:, columns]) + up_bias_ref[:, columns]
+        u = dot(moved, up_sc[:, columns]) + up_bias_ref[0:1, columns]
         square = u * u
         t = jnp.tanh(0.7978845608028654 * (u + 0.044715 * u * square))
         active = (0.5 * u * (1.0 + t)).astype(bf16)
@@ -459,20 +503,20 @@
             1.0 + 0.134145 * square
         )
         pack_ref[:, pl.ds(2 * width + f * width, width)] = active
-        if f == 0:
-            down_copy.wait()
         term = dot(active, down_sc[columns, :])
         lower = term if lower is None else lower + term
-    lower = lower + down_bias_ref[...]
+    lower = lower + gains_ref[2:3]
     gate = wide(5)
     final = hidden + gate * lower
     for s in range(seqs):
         final_ref[s] = final[s * tokens : (s + 1) * tokens].astype(bf16)
     teacher = jnp.concatenate([teacher_ref[s].astype(f32) for s in range(seqs)])
     mismatch = final - teacher
-    sums_ref[14:15] = jnp.sum(mask_ref[...] * mismatch * mismatch, axis=0, keepdims=True)
+    sums_ref[14:15] = jnp.sum(
+        mask_ref[:, 0:1] * mismatch * mismatch, axis=0, keepdims=True
+    )
     sums_ref[15:16] = jnp.zeros((1, width), f32)
-    grad_final = weight_ref[...] * mismatch
+    grad_final = mask_ref[:, 1:2] * mismatch
     add_rows(6, grad_final * lower)
     grad_lower = (gate * grad_final).astype(bf16)
     base = 2 * width + units
@@ -491,12 +535,12 @@
     add_rows(4, grad_moved * scaled)
     grad_scaled = grad_moved * (1.0 + wide(4))
     sums_ref[8:9] = jnp.sum(grad_scaled * normed, axis=0, keepdims=True)
-    grad_hidden = grad_final + norm_back(grad_scaled * gain_ref[...], normed, inverse)
+    grad_hidden = grad_final + norm_back(grad_scaled * gains_ref[1:2], normed, inverse)
     hidden_ref[...] = grad_hidden
     add_rows(0, grad_hidden * branch)
     grad_branch = (wide(2) * grad_hidden).astype(bf16)
     pack_ref[:, pl.ds(base, width)] = grad_branch
-    grad_mixed = dot_nt(grad_branch, out_ref[...]).astype(bf16)
+    grad_mixed = dot_nt(grad_branch, out_sc[...]).astype(bf16)
     for s in range(seqs):
         for g in range(GROUPS):
             piece = grad_mixed[s * tokens : (s + 1) * tokens, g * WIDTH : (g + 1) * WIDTH]
@@ -504,12 +548,21 @@
             leave_ref[s * GROUPS + g, :, pl.ds(WIDTH, WIDTH)] = piece[half:]
 
 
-def middle(came, inputs, teacher, mask, weight, pieces, gain, up_bias, down_bias, out, up, down):
+def middle(came, inputs, teacher, masks, modulation, gains, up_bias, later):
     seqs, tokens, width = inputs.shape
-    units = up.shape[1]
+    units = up_bias.shape[1]
     rows = seqs * tokens
+    gathered = len(later) == 1
+    scratch = [
+        pltpu.VMEM((width, width), bf16),
+        pltpu.VMEM((width, units), bf16),
+        pltpu.VMEM((units, width), bf16),
+        pltpu.VMEM((rows, units), f32),
+    ]
+    if gathered:
+        scratch.append(pltpu.VMEM((9, 32, 24, width), bf16))
     return pl.pallas_call(
-        middle_kernel,
+        partial(middle_kernel, gathered),
         out_shape=(
             jax.ShapeDtypeStruct((seqs, tokens, width), bf16),
             jax.ShapeDtypeStruct((rows, width), f32),
@@ -517,16 +570,11 @@
             jax.ShapeDtypeStruct((rows, 4 * width + 2 * units), bf16),
             jax.ShapeDtypeStruct((16, width), f32),
         ),
-        in_specs=[VMEM] * 10 + [ANY] * 2,
+        in_specs=[VMEM] * 7 + [ANY] * len(later),
         out_specs=(VMEM,) * 5,
-        scratch_shapes=[
-            pltpu.VMEM((width, units), bf16),
-            pltpu.VMEM((units, width), bf16),
-            pltpu.VMEM((rows, units), f32),
-            pltpu.SemaphoreType.DMA((2,)),
-        ],
-        compiler_params=pltpu.CompilerParams(vmem_limit_bytes=56 << 20),
-    )(came, inputs, teacher, mask, weight, pieces, gain, up_bias, down_bias, out, up, down)
+        scratch_shapes=scratch + [pltpu.SemaphoreType.DMA((9,))],
+        compiler_params=pltpu.CompilerParams(vmem_limit_bytes=60 << 20),
+    )(came, inputs, teacher, masks, modulation, gains, up_bias, *later)
 
 
 def weights_kernel(
@@ -579,29 +627,30 @@
     )(here, own, other)
 
 
-def flat_rows(came_ref, target, first_row, seqs, tokens, width):
+def flat_rows(query_ref, pair_ref, target, first_row, seqs, tokens, width):
     half = tokens // 2
     for s in range(seqs):
         for g in range(GROUPS):
             slot = s * GROUPS + g
             row = first_row + s * tokens
-            left, right = load_pairs(came_ref, slot, tokens, half)
+            left, right = load_pairs(query_ref, slot, 0, half)
             target[pl.ds(row, half), pl.ds(g * WIDTH, WIDTH)] = left
             target[pl.ds(row + half, half), pl.ds(g * WIDTH, WIDTH)] = right
-            left, right = load_pairs(came_ref, slot, 0, tokens)
+            left, right = load_pairs(pair_ref, slot, 0, tokens)
             target[pl.ds(row, tokens), pl.ds(width + g * WIDTH, WIDTH)] = left
             target[pl.ds(row, tokens), pl.ds(2 * width + g * WIDTH, WIDTH)] = right
 
 
 def qkv_kernel(
-    seqs, place_ref, entered_ref, entered_other, own_ref, other_ref,
+    seqs, place_ref, entered_ref, entered_other, query_ref, query_other, pair_ref, pair_other,
     keep_a, send_a, keep_b, send_b, left_sc, right_sc, block_sc, sems,
 ):
     rows, width = entered_ref.shape
     hc = place_ref[1]
-    for which, (left, right) in enumerate(((entered_ref, own_ref), (entered_other, other_ref))):
+    both = ((entered_ref, query_ref, pair_ref), (entered_other, query_other, pair_other))
+    for which, (left, query, pair) in enumerate(both):
         left_sc[:, pl.ds(which * rows, rows)] = left[...].T
-        flat_rows(right, right_sc, which * rows, seqs, rows // seqs, width)
+        flat_rows(query, pair, right_sc, which * rows, seqs, rows // seqs, width)
     for hx in range(2):
         begin = pl.multiple_of(hx * 384 + hc * 192, 64)
         for j in range(3):
@@ -617,13 +666,13 @@
         copy.wait()
 
 
-def qkv_terms(here, seqs, entered, entered_other, own, other):
-    rows, width = entered.shape
+def qkv_terms(here, seqs, *values):
+    rows, width = values[0].shape
     side = jax.ShapeDtypeStruct((2, 4, 24, 3 * width // 2), bf16)
     return pl.pallas_call(
         partial(qkv_kernel, seqs),
         out_shape=(side,) * 4,
-        in_specs=[SMEM] + [VMEM] * 4,
+        in_specs=[SMEM] + [VMEM] * 6,
         out_specs=(ANY,) * 4,
         scratch_shapes=[
             pltpu.VMEM((width, 2 * rows), bf16),
@@ -632,47 +681,148 @@
             pltpu.SemaphoreType.DMA((2, 16)),
         ],
         compiler_params=pltpu.CompilerParams(vmem_limit_bytes=40 << 20),
-    )(here, entered, entered_other, own, other)
+    )(here, *values)
 
 
 def leave_kernel(
-    came_ref, x_ref, hidden_ref, mod_ref, gain_ref, weight_ref, grad_ref, sums_ref, flat_ref
+    query_ref, pair_ref, x_ref, hidden_ref, mod_ref, gains_ref, weight_ref, middle_ref,
+    grad_ref, small_ref, flat_ref,
 ):
     seqs, tokens, width = x_ref.shape
-    flat_rows(came_ref, flat_ref, 0, seqs, tokens, width)
+    devices = small_ref.shape[0]
+    flat_rows(query_ref, pair_ref, flat_ref, 0, seqs, tokens, width)
     grad_entered = None
     for which in range(3):
         columns = pl.ds(which * width, width)
         term = dot_nt(flat_ref[:, columns], weight_ref[:, columns])
         grad_entered = term if grad_entered is None else grad_entered + term
-    sums_ref[...] = jnp.zeros(sums_ref.shape, f32)
     gain_sum = None
+    sums = []
     for s in range(seqs):
         normed, inverse = normalize(x_ref[s].astype(f32))
         rows = slice(s * tokens, (s + 1) * tokens)
         grad = grad_entered[rows]
-        sums_ref[s : s + 1] = jnp.sum(grad, axis=0, keepdims=True)
-        sums_ref[2 + s : 3 + s] = jnp.sum(grad * (normed * gain_ref[...]), axis=0, keepdims=True)
-        grad_scaled = grad * (1.0 + mod_ref[s, 1:2])
+        shift_sum = jnp.sum(grad, axis=0, keepdims=True)
+        scale_sum = jnp.sum(grad * (normed * gains_ref[0:1]), axis=0, keepdims=True)
+        grad_scaled = grad * (1.0 + mod_ref[s : s + 1, pl.ds(width, width)])
         term = jnp.sum(grad_scaled * normed, axis=0, keepdims=True)
         gain_sum = term if gain_sum is None else gain_sum + term
-        grad_ref[s] = hidden_ref[rows] + norm_back(grad_scaled * gain_ref[...], normed, inverse)
-    sums_ref[4:5] = gain_sum
-
-
-def leave(came, inputs, grad_hidden, pieces, gain, weight):
+        grad_ref[s] = hidden_ref[rows] + norm_back(grad_scaled * gains_ref[0:1], normed, inverse)
+        later = [middle_ref[i + s : i + s + 1] for i in (0, 2, 4, 6)]
+        sums.append(jnp.concatenate([shift_sum, scale_sum, *later], axis=1))
+    up_bias = jnp.concatenate([middle_ref[i : i + 1] for i in range(10, 14)], axis=1)
+    fields = [*sums, gain_sum, middle_ref[8:9], up_bias, middle_ref[9:10]]
+    error = jnp.sum(middle_ref[14:15], axis=1, keepdims=True)
+    small_ref[...] = jnp.zeros(small_ref.shape, f32)
+    begin = 0
+    for field in fields:
+        size = field.shape[1] // devices
+        for i in range(devices):
+            small_ref[i : i + 1, pl.ds(begin, size)] = field[:, i * size : (i + 1) * size]
+        begin += size
+    small_ref[:, pl.ds(begin, 1)] = jnp.broadcast_to(error, (devices, 1))
+
+
+def leave(query, pair, inputs, grad_hidden, modulation, gains, weight, sums, devices):
     seqs, tokens, width = inputs.shape
     return pl.pallas_call(
         leave_kernel,
         out_shape=(
             jax.ShapeDtypeStruct((seqs, tokens, width), f32),
-            jax.ShapeDtypeStruct((8, width), f32),
+            jax.ShapeDtypeStruct((devices, 512), f32),
             jax.ShapeDtypeStruct((seqs * tokens, 3 * width), bf16),
         ),
-        in_specs=[VMEM] * 6,
+        in_specs=[VMEM] * 8,
         out_specs=(VMEM,) * 3,
         compiler_params=pltpu.CompilerParams(vmem_limit_bytes=40 << 20),
-    )(came, inputs, grad_hidden, pieces, gain, weight)
+    )(query, pair, inputs, grad_hidden, modulation, gains, weight, sums)
+
+
+def unpack_kernel(
+    parts, sizes, factor, place_ref, every_ref, valid_ref,
+    mod_ref, gains_ref, up_ref, key_docs_ref, query_docs_ref, masks_ref,
+):
+    devices = every_ref.shape[0]
+    seqs, tokens = valid_ref.shape
+    size_mod, size_gain, size_up = sizes
+    mod_ref[...] = jnp.zeros(mod_ref.shape, f32)
+    gains_ref[...] = jnp.zeros(gains_ref.shape, f32)
+    up_ref[...] = jnp.zeros(up_ref.shape, f32)
+    begin = 0
+    targets = [(mod_ref, s, size_mod) for s in range(seqs)]
+    targets += [(gains_ref, 0, size_gain), (gains_ref, 1, size_gain)]
+    targets += [(up_ref, 0, size_up), (gains_ref, 2, size_gain)]
+    for target, row, size in targets:
+        for i in range(devices):
+            target[row : row + 1, pl.ds(i * size, size)] = every_ref[
+                i : i + 1, pl.ds(begin, size)
+            ]
+        begin += size
+    hx, hc, sz, sy, rb = (place_ref[i] for i in range(5))
+    second = sz * 2 + sy >= GROUPS
+    row = 0
+    for core in range(2):
+        for across in range(2):
+            for part in range(parts):
+                block = ((hx ^ across) * 2 + (hc ^ core)) * parts + part
+                lines = every_ref[pl.ds(pl.multiple_of(block * 8, 8), 8), pl.ds(begin, 2 * tokens)]
+                lines = jnp.where(second, lines[:, tokens:], lines[:, :tokens])
+                turned = lines.T
+                for spot in range(8):
+                    key_docs_ref[pl.ds(row, tokens), :] = turned[:, spot : spot + 1]
+                    row += tokens
+    lines = every_ref[
+        pl.ds(pl.multiple_of(((hx * 2 + hc) * parts + rb) * 8, 8), 8), pl.ds(begin, 2 * tokens)
+    ]
+    lines = jnp.where(second, lines[:, tokens:], lines[:, :tokens])
+    for spot in range(8):
+        query_docs_ref[:, pl.ds(spot * tokens, tokens)] = lines[spot : spot + 1]
+    begin += 2 * tokens
+    count = jnp.sum(every_ref[:, pl.ds(begin, 1)], axis=0, keepdims=True)
+    gains_ref[3:4, pl.ds(0, 1)] = count
+    turned = valid_ref[...].astype(f32).T
+    for s in range(seqs):
+        rows = pl.ds(s * tokens, tokens)
+        masks_ref[rows, pl.ds(0, 1)] = turned[:, s : s + 1]
+        masks_ref[rows, pl.ds(1, 1)] = turned[:, s : s + 1] * (factor / count)
+
+
+def unpack(here, every, valid_mask, width, units, parts, length):
+    seqs, tokens = valid_mask.shape
+    devices = every.shape[0]
+    sizes = (6 * width // devices, width // devices, units // devices)
+    return pl.pallas_call(
+        partial(unpack_kernel, parts, sizes, float(seqs * length)),
+        out_shape=(
+            jax.ShapeDtypeStruct((8, 6 * width), f32),
+            jax.ShapeDtypeStruct((8, width), f32),
+            jax.ShapeDtypeStruct((8, units), f32),
+            jax.ShapeDtypeStruct((4 * parts * 8 * tokens, 1), f32),
+            jax.ShapeDtypeStruct((1, 8 * tokens), f32),
+            jax.ShapeDtypeStruct((seqs * tokens, 2), f32),
+        ),
+        in_specs=[SMEM, VMEM, VMEM],
+        out_specs=(VMEM,) * 6,
+        compiler_params=pltpu.CompilerParams(vmem_limit_bytes=40 << 20),
+    )(here, every, valid_mask)
+
+
+def block_kernel(out_ref, up_ref, down_ref, later_ref):
+    width = out_ref.shape[1]
+    later_ref[0] = out_ref[...]
+    for j in range(4):
+        later_ref[1 + j] = up_ref[:, pl.ds(j * width, width)]
+        later_ref[5 + j] = down_ref[pl.ds(j * 24, 24), :]
+
+
+def block(out_weight, up_weight, down_weight):
+    width = out_weight.shape[1]
+    return pl.pallas_call(
+        block_kernel,
+        out_shape=jax.ShapeDtypeStruct((9, 24, width), bf16),
+        in_specs=[VMEM] * 3,
+        out_specs=VMEM,
+    )(out_weight, up_weight, down_weight)
 
 
 def exchange(rows):
@@ -703,13 +853,10 @@
     length = tokens * devices
     queries = 8 * tokens
     here = place()
-    hx, hc, rb = lax.axis_index("hx"), lax.axis_index("hc"), lax.axis_index("rb")
-    own_seq = (lax.axis_index("sz") * 2 + lax.axis_index("sy")) // GROUPS
 
     own_modulation = jnp.dot(
         time_embed, ada_weight.astype(f32), precision=precise
     ) + ada_bias.astype(f32)
-    mask_float = valid_mask.astype(f32)
     fields = [
         own_modulation.reshape(-1),
         gain_attn.astype(f32),
@@ -717,84 +864,87 @@
         up_bias.astype(f32),
         down_bias.astype(f32),
         segments.astype(f32).reshape(-1),
-        jnp.sum(mask_float).reshape(1),
+        jnp.sum(valid_mask.astype(f32)).reshape(1),
     ]
-    sizes = [field.shape[0] for field in fields]
     packed = jnp.concatenate(fields)
-    everyone = lax.all_to_all(
+    packed = jnp.pad(packed, (0, -packed.shape[0] % 128))
+    every = lax.all_to_all(
         jnp.broadcast_to(packed, (devices, packed.shape[0])), EVERY, 0, 0, tiled=True
     )
-    columns = []
-    begin = 0
-    for size in sizes:
-        columns.append(everyone[:, begin : begin + size])
-        begin += size
-    modulation = columns[0].reshape(devices, seqs, -1).transpose(1, 0, 2)
-    pieces = modulation.reshape(seqs, 6, width)
-    gain_one, gain_two, full_up_bias, full_down_bias = (c.reshape(1, -1) for c in columns[1:5])
-    docs = columns[5].reshape(2, 2, parts, 8, seqs, tokens)
-    count_all = jnp.sum(columns[6])
-
-    full_qkv = gather_rows(here, qkv_weight)
     if parts > 1:
-        full_out, full_up, full_down = (
+        full_qkv, *later = (
             lax.all_gather(w, EVERY, axis=0, tiled=True)
-            for w in (out_weight, up_weight, down_weight)
+            for w in (qkv_weight, out_weight, up_weight, down_weight)
         )
     else:
-        later = jnp.concatenate(
-            [out_weight[None]]
-            + [up_weight[None, :, j * width : (j + 1) * width] for j in range(4)]
-            + [down_weight.reshape(4, 24, width)]
-        )
-        later = lax.all_gather(later, EVERY, axis=0, tiled=False)
-        full_out = later[:, 0].reshape(width, width)
-        full_up = later[:, 1:5].transpose(0, 2, 1, 3).reshape(width, units)
-        full_down = later[:, 5:].reshape(units, width)
-
-    entered, leaving = enter(inputs, pieces, gain_one, full_qkv)
-    came = exchange(leaving)
-    pair = came[:, :tokens].reshape(queries, 2 * WIDTH)
+        later = [
+            lax.all_gather(block(out_weight, up_weight, down_weight), EVERY, axis=0, tiled=False)
+        ]
+        full_qkv, every = gather_rows(here, qkv_weight, every)
+    modulation, gains, full_up_bias, key_docs, query_docs, masks = unpack(
+        here, every, valid_mask, width, units, parts, length
+    )
+    count_all = gains[3, 0]
+
+    entered, pair, query = enter(inputs, modulation, gains, full_qkv)
+    pair = exchange(pair).reshape(queries, 2 * WIDTH)
+    query = exchange(query)
     if parts > 1:
         pair = lax.all_gather(pair, "rb", axis=0, tiled=True)
     pair_x = swap(pair, "hx")
-    pair_c = jnp.concatenate([swap(pair, "hc"), swap(pair_x, "hc")])
-    pairs = (pair, pair_x, pair_c)
-
-    docs_here = lax.dynamic_index_in_dim(docs, own_seq, 4, keepdims=False)
-    docs_here = jnp.where(hx == 1, docs_here[::-1], docs_here)
-    docs_here = jnp.where(hc == 1, docs_here[:, ::-1], docs_here)
-    key_docs = docs_here.transpose(1, 0, 2, 3, 4).reshape(-1, 1)
-    query_docs = lax.dynamic_index_in_dim(docs_here[0, 0], rb, 0, keepdims=False).reshape(1, -1)
-    attended, turned, total = attend(came, pairs, key_docs, query_docs)
-
-    mask_column = mask_float.reshape(-1, 1)
+    pairs = (pair, pair_x, swap(pair, "hc"), swap(pair_x, "hc"))
+    attended, turned, total = attend(query, pairs, key_docs, query_docs)
+
     final, grad_hidden, grad_leaving, pack, sums = middle(
-        exchange(attended),
-        inputs,
-        teacher,
-        mask_column,
-        mask_column * (seqs * length / count_all),
-        pieces,
-        gain_two,
-        full_up_bias,
-        full_down_bias,
-        full_out,
-        full_up,
-        full_down,
+        exchange(attended), inputs, teacher, masks, modulation, gains, full_up_bias, later
     )
     grad_came = exchange(grad_leaving)
     if parts == 1:
         terms = weight_terms(here, pack, swap(pack, "hc"), width)
-        side_a = collect(terms[0], terms[1], ORDERS[0])
-        side_b = collect(terms[2], terms[3], ORDERS[1])
+        grad_came, terms = lax.optimization_barrier((grad_came, terms))
+        first_a = reduce_first(terms[0], terms[1], ORDERS[0])
+        first_b = reduce_first(terms[2], terms[3], ORDERS[1])
+
+    grad_query, keep, send = attend_back(
+        query, grad_came, pairs, key_docs, query_docs, turned, total
+    )
+    home_query = exchange(grad_query)
+    grad_pair = keep + swap(send, "hc").astype(f32)
+    middle_row = grad_pair.shape[0] // 2
+    grad_pair = grad_pair[:middle_row] + swap(grad_pair[middle_row:].astype(bf16), "hx").astype(f32)
+    if parts > 1:
+        grad_pair = lax.psum_scatter(grad_pair, "rb", scatter_dimension=0, tiled=True)
+    grad_pair = grad_pair.astype(bf16).reshape(8, tokens, 2 * WIDTH)
+    if parts == 1:
+        grad_pair, first_a, first_b = lax.optimization_barrier((grad_pair, first_a, first_b))
+        second_a = reduce_second(first_a, ORDERS[0])
+        second_b = reduce_second(first_b, ORDERS[1])
+    home_pair = exchange(grad_pair)
+    grad_input, small, flat = leave(
+        home_query, home_pair, inputs, grad_hidden, modulation, gains, full_qkv, sums, devices
+    )
+    if parts == 1:
+        others = swap(entered, "hc"), swap(home_query, "hc"), swap(home_pair, "hc")
+        others, second_a, second_b = lax.optimization_barrier((others, second_a, second_b))
+        terms = qkv_terms(
+            here, seqs, entered, others[0], home_query, others[1], home_pair, others[2]
+        )
+        shard_qkv = jnp.concatenate(
+            [
+                reduce_third(reduce_second(reduce_first(keep, send, order), order))
+                for keep, send, order in zip(terms[::2], terms[1::2], ORDERS)
+            ],
+            axis=1,
+        )
+        side_a = reduce_third(second_a)
+        side_b = reduce_third(second_b)
         shard_out = side_a[0]
         shard_up = side_a[1:].transpose(1, 0, 2).reshape(24, units)
         shard_down = side_b.reshape(96, width)
     else:
         base = 2 * width + units
         ends = (base + width, base + width + units)
-        shard_out, shard_up, shard_down = (
+        shard_qkv, shard_out, shard_up, shard_down = (
             lax.psum_scatter(
                 jnp.einsum("tk,tn->kn", left, right, preferred_element_type=f32),
                 EVERY,
@@ -802,60 +952,17 @@
                 tiled=True,
             )
             for left, right in (
+                (entered, flat),
                 (pack[:, :width], pack[:, base : ends[0]]),
                 (pack[:, width : 2 * width], pack[:, ends[0] : ends[1]]),
                 (pack[:, 2 * width : base], pack[:, ends[1] :]),
             )
         )
-
-    grad_query, keep, send = attend_back(
-        came, grad_came, pairs, key_docs, query_docs, turned, total
-    )
-    grad_pair = keep + swap(send, "hc").astype(f32)
-    middle_row = grad_pair.shape[0] // 2
-    grad_pair = grad_pair[:middle_row] + swap(grad_pair[middle_row:].astype(bf16), "hx").astype(f32)
-    if parts > 1:
-        grad_pair = lax.psum_scatter(grad_pair, "rb", scatter_dimension=0, tiled=True)
-    home = exchange(
-        jnp.concatenate(
-            [grad_pair.astype(bf16).reshape(8, tokens, 2 * WIDTH), grad_query], axis=1
-        )
-    )
-    grad_input, sums_one, flat = leave(home, inputs, grad_hidden, pieces, gain_one, full_qkv)
-    if parts == 1:
-        terms = qkv_terms(here, seqs, entered, swap(entered, "hc"), home, swap(home, "hc"))
-        shard_qkv = jnp.concatenate(
-            [collect(terms[0], terms[1], ORDERS[0]), collect(terms[2], terms[3], ORDERS[1])],
-            axis=1,
-        )
-    else:
-        shard_qkv = lax.psum_scatter(
-            jnp.einsum("tk,tn->kn", entered, flat, preferred_element_type=f32),
-            EVERY,
-            scatter_dimension=0,
-            tiled=True,
-        )
-    grad_modulation = jnp.stack(
-        [
-            jnp.stack([sums_one[s], sums_one[2 + s], sums[s], sums[2 + s], sums[4 + s], sums[6 + s]])
-            for s in range(seqs)
-        ]
-    ).reshape(seqs, devices, -1)
-    fields = [
-        grad_modulation.transpose(1, 0, 2).reshape(devices, -1),
-        sums_one[4].reshape(devices, -1),
-        sums[8].reshape(devices, -1),
-        sums[10:14].reshape(devices, -1),
-        sums[9].reshape(devices, -1),
-        jnp.broadcast_to(jnp.sum(sums[14]), (devices, 1)),
-    ]
-    sizes = [value.shape[1] for value in fields]
-    added = jnp.sum(
-        lax.all_to_all(jnp.concatenate(fields, axis=1), EVERY, 0, 0, tiled=True), axis=0
-    )
+    added = jnp.sum(lax.all_to_all(small, EVERY, 0, 0, tiled=True), axis=0)
     owned = []
     begin = 0
-    for size in sizes:
+    sizes = [6 * width // devices * seqs] + [size // devices for size in (width, width, units, width)]
+    for size in sizes + [1]:
         owned.append(added[begin : begin + size])
         begin += size
     own_grad = owned[0].reshape(seqs, -1)

time: 382 us -> 349 us (0.914)
  waiting for transfers between devices: 148 us -> 108 us
  blocking collectives: 14.1 us -> 50.1 us
  local copies, waits for them, and re-layouts: 59 us -> 39.2 us
  starting transfers between devices: 65.7 us -> 58 us
    all_to_all x1 -> x3, blocking collectives: 14.1 us -> 50.1 us  [exchange(): return lax.all_to_all(rows, SPOT, 0, 0, tiled=True)]
    all_to_all x3, waiting for transfers between devices: 28.7 us -> 0.93 us  [exchange(): return lax.all_to_all(rows, SPOT, 0, 0, tiled=True)]
    slice x10 -> x1, local copies, waits for them, and re-layouts: 14.9 us -> 1.18 us  [on_device(): count_all = gains[3, 0]]
    reshape x13 -> x0, local copies, waits for them, and re-layouts: 10.9 us -> none  [the longest x4 4.27 us: on_device(): c.reshape(1, -1)]
    unnamed x79 -> x100, local copies, waits for them, and re-layouts: 16.2 us -> 25.5 us
    ppermute x22 -> x23, starting transfers between devices: 19.8 us -> 11.7 us  [swap(): return lax.ppermute(value, axis, [(0, 1), (1, 0)])]
    add x8 -> x10, other arithmetic: 3.28 us -> 11.2 us  [the longest x4 5.9 us: reduce_first(): return keep.astype(f32) + swap(send, order[0]).astype(f32)]
    ppermute x22 -> x23, waiting for transfers between devices: 82.8 us -> 75.8 us  [swap(): return lax.ppermute(value, axis, [(0, 1), (1, 0)])]
  transfers between devices with their start and end apart: 43 -> 44, of which waited for: 21 -> 19; matrix products, arithmetic and copies ran while one was open for 18% -> 10% of each run, Pallas kernels for 7% -> 8%
where the time goes in v4:
time: 349 us; the launch traced here: 347 us
  waiting for transfers between devices  108 us (31%)
  starting transfers between devices  58 us (17%)
  Pallas kernels  54.1 us (16%)
  blocking collectives  50.1 us (14%)
  local copies, waits for them, and re-layouts  39.2 us (11%)
  other arithmetic  19.6 us (6%)
  between operations  17.1 us (5%)
    ppermute x23, waiting for transfers between devices, swap(): return lax.ppermute(value, axis, [(0, 1), (1, 0)])  75.8 us
    all_to_all x3, blocking collectives, exchange(): return lax.all_to_all(rows, SPOT, 0, 0, tiled=True)  50.1 us
    ppermute x15, starting transfers between devices, turn(): lax.ppermute(value, axis, [(i, (i - step) % size) for i in range(size)])  25.7 us
    unnamed x100, local copies, waits for them, and re-layouts  25.5 us
    ppermute x15, waiting for transfers between devices, turn(): lax.ppermute(value, axis, [(i, (i - step) % size) for i in range(size)])  18 us
    all_to_all x3, starting transfers between devices, exchange(): return lax.all_to_all(rows, SPOT, 0, 0, tiled=True)  12.4 us
    pallas_call x1, Pallas kernels, middle(): pl.pallas_call(partial(middle_kernel, gathered), out_shape=(jax.ShapeDtyp...  12.2 us
    pallas_call x1, Pallas kernels, attend_back(): pl.pallas_call(partial(backward_kernel, starts), grid=(steps,), out_shape...  12 us
  transfers between devices with their start and end apart: 44, of which 19 were waited for; matrix products, arithmetic and copies ran while one was open for 10% of the time, Pallas kernels for 8%

profile of v4, /device:TPU:0, one launch (start us, length us, event | category | flops | bytes accessed | tf_op | source)
XLA Modules:
  0.0 346.9 jit_solution(9549099389380489018)
XLA Ops:
  9.0 5.1 %collective-permute-start = (bf16[24,2304]{1,0:T(8,128)(2,1)}, bf16[24,2304]{1,0:T(8,128)(2,1)S(1)}, u32[]{:S(2)}, u32[]{:S(2)}) collective-permute-start(bf16[24,2304]{1,0:T(8,128)(2,1)} %param.23), channel_id=1, source_target_pairs={{0,6},{2,0},{4,2},{6,4},{1,7},{3,1},{5,3},{7,5},{8,14},{10,8},{12,... | collective-permute-start | bytes 331784 | tf_op jit(solution)/shard_map/ppermute | solution.py:49
  18.8 3.4 concatenate.6
  22.9 5.1 %all-to-all-start = ((f32[32,1,640]{2,1,0:T(1,128)}), f32[32,1,640]{2,1,0:T(1,128)S(1)}, u32[]{:S(2)}, u32[]{:S(2)}) async-start(f32[32,1,640]{2,1,0:T(1,128)} %broadcast_in_dim.2), calls=%async_computation | async-start | bytes 163840 | tf_op jit(solution)/shard_map/all_to_all | solution.py:871
  29.0 8.1 %all-to-all-done = f32[32,1,640]{2,1,0:T(1,128)S(1)} async-done(((f32[32,1,640]{2,1,0:T(1,128)}), f32[32,1,640]{2,1,0:T(1,128)S(1)}, u32[]{:S(2)}, u32[]{:S(2)}) %all-to-all-start) | async-done | bytes 81952 | tf_op jit(solution)/shard_map/all_to_all | solution.py:871
  39.1 5.3 %collective-permute-done.6 = bf16[4,24,1152]{2,1,0:T(8,128)(2,1)S(1)} collective-permute-done((bf16[4,24,1152]{2,1,0:T(8,128)(2,1)S(1)}, bf16[4,24,1152]{2,1,0:T(8,128)(2,1)S(1)}, u32[]{:S(2)}, u32[]{:S(2)}) %collective-permute-start.6) | collective-permute-done | bytes 221216 | tf_op jit(solution)/shard_map/ppermute | solution.py:44
  47.2 17.3 %collective-permute-done.7 = bf16[2,4,24,1152]{3,2,1,0:T(8,128)(2,1)S(1)} collective-permute-done((bf16[2,4,24,1152]{3,2,1,0:T(8,128)(2,1)S(1)}, bf16[2,4,24,1152]{3,2,1,0:T(8,128)(2,1)S(1)}, u32[]{:S(2)}, u32[]{:S(2)}) %collective-permute-start.7) | collective-permute-done | bytes 442400 | tf_op jit(solution)/shard_map/ppermute | solution.py:44
  77.6 3.1 shard_map.247
  81.7 26.3 %all_to_all.48 = bf16[8,64,384]{2,1,0:T(8,128)(2,1)S(1)} all-to-all(bf16[8,64,384]{2,1,0:T(8,128)(2,1)S(1)} %get-tuple-element.63), channel_id=1, replica_groups=mesh['hx'=2,'hc'=2,'rb'=1,'sz'=4,'sy'=2] {'sz','sy'}, dimensions={0} | all-to-all | bytes 786432 | tf_op jit(solution)/shard_map/all_to_all | solution.py:829
  108.8 9.5 %collective-permute-done.9.second_ref = bf16[512,384]{1,0:T(8,128)(2,1)S(1)} collective-permute-done((bf16[512,384]{1,0:T(8,128)(2,1)S(1)}, bf16[512,384]{1,0:T(8,128)(2,1)S(1)}, u32[]{:S(2)}, u32[]{:S(2)}) %collective-permute-start.9) | collective-permute-done | bytes 393248 | tf_op jit(solution)/shard_map/ppermute | solution.py:44
  118.3 12.8 %all_to_all.49.came_ref = bf16[8,32,384]{2,1,0:T(8,128)(2,1)S(1)} all-to-all(bf16[8,32,384]{2,1,0:T(8,128)(2,1)S(1)} %get-tuple-element.62), channel_id=1, replica_groups=mesh['hx'=2,'hc'=2,'rb'=1,'sz'=4,'sy'=2] {'sz','sy'}, dimensions={0} | all-to-all | bytes 393216 | tf_op jit(solution)/shard_map/all_to_all | solution.py:829
  131.1 8.2 %shard_map.249 = (bf16[8,32,384]{2,1,0:T(8,128)(2,1)S(1)}, f32[192,512]{1,0:T(8,128)S(1)}, f32[8,512]{1,0:T(8,128)S(1)}) custom-call(bf16[8,32,384]{2,1,0:T(8,128)(2,1)S(1)} %all_to_all.49.came_ref, bf16[512,384]{1,0:T(8,128)(2,1)S(1)} %bitcast.119, bf16[512,384]{1,0:T(8,128)(2,1)S(1)} %collective-permute-done.9.second_ref, ...), custom_call_target="tpu_custom_call" | custom-call | tf_op jit(solution)/shard_map/pallas_call | solution.py:293
  140.7 11.1 %all_to_all.50.came_ref = bf16[8,32,384]{2,1,0:T(8,128)(2,1)} all-to-all(bf16[8,32,384]{2,1,0:T(8,128)(2,1)S(1)} %get-tuple-element.66), channel_id=1, replica_groups=mesh['hx'=2,'hc'=2,'rb'=1,'sz'=4,'sy'=2] {'sz','sy'}, dimensions={0} | all-to-all | bytes 393216 | tf_op jit(solution)/shard_map/all_to_all | solution.py:829
  151.7 12.2 %shard_map.251 = (bf16[2,64,768]{2,1,0:T(8,128)(2,1)}, f32[128,768]{1,0:T(8,128)}, bf16[8,32,384]{2,1,0:T(8,128)(2,1)}, bf16[128,9216]{1,0:T(8,128)(2,1)}, f32[16,768]{1,0:T(8,128)}) custom-call(bf16[8,32,384]{2,1,0:T(8,128)(2,1)} %all_to_all.50.came_ref, bf16[2,64,768]{2,1,0:T(8,128)(2,1)} %x_ref.5, bf16[2,64,768]{2,1,0:T(8,128)(2,1)} %teacher_ref.1, ...), custom_call_target="tpu_custom_call" | custom-call | tf_op jit(solution)/shard_map/pallas_call | solution.py:564
  164.0 4.0 %all-to-all-start.4 = ((bf16[8,32,384]{2,1,0:T(8,128)(2,1)}), bf16[8,32,384]{2,1,0:T(8,128)(2,1)}, u32[]{:S(2)}, u32[]{:S(2)}) async-start(bf16[8,32,384]{2,1,0:T(8,128)(2,1)} %get-tuple-element.70), calls=%async_computation.4 | async-start | bytes 393216 | tf_op jit(solution)/shard_map/all_to_all | solution.py:829
  168.8 7.1 %shard_map.252 = (bf16[2,4,5,24,768]{4,3,2,1,0:T(8,128)(2,1)}, bf16[2,4,5,24,768]{4,3,2,1,0:T(8,128)(2,1)}, bf16[2,4,4,24,768]{4,3,2,1,0:T(8,128)(2,1)}, bf16[2,4,4,24,768]{4,3,2,1,0:T(8,128)(2,1)}) custom-call(s32[5]{0:T(128)} %copy-done.38, bf16[128,9216]{1,0:T(8,128)(2,1)} %get-tuple-element.71.own_ref, bf16[128,9216]{1,0:T(8,128)(2,1)} %collective-permute-done.12.other_ref), custom_call_target="tpu_custom_call" | custom-call | tf_op jit(solution)/shard_map/pallas_call | solution.py:614
  184.7 12.0 %shard_map.253 = (bf16[8,32,384]{2,1,0:T(8,128)(2,1)S(1)}, f32[1024,384]{1,0:T(8,128)S(1)}, bf16[1024,384]{1,0:T(8,128)(2,1)S(1)}) custom-call(bf16[8,32,384]{2,1,0:T(8,128)(2,1)S(1)} %copy-done.11, bf16[8,32,384]{2,1,0:T(8,128)(2,1)} %all-to-all-done.4.grad_ref, bf16[512,384]{1,0:T(8,128)(2,1)S(1)} %bitcast.120, bf16[512,384]{1,0:T(8,128)(2,1)S(1)} %copy-done.15, ...), custom_call_target="tpu_custom_call" | custom-call | tf_op jit(solution)/shard_map/pallas_call | solution.py:382
  202.0 4.2 %all-to-all-start.5 = ((bf16[8,32,384]{2,1,0:T(8,128)(2,1)}), bf16[8,32,384]{2,1,0:T(8,128)(2,1)}, u32[]{:S(2)}, u32[]{:S(2)}) async-start(bf16[8,32,384]{2,1,0:T(8,128)(2,1)} %copy-done.32), calls=%async_computation.5 | async-start | bytes 393216 | tf_op jit(solution)/shard_map/all_to_all | solution.py:829
  206.2 27.7 %collective-permute-done.14 = bf16[512,384]{1,0:T(8,128)(2,1)} collective-permute-done((bf16[512,384]{1,0:T(8,128)(2,1)}, bf16[512,384]{1,0:T(8,128)(2,1)}, u32[]{:S(2)}, u32[]{:S(2)}) %collective-permute-start.14) | collective-permute-done | bytes 393248 | tf_op jit(solution)/shard_map/ppermute | solution.py:44
  237.7 4.1 %convert_add_fusion = f32[2,4,5,24,768]{4,3,2,1,0:T(8,128)} fusion(bf16[2,4,5,24,768]{4,3,2,1,0:T(8,128)(2,1)} %collective-permute-done.15, bf16[2,4,5,24,768]{4,3,2,1,0:T(8,128)(2,1)S(1)} %copy-done.46), kind=kLoop, calls=%fused_computation | loop fusion | flops 2211840 | bytes 5898240 | tf_op jit(solution)/shard_map/add | solution.py:137
  246.3 4.1 %all-to-all-start.6 = ((bf16[8,64,384]{2,1,0:T(8,128)(2,1)}), bf16[8,64,384]{2,1,0:T(8,128)(2,1)}, u32[]{:S(2)}, u32[]{:S(2)}) async-start(bf16[8,64,384]{2,1,0:T(8,128)(2,1)} %bitcast.124), calls=%async_computation.6 | async-start | bytes 786432 | tf_op jit(solution)/shard_map/all_to_all | solution.py:829
  252.8 8.8 %collective-permute-done.21 = bf16[4,4,24,768]{3,2,1,0:T(8,128)(2,1)} collective-permute-done((bf16[4,4,24,768]{3,2,1,0:T(8,128)(2,1)}, bf16[4,4,24,768]{3,2,1,0:T(8,128)(2,1)}, u32[]{:S(2)}, u32[]{:S(2)}) %collective-permute-start.21) | collective-permute-done | bytes 589856 | tf_op jit(solution)/shard_map/ppermute | solution.py:44
  261.5 2.6 bitcast_add_fusion.1
  268.5 3.4 shard_map.254
  272.6 3.1 all-to-all-start.7
  277.8 5.2 %all-to-all-done.7 = f32[32,1,512]{2,1,0:T(1,128)S(1)} async-done(((f32[32,1,512]{2,1,0:T(1,128)}), f32[32,1,512]{2,1,0:T(1,128)S(1)}, u32[]{:S(2)}, u32[]{:S(2)}) %all-to-all-start.7) | async-done | bytes 65568 | tf_op jit(solution)/shard_map/all_to_all | solution.py:961
  288.4 2.5 collective-permute-start.37
  293.1 3.4 shard_map.255
  296.6 2.9 collective-permute-start.34
  299.5 2.5 collective-permute-done.36
  306.0 10.2 %collective-permute-done.33 = bf16[5,24,768]{2,1,0:T(8,128)(2,1)S(1)} collective-permute-done((bf16[5,24,768]{2,1,0:T(8,128)(2,1)S(1)}, bf16[5,24,768]{2,1,0:T(8,128)(2,1)S(1)}, u32[]{:S(2)}, u32[]{:S(2)}) %collective-permute-start.33) | collective-permute-done | bytes 184352 | tf_op jit(solution)/shard_map/ppermute | solution.py:49
  319.4 4.4 %collective-permute-done.23 = bf16[4,24,1152]{2,1,0:T(8,128)(2,1)S(1)} collective-permute-done((bf16[4,24,1152]{2,1,0:T(8,128)(2,1)S(1)}, bf16[4,24,1152]{2,1,0:T(8,128)(2,1)S(1)}, u32[]{:S(2)}, u32[]{:S(2)}) %collective-permute-start.23) | collective-permute-done | bytes 221216 | tf_op jit(solution)/shard_map/ppermute | solution.py:44
  323.9 4.3 %collective-permute-start.24 = (bf16[24,1152]{1,0:T(8,128)(2,1)S(1)}, bf16[24,1152]{1,0:T(8,128)(2,1)S(1)}, u32[]{:S(2)}, u32[]{:S(2)}) collective-permute-start(bf16[24,1152]{1,0:T(8,128)(2,1)S(1)} %get-tuple-element.121), channel_id=1, source_target_pairs={{0,2},{2,4},{4,6},{6,0},{1,3},{3,5},{5,7},{7,1},{8,10},{10,12},{12... | collective-permute-start | bytes 165896 | tf_op jit(solution)/shard_map/ppermute | solution.py:49
  (223 shorter events, 86.0 us)
Async XLA Ops:
  7.2 144.5 %all-gather.3.cloned.1.call-start = ((), (), s32[]{:S(2)}) async-start(), calls=%async_computation.8 | async-start | bytes 10948608 | tf_op jit(solution)/shard_map/all_gather | solution.py:881
  9.0 18.9 %collective-permute-start = (bf16[24,2304]{1,0:T(8,128)(2,1)}, bf16[24,2304]{1,0:T(8,128)(2,1)S(1)}, u32[]{:S(2)}, u32[]{:S(2)}) collective-permute-start(bf16[24,2304]{1,0:T(8,128)(2,1)} %param.23), channel_id=1, source_target_pairs={{0,6},{2,0},{4,2},{6,4},{1,7},{3,1},{5,3},{7,5},{8,14},{10,8},{12,... | collective-permute-start | bytes 331784 | tf_op jit(solution)/shard_map/ppermute | solution.py:49
  14.1 13.9 %collective-permute-start.1 = (bf16[24,2304]{1,0:T(8,128)(2,1)}, bf16[24,2304]{1,0:T(8,128)(2,1)S(1)}, u32[]{:S(2)}, u32[]{:S(2)}) collective-permute-start(bf16[24,2304]{1,0:T(8,128)(2,1)} %param.23), channel_id=1, source_target_pairs={{0,4},{2,6},{4,0},{6,2},{1,5},{3,7},{5,1},{7,3},{8,12},{10,14},{12... | collective-permute-start | bytes 331784 | tf_op jit(solution)/shard_map/ppermute | solution.py:49
  14.1 13.9 %collective-permute-start.2 = (bf16[24,2304]{1,0:T(8,128)(2,1)}, bf16[24,2304]{1,0:T(8,128)(2,1)S(1)}, u32[]{:S(2)}, u32[]{:S(2)}) collective-permute-start(bf16[24,2304]{1,0:T(8,128)(2,1)} %param.23), channel_id=1, source_target_pairs={{0,2},{2,4},{4,6},{6,0},{1,3},{3,5},{5,7},{7,1},{8,10},{10,12},{12... | collective-permute-start | bytes 331784 | tf_op jit(solution)/shard_map/ppermute | solution.py:49
  22.9 14.1 %all-to-all-start = ((f32[32,1,640]{2,1,0:T(1,128)}), f32[32,1,640]{2,1,0:T(1,128)S(1)}, u32[]{:S(2)}, u32[]{:S(2)}) async-start(f32[32,1,640]{2,1,0:T(1,128)} %broadcast_in_dim.2), calls=%async_computation | async-start | bytes 163840 | tf_op jit(solution)/shard_map/all_to_all | solution.py:871
  44.5 20.0 %collective-permute-start.7 = (bf16[2,4,24,1152]{3,2,1,0:T(8,128)(2,1)S(1)}, bf16[2,4,24,1152]{3,2,1,0:T(8,128)(2,1)S(1)}, u32[]{:S(2)}, u32[]{:S(2)}) collective-permute-start(bf16[2,4,24,1152]{3,2,1,0:T(8,128)(2,1)S(1)} %get-tuple-element.114), channel_id=1, source_target_pairs={{0,16},{16,0},{1,17},{17,1},{2,18},{18,2},{3,19},{19,3},{4,20},{20... | collective-permute-start | bytes 1327112 | tf_op jit(solution)/shard_map/ppermute | solution.py:44
  47.0 17.6 %collective-permute-start.4 = (bf16[2,4,24,1152]{3,2,1,0:T(8,128)(2,1)S(1)}, bf16[2,4,24,1152]{3,2,1,0:T(8,128)(2,1)S(1)}, u32[]{:S(2)}, u32[]{:S(2)}) collective-permute-start(bf16[2,4,24,1152]{3,2,1,0:T(8,128)(2,1)S(1)} %get-tuple-element.120), channel_id=1, source_target_pairs={{0,1},{1,0},{2,3},{3,2},{4,5},{5,4},{6,7},{7,6},{8,9},{9,8},{10,11... | collective-permute-start | bytes 1327112 | tf_op jit(solution)/shard_map/ppermute | solution.py:44
  108.0 10.3 %collective-permute-start.9 = (bf16[512,384]{1,0:T(8,128)(2,1)S(1)}, bf16[512,384]{1,0:T(8,128)(2,1)S(1)}, u32[]{:S(2)}, u32[]{:S(2)}) collective-permute-start(bf16[512,384]{1,0:T(8,128)(2,1)S(1)} %bitcast.117), channel_id=1, source_target_pairs={{0,16},{16,0},{1,17},{17,1},{2,18},{18,2},{3,19},{19,3},{4,20},{20... | collective-permute-start | bytes 1179656 | tf_op jit(solution)/shard_map/ppermute | solution.py:44
  108.8 22.2 %collective-permute-start.10 = (bf16[512,384]{1,0:T(8,128)(2,1)S(1)}, bf16[512,384]{1,0:T(8,128)(2,1)S(1)}, u32[]{:S(2)}, u32[]{:S(2)}) collective-permute-start(bf16[512,384]{1,0:T(8,128)(2,1)S(1)} %bitcast.118), channel_id=1, source_target_pairs={{0,8},{8,0},{1,9},{9,1},{2,10},{10,2},{3,11},{11,3},{4,12},{12,4},... | collective-permute-start | bytes 1179656 | tf_op jit(solution)/shard_map/ppermute | solution.py:44
  118.3 12.8 %collective-permute-start.11 = (bf16[512,384]{1,0:T(8,128)(2,1)S(1)}, bf16[512,384]{1,0:T(8,128)(2,1)S(1)}, u32[]{:S(2)}, u32[]{:S(2)}) collective-permute-start(bf16[512,384]{1,0:T(8,128)(2,1)S(1)} %collective-permute-done.9.second_ref), channel_id=1, source_target_pairs={{0,8},{8,0},{1,9},{9,1},{2,10},{10,2},{3,11},{11,3},{4,12},{12,4},... | collective-permute-start | bytes 1179656 | tf_op jit(solution)/shard_map/ppermute | solution.py:44
  164.0 12.9 %all-to-all-start.4 = ((bf16[8,32,384]{2,1,0:T(8,128)(2,1)}), bf16[8,32,384]{2,1,0:T(8,128)(2,1)}, u32[]{:S(2)}, u32[]{:S(2)}) async-start(bf16[8,32,384]{2,1,0:T(8,128)(2,1)} %get-tuple-element.70), calls=%async_computation.4 | async-start | bytes 393216 | tf_op jit(solution)/shard_map/all_to_all | solution.py:829
  196.8 39.2 %collective-permute-start.16 = (bf16[2,4,4,24,768]{4,3,2,1,0:T(8,128)(2,1)}, bf16[2,4,4,24,768]{4,3,2,1,0:T(8,128)(2,1)}, u32[]{:S(2)}, u32[]{:S(2)}) collective-permute-start(bf16[2,4,4,24,768]{4,3,2,1,0:T(8,128)(2,1)} %get-tuple-element.85), channel_id=1, source_target_pairs={{0,16},{16,0},{1,17},{17,1},{2,18},{18,2},{3,19},{19,3},{4,20},{20... | collective-permute-start | bytes 3538952 | tf_op jit(solution)/shard_map/ppermute | solution.py:44
  197.2 40.5 %collective-permute-start.15 = (bf16[2,4,5,24,768]{4,3,2,1,0:T(8,128)(2,1)}, bf16[2,4,5,24,768]{4,3,2,1,0:T(8,128)(2,1)}, u32[]{:S(2)}, u32[]{:S(2)}) collective-permute-start(bf16[2,4,5,24,768]{4,3,2,1,0:T(8,128)(2,1)} %get-tuple-element.83), channel_id=1, source_target_pairs={{0,1},{1,0},{2,3},{3,2},{4,5},{5,4},{6,7},{7,6},{8,9},{9,8},{10,11... | collective-permute-start | bytes 4423688 | tf_op jit(solution)/shard_map/ppermute | solution.py:44
  201.2 32.8 %collective-permute-start.14 = (bf16[512,384]{1,0:T(8,128)(2,1)}, bf16[512,384]{1,0:T(8,128)(2,1)}, u32[]{:S(2)}, u32[]{:S(2)}) collective-permute-start(bf16[512,384]{1,0:T(8,128)(2,1)} %slice.245), channel_id=1, source_target_pairs={{0,16},{16,0},{1,17},{17,1},{2,18},{18,2},{3,19},{19,3},{4,20},{20... | collective-permute-start | bytes 1179656 | tf_op jit(solution)/shard_map/ppermute | solution.py:44
  202.0 44.3 %all-to-all-start.5 = ((bf16[8,32,384]{2,1,0:T(8,128)(2,1)}), bf16[8,32,384]{2,1,0:T(8,128)(2,1)}, u32[]{:S(2)}, u32[]{:S(2)}) async-start(bf16[8,32,384]{2,1,0:T(8,128)(2,1)} %copy-done.32), calls=%async_computation.5 | async-start | bytes 393216 | tf_op jit(solution)/shard_map/all_to_all | solution.py:829
  242.6 18.9 %collective-permute-start.21 = (bf16[4,4,24,768]{3,2,1,0:T(8,128)(2,1)}, bf16[4,4,24,768]{3,2,1,0:T(8,128)(2,1)}, u32[]{:S(2)}, u32[]{:S(2)}) collective-permute-start(bf16[4,4,24,768]{3,2,1,0:T(8,128)(2,1)} %fusion.2), channel_id=1, source_target_pairs={{0,1},{1,0},{2,3},{3,2},{4,5},{5,4},{6,7},{7,6},{8,9},{9,8},{10,11... | collective-permute-start | bytes 1769480 | tf_op jit(solution)/shard_map/ppermute | solution.py:44
  246.0 30.0 %collective-permute-start.20 = (bf16[4,5,24,768]{3,2,1,0:T(8,128)(2,1)}, bf16[4,5,24,768]{3,2,1,0:T(8,128)(2,1)}, u32[]{:S(2)}, u32[]{:S(2)}) collective-permute-start(bf16[4,5,24,768]{3,2,1,0:T(8,128)(2,1)} %fusion.1), channel_id=1, source_target_pairs={{0,16},{16,0},{1,17},{17,1},{2,18},{18,2},{3,19},{19,3},{4,20},{20... | collective-permute-start | bytes 2211848 | tf_op jit(solution)/shard_map/ppermute | solution.py:44
  246.3 17.9 %all-to-all-start.6 = ((bf16[8,64,384]{2,1,0:T(8,128)(2,1)}), bf16[8,64,384]{2,1,0:T(8,128)(2,1)}, u32[]{:S(2)}, u32[]{:S(2)}) async-start(bf16[8,64,384]{2,1,0:T(8,128)(2,1)} %bitcast.124), calls=%async_computation.6 | async-start | bytes 786432 | tf_op jit(solution)/shard_map/all_to_all | solution.py:829
  252.2 34.6 %collective-permute-start.17 = (bf16[128,768]{1,0:T(8,128)(2,1)}, bf16[128,768]{1,0:T(8,128)(2,1)}, u32[]{:S(2)}, u32[]{:S(2)}) collective-permute-start(bf16[128,768]{1,0:T(8,128)(2,1)} %copy-done.33), channel_id=1, source_target_pairs={{0,8},{8,0},{1,9},{9,1},{2,10},{10,2},{3,11},{11,3},{4,12},{12,4},... | collective-permute-start | bytes 589832 | tf_op jit(solution)/shard_map/ppermute | solution.py:44
  252.3 34.5 %collective-permute-start.18 = (bf16[8,32,384]{2,1,0:T(8,128)(2,1)}, bf16[8,32,384]{2,1,0:T(8,128)(2,1)}, u32[]{:S(2)}, u32[]{:S(2)}) collective-permute-start(bf16[8,32,384]{2,1,0:T(8,128)(2,1)} %all-to-all-done.5.query_ref), channel_id=1, source_target_pairs={{0,8},{8,0},{1,9},{9,1},{2,10},{10,2},{3,11},{11,3},{4,12},{12,4},... | collective-permute-start | bytes 589832 | tf_op jit(solution)/shard_map/ppermute | solution.py:44
  272.6 10.4 %all-to-all-start.7 = ((f32[32,1,512]{2,1,0:T(1,128)}), f32[32,1,512]{2,1,0:T(1,128)S(1)}, u32[]{:S(2)}, u32[]{:S(2)}) async-start(f32[32,1,512]{2,1,0:T(1,128)} %copy.31), calls=%async_computation.7 | async-start | bytes 131072 | tf_op jit(solution)/shard_map/all_to_all | solution.py:961
  275.7 11.2 %collective-permute-start.19 = (bf16[8,64,384]{2,1,0:T(8,128)(2,1)}, bf16[8,64,384]{2,1,0:T(8,128)(2,1)S(1)}, u32[]{:S(2)}, u32[]{:S(2)}) collective-permute-start(bf16[8,64,384]{2,1,0:T(8,128)(2,1)} %all-to-all-done.6.pair_ref), channel_id=1, source_target_pairs={{0,8},{8,0},{1,9},{9,1},{2,10},{10,2},{3,11},{11,3},{4,12},{12,4},... | collective-permute-start | bytes 1179656 | tf_op jit(solution)/shard_map/ppermute | solution.py:44
  287.0 9.6 %collective-permute-start.35 = (bf16[4,24,768]{2,1,0:T(8,128)(2,1)S(1)}, bf16[4,24,768]{2,1,0:T(8,128)(2,1)S(1)}, u32[]{:S(2)}, u32[]{:S(2)}) collective-permute-start(bf16[4,24,768]{2,1,0:T(8,128)(2,1)S(1)} %get-tuple-element.110), channel_id=1, source_target_pairs={{0,2},{2,4},{4,6},{6,0},{1,3},{3,5},{5,7},{7,1},{8,10},{10,12},{12... | collective-permute-start | bytes 442376 | tf_op jit(solution)/shard_map/ppermute | solution.py:49
  287.4 14.6 %collective-permute-start.36 = (bf16[4,24,768]{2,1,0:T(8,128)(2,1)S(1)}, bf16[4,24,768]{2,1,0:T(8,128)(2,1)S(1)}, u32[]{:S(2)}, u32[]{:S(2)}) collective-permute-start(bf16[4,24,768]{2,1,0:T(8,128)(2,1)S(1)} %get-tuple-element.112), channel_id=1, source_target_pairs={{0,4},{2,6},{4,0},{6,2},{1,5},{3,7},{5,1},{7,3},{8,12},{10,14},{12... | collective-permute-start | bytes 442376 | tf_op jit(solution)/shard_map/ppermute | solution.py:49
  288.4 14.4 %collective-permute-start.37 = (bf16[4,24,768]{2,1,0:T(8,128)(2,1)S(1)}, bf16[4,24,768]{2,1,0:T(8,128)(2,1)S(1)}, u32[]{:S(2)}, u32[]{:S(2)}) collective-permute-start(bf16[4,24,768]{2,1,0:T(8,128)(2,1)S(1)} %get-tuple-element.111), channel_id=1, source_target_pairs={{0,6},{2,0},{4,2},{6,4},{1,7},{3,1},{5,3},{7,5},{8,14},{10,8},{12,... | collective-permute-start | bytes 442376 | tf_op jit(solution)/shard_map/ppermute | solution.py:49
  291.0 15.0 %collective-permute-start.32 = (bf16[5,24,768]{2,1,0:T(8,128)(2,1)S(1)}, bf16[5,24,768]{2,1,0:T(8,128)(2,1)S(1)}, u32[]{:S(2)}, u32[]{:S(2)}) collective-permute-start(bf16[5,24,768]{2,1,0:T(8,128)(2,1)S(1)} %get-tuple-element.107), channel_id=1, source_target_pairs={{0,2},{2,4},{4,6},{6,0},{1,3},{3,5},{5,7},{7,1},{8,10},{10,12},{12... | collective-permute-start | bytes 552968 | tf_op jit(solution)/shard_map/ppermute | solution.py:49
  291.6 24.6 %collective-permute-start.33 = (bf16[5,24,768]{2,1,0:T(8,128)(2,1)S(1)}, bf16[5,24,768]{2,1,0:T(8,128)(2,1)S(1)}, u32[]{:S(2)}, u32[]{:S(2)}) collective-permute-start(bf16[5,24,768]{2,1,0:T(8,128)(2,1)S(1)} %get-tuple-element.109), channel_id=1, source_target_pairs={{0,4},{2,6},{4,0},{6,2},{1,5},{3,7},{5,1},{7,3},{8,12},{10,14},{12... | collective-permute-start | bytes 552968 | tf_op jit(solution)/shard_map/ppermute | solution.py:49
  296.6 19.6 %collective-permute-start.34 = (bf16[5,24,768]{2,1,0:T(8,128)(2,1)S(1)}, bf16[5,24,768]{2,1,0:T(8,128)(2,1)S(1)}, u32[]{:S(2)}, u32[]{:S(2)}) collective-permute-start(bf16[5,24,768]{2,1,0:T(8,128)(2,1)S(1)} %get-tuple-element.108), channel_id=1, source_target_pairs={{0,6},{2,0},{4,2},{6,4},{1,7},{3,1},{5,3},{7,5},{8,14},{10,8},{12,... | collective-permute-start | bytes 552968 | tf_op jit(solution)/shard_map/ppermute | solution.py:49
  302.0 15.7 %collective-permute-start.22 = (bf16[2,4,24,1152]{3,2,1,0:T(8,128)(2,1)S(1)}, bf16[2,4,24,1152]{3,2,1,0:T(8,128)(2,1)S(1)}, u32[]{:S(2)}, u32[]{:S(2)}) collective-permute-start(bf16[2,4,24,1152]{3,2,1,0:T(8,128)(2,1)S(1)} %get-tuple-element.98), channel_id=1, source_target_pairs={{0,1},{1,0},{2,3},{3,2},{4,5},{5,4},{6,7},{7,6},{8,9},{9,8},{10,11... | collective-permute-start | bytes 1327112 | tf_op jit(solution)/shard_map/ppermute | solution.py:44
  302.8 15.7 %collective-permute-start.27 = (bf16[2,4,24,1152]{3,2,1,0:T(8,128)(2,1)S(1)}, bf16[2,4,24,1152]{3,2,1,0:T(8,128)(2,1)S(1)}, u32[]{:S(2)}, u32[]{:S(2)}) collective-permute-start(bf16[2,4,24,1152]{3,2,1,0:T(8,128)(2,1)S(1)} %get-tuple-element.100), channel_id=1, source_target_pairs={{0,16},{16,0},{1,17},{17,1},{2,18},{18,2},{3,19},{19,3},{4,20},{20... | collective-permute-start | bytes 1327112 | tf_op jit(solution)/shard_map/ppermute | solution.py:44
  318.6 12.1 %collective-permute-start.28 = (bf16[4,24,1152]{2,1,0:T(8,128)(2,1)S(1)}, bf16[4,24,1152]{2,1,0:T(8,128)(2,1)S(1)}, u32[]{:S(2)}, u32[]{:S(2)}) collective-permute-start(bf16[4,24,1152]{2,1,0:T(8,128)(2,1)S(1)} %fusion.10), channel_id=1, source_target_pairs={{0,1},{1,0},{2,3},{3,2},{4,5},{5,4},{6,7},{7,6},{8,9},{9,8},{10,11... | collective-permute-start | bytes 663560 | tf_op jit(solution)/shard_map/ppermute | solution.py:44
  323.9 9.4 %collective-permute-start.24 = (bf16[24,1152]{1,0:T(8,128)(2,1)S(1)}, bf16[24,1152]{1,0:T(8,128)(2,1)S(1)}, u32[]{:S(2)}, u32[]{:S(2)}) collective-permute-start(bf16[24,1152]{1,0:T(8,128)(2,1)S(1)} %get-tuple-element.121), channel_id=1, source_target_pairs={{0,2},{2,4},{4,6},{6,0},{1,3},{3,5},{5,7},{7,1},{8,10},{10,12},{12... | collective-permute-start | bytes 165896 | tf_op jit(solution)/shard_map/ppermute | solution.py:49
  (61 other events, 429.1 us)
Sparse Core Ops, SparseCore 0:
  11.5 106.1 all-gather.2

commit v5 on v4

--- a/solution.py
+++ b/solution.py
@@ -58,6 +58,31 @@
 ANY = pl.BlockSpec(memory_space=pl.ANY)
 SMEM = pl.BlockSpec(memory_space=pltpu.SMEM)
 VMEM = pl.BlockSpec(memory_space=pltpu.VMEM)
+
+
+def hbm(value):
+    return pltpu.with_memory_space_constraint(value, pltpu.HBM)
+
+
+def whole_spec(shape):
+    return pl.BlockSpec(shape, lambda *_: (0,) * len(shape))
+
+
+def single(kernel, outs, values, scratch=(), limit=40, place=None, raw=0, raw_out=False):
+    blocked = len(values) - raw
+    specs = [whole_spec(v.shape) for v in values[:blocked]] + [ANY] * raw
+    values = [hbm(v) for v in values]
+    if place is not None:
+        specs, values = [SMEM] + specs, [place] + values
+    return pl.pallas_call(
+        kernel,
+        grid=(1,),
+        out_shape=tuple(jax.ShapeDtypeStruct(*o) for o in outs),
+        in_specs=specs,
+        out_specs=tuple(ANY if raw_out else whole_spec(o[0]) for o in outs),
+        scratch_shapes=list(scratch),
+        compiler_params=pltpu.CompilerParams(vmem_limit_bytes=limit << 20),
+    )(*values)
 
 
 def run_all(copies):
@@ -91,30 +116,34 @@
 
 def join(here, *sides):
     rows, half = sides[0].shape[-2:]
-    return pl.pallas_call(
+    (whole,) = single(
         join_kernel,
-        out_shape=jax.ShapeDtypeStruct((32, rows, half * 2), bf16),
-        in_specs=[SMEM] + [ANY] * 4,
-        out_specs=VMEM,
-        scratch_shapes=[pltpu.SemaphoreType.DMA((64,))],
-        compiler_params=pltpu.CompilerParams(vmem_limit_bytes=40 << 20),
-    )(here, *sides).reshape(rows * 32, half * 2)
-
-
-def gather_rows(here, shard, first):
+        [((32, rows, half * 2), bf16)],
+        sides,
+        [pltpu.SemaphoreType.DMA((64,))],
+        place=here,
+        raw=4,
+    )
+    return whole.reshape(rows * 32, half * 2)
+
+
+def gather_rows(here, shard, every, use):
     half = shard.shape[1] // 2
     sides = []
     deep = jnp.stack([shard] + [turn(shard, "sz", k) for k in (1, 2, 3)])
-    deep, first = lax.optimization_barrier((deep, first))
-    for side, order in ((0, ("hx", "sy")), (1, ("sy", "hx"))):
-        level = deep[:, :, side * half : (side + 1) * half]
-        for axis in order:
-            level = jnp.stack([level, swap(level, axis)])
+    orders = (("hx", "sy"), ("sy", "hx"))
+    levels = [deep[:, :, :half], deep[:, :, half:]]
+    levels = [jnp.stack([v, swap(v, order[0])]) for v, order in zip(levels, orders)]
+    levels, every = lax.optimization_barrier((levels, every))
+    levels = [jnp.stack([v, swap(v, order[1])]) for v, order in zip(levels, orders)]
+    used = use(every)
+    levels, used = lax.optimization_barrier((levels, used))
+    for level in levels:
         sides += [level, swap(level, "hc")]
-    return join(here, *sides), first
-
-
-def piece_copies(place_ref, blocks, keep, send, sems, side, columns=None):
+    return join(here, *sides), used
+
+
+def piece_copies(place_ref, blocks, keep, send, sems, side, columns):
     hx, sz, sy = place_ref[0], place_ref[2], place_ref[3]
     copies = []
     for second in range(2):
@@ -122,29 +151,34 @@
             for deep in range(4):
                 across, down = (first, second) if side == 0 else (second, first)
                 spot = ((hx ^ across) * 4 + lax.rem(sz + deep, 4)) * 2 + (sy ^ down)
-                source = blocks.at[spot] if columns is None else blocks.at[spot, :, columns]
+                source = blocks.at[(spot,) + (slice(None),) * (len(blocks.shape) - 2) + (columns,)]
                 target = (keep, send)[second].at[first, deep]
-                copies.append(pltpu.make_async_copy(source, target, sems.at[side, len(copies)]))
+                copies.append(pltpu.make_async_copy(source, target, sems.at[len(copies)]))
     for copy in copies:
         copy.start()
     return copies
 
 
 ORDERS = (("sy", "hx"), ("hx", "sy"))
-
-
-def reduce_first(keep, send, order):
-    return keep.astype(f32) + swap(send, order[0]).astype(f32)
-
-
-def reduce_second(total, order):
-    return total[0] + swap(total[1].astype(bf16), order[1]).astype(f32)
-
-
-def reduce_third(total):
+COLUMN_GROUPS = ((1, 0), (2, 0), (1, 1), (2, 1))
+
+
+def second_send(keep, recv):
+    return (keep[1].astype(f32) + recv[1].astype(f32)).astype(bf16)
+
+
+def second_total(keep, recv, recv_second):
+    return keep[0].astype(f32) + recv[0].astype(f32) + recv_second.astype(f32)
+
+
+def third_recvs(total):
+    return [turn(total[k].astype(bf16), "sz", -k) for k in (1, 2, 3)]
+
+
+def third_total(total, recvs):
     result = total[0]
-    for k in (1, 2, 3):
-        result = result + turn(total[k].astype(bf16), "sz", -k).astype(f32)
+    for recv in recvs:
+        result = result + recv.astype(f32)
     return result
 
 
@@ -172,17 +206,15 @@
 
 def enter(inputs, modulation, gains, weight):
     seqs, tokens, width = inputs.shape
-    return pl.pallas_call(
+    return single(
         enter_kernel,
-        out_shape=(
-            jax.ShapeDtypeStruct((seqs * tokens, width), bf16),
-            jax.ShapeDtypeStruct((8, tokens, 2 * WIDTH), bf16),
-            jax.ShapeDtypeStruct((8, tokens // 2, 2 * WIDTH), bf16),
-        ),
-        in_specs=[VMEM] * 4,
-        out_specs=(VMEM,) * 3,
-        compiler_params=pltpu.CompilerParams(vmem_limit_bytes=40 << 20),
-    )(inputs, modulation, gains, weight)
+        [
+            ((seqs * tokens, width), bf16),
+            ((8, tokens, 2 * WIDTH), bf16),
+            ((8, tokens // 2, 2 * WIDTH), bf16),
+        ],
+        [inputs, modulation, gains, weight],
+    )
 
 
 def head_lanes(rows, head):
@@ -273,10 +305,6 @@
         starts.append((begin, begin + count))
         begin += count
     return specs, starts, begin
-
-
-def whole_spec(shape):
-    return pl.BlockSpec(shape, lambda i: (0,) * len(shape))
 
 
 def attend(came, pairs, key_docs, query_docs):
@@ -309,12 +337,12 @@
             pltpu.VMEM((WIDTH, queries), f32),
         ],
         compiler_params=pltpu.CompilerParams(vmem_limit_bytes=48 << 20),
-    )(came, *pairs, key_docs, query_docs)
+    )(*map(hbm, (came, *pairs, key_docs, query_docs)))
 
 
 def backward_kernel(
     starts, came_ref, grad_ref, first_ref, second_ref, third_ref, fourth_ref, key_docs_ref, query_docs_ref,
-    turned_ref, total_ref, query_out, keep_ref, send_ref,
+    turned_ref, total_ref, query_out, keep_ref, keep_other, send_ref,
     query_sc, grad_sc, pair_sc, delta_sc, acc_sc,
 ):
     step = pl.program_id(0)
@@ -351,12 +379,14 @@
         acc_sc[rows] = acc_sc[rows] + dot(
             key_turned[h * HEAD_DIM : (h + 1) * HEAD_DIM], grad_scores
         )
-    middle = pl.num_programs(0) // 2
-
-    @pl.when(step < middle)
-    def mine():
-        keep_ref[:, pl.ds(0, WIDTH)] = grad_key
-        keep_ref[:, pl.ds(WIDTH, WIDTH)] = grad_value
+    quarter = pl.num_programs(0) // 4
+    middle = 2 * quarter
+
+    for number, ref in enumerate((keep_ref, keep_other)):
+        @pl.when((step >= number * quarter) & (step < (number + 1) * quarter))
+        def mine(ref=ref):
+            ref[:, pl.ds(0, WIDTH)] = grad_key
+            ref[:, pl.ds(WIDTH, WIDTH)] = grad_value
 
     @pl.when(step >= middle)
     def theirs():
@@ -378,13 +408,15 @@
     heads = WIDTH // HEAD_DIM
     chunk = 512
     specs, starts, steps = pair_specs(pairs, chunk)
-    middle = steps // 2
+    quarter = steps // 4
+    middle = 2 * quarter
     return pl.pallas_call(
         partial(backward_kernel, starts),
         grid=(steps,),
         out_shape=(
             jax.ShapeDtypeStruct((slots, half, columns), bf16),
-            jax.ShapeDtypeStruct((middle * chunk, columns), f32),
+            jax.ShapeDtypeStruct((quarter * chunk, columns), f32),
+            jax.ShapeDtypeStruct((quarter * chunk, columns), f32),
             jax.ShapeDtypeStruct((middle * chunk, columns), bf16),
         ),
         in_specs=[
@@ -398,7 +430,8 @@
         ],
         out_specs=(
             whole_spec((slots, half, columns)),
-            pl.BlockSpec((chunk, columns), lambda i: (jnp.minimum(i, middle - 1), 0)),
+            pl.BlockSpec((chunk, columns), lambda i: (jnp.minimum(i, quarter - 1), 0)),
+            pl.BlockSpec((chunk, columns), lambda i: (jnp.clip(i - quarter, 0, quarter - 1), 0)),
             pl.BlockSpec((chunk, columns), lambda i: (jnp.maximum(i - middle, 0), 0)),
         ),
         scratch_shapes=[
@@ -409,7 +442,7 @@
             pltpu.VMEM((WIDTH, queries), f32),
         ],
         compiler_params=pltpu.CompilerParams(vmem_limit_bytes=48 << 20),
-    )(came, grad, *pairs, key_docs, query_docs, turned, total)
+    )(*map(hbm, (came, grad, *pairs, key_docs, query_docs, turned, total)))
 
 
 def middle_kernel(
@@ -561,26 +594,27 @@
     ]
     if gathered:
         scratch.append(pltpu.VMEM((9, 32, 24, width), bf16))
-    return pl.pallas_call(
+    return single(
         partial(middle_kernel, gathered),
-        out_shape=(
-            jax.ShapeDtypeStruct((seqs, tokens, width), bf16),
-            jax.ShapeDtypeStruct((rows, width), f32),
-            jax.ShapeDtypeStruct(came.shape, bf16),
-            jax.ShapeDtypeStruct((rows, 4 * width + 2 * units), bf16),
-            jax.ShapeDtypeStruct((16, width), f32),
-        ),
-        in_specs=[VMEM] * 7 + [ANY] * len(later),
-        out_specs=(VMEM,) * 5,
-        scratch_shapes=scratch + [pltpu.SemaphoreType.DMA((9,))],
-        compiler_params=pltpu.CompilerParams(vmem_limit_bytes=60 << 20),
-    )(came, inputs, teacher, masks, modulation, gains, up_bias, *later)
+        [
+            ((seqs, tokens, width), bf16),
+            ((rows, width), f32),
+            (came.shape, bf16),
+            ((rows, 4 * width + 2 * units), bf16),
+            ((16, width), f32),
+        ],
+        [came, inputs, teacher, masks, modulation, gains, up_bias, *later],
+        scratch + [pltpu.SemaphoreType.DMA((9,))],
+        limit=60,
+        raw=len(later),
+    )
 
 
 def weights_kernel(
-    place_ref, own_ref, other_ref, keep_a, send_a, keep_b, send_b, left_sc, right_sc, a_sc, b_sc, sems
+    place_ref, own_ref, other_ref, *refs
 ):
-    rows, width = own_ref.shape[0], a_sc.shape[-1]
+    *groups, left_sc, right_sc, block_sc, sems = refs
+    rows, width = own_ref.shape[0], block_sc.shape[-1]
     units = 4 * width
     hc = place_ref[1]
     base = 2 * width + units
@@ -593,64 +627,65 @@
             offset = 0 if j == 0 else width
             value = dot(left_sc[pl.ds(begin + offset, 192), :], right_sc[:, pl.ds(j * width, width)])
             for i in range(8):
-                a_sc[hx * 8 + i, j] = value[i * 24 : (i + 1) * 24].astype(bf16)
-    copies = piece_copies(place_ref, a_sc, keep_a, send_a, sems, 0)
-    for hx in range(2):
+                block_sc[hx * 8 + i, j] = value[i * 24 : (i + 1) * 24].astype(bf16)
         begin = pl.multiple_of(2 * width + hx * 1536 + hc * 768, 256)
         value = dot(left_sc[pl.ds(begin, 768), :], right_sc[:, pl.ds(width + units, width)])
         for i in range(8):
             for j in range(4):
                 first = i * 96 + j * 24
-                b_sc[hx * 8 + i, j] = value[first : first + 24].astype(bf16)
-    copies += piece_copies(place_ref, b_sc, keep_b, send_b, sems, 1)
+                block_sc[hx * 8 + i, 5 + j] = value[first : first + 24].astype(bf16)
+    copies = []
+    begin = 0
+    for number, (_, side) in enumerate(COLUMN_GROUPS):
+        keep, send = groups[2 * number : 2 * number + 2]
+        columns = pl.ds(begin, keep.shape[-1])
+        copies += piece_copies(place_ref, block_sc, keep, send, sems.at[number], side, columns)
+        begin += keep.shape[-1]
     for copy in copies:
         copy.wait()
 
 
 def weight_terms(here, own, other, width):
     rows, total = own.shape
-    a = jax.ShapeDtypeStruct((2, 4, 5, 24, width), bf16)
-    b = jax.ShapeDtypeStruct((2, 4, 4, 24, width), bf16)
-    return pl.pallas_call(
+    return single(
         weights_kernel,
-        out_shape=(a, a, b, b),
-        in_specs=[SMEM, VMEM, VMEM],
-        out_specs=(ANY,) * 4,
-        scratch_shapes=[
+        [((2, 4, 9, 24, 128 * size), bf16) for size, _ in COLUMN_GROUPS for _ in range(2)],
+        [own, other],
+        [
             pltpu.VMEM((total // 2, 2 * rows), bf16),
             pltpu.VMEM((2 * rows, total // 2), bf16),
-            pltpu.VMEM((16, 5, 24, width), bf16),
-            pltpu.VMEM((16, 4, 24, width), bf16),
-            pltpu.SemaphoreType.DMA((2, 16)),
+            pltpu.VMEM((16, 9, 24, width), bf16),
+            pltpu.SemaphoreType.DMA((len(COLUMN_GROUPS), 16)),
         ],
-        compiler_params=pltpu.CompilerParams(vmem_limit_bytes=56 << 20),
-    )(here, own, other)
-
-
-def flat_rows(query_ref, pair_ref, target, first_row, seqs, tokens, width):
+        limit=56,
+        place=here,
+        raw_out=True,
+    )
+
+
+def flat_rows(home_ref, target, first_row, seqs, tokens, width):
     half = tokens // 2
     for s in range(seqs):
         for g in range(GROUPS):
             slot = s * GROUPS + g
             row = first_row + s * tokens
-            left, right = load_pairs(query_ref, slot, 0, half)
+            left, right = load_pairs(home_ref, slot, tokens, half)
             target[pl.ds(row, half), pl.ds(g * WIDTH, WIDTH)] = left
             target[pl.ds(row + half, half), pl.ds(g * WIDTH, WIDTH)] = right
-            left, right = load_pairs(pair_ref, slot, 0, tokens)
+            left, right = load_pairs(home_ref, slot, 0, tokens)
             target[pl.ds(row, tokens), pl.ds(width + g * WIDTH, WIDTH)] = left
             target[pl.ds(row, tokens), pl.ds(2 * width + g * WIDTH, WIDTH)] = right
 
 
 def qkv_kernel(
-    seqs, place_ref, entered_ref, entered_other, query_ref, query_other, pair_ref, pair_other,
+    seqs, place_ref, entered_ref, entered_other, home_ref, home_other,
     keep_a, send_a, keep_b, send_b, left_sc, right_sc, block_sc, sems,
 ):
     rows, width = entered_ref.shape
     hc = place_ref[1]
-    both = ((entered_ref, query_ref, pair_ref), (entered_other, query_other, pair_other))
-    for which, (left, query, pair) in enumerate(both):
+    for which, (left, home) in enumerate(((entered_ref, home_ref), (entered_other, home_other))):
         left_sc[:, pl.ds(which * rows, rows)] = left[...].T
-        flat_rows(query, pair, right_sc, which * rows, seqs, rows // seqs, width)
+        flat_rows(home, right_sc, which * rows, seqs, rows // seqs, width)
     for hx in range(2):
         begin = pl.multiple_of(hx * 384 + hc * 192, 64)
         for j in range(3):
@@ -660,37 +695,36 @@
                     i * 24 : (i + 1) * 24
                 ].astype(bf16)
     half = 3 * width // 2
-    copies = piece_copies(place_ref, block_sc, keep_a, send_a, sems, 0, pl.ds(0, half))
-    copies += piece_copies(place_ref, block_sc, keep_b, send_b, sems, 1, pl.ds(half, half))
+    copies = piece_copies(place_ref, block_sc, keep_a, send_a, sems.at[0], 0, pl.ds(0, half))
+    copies += piece_copies(place_ref, block_sc, keep_b, send_b, sems.at[1], 1, pl.ds(half, half))
     for copy in copies:
         copy.wait()
 
 
 def qkv_terms(here, seqs, *values):
     rows, width = values[0].shape
-    side = jax.ShapeDtypeStruct((2, 4, 24, 3 * width // 2), bf16)
-    return pl.pallas_call(
+    return single(
         partial(qkv_kernel, seqs),
-        out_shape=(side,) * 4,
-        in_specs=[SMEM] + [VMEM] * 6,
-        out_specs=(ANY,) * 4,
-        scratch_shapes=[
+        [((2, 4, 24, 3 * width // 2), bf16)] * 4,
+        values,
+        [
             pltpu.VMEM((width, 2 * rows), bf16),
             pltpu.VMEM((2 * rows, 3 * width), bf16),
             pltpu.VMEM((16, 24, 3 * width), bf16),
             pltpu.SemaphoreType.DMA((2, 16)),
         ],
-        compiler_params=pltpu.CompilerParams(vmem_limit_bytes=40 << 20),
-    )(here, *values)
+        place=here,
+        raw_out=True,
+    )
 
 
 def leave_kernel(
-    query_ref, pair_ref, x_ref, hidden_ref, mod_ref, gains_ref, weight_ref, middle_ref,
+    home_ref, x_ref, hidden_ref, mod_ref, gains_ref, weight_ref, middle_ref,
     grad_ref, small_ref, flat_ref,
 ):
     seqs, tokens, width = x_ref.shape
     devices = small_ref.shape[0]
-    flat_rows(query_ref, pair_ref, flat_ref, 0, seqs, tokens, width)
+    flat_rows(home_ref, flat_ref, 0, seqs, tokens, width)
     grad_entered = None
     for which in range(3):
         columns = pl.ds(which * width, width)
@@ -723,19 +757,17 @@
     small_ref[:, pl.ds(begin, 1)] = jnp.broadcast_to(error, (devices, 1))
 
 
-def leave(query, pair, inputs, grad_hidden, modulation, gains, weight, sums, devices):
+def leave(home, inputs, grad_hidden, modulation, gains, weight, sums, devices):
     seqs, tokens, width = inputs.shape
-    return pl.pallas_call(
+    return single(
         leave_kernel,
-        out_shape=(
-            jax.ShapeDtypeStruct((seqs, tokens, width), f32),
-            jax.ShapeDtypeStruct((devices, 512), f32),
-            jax.ShapeDtypeStruct((seqs * tokens, 3 * width), bf16),
-        ),
-        in_specs=[VMEM] * 8,
-        out_specs=(VMEM,) * 3,
-        compiler_params=pltpu.CompilerParams(vmem_limit_bytes=40 << 20),
-    )(query, pair, inputs, grad_hidden, modulation, gains, weight, sums)
+        [
+            ((seqs, tokens, width), f32),
+            ((devices, 512), f32),
+            ((seqs * tokens, 3 * width), bf16),
+        ],
+        [home, inputs, grad_hidden, modulation, gains, weight, sums],
+    )
 
 
 def unpack_kernel(
@@ -791,38 +823,67 @@
     seqs, tokens = valid_mask.shape
     devices = every.shape[0]
     sizes = (6 * width // devices, width // devices, units // devices)
-    return pl.pallas_call(
+    return single(
         partial(unpack_kernel, parts, sizes, float(seqs * length)),
-        out_shape=(
-            jax.ShapeDtypeStruct((8, 6 * width), f32),
-            jax.ShapeDtypeStruct((8, width), f32),
-            jax.ShapeDtypeStruct((8, units), f32),
-            jax.ShapeDtypeStruct((4 * parts * 8 * tokens, 1), f32),
-            jax.ShapeDtypeStruct((1, 8 * tokens), f32),
-            jax.ShapeDtypeStruct((seqs * tokens, 2), f32),
-        ),
-        in_specs=[SMEM, VMEM, VMEM],
-        out_specs=(VMEM,) * 6,
-        compiler_params=pltpu.CompilerParams(vmem_limit_bytes=40 << 20),
-    )(here, every, valid_mask)
-
-
-def block_kernel(out_ref, up_ref, down_ref, later_ref):
-    width = out_ref.shape[1]
-    later_ref[0] = out_ref[...]
-    for j in range(4):
-        later_ref[1 + j] = up_ref[:, pl.ds(j * width, width)]
-        later_ref[5 + j] = down_ref[pl.ds(j * 24, 24), :]
-
-
-def block(out_weight, up_weight, down_weight):
-    width = out_weight.shape[1]
-    return pl.pallas_call(
-        block_kernel,
-        out_shape=jax.ShapeDtypeStruct((9, 24, width), bf16),
-        in_specs=[VMEM] * 3,
-        out_specs=VMEM,
-    )(out_weight, up_weight, down_weight)
+        [
+            ((8, 6 * width), f32),
+            ((8, width), f32),
+            ((8, units), f32),
+            ((4 * parts * 8 * tokens, 1), f32),
+            ((1, 8 * tokens), f32),
+            ((seqs * tokens, 2), f32),
+        ],
+        [every, valid_mask],
+        place=here,
+    )
+
+
+def begin_kernel(embed_ref, ada_ref, vectors_ref, segments_ref, valid_ref, *refs):
+    *weights, packed_ref = refs[:-1] if len(refs) > 1 else refs
+    seqs, tokens = segments_ref.shape
+    modulation = jnp.dot(
+        embed_ref[...], ada_ref[...].astype(f32), precision=precise, preferred_element_type=f32
+    )
+    size = modulation.shape[1]
+    modulation = modulation + vectors_ref[:, pl.ds(0, size)]
+    rest = vectors_ref.shape[1] - size
+    count = jnp.sum(valid_ref[...].astype(f32), axis=1, keepdims=True)
+    count = jnp.sum(count, axis=0, keepdims=True)
+    fields = [modulation[s : s + 1] for s in range(seqs)]
+    fields.append(vectors_ref[:, pl.ds(size, rest)])
+    fields += [segments_ref[s : s + 1, :].astype(f32) for s in range(seqs)]
+    fields.append(count)
+    packed_ref[...] = jnp.zeros(packed_ref.shape, f32)
+    begin = 0
+    for field in fields:
+        columns = pl.ds(begin, field.shape[1])
+        packed_ref[:, columns] = jnp.broadcast_to(
+            field, (packed_ref.shape[0], field.shape[1])
+        )
+        begin += field.shape[1]
+    if weights:
+        out_ref, up_ref, down_ref = weights
+        later_ref = refs[-1]
+        width = out_ref.shape[1]
+        later_ref[0] = out_ref[...]
+        for j in range(4):
+            later_ref[1 + j] = up_ref[:, pl.ds(j * width, width)]
+            later_ref[5 + j] = down_ref[pl.ds(j * 24, 24), :]
+
+
+def begin_with(time_embed, ada_weight, vectors, segments, valid_mask, weights, devices):
+    seqs, tokens = segments.shape
+    columns = seqs * ada_weight.shape[1] + vectors.shape[1] - ada_weight.shape[1] + seqs * tokens + 1
+    outs = [((devices, columns + -columns % 128), f32)]
+    if weights:
+        outs.append(((9, 24, weights[0].shape[1]), bf16))
+    return single(
+        begin_kernel, outs, [time_embed, ada_weight, vectors, segments, valid_mask, *weights]
+    )
+
+
+def after(value, *others):
+    return lax.optimization_barrier((value, others))[0]
 
 
 def exchange(rows):
@@ -854,36 +915,30 @@
     queries = 8 * tokens
     here = place()
 
-    own_modulation = jnp.dot(
-        time_embed, ada_weight.astype(f32), precision=precise
-    ) + ada_bias.astype(f32)
-    fields = [
-        own_modulation.reshape(-1),
-        gain_attn.astype(f32),
-        gain_mlp.astype(f32),
-        up_bias.astype(f32),
-        down_bias.astype(f32),
-        segments.astype(f32).reshape(-1),
-        jnp.sum(valid_mask.astype(f32)).reshape(1),
-    ]
-    packed = jnp.concatenate(fields)
-    packed = jnp.pad(packed, (0, -packed.shape[0] % 128))
-    every = lax.all_to_all(
-        jnp.broadcast_to(packed, (devices, packed.shape[0])), EVERY, 0, 0, tiled=True
-    )
+    vectors = jnp.concatenate([ada_bias, gain_attn, gain_mlp, up_bias, down_bias])
+    vectors = vectors.astype(f32).reshape(1, -1)
+    weights = [] if parts > 1 else [out_weight, up_weight, down_weight]
+    packed, *later = begin_with(
+        time_embed, ada_weight, vectors, segments, valid_mask, weights, devices
+    )
+    every = lax.all_to_all(packed, EVERY, 0, 0, tiled=True)
     if parts > 1:
         full_qkv, *later = (
             lax.all_gather(w, EVERY, axis=0, tiled=True)
             for w in (qkv_weight, out_weight, up_weight, down_weight)
         )
     else:
-        later = [
-            lax.all_gather(block(out_weight, up_weight, down_weight), EVERY, axis=0, tiled=False)
-        ]
-        full_qkv, every = gather_rows(here, qkv_weight, every)
-    modulation, gains, full_up_bias, key_docs, query_docs, masks = unpack(
-        here, every, valid_mask, width, units, parts, length
-    )
+        later = [lax.all_gather(later[0], EVERY, axis=0, tiled=False)]
+        shard, packed = lax.optimization_barrier((qkv_weight, packed))
+
+    def use(every):
+        return unpack(here, every, valid_mask, width, units, parts, length)
+
+    if parts > 1:
+        used = use(every)
+    else:
+        full_qkv, used = gather_rows(here, shard, every, use)
+    modulation, gains, full_up_bias, key_docs, query_docs, masks = used
     count_all = gains[3, 0]
 
     entered, pair, query = enter(inputs, modulation, gains, full_qkv)
@@ -892,6 +947,7 @@
     if parts > 1:
         pair = lax.all_gather(pair, "rb", axis=0, tiled=True)
     pair_x = swap(pair, "hx")
+    pair_x, query = lax.optimization_barrier((pair_x, query))
     pairs = (pair, pair_x, swap(pair, "hc"), swap(pair_x, "hc"))
     attended, turned, total = attend(query, pairs, key_docs, query_docs)
 
@@ -902,46 +958,73 @@
     if parts == 1:
         terms = weight_terms(here, pack, swap(pack, "hc"), width)
         grad_came, terms = lax.optimization_barrier((grad_came, terms))
-        first_a = reduce_first(terms[0], terms[1], ORDERS[0])
-        first_b = reduce_first(terms[2], terms[3], ORDERS[1])
-
-    grad_query, keep, send = attend_back(
+        held = terms[::2]
+        firsts = [
+            swap(send, ORDERS[side][0]) for send, (_, side) in zip(terms[1::2], COLUMN_GROUPS)
+        ]
+
+    grad_query, keep, keep_x, send = attend_back(
         query, grad_came, pairs, key_docs, query_docs, turned, total
     )
-    home_query = exchange(grad_query)
-    grad_pair = keep + swap(send, "hc").astype(f32)
-    middle_row = grad_pair.shape[0] // 2
-    grad_pair = grad_pair[:middle_row] + swap(grad_pair[middle_row:].astype(bf16), "hx").astype(f32)
+    if parts == 1:
+        send, firsts[0], firsts[2] = lax.optimization_barrier((send, firsts[0], firsts[2]))
+    recv = swap(send, "hc")
+    own_rows = keep.shape[0]
+    send_x = (keep_x + recv[own_rows:].astype(f32)).astype(bf16)
+    grad_pair = keep + recv[:own_rows].astype(f32) + swap(send_x, "hx").astype(f32)
     if parts > 1:
         grad_pair = lax.psum_scatter(grad_pair, "rb", scatter_dimension=0, tiled=True)
-    grad_pair = grad_pair.astype(bf16).reshape(8, tokens, 2 * WIDTH)
+    home = jnp.concatenate(
+        [grad_pair.astype(bf16).reshape(8, tokens, 2 * WIDTH), grad_query], axis=1
+    )
     if parts == 1:
-        grad_pair, first_a, first_b = lax.optimization_barrier((grad_pair, first_a, first_b))
-        second_a = reduce_second(first_a, ORDERS[0])
-        second_b = reduce_second(first_b, ORDERS[1])
-    home_pair = exchange(grad_pair)
+        home, firsts[1] = lax.optimization_barrier((home, firsts[1]))
+        seconds = [
+            swap(
+                jnp.concatenate(
+                    [
+                        second_send(keep, recv)
+                        for keep, recv, (_, own) in zip(held, firsts, COLUMN_GROUPS)
+                        if own == side
+                    ],
+                    axis=3,
+                ),
+                ORDERS[side][1],
+            )
+            for side in (0, 1)
+        ]
+    home = exchange(home)
+    if parts == 1:
+        others = swap(entered, "hc"), swap(home, "hc")
+        terms = qkv_terms(here, seqs, entered, others[0], home, others[1])
+        seconds = after(seconds, terms)
+        second = jnp.concatenate(
+            [
+                keep[0].astype(f32) + recv[0].astype(f32)
+                for keep, recv in zip(held, firsts)
+            ],
+            axis=3,
+        ) + jnp.concatenate(seconds, axis=3).astype(f32)
+        third = third_recvs(second)
+        recvs = [swap(send, order[0]) for send, order in zip(terms[1::2], ORDERS)]
+        home = after(home, recvs)
+        second_qkv = jnp.concatenate(
+            [
+                second_total(keep, recv, swap(second_send(keep, recv), order[1]))
+                for keep, recv, order in zip(terms[::2], recvs, ORDERS)
+            ],
+            axis=2,
+        )
+        third, third_qkv = lax.optimization_barrier((third, third_recvs(second_qkv)))
+        owned_later = third_total(second, third)
+        shard_qkv = third_total(second_qkv, third_qkv)
+        shard_out = owned_later[0]
+        shard_up = owned_later[1:5].transpose(1, 0, 2).reshape(24, units)
+        shard_down = owned_later[5:].reshape(96, width)
     grad_input, small, flat = leave(
-        home_query, home_pair, inputs, grad_hidden, modulation, gains, full_qkv, sums, devices
-    )
-    if parts == 1:
-        others = swap(entered, "hc"), swap(home_query, "hc"), swap(home_pair, "hc")
-        others, second_a, second_b = lax.optimization_barrier((others, second_a, second_b))
-        terms = qkv_terms(
-            here, seqs, entered, others[0], home_query, others[1], home_pair, others[2]
-        )
-        shard_qkv = jnp.concatenate(
-            [
-                reduce_third(reduce_second(reduce_first(keep, send, order), order))
-                for keep, send, order in zip(terms[::2], terms[1::2], ORDERS)
-            ],
-            axis=1,
-        )
-        side_a = reduce_third(second_a)
-        side_b = reduce_third(second_b)
-        shard_out = side_a[0]
-        shard_up = side_a[1:].transpose(1, 0, 2).reshape(24, units)
-        shard_down = side_b.reshape(96, width)
-    else:
+        home, inputs, grad_hidden, modulation, gains, full_qkv, sums, devices
+    )
+    if parts > 1:
         base = 2 * width + units
         ends = (base + width, base + width + units)
         shard_qkv, shard_out, shard_up, shard_down = (
@@ -958,7 +1041,10 @@
                 (pack[:, 2 * width : base], pack[:, ends[1] :]),
             )
         )
-    added = jnp.sum(lax.all_to_all(small, EVERY, 0, 0, tiled=True), axis=0)
+    small = lax.all_to_all(small, EVERY, 0, 0, tiled=True)
+    if parts == 1:
+        small = after(small, second_qkv)
+    added = jnp.sum(small, axis=0)
     owned = []
     begin = 0
     sizes = [6 * width // devices * seqs] + [size // devices for size in (width, width, units, width)]

time: 349 us -> 309 us (0.89)
  waiting for transfers between devices: 108 us -> 86.5 us
  local copies, waits for them, and re-layouts: 39.2 us -> 21.4 us
  blocking collectives: 50.1 us -> 40 us
  Pallas kernels: 54.1 us -> 62.8 us
    ppermute x23 -> x24, waiting for transfers between devices: 75.8 us -> 39.7 us  [swap(): return lax.ppermute(value, axis, [(0, 1), (1, 0)])]
    unnamed x100 -> x73, local copies, waits for them, and re-layouts: 25.5 us -> 12.2 us
    all_to_all x3, waiting for transfers between devices: 0.93 us -> 12.6 us  [exchange(): return lax.all_to_all(rows, SPOT, 0, 0, tiled=True)]
    ppermute x23 -> x24, starting transfers between devices: 11.7 us -> 22.4 us  [swap(): return lax.ppermute(value, axis, [(0, 1), (1, 0)])]
    all_to_all x3 -> x2, blocking collectives: 50.1 us -> 40 us  [exchange(): return lax.all_to_all(rows, SPOT, 0, 0, tiled=True)]
    ppermute x15 -> x9, starting transfers between devices: 25.7 us -> 16.4 us  [turn(): lax.ppermute(value, axis, [(i, (i - step) % size) for i in range(size)])]
    pallas_call x8, Pallas kernels: 33.9 us -> 40.1 us  [single(): pl.pallas_call(kernel, grid=(1,), out_shape=tuple((jax.ShapeDtypeStruct(*...]
    all_to_all x2, waiting for transfers between devices: 13.2 us -> 18.1 us  [the longest x1 12.5 us: on_device(): small = lax.all_to_all(small, EVERY, 0, 0, tiled=True)]
  transfers between devices with their start and end apart: 44 -> 39, of which waited for: 19 -> 18; matrix products, arithmetic and copies ran while one was open for 10% -> 8% of each run, Pallas kernels for 8% -> 16%
where the time goes in v5:
time: 309 us; the launch traced here: 307 us
  waiting for transfers between devices  86.5 us (28%)
  Pallas kernels  62.8 us (20%)
  starting transfers between devices  59.9 us (19%)
  blocking collectives  40 us (13%)
  local copies, waits for them, and re-layouts  21.4 us (7%)
  other arithmetic  19.9 us (6%)
  between operations  17 us (6%)
    pallas_call x8, Pallas kernels, single(): pl.pallas_call(kernel, grid=(1,), out_shape=tuple((jax.ShapeDtypeStruct(*...  40.1 us
    all_to_all x2, blocking collectives, exchange(): return lax.all_to_all(rows, SPOT, 0, 0, tiled=True)  40 us
    ppermute x24, waiting for transfers between devices, swap(): return lax.ppermute(value, axis, [(0, 1), (1, 0)])  39.7 us
    ppermute x24, starting transfers between devices, swap(): return lax.ppermute(value, axis, [(0, 1), (1, 0)])  22.4 us
    ppermute x9, starting transfers between devices, turn(): lax.ppermute(value, axis, [(i, (i - step) % size) for i in range(size)])  16.4 us
    ppermute x9, waiting for transfers between devices, turn(): lax.ppermute(value, axis, [(i, (i - step) % size) for i in range(size)])  16.1 us
    pallas_call x1, Pallas kernels, attend_back(): pl.pallas_call(partial(backward_kernel, starts), grid=(steps,), out_shape...  12.8 us
    all_to_all x3, waiting for transfers between devices, exchange(): return lax.all_to_all(rows, SPOT, 0, 0, tiled=True)  12.6 us
  transfers between devices with their start and end apart: 39, of which 18 were waited for; matrix products, arithmetic and copies ran while one was open for 8% of the time, Pallas kernels for 16%

profile of v5, /device:TPU:0, one launch (start us, length us, event | category | flops | bytes accessed | tf_op | source)
XLA Modules:
  0.0 307.4 jit_solution(4890140828042984528)
XLA Ops:
  12.8 5.1 %collective-permute-start = (bf16[24,2304]{1,0:T(8,128)(2,1)}, bf16[24,2304]{1,0:T(8,128)(2,1)S(1)}, u32[]{:S(2)}, u32[]{:S(2)}) collective-permute-start(bf16[24,2304]{1,0:T(8,128)(2,1)} %param.23), channel_id=1, source_target_pairs={{0,6},{2,0},{4,2},{6,4},{1,7},{3,1},{5,3},{7,5},{8,14},{10,8},{12,... | collective-permute-start | bytes 331784 | tf_op jit(solution)/shard_map/ppermute | solution.py:49
  18.9 2.8 collective-permute-done
  21.7 6.2 %collective-permute-done.1 = bf16[24,2304]{1,0:T(8,128)(2,1)S(1)} collective-permute-done((bf16[24,2304]{1,0:T(8,128)(2,1)}, bf16[24,2304]{1,0:T(8,128)(2,1)S(1)}, u32[]{:S(2)}, u32[]{:S(2)}) %collective-permute-start.1) | collective-permute-done | bytes 110624 | tf_op jit(solution)/shard_map/ppermute | solution.py:49
  31.2 6.3 %all-to-all-start = ((f32[32,1,640]{2,1,0:T(1,128)}), f32[32,1,640]{2,1,0:T(1,128)S(1)}, u32[]{:S(2)}, u32[]{:S(2)}) async-start(f32[32,1,640]{2,1,0:T(1,128)} %copy.36), calls=%async_computation | async-start | bytes 163840 | tf_op jit(solution)/shard_map/all_to_all | solution.py:924
  39.3 5.6 %all-to-all-done = f32[32,1,640]{2,1,0:T(1,128)S(1)} async-done(((f32[32,1,640]{2,1,0:T(1,128)}), f32[32,1,640]{2,1,0:T(1,128)S(1)}, u32[]{:S(2)}, u32[]{:S(2)}) %all-to-all-start) | async-done | bytes 81952 | tf_op jit(solution)/shard_map/all_to_all | solution.py:924
  47.0 2.5 collective-permute-start.6
  50.8 2.4 shard_map.247
  53.3 11.6 %collective-permute-done.6 = bf16[2,4,24,1152]{3,2,1,0:T(8,128)(2,1)S(1)} collective-permute-done((bf16[2,4,24,1152]{3,2,1,0:T(8,128)(2,1)S(1)}, bf16[2,4,24,1152]{3,2,1,0:T(8,128)(2,1)S(1)}, u32[]{:S(2)}, u32[]{:S(2)}) %collective-permute-start.6) | collective-permute-done | bytes 442400 | tf_op jit(solution)/shard_map/ppermute | solution.py:44
  69.8 3.1 %shard_map.248 = bf16[32,24,2304]{2,1,0:T(8,128)(2,1)S(1)} custom-call(s32[5]{0:T(128)S(1)} %stack.88.place_ref, bf16[2,2,4,24,1152]{4,3,2,1,0:T(8,128)(2,1)} %copy-done.15, bf16[2,2,4,24,1152]{4,3,2,1,0:T(8,128)(2,1)} %copy-done.23, bf16[2,2,4,24,1152]{4,3,2,1,0:T(8,128)(2,1)} %copy-done.14, bf16[2,2,4,24,1152]{4,3,2,1,0:T(8,128)(2,1)} %copy-done.24), custom_call_target="tpu_custom_call" | custom-call | tf_op jit(solution)/shard_map/pallas_call | solution.py:77
  74.8 4.6 %shard_map.249 = (bf16[128,768]{1,0:T(8,128)(2,1)S(1)}, bf16[8,64,384]{2,1,0:T(8,128)(2,1)S(1)}, bf16[8,32,384]{2,1,0:T(8,128)(2,1)}) custom-call(bf16[2,64,768]{2,1,0:T(8,128)(2,1)} %x_ref.5, f32[8,4608]{1,0:T(8,128)} %copy-done.2, f32[8,768]{1,0:T(8,128)} %copy-done.4, bf16[768,2304]{1,0:T(8,128)(2,1)} %bitcast.96), custom_call_target="tpu_custom_call" | custom-call | tf_op jit(solution)/shard_map/pallas_call | solution.py:77
  79.4 28.4 %all_to_all.49 = bf16[8,64,384]{2,1,0:T(8,128)(2,1)S(1)} all-to-all(bf16[8,64,384]{2,1,0:T(8,128)(2,1)S(1)} %get-tuple-element.103), channel_id=1, replica_groups=mesh['hx'=2,'hc'=2,'rb'=1,'sz'=4,'sy'=2] {'sz','sy'}, dimensions={0} | all-to-all | bytes 786432 | tf_op jit(solution)/shard_map/all_to_all | solution.py:890
  108.8 3.5 %all-to-all-start.2 = ((bf16[8,32,384]{2,1,0:T(8,128)(2,1)}), bf16[8,32,384]{2,1,0:T(8,128)(2,1)S(1)}, u32[]{:S(2)}, u32[]{:S(2)}) async-start(bf16[8,32,384]{2,1,0:T(8,128)(2,1)} %get-tuple-element.104), calls=%async_computation.2 | async-start | bytes 393216 | tf_op jit(solution)/shard_map/all_to_all | solution.py:890
  112.4 7.8 %all-to-all-done.2.came_ref = bf16[8,32,384]{2,1,0:T(8,128)(2,1)S(1)} async-done(((bf16[8,32,384]{2,1,0:T(8,128)(2,1)}), bf16[8,32,384]{2,1,0:T(8,128)(2,1)S(1)}, u32[]{:S(2)}, u32[]{:S(2)}) %all-to-all-start.2) | async-done | bytes 196640 | tf_op jit(solution)/shard_map/all_to_all | solution.py:890
  122.8 9.8 %shard_map.250 = (bf16[8,32,384]{2,1,0:T(8,128)(2,1)S(1)}, f32[192,512]{1,0:T(8,128)S(1)}, f32[8,512]{1,0:T(8,128)S(1)}) custom-call(bf16[8,32,384]{2,1,0:T(8,128)(2,1)} %copy-done.17, bf16[512,384]{1,0:T(8,128)(2,1)} %bitcast.103, bf16[512,384]{1,0:T(8,128)(2,1)} %copy-done.18, bf16[512,384]{1,0:T(8,128)(2,1)} %copy-done.19, bf16[512,384]{1,0:T(8,128)(2,1)} %copy-done.20, ...), custom_call_target="tpu_custom_call" | custom-call | tf_op jit(solution)/shard_map/pallas_call | solution.py:321
  133.9 11.6 %all_to_all.50.came_ref = bf16[8,32,384]{2,1,0:T(8,128)(2,1)} all-to-all(bf16[8,32,384]{2,1,0:T(8,128)(2,1)S(1)} %get-tuple-element.109), channel_id=1, replica_groups=mesh['hx'=2,'hc'=2,'rb'=1,'sz'=4,'sy'=2] {'sz','sy'}, dimensions={0} | all-to-all | bytes 393216 | tf_op jit(solution)/shard_map/all_to_all | solution.py:890
  145.5 12.2 %shard_map.251 = (bf16[2,64,768]{2,1,0:T(8,128)(2,1)}, f32[128,768]{1,0:T(8,128)}, bf16[8,32,384]{2,1,0:T(8,128)(2,1)}, bf16[128,9216]{1,0:T(8,128)(2,1)}, f32[16,768]{1,0:T(8,128)}) custom-call(bf16[8,32,384]{2,1,0:T(8,128)(2,1)} %all_to_all.50.came_ref, bf16[2,64,768]{2,1,0:T(8,128)(2,1)} %x_ref.5, bf16[2,64,768]{2,1,0:T(8,128)(2,1)} %teacher_ref.1, ...), custom_call_target="tpu_custom_call" | custom-call | tf_op jit(solution)/shard_map/pallas_call | solution.py:77
  157.7 3.6 %all-to-all-start.4 = ((bf16[8,32,384]{2,1,0:T(8,128)(2,1)}), bf16[8,32,384]{2,1,0:T(8,128)(2,1)S(1)}, u32[]{:S(2)}, u32[]{:S(2)}) async-start(bf16[8,32,384]{2,1,0:T(8,128)(2,1)} %get-tuple-element.114), calls=%async_computation.4 | async-start | bytes 393216 | tf_op jit(solution)/shard_map/all_to_all | solution.py:890
  163.8 7.5 %shard_map.252 = (bf16[2,4,9,24,128]{4,3,2,1,0:T(8,128)(2,1)}, bf16[2,4,9,24,128]{4,3,2,1,0:T(8,128)(2,1)}, bf16[2,4,9,24,256]{4,3,2,1,0:T(8,128)(2,1)}, bf16[2,...) custom-call(s32[5]{0:T(128)} %copy-done.9, ...), custom_call_target="tpu_custom_call" | custom-call | tf_op jit(solution)/shard_map/pallas_call | solution.py:77
  173.4 12.8 %shard_map.253 = (bf16[8,32,384]{2,1,0:T(8,128)(2,1)S(1)}, f32[512,384]{1,0:T(8,128)S(1)}, f32[512,384]{1,0:T(8,128)S(1)}, bf16[1024,384]{1,0:T(8,128)(2,1)S(1)}) custom-call(bf16[8,32,384]{2,1,0:T(8,128)(2,1)} %copy-done.17, bf16[8,32,384]{2,1,0:T(8,128)(2,1)} %copy-done.26, bf16[512,384]{1,0:T(8,128)(2,1)} %bitcast.104, bf16[512,384]{1,0:T(8,128)(2,1)} %copy-done.18, ...), custom_call_target="tpu_custom_call" | custom-call | tf_op jit(solution)/shard_map/pallas_call | solution.py:413
  191.7 9.0 %collective-permute-done.16 = bf16[512,384]{1,0:T(8,128)(2,1)S(1)} collective-permute-done((bf16[512,384]{1,0:T(8,128)(2,1)S(1)}, bf16[512,384]{1,0:T(8,128)(2,1)S(1)}, u32[]{:S(2)}, u32[]{:S(2)}) %collective-permute-start.16) | collective-permute-done | bytes 393248 | tf_op jit(solution)/shard_map/ppermute | solution.py:44
  201.7 6.7 %collective-permute-done.17 = bf16[2,4,9,24,256]{4,3,2,1,0:T(8,128)(2,1)S(1)} collective-permute-done((bf16[2,4,9,24,256]{4,3,2,1,0:T(8,128)(2,1)S(1)}, bf16[2,4,9,24,256]{4,3,2,1,0:T(8,128)(2,1)S(1)}, u32[]{:S(2)}, u32[]{:S(2)}) %collective-permute-start.17) | collective-permute-done | bytes 884768 | tf_op jit(solution)/shard_map/ppermute | solution.py:44
  208.4 4.2 %all-to-all-start.5 = ((bf16[8,96,384]{2,1,0:T(8,128)(2,1)}), bf16[8,96,384]{2,1,0:T(8,128)(2,1)S(1)}, u32[]{:S(2)}, u32[]{:S(2)}) async-start(bf16[8,96,384]{2,1,0:T(8,128)(2,1)} %pad_maximum_fusion.5), calls=%async_computation.5 | async-start | bytes 1179648 | tf_op jit(solution)/shard_map/all_to_all | solution.py:890
  214.9 4.0 %collective-permute-done.24 = bf16[2,4,9,24,256]{4,3,2,1,0:T(8,128)(2,1)S(1)} collective-permute-done((bf16[2,4,9,24,256]{4,3,2,1,0:T(8,128)(2,1)}, bf16[2,4,9,24,256]{4,3,2,1,0:T(8,128)(2,1)S(1)}, u32[]{:S(2)}, u32[]{:S(2)}) %collective-permute-start.24) | collective-permute-done | bytes 884768 | tf_op jit(solution)/shard_map/ppermute | solution.py:44
  223.6 4.8 %all-to-all-done.5.home_ref = bf16[8,96,384]{2,1,0:T(8,128)(2,1)S(1)} async-done(((bf16[8,96,384]{2,1,0:T(8,128)(2,1)}), bf16[8,96,384]{2,1,0:T(8,128)(2,1)S(1)}, u32[]{:S(2)}, u32[]{:S(2)}) %all-to-all-start.5) | async-done | bytes 589856 | tf_op jit(solution)/shard_map/all_to_all | solution.py:890
  232.2 3.6 %shard_map.254 = (bf16[2,4,24,1152]{3,2,1,0:T(8,128)(2,1)S(1)}, bf16[2,4,24,1152]{3,2,1,0:T(8,128)(2,1)S(1)}, bf16[2,4,24,1152]{3,2,1,0:T(8,128)(2,1)S(1)}, bf16[2,4,24,1152]{3,2,1,0:T(8,128)(2,1)S(1)}) custom-call(s32[5]{0:T(128)S(1)} %copy-done.10, bf16[128,768]{1,0:T(8,128)(2,1)} %copy-done.5, bf16[128,768]{1,0:T(8,128)(2,1)} %copy-done.32, ...), custom_call_target="tpu_custom_call" | custom-call | tf_op jit(solution)/shard_map/pallas_call | solution.py:77
  242.6 3.2 %collective-permute-start.28 = (bf16[9,24,768]{2,1,0:T(8,128)(2,1)}, bf16[9,24,768]{2,1,0:T(8,128)(2,1)}, u32[]{:S(2)}, u32[]{:S(2)}) collective-permute-start(bf16[9,24,768]{2,1,0:T(8,128)(2,1)} %get-tuple-element.170), channel_id=1, source_target_pairs={{0,4},{2,6},{4,0},{6,2},{1,5},{3,7},{5,1},{7,3},{8,12},{10,14},{12... | collective-permute-start | bytes 995336 | tf_op jit(solution)/shard_map/ppermute | solution.py:49
  245.8 2.5 collective-permute-start.29
  251.1 4.8 %shard_map.255 = (f32[2,64,768]{2,1,0:T(8,128)}, f32[32,512]{1,0:T(8,128)S(1)}, bf16[128,2304]{1,0:T(8,128)(2,1)}) custom-call(bf16[8,96,384]{2,1,0:T(8,128)(2,1)} %copy-done.12, bf16[2,64,768]{2,1,0:T(8,128)(2,1)} %x_ref.5, f32[128,768]{1,0:T(8,128)} %get-tuple-element.140.hidden_ref, f32[8,4608]{1,0:T(8,128)} %copy-done.2, f32[8,768]{1,0:T(8,128)} %copy-done.4, ...), custom_call_target="tpu_custom_call" | custom-call | tf_op jit(solution)/shard_map/pallas_call | solution.py:77
  256.6 3.3 %all-to-all-start.6 = ((f32[32,1,512]{2,1,0:T(1,128)}), f32[32,1,512]{2,1,0:T(1,128)}, u32[]{:S(2)}, u32[]{:S(2)}) async-start(f32[32,1,512]{2,1,0:T(1,128)} %copy.37), calls=%async_computation.6 | async-start | bytes 131072 | tf_op jit(solution)/shard_map/all_to_all | solution.py:1044
  263.2 12.5 %all-to-all-done.6 = f32[32,1,512]{2,1,0:T(1,128)} async-done(((f32[32,1,512]{2,1,0:T(1,128)}), f32[32,1,512]{2,1,0:T(1,128)}, u32[]{:S(2)}, u32[]{:S(2)}) %all-to-all-start.6) | async-done | bytes 65568 | tf_op jit(solution)/shard_map/all_to_all | solution.py:1044
  288.1 3.2 %collective-permute-done.30 = bf16[24,2304]{1,0:T(8,128)(2,1)S(1)} collective-permute-done((bf16[24,2304]{1,0:T(8,128)(2,1)S(1)}, bf16[24,2304]{1,0:T(8,128)(2,1)S(1)}, u32[]{:S(2)}, u32[]{:S(2)}) %collective-permute-start.30) | collective-permute-done | bytes 110624 | tf_op jit(solution)/shard_map/ppermute | solution.py:49
  291.3 3.9 %collective-permute-done.31 = bf16[24,2304]{1,0:T(8,128)(2,1)S(1)} collective-permute-done((bf16[24,2304]{1,0:T(8,128)(2,1)S(1)}, bf16[24,2304]{1,0:T(8,128)(2,1)S(1)}, u32[]{:S(2)}, u32[]{:S(2)}) %collective-permute-start.31) | collective-permute-done | bytes 110624 | tf_op jit(solution)/shard_map/ppermute | solution.py:49
  (174 shorter events, 77.3 us)
Async XLA Ops:
  7.2 138.3 %all-gather.3.cloned.1.call-start = ((), (), s32[]{:S(2)}) async-start(), calls=%async_computation.7 | async-start | bytes 10948608 | tf_op jit(solution)/shard_map/all_gather | solution.py:931
  12.8 8.9 %collective-permute-start = (bf16[24,2304]{1,0:T(8,128)(2,1)}, bf16[24,2304]{1,0:T(8,128)(2,1)S(1)}, u32[]{:S(2)}, u32[]{:S(2)}) collective-permute-start(bf16[24,2304]{1,0:T(8,128)(2,1)} %param.23), channel_id=1, source_target_pairs={{0,6},{2,0},{4,2},{6,4},{1,7},{3,1},{5,3},{7,5},{8,14},{10,8},{12,... | collective-permute-start | bytes 331784 | tf_op jit(solution)/shard_map/ppermute | solution.py:49
  17.9 9.9 %collective-permute-start.1 = (bf16[24,2304]{1,0:T(8,128)(2,1)}, bf16[24,2304]{1,0:T(8,128)(2,1)S(1)}, u32[]{:S(2)}, u32[]{:S(2)}) collective-permute-start(bf16[24,2304]{1,0:T(8,128)(2,1)} %param.23), channel_id=1, source_target_pairs={{0,4},{2,6},{4,0},{6,2},{1,5},{3,7},{5,1},{7,3},{8,12},{10,14},{12... | collective-permute-start | bytes 331784 | tf_op jit(solution)/shard_map/ppermute | solution.py:49
  17.9 9.9 %collective-permute-start.2 = (bf16[24,2304]{1,0:T(8,128)(2,1)}, bf16[24,2304]{1,0:T(8,128)(2,1)S(1)}, u32[]{:S(2)}, u32[]{:S(2)}) collective-permute-start(bf16[24,2304]{1,0:T(8,128)(2,1)} %param.23), channel_id=1, source_target_pairs={{0,2},{2,4},{4,6},{6,0},{1,3},{3,5},{5,7},{7,1},{8,10},{10,12},{12... | collective-permute-start | bytes 331784 | tf_op jit(solution)/shard_map/ppermute | solution.py:49
  28.9 16.7 %collective-permute-start.4 = (bf16[4,24,1152]{2,1,0:T(8,128)(2,1)S(1)}, bf16[4,24,1152]{2,1,0:T(8,128)(2,1)S(1)}, u32[]{:S(2)}, u32[]{:S(2)}) collective-permute-start(bf16[4,24,1152]{2,1,0:T(8,128)(2,1)S(1)} %get-tuple-element.183), channel_id=1, source_target_pairs={{0,1},{1,0},{2,3},{3,2},{4,5},{5,4},{6,7},{7,6},{8,9},{9,8},{10,11... | collective-permute-start | bytes 663560 | tf_op jit(solution)/shard_map/ppermute | solution.py:44
  31.2 13.7 %all-to-all-start = ((f32[32,1,640]{2,1,0:T(1,128)}), f32[32,1,640]{2,1,0:T(1,128)S(1)}, u32[]{:S(2)}, u32[]{:S(2)}) async-start(f32[32,1,640]{2,1,0:T(1,128)} %copy.36), calls=%async_computation | async-start | bytes 163840 | tf_op jit(solution)/shard_map/all_to_all | solution.py:924
  37.5 9.5 %collective-permute-start.3 = (bf16[4,24,1152]{2,1,0:T(8,128)(2,1)S(1)}, bf16[4,24,1152]{2,1,0:T(8,128)(2,1)S(1)}, u32[]{:S(2)}, u32[]{:S(2)}) collective-permute-start(bf16[4,24,1152]{2,1,0:T(8,128)(2,1)S(1)} %get-tuple-element.184), channel_id=1, source_target_pairs={{0,16},{16,0},{1,17},{17,1},{2,18},{18,2},{3,19},{19,3},{4,20},{20... | collective-permute-start | bytes 663560 | tf_op jit(solution)/shard_map/ppermute | solution.py:44
  47.0 18.0 %collective-permute-start.6 = (bf16[2,4,24,1152]{3,2,1,0:T(8,128)(2,1)S(1)}, bf16[2,4,24,1152]{3,2,1,0:T(8,128)(2,1)S(1)}, u32[]{:S(2)}, u32[]{:S(2)}) collective-permute-start(bf16[2,4,24,1152]{3,2,1,0:T(8,128)(2,1)S(1)} %pad_maximum_fusion.8), channel_id=1, source_target_pairs={{0,16},{16,0},{1,17},{17,1},{2,18},{18,2},{3,19},{19,3},{4,20},{20... | collective-permute-start | bytes 1327112 | tf_op jit(solution)/shard_map/ppermute | solution.py:44
  49.5 15.5 %collective-permute-start.5 = (bf16[2,4,24,1152]{3,2,1,0:T(8,128)(2,1)S(1)}, bf16[2,4,24,1152]{3,2,1,0:T(8,128)(2,1)S(1)}, u32[]{:S(2)}, u32[]{:S(2)}) collective-permute-start(bf16[2,4,24,1152]{3,2,1,0:T(8,128)(2,1)S(1)} %pad_maximum_fusion.7), channel_id=1, source_target_pairs={{0,1},{1,0},{2,3},{3,2},{4,5},{5,4},{6,7},{7,6},{8,9},{9,8},{10,11... | collective-permute-start | bytes 1327112 | tf_op jit(solution)/shard_map/ppermute | solution.py:44
  107.7 12.4 %collective-permute-start.9 = (bf16[512,384]{1,0:T(8,128)(2,1)S(1)}, bf16[512,384]{1,0:T(8,128)(2,1)S(1)}, u32[]{:S(2)}, u32[]{:S(2)}) collective-permute-start(bf16[512,384]{1,0:T(8,128)(2,1)S(1)} %bitcast.101), channel_id=1, source_target_pairs={{0,16},{16,0},{1,17},{17,1},{2,18},{18,2},{3,19},{19,3},{4,20},{20... | collective-permute-start | bytes 1179656 | tf_op jit(solution)/shard_map/ppermute | solution.py:44
  108.8 11.4 %all-to-all-start.2 = ((bf16[8,32,384]{2,1,0:T(8,128)(2,1)}), bf16[8,32,384]{2,1,0:T(8,128)(2,1)S(1)}, u32[]{:S(2)}, u32[]{:S(2)}) async-start(bf16[8,32,384]{2,1,0:T(8,128)(2,1)} %get-tuple-element.104), calls=%async_computation.2 | async-start | bytes 393216 | tf_op jit(solution)/shard_map/all_to_all | solution.py:890
  112.3 7.9 %collective-permute-start.10 = (bf16[512,384]{1,0:T(8,128)(2,1)S(1)}, bf16[512,384]{1,0:T(8,128)(2,1)S(1)}, u32[]{:S(2)}, u32[]{:S(2)}) collective-permute-start(bf16[512,384]{1,0:T(8,128)(2,1)S(1)} %bitcast.102), channel_id=1, source_target_pairs={{0,8},{8,0},{1,9},{9,1},{2,10},{10,2},{3,11},{11,3},{4,12},{12,4},... | collective-permute-start | bytes 1179656 | tf_op jit(solution)/shard_map/ppermute | solution.py:44
  157.7 13.7 %all-to-all-start.4 = ((bf16[8,32,384]{2,1,0:T(8,128)(2,1)}), bf16[8,32,384]{2,1,0:T(8,128)(2,1)S(1)}, u32[]{:S(2)}, u32[]{:S(2)}) async-start(bf16[8,32,384]{2,1,0:T(8,128)(2,1)} %get-tuple-element.114), calls=%async_computation.4 | async-start | bytes 393216 | tf_op jit(solution)/shard_map/all_to_all | solution.py:890
  171.4 14.9 %collective-permute-start.13 = (bf16[2,4,9,24,128]{4,3,2,1,0:T(8,128)(2,1)}, bf16[2,4,9,24,128]{4,3,2,1,0:T(8,128)(2,1)S(1)}, u32[]{:S(2)}, u32[]{:S(2)}) collective-permute-start(bf16[2,4,9,24,128]{4,3,2,1,0:T(8,128)(2,1)} %get-tuple-element.129), channel_id=1, source_target_pairs={{0,1},{1,0},{2,3},{3,2},{4,5},{5,4},{6,7},{7,6},{8,9},{9,8},{10,11... | collective-permute-start | bytes 1327112 | tf_op jit(solution)/shard_map/ppermute | solution.py:44
  172.4 13.8 %collective-permute-start.14 = (bf16[2,4,9,24,128]{4,3,2,1,0:T(8,128)(2,1)}, bf16[2,4,9,24,128]{4,3,2,1,0:T(8,128)(2,1)S(1)}, u32[]{:S(2)}, u32[]{:S(2)}) collective-permute-start(bf16[2,4,9,24,128]{4,3,2,1,0:T(8,128)(2,1)} %get-tuple-element.130), channel_id=1, source_target_pairs={{0,16},{16,0},{1,17},{17,1},{2,18},{18,2},{3,19},{19,3},{4,20},{20... | collective-permute-start | bytes 1327112 | tf_op jit(solution)/shard_map/ppermute | solution.py:44
  186.4 22.1 %collective-permute-start.17 = (bf16[2,4,9,24,256]{4,3,2,1,0:T(8,128)(2,1)S(1)}, bf16[2,4,9,24,256]{4,3,2,1,0:T(8,128)(2,1)S(1)}, u32[]{:S(2)}, u32[]{:S(2)}) collective-permute-start(bf16[2,4,9,24,256]{4,3,2,1,0:T(8,128)(2,1)S(1)} %copy-done.34), channel_id=1, source_target_pairs={{0,1},{1,0},{2,3},{3,2},{4,5},{5,4},{6,7},{7,6},{8,9},{9,8},{10,11... | collective-permute-start | bytes 2654216 | tf_op jit(solution)/shard_map/ppermute | solution.py:44
  188.7 12.0 %collective-permute-start.16 = (bf16[512,384]{1,0:T(8,128)(2,1)S(1)}, bf16[512,384]{1,0:T(8,128)(2,1)S(1)}, u32[]{:S(2)}, u32[]{:S(2)}) collective-permute-start(bf16[512,384]{1,0:T(8,128)(2,1)S(1)} %add_convert_fusion.3), channel_id=1, source_target_pairs={{0,16},{16,0},{1,17},{17,1},{2,18},{18,2},{3,19},{19,3},{4,20},{20... | collective-permute-start | bytes 1179656 | tf_op jit(solution)/shard_map/ppermute | solution.py:44
  189.9 29.0 %collective-permute-start.24 = (bf16[2,4,9,24,256]{4,3,2,1,0:T(8,128)(2,1)}, bf16[2,4,9,24,256]{4,3,2,1,0:T(8,128)(2,1)S(1)}, u32[]{:S(2)}, u32[]{:S(2)}) collective-permute-start(bf16[2,4,9,24,256]{4,3,2,1,0:T(8,128)(2,1)} %get-tuple-element.154), channel_id=1, source_target_pairs={{0,16},{16,0},{1,17},{17,1},{2,18},{18,2},{3,19},{19,3},{4,20},{20... | collective-permute-start | bytes 2654216 | tf_op jit(solution)/shard_map/ppermute | solution.py:44
  208.4 19.9 %all-to-all-start.5 = ((bf16[8,96,384]{2,1,0:T(8,128)(2,1)}), bf16[8,96,384]{2,1,0:T(8,128)(2,1)S(1)}, u32[]{:S(2)}, u32[]{:S(2)}) async-start(bf16[8,96,384]{2,1,0:T(8,128)(2,1)} %pad_maximum_fusion.5), calls=%async_computation.5 | async-start | bytes 1179648 | tf_op jit(solution)/shard_map/all_to_all | solution.py:890
  220.1 18.3 %collective-permute-start.26 = (bf16[4,9,24,384]{3,2,1,0:T(8,128)(2,1)S(1)}, bf16[4,9,24,384]{3,2,1,0:T(8,128)(2,1)}, u32[]{:S(2)}, u32[]{:S(2)}) collective-permute-start(bf16[4,9,24,384]{3,2,1,0:T(8,128)(2,1)S(1)} %pad_maximum_fusion.4), channel_id=1, source_target_pairs={{0,1},{1,0},{2,3},{3,2},{4,5},{5,4},{6,7},{7,6},{8,9},{9,8},{10,11... | collective-permute-start | bytes 1990664 | tf_op jit(solution)/shard_map/ppermute | solution.py:44
  222.4 16.0 %collective-permute-start.25 = (bf16[4,9,24,384]{3,2,1,0:T(8,128)(2,1)S(1)}, bf16[4,9,24,384]{3,2,1,0:T(8,128)(2,1)}, u32[]{:S(2)}, u32[]{:S(2)}) collective-permute-start(bf16[4,9,24,384]{3,2,1,0:T(8,128)(2,1)S(1)} %pad_maximum_fusion.3), channel_id=1, source_target_pairs={{0,16},{16,0},{1,17},{17,1},{2,18},{18,2},{3,19},{19,3},{4,20},{20... | collective-permute-start | bytes 1990664 | tf_op jit(solution)/shard_map/ppermute | solution.py:44
  235.8 12.4 %collective-permute-start.21 = (bf16[2,4,24,1152]{3,2,1,0:T(8,128)(2,1)S(1)}, bf16[2,4,24,1152]{3,2,1,0:T(8,128)(2,1)S(1)}, u32[]{:S(2)}, u32[]{:S(2)}) collective-permute-start(bf16[2,4,24,1152]{3,2,1,0:T(8,128)(2,1)S(1)} %get-tuple-element.138), channel_id=1, source_target_pairs={{0,16},{16,0},{1,17},{17,1},{2,18},{18,2},{3,19},{19,3},{4,20},{20... | collective-permute-start | bytes 1327112 | tf_op jit(solution)/shard_map/ppermute | solution.py:44
  237.0 13.4 %collective-permute-start.20 = (bf16[2,4,24,1152]{3,2,1,0:T(8,128)(2,1)S(1)}, bf16[2,4,24,1152]{3,2,1,0:T(8,128)(2,1)S(1)}, u32[]{:S(2)}, u32[]{:S(2)}) collective-permute-start(bf16[2,4,24,1152]{3,2,1,0:T(8,128)(2,1)S(1)} %get-tuple-element.137), channel_id=1, source_target_pairs={{0,1},{1,0},{2,3},{3,2},{4,5},{5,4},{6,7},{7,6},{8,9},{9,8},{10,11... | collective-permute-start | bytes 1327112 | tf_op jit(solution)/shard_map/ppermute | solution.py:44
  241.9 43.7 %collective-permute-start.27 = (bf16[9,24,768]{2,1,0:T(8,128)(2,1)}, bf16[9,24,768]{2,1,0:T(8,128)(2,1)}, u32[]{:S(2)}, u32[]{:S(2)}) collective-permute-start(bf16[9,24,768]{2,1,0:T(8,128)(2,1)} %get-tuple-element.171), channel_id=1, source_target_pairs={{0,2},{2,4},{4,6},{6,0},{1,3},{3,5},{5,7},{7,1},{8,10},{10,12},{12... | collective-permute-start | bytes 995336 | tf_op jit(solution)/shard_map/ppermute | solution.py:49
  242.6 45.4 %collective-permute-start.28 = (bf16[9,24,768]{2,1,0:T(8,128)(2,1)}, bf16[9,24,768]{2,1,0:T(8,128)(2,1)}, u32[]{:S(2)}, u32[]{:S(2)}) collective-permute-start(bf16[9,24,768]{2,1,0:T(8,128)(2,1)} %get-tuple-element.170), channel_id=1, source_target_pairs={{0,4},{2,6},{4,0},{6,2},{1,5},{3,7},{5,1},{7,3},{8,12},{10,14},{12... | collective-permute-start | bytes 995336 | tf_op jit(solution)/shard_map/ppermute | solution.py:49
  245.8 42.3 %collective-permute-start.29 = (bf16[9,24,768]{2,1,0:T(8,128)(2,1)}, bf16[9,24,768]{2,1,0:T(8,128)(2,1)}, u32[]{:S(2)}, u32[]{:S(2)}) collective-permute-start(bf16[9,24,768]{2,1,0:T(8,128)(2,1)} %get-tuple-element.169), channel_id=1, source_target_pairs={{0,6},{2,0},{4,2},{6,4},{1,7},{3,1},{5,3},{7,5},{8,14},{10,8},{12,... | collective-permute-start | bytes 995336 | tf_op jit(solution)/shard_map/ppermute | solution.py:49
  249.1 32.0 %collective-permute-start.23 = (bf16[4,24,1152]{2,1,0:T(8,128)(2,1)}, bf16[4,24,1152]{2,1,0:T(8,128)(2,1)}, u32[]{:S(2)}, u32[]{:S(2)}) collective-permute-start(bf16[4,24,1152]{2,1,0:T(8,128)(2,1)} %fusion.6), channel_id=1, source_target_pairs={{0,1},{1,0},{2,3},{3,2},{4,5},{5,4},{6,7},{7,6},{8,9},{9,8},{10,11... | collective-permute-start | bytes 663560 | tf_op jit(solution)/shard_map/ppermute | solution.py:44
  256.6 19.1 %all-to-all-start.6 = ((f32[32,1,512]{2,1,0:T(1,128)}), f32[32,1,512]{2,1,0:T(1,128)}, u32[]{:S(2)}, u32[]{:S(2)}) async-start(f32[32,1,512]{2,1,0:T(1,128)} %copy.37), calls=%async_computation.6 | async-start | bytes 131072 | tf_op jit(solution)/shard_map/all_to_all | solution.py:1044
  261.6 20.6 %collective-permute-start.22 = (bf16[4,24,1152]{2,1,0:T(8,128)(2,1)}, bf16[4,24,1152]{2,1,0:T(8,128)(2,1)}, u32[]{:S(2)}, u32[]{:S(2)}) collective-permute-start(bf16[4,24,1152]{2,1,0:T(8,128)(2,1)} %fusion.5), channel_id=1, source_target_pairs={{0,16},{16,0},{1,17},{17,1},{2,18},{18,2},{3,19},{19,3},{4,20},{20... | collective-permute-start | bytes 663560 | tf_op jit(solution)/shard_map/ppermute | solution.py:44
  283.4 7.9 %collective-permute-start.30 = (bf16[24,2304]{1,0:T(8,128)(2,1)S(1)}, bf16[24,2304]{1,0:T(8,128)(2,1)S(1)}, u32[]{:S(2)}, u32[]{:S(2)}) collective-permute-start(bf16[24,2304]{1,0:T(8,128)(2,1)S(1)} %get-tuple-element.180), channel_id=1, source_target_pairs={{0,2},{2,4},{4,6},{6,0},{1,3},{3,5},{5,7},{7,1},{8,10},{10,12},{12... | collective-permute-start | bytes 331784 | tf_op jit(solution)/shard_map/ppermute | solution.py:49
  284.3 10.9 %collective-permute-start.31 = (bf16[24,2304]{1,0:T(8,128)(2,1)S(1)}, bf16[24,2304]{1,0:T(8,128)(2,1)S(1)}, u32[]{:S(2)}, u32[]{:S(2)}) collective-permute-start(bf16[24,2304]{1,0:T(8,128)(2,1)S(1)} %get-tuple-element.179), channel_id=1, source_target_pairs={{0,4},{2,6},{4,0},{6,2},{1,5},{3,7},{5,1},{7,3},{8,12},{10,14},{12... | collective-permute-start | bytes 331784 | tf_op jit(solution)/shard_map/ppermute | solution.py:49
  285.5 9.7 %collective-permute-start.32 = (bf16[24,2304]{1,0:T(8,128)(2,1)S(1)}, bf16[24,2304]{1,0:T(8,128)(2,1)S(1)}, u32[]{:S(2)}, u32[]{:S(2)}) collective-permute-start(bf16[24,2304]{1,0:T(8,128)(2,1)S(1)} %get-tuple-element.178), channel_id=1, source_target_pairs={{0,6},{2,0},{4,2},{6,4},{1,7},{3,1},{5,3},{7,5},{8,14},{10,8},{12,... | collective-permute-start | bytes 331784 | tf_op jit(solution)/shard_map/ppermute | solution.py:49
  (42 other events, 453.6 us)
Sparse Core Ops, SparseCore 0:
  12.9 103.9 all-gather.2

commit v6 on v5

--- a/solution.py
+++ b/solution.py
@@ -68,63 +68,49 @@
     return pl.BlockSpec(shape, lambda *_: (0,) * len(shape))
 
 
-def single(kernel, outs, values, scratch=(), limit=40, place=None, raw=0, raw_out=False):
-    blocked = len(values) - raw
-    specs = [whole_spec(v.shape) for v in values[:blocked]] + [ANY] * raw
-    values = [hbm(v) for v in values]
+def result(shape, kind, free=False):
+    return jax.ShapeDtypeStruct(shape, kind) if free else pltpu.HBM(shape, kind)
+
+
+def single(kernel, outs, values, raw=(), held=(), scratch=(), limit=40, place=None, raw_outs=0):
+    specs = [whole_spec(v.shape) for v in values] + [ANY] * len(raw) + [VMEM] * len(held)
+    values = [hbm(v) for v in values] + list(raw) + list(held)
+    blocked_outs = len(outs) - raw_outs
     if place is not None:
         specs, values = [SMEM] + specs, [place] + values
     return pl.pallas_call(
         kernel,
         grid=(1,),
-        out_shape=tuple(jax.ShapeDtypeStruct(*o) for o in outs),
+        out_shape=tuple(result(*o) for o in outs),
         in_specs=specs,
-        out_specs=tuple(ANY if raw_out else whole_spec(o[0]) for o in outs),
+        out_specs=tuple(
+            whole_spec(o[0]) if i < blocked_outs else ANY for i, o in enumerate(outs)
+        ),
         scratch_shapes=list(scratch),
         compiler_params=pltpu.CompilerParams(vmem_limit_bytes=limit << 20),
     )(*values)
 
 
-def run_all(copies):
-    for copy in copies:
-        copy.start()
-    for copy in copies:
-        copy.wait()
-
-
-def join_kernel(place_ref, left, left_other, right, right_other, whole, sems):
+def join_copies(place_ref, sides, blocks, sems):
     hx, hc, sz, sy = (place_ref[i] for i in range(4))
-    half = left.shape[-1]
+    half = sides[0].shape[-1]
     copies = []
-    for side, cores in enumerate(((left, left_other), (right, right_other))):
-        for core, pieces in enumerate(cores):
-            for second in range(2):
-                for first in range(2):
-                    for deep in range(4):
-                        across, down = (first, second) if side == 0 else (second, first)
-                        block = (hx ^ across) * 2 + (hc ^ core)
-                        spot = (block * 4 + lax.rem(sz + deep, 4)) * 2 + (sy ^ down)
-                        copies.append(
-                            pltpu.make_async_copy(
-                                pieces.at[second, first, deep],
-                                whole.at[spot, :, pl.ds(side * half, half)],
-                                sems.at[len(copies)],
-                            )
+    for number, pieces in enumerate(sides):
+        side, core = divmod(number, 2)
+        for second in range(2):
+            for first in range(2):
+                for deep in range(4):
+                    across, down = (first, second) if side == 0 else (second, first)
+                    block = (hx ^ across) * 2 + (hc ^ core)
+                    spot = (block * 4 + lax.rem(sz + deep, 4)) * 2 + (sy ^ down)
+                    copies.append(
+                        pltpu.make_async_copy(
+                            pieces.at[second, first, deep],
+                            blocks.at[spot, :, pl.ds(side * half, half)],
+                            sems.at[len(copies)],
                         )
-    run_all(copies)
-
-
-def join(here, *sides):
-    rows, half = sides[0].shape[-2:]
-    (whole,) = single(
-        join_kernel,
-        [((32, rows, half * 2), bf16)],
-        sides,
-        [pltpu.SemaphoreType.DMA((64,))],
-        place=here,
-        raw=4,
-    )
-    return whole.reshape(rows * 32, half * 2)
+                    )
+    return copies
 
 
 def gather_rows(here, shard, every, use):
@@ -140,7 +126,7 @@
     levels, used = lax.optimization_barrier((levels, used))
     for level in levels:
         sides += [level, swap(level, "hc")]
-    return join(here, *sides), used
+    return sides, used
 
 
 def piece_copies(place_ref, blocks, keep, send, sems, side, columns):
@@ -182,17 +168,36 @@
     return result
 
 
-def enter_kernel(x_ref, mod_ref, gains_ref, weight_ref, entered_ref, pair_ref, query_ref):
+def enter_kernel(place_ref, x_ref, mod_ref, gains_ref, *refs):
+    *sides, entered_ref, pair_ref, query_ref, whole_ref, block_sc, weight_sc, sems, sem = refs
     seqs, tokens, width = x_ref.shape
     half = tokens // 2
+    pieced = len(sides) > 1
+    if pieced:
+        copies = join_copies(place_ref, sides, block_sc, sems)
+    else:
+        copies = [pltpu.make_async_copy(sides[0], weight_sc, sem)]
+    for copy in copies:
+        copy.start()
     for s in range(seqs):
         normed = normalize(x_ref[s].astype(f32))[0]
         shift, scale = (mod_ref[s : s + 1, pl.ds(i * width, width)] for i in (0, 1))
         value = normed * gains_ref[0:1] * (1.0 + scale) + shift
         entered_ref[pl.ds(s * tokens, tokens), :] = value.astype(bf16)
     entered = entered_ref[...]
+    for copy in copies:
+        copy.wait()
+    if pieced:
+        rows = block_sc.shape[1]
+        for i in range(block_sc.shape[0]):
+            weight_sc[pl.ds(i * rows, rows), :] = block_sc[i]
+    leaving = pltpu.make_async_copy(weight_sc, whole_ref, sem)
+    leaving.start()
     for which in (1, 2, 0):
-        triple = dot(entered, weight_ref[:, pl.ds(which * width, width)]).astype(bf16)
+        triple = dot(entered, weight_sc[:, pl.ds(which * width, width)])
+        if which == 0:
+            triple = triple * HEAD_DIM ** (-0.5)
+        triple = triple.astype(bf16)
         for s in range(seqs):
             for g in range(GROUPS):
                 rows = triple[s * tokens : (s + 1) * tokens, g * WIDTH : (g + 1) * WIDTH]
@@ -202,24 +207,31 @@
                     query_ref[slot, :, pl.ds(WIDTH, WIDTH)] = rows[half:]
                 else:
                     pair_ref[slot, :, pl.ds((which - 1) * WIDTH, WIDTH)] = rows
-
-
-def enter(inputs, modulation, gains, weight):
+    leaving.wait()
+
+
+def enter(here, inputs, modulation, gains, sides):
     seqs, tokens, width = inputs.shape
+    rows = sides[0].shape[-2] if len(sides) > 1 else width // 32
     return single(
         enter_kernel,
         [
             ((seqs * tokens, width), bf16),
-            ((8, tokens, 2 * WIDTH), bf16),
-            ((8, tokens // 2, 2 * WIDTH), bf16),
+            ((8, tokens, 2 * WIDTH), bf16, True),
+            ((8, tokens // 2, 2 * WIDTH), bf16, True),
+            ((width, 3 * width), bf16),
         ],
-        [inputs, modulation, gains, weight],
-    )
-
-
-def head_lanes(rows, head):
-    lane = lax.broadcasted_iota(jnp.int32, (rows, WIDTH), 1)
-    return (lane >= head * HEAD_DIM) & (lane < (head + 1) * HEAD_DIM)
+        [inputs, modulation, gains],
+        raw=sides,
+        scratch=[
+            pltpu.VMEM((32, rows, 3 * width), bf16),
+            pltpu.VMEM((width, 3 * width), bf16),
+            pltpu.SemaphoreType.DMA((64,)),
+            pltpu.SemaphoreType.DMA,
+        ],
+        place=here,
+        raw_outs=1,
+    )
 
 
 def load_pairs(pair_ref, slot, first_row, half):
@@ -227,16 +239,23 @@
     return value[:, :WIDTH], value[:, WIDTH:]
 
 
-def spread_heads(pair_ref, first_row, half, target, factor):
-    heads = target.shape[0]
-    zero = jnp.zeros((half, WIDTH), bf16)
-    for slot in range(8):
-        for part, rows in enumerate(load_pairs(pair_ref, slot, first_row, half)):
-            rows = (rows.astype(f32) * factor).astype(bf16)
-            for h in range(heads):
-                target[h, pl.ds((slot * 2 + part) * half, half), :] = jnp.where(
-                    head_lanes(half, h), rows, zero
-                )
+def key_column(docs_ref, step):
+    row = docs_ref[pl.ds(step, 1), :]
+    return jnp.broadcast_to(row, (8, row.shape[1])).T[:, 0:1]
+
+
+def gather_pairs(pair_ref, target):
+    half = pair_ref.shape[1]
+    for slot in range(pair_ref.shape[0]):
+        for part, rows in enumerate(load_pairs(pair_ref, slot, 0, half)):
+            target[pl.ds((slot * 2 + part) * half, half), :] = rows
+
+
+def spread_heads(rows, target):
+    lane = lax.broadcasted_iota(jnp.int32, (1, WIDTH), 1)
+    for h in range(target.shape[0]):
+        own = (lane >= h * HEAD_DIM) & (lane < (h + 1) * HEAD_DIM)
+        target[h] = rows * jnp.where(own, 1.0, 0.0).astype(bf16)
 
 
 def fetch(step, pair_refs, starts, pair_sc):
@@ -248,7 +267,7 @@
 
 def forward_kernel(
     starts, came_ref, first_ref, second_ref, third_ref, fourth_ref, key_docs_ref, query_docs_ref,
-    out_ref, turned_ref, total_ref, query_sc, pair_sc, top_sc, sum_sc, acc_sc,
+    out_ref, turned_ref, total_ref, query_sc, flat_sc, pair_sc, top_sc, sum_sc, acc_sc,
 ):
     step = pl.program_id(0)
     heads, queries = query_sc.shape[:2]
@@ -256,7 +275,8 @@
 
     @pl.when(step == 0)
     def start():
-        spread_heads(came_ref, 0, half, query_sc, HEAD_DIM ** (-0.5))
+        gather_pairs(came_ref, flat_sc)
+        spread_heads(flat_sc[...], query_sc)
         top_sc[...] = jnp.full(top_sc.shape, -1e30, f32)
         sum_sc[...] = jnp.zeros(sum_sc.shape, f32)
         acc_sc[...] = jnp.zeros(acc_sc.shape, f32)
@@ -264,19 +284,23 @@
     fetch(step, (first_ref, second_ref, third_ref, fourth_ref), starts, pair_sc)
     key_part = pair_sc[:, :WIDTH]
     value_turned = pair_sc[:, WIDTH:].T
-    allowed = key_docs_ref[...] == query_docs_ref[...]
+    allowed = key_column(key_docs_ref, step) == query_docs_ref[...]
+    old = [top_sc[h : h + 1] for h in range(heads)]
+    raw = [dot_nt(key_part, query_sc[h]) for h in range(heads)]
+    scores = [jnp.where(allowed, value, -1e30) for value in raw]
+    new = [jnp.maximum(o, jnp.max(v, axis=0, keepdims=True)) for o, v in zip(old, scores)]
+    exponent = [jnp.exp(v - n) for v, n in zip(scores, new)]
+    terms = [
+        dot(value_turned[h * HEAD_DIM : (h + 1) * HEAD_DIM], exponent[h].astype(bf16))
+        for h in range(heads)
+    ]
+    sums = [jnp.sum(v, axis=0, keepdims=True) for v in exponent]
     for h in range(heads):
         rows = pl.ds(h * HEAD_DIM, HEAD_DIM)
-        scores = jnp.where(allowed, dot_nt(key_part, query_sc[h]), -1e30)
-        old = top_sc[h : h + 1]
-        new = jnp.maximum(old, jnp.max(scores, axis=0, keepdims=True))
-        exponent = jnp.exp(scores - new)
-        fade = jnp.exp(old - new)
-        top_sc[h : h + 1] = new
-        sum_sc[h : h + 1] = sum_sc[h : h + 1] * fade + jnp.sum(exponent, axis=0, keepdims=True)
-        acc_sc[rows] = acc_sc[rows] * fade + dot(
-            value_turned[h * HEAD_DIM : (h + 1) * HEAD_DIM], exponent.astype(bf16)
-        )
+        fade = jnp.exp(old[h] - new[h])
+        top_sc[h : h + 1] = new[h]
+        sum_sc[h : h + 1] = sum_sc[h : h + 1] * fade + sums[h]
+        acc_sc[rows] = acc_sc[rows] * fade + terms[h]
 
     @pl.when(step == pl.num_programs(0) - 1)
     def finish():
@@ -285,7 +309,7 @@
             rows = pl.ds(h * HEAD_DIM, HEAD_DIM)
             turned_ref[rows] = acc_sc[rows] / sum_sc[h : h + 1]
             total_ref[h : h + 1] = top_sc[h : h + 1] + jnp.log(sum_sc[h : h + 1])
-        whole = turned_ref[...].T.astype(bf16)
+        whole = turned_ref[...].astype(bf16).T
         for slot in range(8):
             for part in range(2):
                 begin = (slot * 2 + part) * half
@@ -314,9 +338,9 @@
     chunk = 512
     specs, starts, steps = pair_specs(pairs, chunk)
     outs = (
-        jax.ShapeDtypeStruct((slots, half, columns), bf16),
-        jax.ShapeDtypeStruct((WIDTH, queries), f32),
-        jax.ShapeDtypeStruct((8, queries), f32),
+        result((slots, half, columns), bf16, True),
+        result((WIDTH, queries), f32),
+        result((8, queries), f32),
     )
     return pl.pallas_call(
         partial(forward_kernel, starts),
@@ -325,12 +349,13 @@
         in_specs=[
             whole_spec(came.shape),
             *specs,
-            pl.BlockSpec((chunk, 1), lambda i: (i, 0)),
+            whole_spec(key_docs.shape),
             whole_spec(query_docs.shape),
         ],
         out_specs=tuple(whole_spec(o.shape) for o in outs),
         scratch_shapes=[
             pltpu.VMEM((heads, queries, WIDTH), bf16),
+            pltpu.VMEM((queries, WIDTH), bf16),
             pltpu.VMEM((chunk, 2 * WIDTH), bf16),
             pltpu.VMEM((8, queries), f32),
             pltpu.VMEM((8, queries), f32),
@@ -343,7 +368,7 @@
 def backward_kernel(
     starts, came_ref, grad_ref, first_ref, second_ref, third_ref, fourth_ref, key_docs_ref, query_docs_ref,
     turned_ref, total_ref, query_out, keep_ref, keep_other, send_ref,
-    query_sc, grad_sc, pair_sc, delta_sc, acc_sc,
+    query_sc, grad_sc, flat_sc, pair_sc, delta_sc, acc_sc,
 ):
     step = pl.program_id(0)
     heads, queries = query_sc.shape[:2]
@@ -351,33 +376,37 @@
 
     @pl.when(step == 0)
     def start():
-        spread_heads(came_ref, 0, half, query_sc, HEAD_DIM ** (-0.5))
-        spread_heads(grad_ref, 0, half, grad_sc, 1.0)
+        gather_pairs(came_ref, flat_sc)
+        spread_heads(flat_sc[...], query_sc)
+        gather_pairs(grad_ref, flat_sc)
+        spread_heads(flat_sc[...], grad_sc)
         acc_sc[...] = jnp.zeros(acc_sc.shape, f32)
+        product = flat_sc[...].T.astype(f32) * turned_ref[...]
         for h in range(heads):
             rows = slice(h * HEAD_DIM, (h + 1) * HEAD_DIM)
-            turned = grad_sc[h].astype(f32).T
-            delta_sc[h : h + 1] = jnp.sum(turned[rows] * turned_ref[rows], axis=0, keepdims=True)
+            delta_sc[h : h + 1] = jnp.sum(product[rows], axis=0, keepdims=True)
 
     fetch(step, (first_ref, second_ref, third_ref, fourth_ref), starts, pair_sc)
     key_part = pair_sc[:, :WIDTH]
     value_part = pair_sc[:, WIDTH:]
     key_turned = key_part.T
-    allowed = key_docs_ref[...] == query_docs_ref[...]
-    grad_key = grad_value = None
+    allowed = key_column(key_docs_ref, step) == query_docs_ref[...]
+    raw = [dot_nt(key_part, query_sc[h]) for h in range(heads)]
+    slopes = [dot_nt(value_part, grad_sc[h]) for h in range(heads)]
+    probabilities = [
+        jnp.exp(jnp.where(allowed, value, -1e30) - total_ref[h : h + 1])
+        for h, value in enumerate(raw)
+    ]
+    grad_scores = [
+        (p * (slope - delta_sc[h : h + 1])).astype(bf16)
+        for h, (p, slope) in enumerate(zip(probabilities, slopes))
+    ]
+    grad_value = sum(dot(probabilities[h].astype(bf16), grad_sc[h]) for h in range(heads))
+    grad_key = sum(dot(grad_scores[h], query_sc[h]) for h in range(heads))
     for h in range(heads):
         rows = pl.ds(h * HEAD_DIM, HEAD_DIM)
-        query, grad = query_sc[h], grad_sc[h]
-        scores = jnp.where(allowed, dot_nt(key_part, query), -1e30)
-        probabilities = jnp.exp(scores - total_ref[h : h + 1])
-        slope = dot_nt(value_part, grad) - delta_sc[h : h + 1]
-        grad_scores = (probabilities * slope).astype(bf16)
-        value_term = dot(probabilities.astype(bf16), grad)
-        key_term = dot(grad_scores, query)
-        grad_value = value_term if grad_value is None else grad_value + value_term
-        grad_key = key_term if grad_key is None else grad_key + key_term
         acc_sc[rows] = acc_sc[rows] + dot(
-            key_turned[h * HEAD_DIM : (h + 1) * HEAD_DIM], grad_scores
+            key_turned[h * HEAD_DIM : (h + 1) * HEAD_DIM], grad_scores[h]
         )
     quarter = pl.num_programs(0) // 4
     middle = 2 * quarter
@@ -395,7 +424,7 @@
 
     @pl.when(step == pl.num_programs(0) - 1)
     def finish():
-        whole = (acc_sc[...] * HEAD_DIM ** (-0.5)).T.astype(bf16)
+        whole = (acc_sc[...] * HEAD_DIM ** (-0.5)).astype(bf16).T
         for slot in range(8):
             for part in range(2):
                 begin = (slot * 2 + part) * half
@@ -423,7 +452,7 @@
             whole_spec(came.shape),
             whole_spec(grad.shape),
             *specs,
-            pl.BlockSpec((chunk, 1), lambda i: (i, 0)),
+            whole_spec(key_docs.shape),
             whole_spec(query_docs.shape),
             whole_spec(turned.shape),
             whole_spec(total.shape),
@@ -437,6 +466,7 @@
         scratch_shapes=[
             pltpu.VMEM((heads, queries, WIDTH), bf16),
             pltpu.VMEM((heads, queries, WIDTH), bf16),
+            pltpu.VMEM((queries, WIDTH), bf16),
             pltpu.VMEM((chunk, 2 * WIDTH), bf16),
             pltpu.VMEM((8, queries), f32),
             pltpu.VMEM((WIDTH, queries), f32),
@@ -445,43 +475,17 @@
     )(*map(hbm, (came, grad, *pairs, key_docs, query_docs, turned, total)))
 
 
-def middle_kernel(
-    gathered, came_ref, x_ref, teacher_ref, mask_ref, mod_ref, gains_ref, up_bias_ref, *refs
+def settle_kernel(
+    later_hbm, out_ref, up_ref, down_ref, block_sc, out_sc, up_sc, down_sc, sems, out_sems
 ):
-    if gathered:
-        later_hbm, *refs = refs
-    else:
-        out_hbm, up_hbm, down_hbm, *refs = refs
-    final_ref, hidden_ref, leave_ref, pack_ref, sums_ref, *refs = refs
-    out_sc, up_sc, down_sc, slope_sc, *refs = refs
-    if gathered:
-        block_sc, sems = refs
-    else:
-        (sems,) = refs
-
-    seqs, tokens, width = x_ref.shape
-    units = up_sc.shape[1]
-    rows = seqs * tokens
-    half = tokens // 2
-    if gathered:
-        copies = [
-            pltpu.make_async_copy(later_hbm.at[:, j], block_sc.at[j], sems.at[j]) for j in range(9)
-        ]
-    else:
-        copies = [
-            pltpu.make_async_copy(source, target, sems.at[i])
-            for i, (source, target) in enumerate(
-                ((out_hbm, out_sc), (up_hbm, up_sc), (down_hbm, down_sc))
-            )
-        ]
+    width = out_ref.shape[1]
+    copies = [
+        pltpu.make_async_copy(later_hbm.at[:, j], block_sc.at[j], sems.at[j]) for j in range(9)
+    ]
     for copy in copies:
         copy.start()
-
-    def settle(j):
-        if not gathered:
-            if j < 2 or j == 5:
-                copies[(0, 1, None, None, None, 2)[j]].wait()
-            return
+    leaving = []
+    for j in range(9):
         copies[j].wait()
         for i in range(32):
             value = block_sc[j, i]
@@ -491,6 +495,60 @@
                 up_sc[pl.ds(i * 24, 24), pl.ds((j - 1) * width, width)] = value
             else:
                 down_sc[pl.ds(i * 96 + (j - 5) * 24, 24), :] = value
+        if j == 0:
+            leaving.append(pltpu.make_async_copy(out_sc, out_ref, out_sems.at[j]))
+        elif j < 5:
+            columns = pl.ds((j - 1) * width, width)
+            leaving.append(
+                pltpu.make_async_copy(up_sc.at[:, columns], up_ref.at[:, columns], out_sems.at[j])
+            )
+        elif j == 8:
+            leaving.append(pltpu.make_async_copy(down_sc, down_ref, out_sems.at[j]))
+        if j < 5 or j == 8:
+            leaving[-1].start()
+    for copy in leaving:
+        copy.wait()
+
+
+def settle(later):
+    width = later.shape[-1]
+    shapes = ((width, width), (width, 4 * width), (4 * width, width))
+    return pl.pallas_call(
+        settle_kernel,
+        out_shape=tuple(result(shape, bf16) for shape in shapes),
+        in_specs=[ANY],
+        out_specs=(ANY,) * 3,
+        scratch_shapes=[
+            pltpu.VMEM((9, 32, 24, width), bf16),
+            *(pltpu.VMEM(shape, bf16) for shape in shapes),
+            pltpu.SemaphoreType.DMA((9,)),
+            pltpu.SemaphoreType.DMA((9,)),
+        ],
+        compiler_params=pltpu.CompilerParams(vmem_limit_bytes=40 << 20),
+    )(hbm(later))
+
+
+def middle_kernel(
+    came_ref, x_ref, teacher_ref, mask_ref, mod_ref, gains_ref, up_bias_ref,
+    out_hbm, up_hbm, down_hbm,
+    final_ref, hidden_ref, leave_ref, pack_ref, sums_ref, out_sc, up_sc, down_sc, slope_sc, sems,
+):
+    seqs, tokens, width = x_ref.shape
+    units = up_sc.shape[1]
+    rows = seqs * tokens
+    half = tokens // 2
+    parts = [pl.ds(f * width, width) for f in range(units // width)]
+    copies = [pltpu.make_async_copy(out_hbm, out_sc, sems.at[0])]
+    for f, part in enumerate(parts):
+        copies.append(
+            pltpu.make_async_copy(up_hbm.at[:, part], up_sc.at[:, part], sems.at[1 + 2 * f])
+        )
+        copies.append(
+            pltpu.make_async_copy(down_hbm.at[part, :], down_sc.at[part, :], sems.at[2 + 2 * f])
+        )
+    for copy in copies:
+        copy.start()
+    masks = mask_ref[...].T
 
     def wide(index):
         return jnp.concatenate(
@@ -516,18 +574,17 @@
             pack_ref[pl.ds(s * tokens + half, half), columns] = right
     mixed = pack_ref[:, pl.ds(0, width)]
     residual = jnp.concatenate([x_ref[s].astype(f32) for s in range(seqs)])
-    settle(0)
+    copies[0].wait()
     branch = dot(mixed, out_sc[...])
     hidden = residual + wide(2) * branch
     normed, inverse = normalize(hidden)
     scaled = normed * gains_ref[1:2]
     moved = (scaled * (1.0 + wide(4)) + wide(3)).astype(bf16)
     pack_ref[:, pl.ds(width, width)] = moved
-    for j in range(1, 9):
-        settle(j)
     lower = None
     for f in range(units // width):
         columns = pl.ds(f * width, width)
+        copies[1 + 2 * f].wait()
         u = dot(moved, up_sc[:, columns]) + up_bias_ref[0:1, columns]
         square = u * u
         t = jnp.tanh(0.7978845608028654 * (u + 0.044715 * u * square))
@@ -536,6 +593,7 @@
             1.0 + 0.134145 * square
         )
         pack_ref[:, pl.ds(2 * width + f * width, width)] = active
+        copies[2 + 2 * f].wait()
         term = dot(active, down_sc[columns, :])
         lower = term if lower is None else lower + term
     lower = lower + gains_ref[2:3]
@@ -546,10 +604,10 @@
     teacher = jnp.concatenate([teacher_ref[s].astype(f32) for s in range(seqs)])
     mismatch = final - teacher
     sums_ref[14:15] = jnp.sum(
-        mask_ref[:, 0:1] * mismatch * mismatch, axis=0, keepdims=True
+        masks[:, 0:1] * mismatch * mismatch, axis=0, keepdims=True
     )
     sums_ref[15:16] = jnp.zeros((1, width), f32)
-    grad_final = mask_ref[:, 1:2] * mismatch
+    grad_final = masks[:, 1:2] * mismatch
     add_rows(6, grad_final * lower)
     grad_lower = (gate * grad_final).astype(bf16)
     base = 2 * width + units
@@ -581,32 +639,29 @@
             leave_ref[s * GROUPS + g, :, pl.ds(WIDTH, WIDTH)] = piece[half:]
 
 
-def middle(came, inputs, teacher, masks, modulation, gains, up_bias, later):
+def middle(came, inputs, teacher, masks, modulation, gains, up_bias, weights):
     seqs, tokens, width = inputs.shape
     units = up_bias.shape[1]
     rows = seqs * tokens
-    gathered = len(later) == 1
-    scratch = [
-        pltpu.VMEM((width, width), bf16),
-        pltpu.VMEM((width, units), bf16),
-        pltpu.VMEM((units, width), bf16),
-        pltpu.VMEM((rows, units), f32),
-    ]
-    if gathered:
-        scratch.append(pltpu.VMEM((9, 32, 24, width), bf16))
     return single(
-        partial(middle_kernel, gathered),
+        middle_kernel,
         [
             ((seqs, tokens, width), bf16),
             ((rows, width), f32),
-            (came.shape, bf16),
-            ((rows, 4 * width + 2 * units), bf16),
+            (came.shape, bf16, True),
+            ((rows, 4 * width + 2 * units), bf16, True),
             ((16, width), f32),
         ],
-        [came, inputs, teacher, masks, modulation, gains, up_bias, *later],
-        scratch + [pltpu.SemaphoreType.DMA((9,))],
-        limit=60,
-        raw=len(later),
+        [came, inputs, teacher, masks, modulation, gains, up_bias],
+        raw=[hbm(w) for w in weights],
+        scratch=[
+            pltpu.VMEM((width, width), bf16),
+            pltpu.VMEM((width, units), bf16),
+            pltpu.VMEM((units, width), bf16),
+            pltpu.VMEM((rows, units), f32),
+            pltpu.SemaphoreType.DMA((9,)),
+        ],
+        limit=40,
     )
 
 
@@ -650,16 +705,17 @@
     return single(
         weights_kernel,
         [((2, 4, 9, 24, 128 * size), bf16) for size, _ in COLUMN_GROUPS for _ in range(2)],
-        [own, other],
-        [
+        [],
+        held=[own, other],
+        scratch=[
             pltpu.VMEM((total // 2, 2 * rows), bf16),
             pltpu.VMEM((2 * rows, total // 2), bf16),
             pltpu.VMEM((16, 9, 24, width), bf16),
             pltpu.SemaphoreType.DMA((len(COLUMN_GROUPS), 16)),
         ],
-        limit=56,
+        limit=40,
         place=here,
-        raw_out=True,
+        raw_outs=2 * len(COLUMN_GROUPS),
     )
 
 
@@ -707,14 +763,14 @@
         partial(qkv_kernel, seqs),
         [((2, 4, 24, 3 * width // 2), bf16)] * 4,
         values,
-        [
+        scratch=[
             pltpu.VMEM((width, 2 * rows), bf16),
             pltpu.VMEM((2 * rows, 3 * width), bf16),
             pltpu.VMEM((16, 24, 3 * width), bf16),
             pltpu.SemaphoreType.DMA((2, 16)),
         ],
         place=here,
-        raw_out=True,
+        raw_outs=4,
     )
 
 
@@ -763,7 +819,7 @@
         leave_kernel,
         [
             ((seqs, tokens, width), f32),
-            ((devices, 512), f32),
+            ((devices, 512), f32, True),
             ((seqs * tokens, 3 * width), bf16),
         ],
         [home, inputs, grad_hidden, modulation, gains, weight, sums],
@@ -799,10 +855,11 @@
                 block = ((hx ^ across) * 2 + (hc ^ core)) * parts + part
                 lines = every_ref[pl.ds(pl.multiple_of(block * 8, 8), 8), pl.ds(begin, 2 * tokens)]
                 lines = jnp.where(second, lines[:, tokens:], lines[:, :tokens])
-                turned = lines.T
                 for spot in range(8):
-                    key_docs_ref[pl.ds(row, tokens), :] = turned[:, spot : spot + 1]
-                    row += tokens
+                    key_docs_ref[row : row + 1, pl.ds(spot * tokens, tokens)] = lines[
+                        spot : spot + 1
+                    ]
+                row += 1
     lines = every_ref[
         pl.ds(pl.multiple_of(((hx * 2 + hc) * parts + rb) * 8, 8), 8), pl.ds(begin, 2 * tokens)
     ]
@@ -812,11 +869,11 @@
     begin += 2 * tokens
     count = jnp.sum(every_ref[:, pl.ds(begin, 1)], axis=0, keepdims=True)
     gains_ref[3:4, pl.ds(0, 1)] = count
-    turned = valid_ref[...].astype(f32).T
+    masks_ref[...] = jnp.zeros(masks_ref.shape, f32)
     for s in range(seqs):
-        rows = pl.ds(s * tokens, tokens)
-        masks_ref[rows, pl.ds(0, 1)] = turned[:, s : s + 1]
-        masks_ref[rows, pl.ds(1, 1)] = turned[:, s : s + 1] * (factor / count)
+        valid = valid_ref[s : s + 1, :].astype(f32)
+        masks_ref[0:1, pl.ds(s * tokens, tokens)] = valid
+        masks_ref[1:2, pl.ds(s * tokens, tokens)] = valid * (factor / count)
 
 
 def unpack(here, every, valid_mask, width, units, parts, length):
@@ -829,12 +886,47 @@
             ((8, 6 * width), f32),
             ((8, width), f32),
             ((8, units), f32),
-            ((4 * parts * 8 * tokens, 1), f32),
+            ((4 * parts, 8 * tokens), f32),
             ((1, 8 * tokens), f32),
-            ((seqs * tokens, 2), f32),
+            ((8, seqs * tokens), f32),
         ],
         [every, valid_mask],
         place=here,
+    )
+
+
+def finish_kernel(width, small_ref, embed_ref, gains_ref, *refs):
+    ada_ref, bias_ref, *vectors, loss_ref = refs
+    seqs = embed_ref.shape[0]
+    columns = ada_ref.shape[1]
+    added = jnp.sum(small_ref[...], axis=0, keepdims=True)
+    turned = embed_ref[...].T
+    begin = 0
+    ada = bias = None
+    for s in range(seqs):
+        grad = added[:, begin : begin + columns]
+        begin += columns
+        term = turned[:, s : s + 1] * grad
+        ada = term if ada is None else ada + term
+        bias = grad if bias is None else bias + grad
+    ada_ref[...] = ada
+    bias_ref[...] = bias
+    for ref in vectors:
+        size = ref.shape[1]
+        ref[...] = added[:, begin : begin + size]
+        begin += size
+    loss_ref[...] = added[:, begin : begin + 1] / (gains_ref[3:4, 0:1] * width)
+
+
+def finish(small, time_embed, gains, width, units):
+    devices = small.shape[0]
+    sizes = [6 * width // devices] + [size // devices for size in (width, width, units, width)]
+    return single(
+        partial(finish_kernel, float(width)),
+        [((time_embed.shape[1], sizes[0]), f32)]
+        + [((1, size), f32, True) for size in sizes]
+        + [((1, 1), f32, True)],
+        [small, time_embed, gains],
     )
 
 
@@ -874,7 +966,7 @@
 def begin_with(time_embed, ada_weight, vectors, segments, valid_mask, weights, devices):
     seqs, tokens = segments.shape
     columns = seqs * ada_weight.shape[1] + vectors.shape[1] - ada_weight.shape[1] + seqs * tokens + 1
-    outs = [((devices, columns + -columns % 128), f32)]
+    outs = [((devices, columns + -columns % 128), f32, True)]
     if weights:
         outs.append(((9, 24, weights[0].shape[1]), bf16))
     return single(
@@ -923,7 +1015,7 @@
     )
     every = lax.all_to_all(packed, EVERY, 0, 0, tiled=True)
     if parts > 1:
-        full_qkv, *later = (
+        sides, *later = (
             lax.all_gather(w, EVERY, axis=0, tiled=True)
             for w in (qkv_weight, out_weight, up_weight, down_weight)
         )
@@ -935,13 +1027,13 @@
         return unpack(here, every, valid_mask, width, units, parts, length)
 
     if parts > 1:
+        sides = [sides]
         used = use(every)
     else:
-        full_qkv, used = gather_rows(here, shard, every, use)
+        sides, used = gather_rows(here, shard, every, use)
     modulation, gains, full_up_bias, key_docs, query_docs, masks = used
-    count_all = gains[3, 0]
-
-    entered, pair, query = enter(inputs, modulation, gains, full_qkv)
+
+    entered, pair, query, full_qkv = enter(here, inputs, modulation, gains, sides)
     pair = exchange(pair).reshape(queries, 2 * WIDTH)
     query = exchange(query)
     if parts > 1:
@@ -951,6 +1043,8 @@
     pairs = (pair, pair_x, swap(pair, "hc"), swap(pair_x, "hc"))
     attended, turned, total = attend(query, pairs, key_docs, query_docs)
 
+    if parts == 1:
+        later = settle(later[0])
     final, grad_hidden, grad_leaving, pack, sums = middle(
         exchange(attended), inputs, teacher, masks, modulation, gains, full_up_bias, later
     )
@@ -998,33 +1092,46 @@
         others = swap(entered, "hc"), swap(home, "hc")
         terms = qkv_terms(here, seqs, entered, others[0], home, others[1])
         seconds = after(seconds, terms)
-        second = jnp.concatenate(
-            [
-                keep[0].astype(f32) + recv[0].astype(f32)
-                for keep, recv in zip(held, firsts)
-            ],
-            axis=3,
-        ) + jnp.concatenate(seconds, axis=3).astype(f32)
+        recvs = [swap(send, order[0]) for send, order in zip(terms[1::2], ORDERS)]
+        grad_input, small, flat = leave(
+            after(home, terms), inputs, grad_hidden, modulation, gains, full_qkv, sums, devices
+        )
+        recvs = after(recvs, small)
+        nexts = [second_send(keep, recv) for keep, recv in zip(terms[::2], recvs)]
+        small = after(small, nexts)
+        next_recvs = [swap(value, order[1]) for value, order in zip(nexts, ORDERS)]
+        totals = [
+            jnp.concatenate(
+                [
+                    keep[0].astype(f32) + recv[0].astype(f32)
+                    for keep, recv, (_, own) in zip(held, firsts, COLUMN_GROUPS)
+                    if own == side
+                ],
+                axis=3,
+            )
+            + seconds[side].astype(f32)
+            for side in (0, 1)
+        ]
+        second = jnp.concatenate(totals, axis=3)
         third = third_recvs(second)
-        recvs = [swap(send, order[0]) for send, order in zip(terms[1::2], ORDERS)]
-        home = after(home, recvs)
         second_qkv = jnp.concatenate(
             [
-                second_total(keep, recv, swap(second_send(keep, recv), order[1]))
-                for keep, recv, order in zip(terms[::2], recvs, ORDERS)
+                second_total(keep, recv, next_recv)
+                for keep, recv, next_recv in zip(terms[::2], recvs, next_recvs)
             ],
             axis=2,
         )
-        third, third_qkv = lax.optimization_barrier((third, third_recvs(second_qkv)))
+        third_qkv = third_recvs(second_qkv)
+        third, third_qkv = lax.optimization_barrier((third, third_qkv))
         owned_later = third_total(second, third)
         shard_qkv = third_total(second_qkv, third_qkv)
         shard_out = owned_later[0]
         shard_up = owned_later[1:5].transpose(1, 0, 2).reshape(24, units)
         shard_down = owned_later[5:].reshape(96, width)
-    grad_input, small, flat = leave(
-        home, inputs, grad_hidden, modulation, gains, full_qkv, sums, devices
-    )
     if parts > 1:
+        grad_input, small, flat = leave(
+            home, inputs, grad_hidden, modulation, gains, full_qkv, sums, devices
+        )
         base = 2 * width + units
         ends = (base + width, base + width + units)
         shard_qkv, shard_out, shard_up, shard_down = (
@@ -1044,30 +1151,22 @@
     small = lax.all_to_all(small, EVERY, 0, 0, tiled=True)
     if parts == 1:
         small = after(small, second_qkv)
-    added = jnp.sum(small, axis=0)
-    owned = []
-    begin = 0
-    sizes = [6 * width // devices * seqs] + [size // devices for size in (width, width, units, width)]
-    for size in sizes + [1]:
-        owned.append(added[begin : begin + size])
-        begin += size
-    own_grad = owned[0].reshape(seqs, -1)
-    grad_ada_weight = jnp.sum(time_embed[:, :, None] * own_grad[:, None, :], axis=0)
-    loss_value = owned[5][0] / (count_all * width)
+    grads = finish(small, time_embed, gains, width, units)
+    loss_value = grads[6].reshape(())
     return (
         final,
         loss_value,
         grad_input,
-        grad_ada_weight,
-        jnp.sum(own_grad, axis=0),
-        owned[1],
+        grads[0],
+        grads[1].reshape(-1),
+        grads[2].reshape(-1),
         shard_qkv,
         shard_out,
-        owned[2],
+        grads[3].reshape(-1),
         shard_up,
-        owned[3],
+        grads[4].reshape(-1),
         shard_down,
-        owned[4],
+        grads[5].reshape(-1),
     )
 
 

time: 309 us -> 298 us (0.964)
  blocking collectives: 40 us -> 28.3 us
  starting transfers between devices: 59.9 us -> 67.5 us
  Pallas kernels: 62.8 us -> 69.5 us
  local copies, waits for them, and re-layouts: 21.4 us -> 16.7 us
  other arithmetic: 19.9 us -> 16.7 us
    all_to_all x2 -> x1, blocking collectives: 40 us -> 28.3 us  [exchange(): return lax.all_to_all(rows, SPOT, 0, 0, tiled=True)]
    ppermute x9, waiting for transfers between devices: 16.1 us -> 6.21 us  [turn(): lax.ppermute(value, axis, [(i, (i - step) % size) for i in range(size)])]
    pallas_call x8 -> x9, Pallas kernels: 40.1 us -> 47.3 us  [the longest x8 38.7 us: single(): pl.pallas_call(kernel, grid=(1,), out_shape=tuple((result(*o) for o in ou...]
    all_to_all x3 -> x4, starting transfers between devices: 11.4 us -> 16.5 us  [exchange(): return lax.all_to_all(rows, SPOT, 0, 0, tiled=True)]
    all_to_all x3 -> x4, waiting for transfers between devices: 12.6 us -> 17.1 us  [exchange(): return lax.all_to_all(rows, SPOT, 0, 0, tiled=True)]
    add x4 -> x2, other arithmetic: 5.41 us -> 2 us  [on_device(): keep[0].astype(f32) + recv[0].astype(f32)]
    ppermute x24, waiting for transfers between devices: 39.7 us -> 43 us  [swap(): return lax.ppermute(value, axis, [(0, 1), (1, 0)])]
    ppermute x9, starting transfers between devices: 16.4 us -> 19.6 us  [turn(): lax.ppermute(value, axis, [(i, (i - step) % size) for i in range(size)])]
  transfers between devices with their start and end apart: 39 -> 40, of which waited for: 18 -> 21; matrix products, arithmetic and copies ran while one was open for 8% -> 7% of each run, Pallas kernels for 16% -> 19%
where the time goes in v6:
time: 298 us; the launch traced here: 297 us
  waiting for transfers between devices  83.9 us (28%)
  Pallas kernels  69.5 us (23%)
  starting transfers between devices  67.5 us (23%)
  blocking collectives  28.3 us (9%)
  local copies, waits for them, and re-layouts  16.7 us (6%)
  other arithmetic  16.7 us (6%)
  between operations  14.5 us (5%)
    ppermute x24, waiting for transfers between devices, swap(): return lax.ppermute(value, axis, [(0, 1), (1, 0)])  43 us
    pallas_call x8, Pallas kernels, single(): pl.pallas_call(kernel, grid=(1,), out_shape=tuple((result(*o) for o in ou...  38.7 us
    all_to_all x1, blocking collectives, exchange(): return lax.all_to_all(rows, SPOT, 0, 0, tiled=True)  28.3 us
    ppermute x9, starting transfers between devices, turn(): lax.ppermute(value, axis, [(i, (i - step) % size) for i in range(size)])  19.6 us
    ppermute x24, starting transfers between devices, swap(): return lax.ppermute(value, axis, [(0, 1), (1, 0)])  19.6 us
    all_to_all x4, waiting for transfers between devices, exchange(): return lax.all_to_all(rows, SPOT, 0, 0, tiled=True)  17.1 us
    all_to_all x4, starting transfers between devices, exchange(): return lax.all_to_all(rows, SPOT, 0, 0, tiled=True)  16.5 us
    pallas_call x1, Pallas kernels, attend_back(): pl.pallas_call(partial(backward_kernel, starts), grid=(steps,), out_shape...  13 us
  transfers between devices with their start and end apart: 40, of which 21 were waited for; matrix products, arithmetic and copies ran while one was open for 7% of the time, Pallas kernels for 19%

profile of v6, /device:TPU:0, one launch (start us, length us, event | category | flops | bytes accessed | tf_op | source)
XLA Modules:
  0.0 297.0 jit_solution(6288425996511756958)
XLA Ops:
  12.8 3.1 %collective-permute-start.2 = (bf16[24,2304]{1,0:T(8,128)(2,1)}, bf16[24,2304]{1,0:T(8,128)(2,1)S(1)}, u32[]{:S(2)}, u32[]{:S(2)}) collective-permute-start(bf16[24,2304]{1,0:T(8,128)(2,1)} %param.23), channel_id=1, source_target_pairs={{0,2},{2,4},{4,6},{6,0},{1,3},{3,5},{5,7},{7,1},{8,10},{10,12},{12... | collective-permute-start | bytes 331784 | tf_op jit(solution)/shard_map/ppermute | solution.py:49
  15.9 2.6 collective-permute-start.1
  19.8 2.3 collective-permute-done.2
  22.1 3.9 %collective-permute-done.1 = bf16[24,2304]{1,0:T(8,128)(2,1)S(1)} collective-permute-done((bf16[24,2304]{1,0:T(8,128)(2,1)}, bf16[24,2304]{1,0:T(8,128)(2,1)S(1)}, u32[]{:S(2)}, u32[]{:S(2)}) %collective-permute-start.1) | collective-permute-done | bytes 110624 | tf_op jit(solution)/shard_map/ppermute | solution.py:49
  29.4 7.1 %all-to-all-start = ((f32[32,1,640]{2,1,0:T(1,128)}), f32[32,1,640]{2,1,0:T(1,128)S(1)}, u32[]{:S(2)}, u32[]{:S(2)}) async-start(f32[32,1,640]{2,1,0:T(1,128)} %copy.34), calls=%async_computation | async-start | bytes 163840 | tf_op jit(solution)/shard_map/all_to_all | solution.py:1016
  38.3 5.6 %all-to-all-done = f32[32,1,640]{2,1,0:T(1,128)S(1)} async-done(((f32[32,1,640]{2,1,0:T(1,128)}), f32[32,1,640]{2,1,0:T(1,128)S(1)}, u32[]{:S(2)}, u32[]{:S(2)}) %all-to-all-start) | async-done | bytes 81952 | tf_op jit(solution)/shard_map/all_to_all | solution.py:1016
  46.7 2.3 collective-permute-start.6
  51.1 8.3 %collective-permute-done.5 = bf16[2,4,24,1152]{3,2,1,0:T(8,128)(2,1)S(1)} collective-permute-done((bf16[2,4,24,1152]{3,2,1,0:T(8,128)(2,1)S(1)}, bf16[2,4,24,1152]{3,2,1,0:T(8,128)(2,1)S(1)}, u32[]{:S(2)}, u32[]{:S(2)}) %collective-permute-start.5) | collective-permute-done | bytes 442400 | tf_op jit(solution)/shard_map/ppermute | solution.py:44
  59.5 4.7 %collective-permute-done.6 = bf16[2,4,24,1152]{3,2,1,0:T(8,128)(2,1)S(1)} collective-permute-done((bf16[2,4,24,1152]{3,2,1,0:T(8,128)(2,1)S(1)}, bf16[2,4,24,1152]{3,2,1,0:T(8,128)(2,1)S(1)}, u32[]{:S(2)}, u32[]{:S(2)}) %collective-permute-start.6) | collective-permute-done | bytes 442400 | tf_op jit(solution)/shard_map/ppermute | solution.py:44
  68.0 6.9 %shard_map.248 = (bf16[128,768]{1,0:T(8,128)(2,1)}, bf16[8,64,384]{2,1,0:T(8,128)(2,1)S(1)}, bf16[8,32,384]{2,1,0:T(8,128)(2,1)}, bf16[768,2304]{1,0:T(8,128)(2,1)}) custom-call(s32[5]{0:T(128)S(1)} %stack.71.place_ref, bf16[2,64,768]{2,1,0:T(8,128)(2,1)} %x_ref.5, f32[8,4608]{1,0:T(8,128)} %get-tuple-element.113.mod_ref, ...), custom_call_target="tpu_custom_call" | custom-call | tf_op jit(solution)/shard_map/pallas_call | solution.py:81
  74.9 28.3 %all_to_all.49 = bf16[8,64,384]{2,1,0:T(8,128)(2,1)S(1)} all-to-all(bf16[8,64,384]{2,1,0:T(8,128)(2,1)S(1)} %get-tuple-element.117), channel_id=1, replica_groups=mesh['hx'=2,'hc'=2,'rb'=1,'sz'=4,'sy'=2] {'sz','sy'}, dimensions={0} | all-to-all | bytes 786432 | tf_op jit(solution)/shard_map/all_to_all | solution.py:982
  104.2 3.4 %all-to-all-start.2 = ((bf16[8,32,384]{2,1,0:T(8,128)(2,1)}), bf16[8,32,384]{2,1,0:T(8,128)(2,1)S(1)}, u32[]{:S(2)}, u32[]{:S(2)}) async-start(bf16[8,32,384]{2,1,0:T(8,128)(2,1)} %get-tuple-element.118), calls=%async_computation.2 | async-start | bytes 393216 | tf_op jit(solution)/shard_map/all_to_all | solution.py:982
  107.7 10.4 %all-to-all-done.2.came_ref = bf16[8,32,384]{2,1,0:T(8,128)(2,1)S(1)} async-done(((bf16[8,32,384]{2,1,0:T(8,128)(2,1)}), bf16[8,32,384]{2,1,0:T(8,128)(2,1)S(1)}, u32[]{:S(2)}, u32[]{:S(2)}) %all-to-all-start.2) | async-done | bytes 196640 | tf_op jit(solution)/shard_map/all_to_all | solution.py:982
  120.7 9.2 %shard_map.249 = (bf16[8,32,384]{2,1,0:T(8,128)(2,1)}, f32[192,512]{1,0:T(8,128)}, f32[8,512]{1,0:T(8,128)}) custom-call(bf16[8,32,384]{2,1,0:T(8,128)(2,1)} %copy-done.2, bf16[512,384]{1,0:T(8,128)(2,1)} %bitcast.103, bf16[512,384]{1,0:T(8,128)(2,1)} %copy-done.3, bf16[512,384]{1,0:T(8,128)(2,1)} %copy-done.4, bf16[512,384]{1,0:T(8,128)(2,1)} %copy-done.5, ...), custom_call_target="tpu_custom_call" | custom-call | tf_op jit(solution)/shard_map/pallas_call | solution.py:345
  129.9 3.6 %all-to-all-start.3 = ((bf16[8,32,384]{2,1,0:T(8,128)(2,1)}), bf16[8,32,384]{2,1,0:T(8,128)(2,1)S(1)}, u32[]{:S(2)}, u32[]{:S(2)}) async-start(bf16[8,32,384]{2,1,0:T(8,128)(2,1)} %get-tuple-element.123), calls=%async_computation.3 | async-start | bytes 393216 | tf_op jit(solution)/shard_map/all_to_all | solution.py:982
  133.6 8.5 %shard_map.250 = (bf16[768,768]{1,0:T(8,128)(2,1)}, bf16[768,3072]{1,0:T(8,128)(2,1)}, bf16[3072,768]{1,0:T(8,128)(2,1)}) custom-call(bf16[32,9,24,768]{3,2,1,0:T(8,128)(2,1)} %bitcast.100), custom_call_target="tpu_custom_call" | custom-call | tf_op jit(solution)/shard_map/pallas_call | solution.py:516
  142.8 10.4 %shard_map.251 = (bf16[2,64,768]{2,1,0:T(8,128)(2,1)}, f32[128,768]{1,0:T(8,128)}, bf16[8,32,384]{2,1,0:T(8,128)(2,1)}, bf16[128,9216]{1,0:T(8,128)(2,1)S(1)}, f32[16,768]{1,0:T(8,128)}) custom-call(bf16[8,32,384]{2,1,0:T(8,128)(2,1)} %copy-done.11, bf16[2,64,768]{2,1,0:T(8,128)(2,1)} %x_ref.5, bf16[2,64,768]{2,1,0:T(8,128)(2,1)} %teacher_ref.1, ...), custom_call_target="tpu_custom_call" | custom-call | tf_op jit(solution)/shard_map/pallas_call | solution.py:81
  153.4 5.6 %all-to-all-start.4 = ((bf16[8,32,384]{2,1,0:T(8,128)(2,1)}), bf16[8,32,384]{2,1,0:T(8,128)(2,1)S(1)}, u32[]{:S(2)}, u32[]{:S(2)}) async-start(bf16[8,32,384]{2,1,0:T(8,128)(2,1)} %get-tuple-element.131), calls=%async_computation.4 | async-start | bytes 393216 | tf_op jit(solution)/shard_map/all_to_all | solution.py:982
  159.0 6.8 %shard_map.252 = (bf16[2,4,9,24,128]{4,3,2,1,0:T(8,128)(2,1)}, bf16[2,4,9,24,128]{4,3,2,1,0:T(8,128)(2,1)}, bf16[2,4,9,24,256]{4,3,2,1,0:T(8,128)(2,1)}, bf16[2,...) custom-call(s32[5]{0:T(128)S(1)} %stack.71.place_ref, ...), custom_call_target="tpu_custom_call" | custom-call | tf_op jit(solution)/shard_map/pallas_call | solution.py:81
  170.2 13.0 %shard_map.253 = (bf16[8,32,384]{2,1,0:T(8,128)(2,1)S(1)}, f32[512,384]{1,0:T(8,128)S(1)}, f32[512,384]{1,0:T(8,128)S(1)}, bf16[1024,384]{1,0:T(8,128)(2,1)S(1)}) custom-call(bf16[8,32,384]{2,1,0:T(8,128)(2,1)} %copy-done.2, bf16[8,32,384]{2,1,0:T(8,128)(2,1)} %copy-done.10, bf16[512,384]{1,0:T(8,128)(2,1)} %bitcast.104, bf16[512,384]{1,0:T(8,128)(2,1)} %copy-done.3, ...), custom_call_target="tpu_custom_call" | custom-call | tf_op jit(solution)/shard_map/pallas_call | solution.py:442
  188.7 9.1 %collective-permute-done.16 = bf16[512,384]{1,0:T(8,128)(2,1)S(1)} collective-permute-done((bf16[512,384]{1,0:T(8,128)(2,1)S(1)}, bf16[512,384]{1,0:T(8,128)(2,1)S(1)}, u32[]{:S(2)}, u32[]{:S(2)}) %collective-permute-start.16) | collective-permute-done | bytes 393248 | tf_op jit(solution)/shard_map/ppermute | solution.py:44
  198.8 6.6 %collective-permute-done.17 = bf16[2,4,9,24,256]{4,3,2,1,0:T(8,128)(2,1)S(1)} collective-permute-done((bf16[2,4,9,24,256]{4,3,2,1,0:T(8,128)(2,1)S(1)}, bf16[2,4,9,24,256]{4,3,2,1,0:T(8,128)(2,1)S(1)}, u32[]{:S(2)}, u32[]{:S(2)}) %collective-permute-start.17) | collective-permute-done | bytes 884768 | tf_op jit(solution)/shard_map/ppermute | solution.py:44
  206.3 3.9 %all-to-all-start.5 = ((bf16[8,96,384]{2,1,0:T(8,128)(2,1)}), bf16[8,96,384]{2,1,0:T(8,128)(2,1)S(1)}, u32[]{:S(2)}, u32[]{:S(2)}) async-start(bf16[8,96,384]{2,1,0:T(8,128)(2,1)} %pad_maximum_fusion.6), calls=%async_computation.5 | async-start | bytes 1179648 | tf_op jit(solution)/shard_map/all_to_all | solution.py:982
  211.1 4.9 %collective-permute-done.25 = bf16[2,4,9,24,256]{4,3,2,1,0:T(8,128)(2,1)} collective-permute-done((bf16[2,4,9,24,256]{4,3,2,1,0:T(8,128)(2,1)}, bf16[2,4,9,24,256]{4,3,2,1,0:T(8,128)(2,1)}, u32[]{:S(2)}, u32[]{:S(2)}) %collective-permute-start.25) | collective-permute-done | bytes 884768 | tf_op jit(solution)/shard_map/ppermute | solution.py:44
  221.2 4.9 %all-to-all-done.5.home_ref = bf16[8,96,384]{2,1,0:T(8,128)(2,1)S(1)} async-done(((bf16[8,96,384]{2,1,0:T(8,128)(2,1)}), bf16[8,96,384]{2,1,0:T(8,128)(2,1)S(1)}, u32[]{:S(2)}, u32[]{:S(2)}) %all-to-all-start.5) | async-done | bytes 589856 | tf_op jit(solution)/shard_map/all_to_all | solution.py:982
  229.7 4.0 %shard_map.254 = (bf16[2,4,24,1152]{3,2,1,0:T(8,128)(2,1)}, bf16[2,4,24,1152]{3,2,1,0:T(8,128)(2,1)}, bf16[2,4,24,1152]{3,2,1,0:T(8,128)(2,1)}, bf16[2,4,24,1152]{3,2,1,0:T(8,128)(2,1)}) custom-call(s32[5]{0:T(128)S(1)} %stack.71.place_ref, bf16[128,768]{1,0:T(8,128)(2,1)} %get-tuple-element.153.entered_ref, bf16[128,768]{1,0:T(8,128)(2,1)} %copy-done.20, ...), custom_call_target="tpu_custom_call" | custom-call | tf_op jit(solution)/shard_map/pallas_call | solution.py:81
  240.6 2.3 collective-permute-start.29
  245.8 4.8 %shard_map.255 = (f32[2,64,768]{2,1,0:T(8,128)}, f32[32,512]{1,0:T(8,128)S(1)}, bf16[128,2304]{1,0:T(8,128)(2,1)}) custom-call(bf16[8,96,384]{2,1,0:T(8,128)(2,1)} %copy-done, bf16[2,64,768]{2,1,0:T(8,128)(2,1)} %x_ref.5, f32[128,768]{1,0:T(8,128)} %get-tuple-element.159.hidden_ref, f32[8,4608]{1,0:T(8,128)} %get-tuple-element.113.mod_ref, ...), custom_call_target="tpu_custom_call" | custom-call | tf_op jit(solution)/shard_map/pallas_call | solution.py:81
  252.8 4.7 %all-to-all-start.6 = ((f32[32,1,512]{2,1,0:T(1,128)}), f32[32,1,512]{2,1,0:T(1,128)}, u32[]{:S(2)}, u32[]{:S(2)}) async-start(f32[32,1,512]{2,1,0:T(1,128)} %copy.35), calls=%async_computation.6 | async-start | bytes 131072 | tf_op jit(solution)/shard_map/all_to_all | solution.py:1151
  260.7 3.5 %collective-permute-start.32 = (bf16[24,2304]{1,0:T(8,128)(2,1)}, bf16[24,2304]{1,0:T(8,128)(2,1)}, u32[]{:S(2)}, u32[]{:S(2)}) collective-permute-start(bf16[24,2304]{1,0:T(8,128)(2,1)} %get-tuple-element.243), channel_id=1, source_target_pairs={{0,6},{2,0},{4,2},{6,4},{1,7},{3,1},{5,3},{7,5},{8,14},{10,8},{12,... | collective-permute-start | bytes 331784 | tf_op jit(solution)/shard_map/ppermute | solution.py:49
  264.2 3.9 %collective-permute-start.30 = (bf16[24,2304]{1,0:T(8,128)(2,1)}, bf16[24,2304]{1,0:T(8,128)(2,1)}, u32[]{:S(2)}, u32[]{:S(2)}) collective-permute-start(bf16[24,2304]{1,0:T(8,128)(2,1)} %get-tuple-element.245), channel_id=1, source_target_pairs={{0,2},{2,4},{4,6},{6,0},{1,3},{3,5},{5,7},{7,1},{8,10},{10,12},{12... | collective-permute-start | bytes 331784 | tf_op jit(solution)/shard_map/ppermute | solution.py:49
  268.1 12.0 %all-to-all-done.6 = f32[32,1,512]{2,1,0:T(1,128)} async-done(((f32[32,1,512]{2,1,0:T(1,128)}), f32[32,1,512]{2,1,0:T(1,128)}, u32[]{:S(2)}, u32[]{:S(2)}) %all-to-all-start.6) | async-done | bytes 65568 | tf_op jit(solution)/shard_map/all_to_all | solution.py:1151
  (144 shorter events, 72.0 us)
Async XLA Ops:
  7.2 126.4 %all-gather.3.cloned.1.call-start = ((), (), s32[]{:S(2)}) async-start(), calls=%async_computation.7 | async-start | bytes 10948608 | tf_op jit(solution)/shard_map/all_gather | solution.py:1023
  12.8 9.3 %collective-permute-start.2 = (bf16[24,2304]{1,0:T(8,128)(2,1)}, bf16[24,2304]{1,0:T(8,128)(2,1)S(1)}, u32[]{:S(2)}, u32[]{:S(2)}) collective-permute-start(bf16[24,2304]{1,0:T(8,128)(2,1)} %param.23), channel_id=1, source_target_pairs={{0,2},{2,4},{4,6},{6,0},{1,3},{3,5},{5,7},{7,1},{8,10},{10,12},{12... | collective-permute-start | bytes 331784 | tf_op jit(solution)/shard_map/ppermute | solution.py:49
  15.9 10.1 %collective-permute-start.1 = (bf16[24,2304]{1,0:T(8,128)(2,1)}, bf16[24,2304]{1,0:T(8,128)(2,1)S(1)}, u32[]{:S(2)}, u32[]{:S(2)}) collective-permute-start(bf16[24,2304]{1,0:T(8,128)(2,1)} %param.23), channel_id=1, source_target_pairs={{0,4},{2,6},{4,0},{6,2},{1,5},{3,7},{5,1},{7,3},{8,12},{10,14},{12... | collective-permute-start | bytes 331784 | tf_op jit(solution)/shard_map/ppermute | solution.py:49
  18.5 7.5 %collective-permute-start = (bf16[24,2304]{1,0:T(8,128)(2,1)}, bf16[24,2304]{1,0:T(8,128)(2,1)S(1)}, u32[]{:S(2)}, u32[]{:S(2)}) collective-permute-start(bf16[24,2304]{1,0:T(8,128)(2,1)} %param.23), channel_id=1, source_target_pairs={{0,6},{2,0},{4,2},{6,4},{1,7},{3,1},{5,3},{7,5},{8,14},{10,8},{12,... | collective-permute-start | bytes 331784 | tf_op jit(solution)/shard_map/ppermute | solution.py:49
  27.1 17.5 %collective-permute-start.4 = (bf16[4,24,1152]{2,1,0:T(8,128)(2,1)S(1)}, bf16[4,24,1152]{2,1,0:T(8,128)(2,1)S(1)}, u32[]{:S(2)}, u32[]{:S(2)}) collective-permute-start(bf16[4,24,1152]{2,1,0:T(8,128)(2,1)S(1)} %get-tuple-element.248), channel_id=1, source_target_pairs={{0,1},{1,0},{2,3},{3,2},{4,5},{5,4},{6,7},{7,6},{8,9},{9,8},{10,11... | collective-permute-start | bytes 663560 | tf_op jit(solution)/shard_map/ppermute | solution.py:44
  29.4 14.5 %all-to-all-start = ((f32[32,1,640]{2,1,0:T(1,128)}), f32[32,1,640]{2,1,0:T(1,128)S(1)}, u32[]{:S(2)}, u32[]{:S(2)}) async-start(f32[32,1,640]{2,1,0:T(1,128)} %copy.34), calls=%async_computation | async-start | bytes 163840 | tf_op jit(solution)/shard_map/all_to_all | solution.py:1016
  36.5 8.8 %collective-permute-start.3 = (bf16[4,24,1152]{2,1,0:T(8,128)(2,1)S(1)}, bf16[4,24,1152]{2,1,0:T(8,128)(2,1)S(1)}, u32[]{:S(2)}, u32[]{:S(2)}) collective-permute-start(bf16[4,24,1152]{2,1,0:T(8,128)(2,1)S(1)} %get-tuple-element.249), channel_id=1, source_target_pairs={{0,16},{16,0},{1,17},{17,1},{2,18},{18,2},{3,19},{19,3},{4,20},{20... | collective-permute-start | bytes 663560 | tf_op jit(solution)/shard_map/ppermute | solution.py:44
  45.3 14.0 %collective-permute-start.5 = (bf16[2,4,24,1152]{3,2,1,0:T(8,128)(2,1)S(1)}, bf16[2,4,24,1152]{3,2,1,0:T(8,128)(2,1)S(1)}, u32[]{:S(2)}, u32[]{:S(2)}) collective-permute-start(bf16[2,4,24,1152]{3,2,1,0:T(8,128)(2,1)S(1)} %pad_maximum_fusion.8), channel_id=1, source_target_pairs={{0,1},{1,0},{2,3},{3,2},{4,5},{5,4},{6,7},{7,6},{8,9},{9,8},{10,11... | collective-permute-start | bytes 1327112 | tf_op jit(solution)/shard_map/ppermute | solution.py:44
  46.7 17.4 %collective-permute-start.6 = (bf16[2,4,24,1152]{3,2,1,0:T(8,128)(2,1)S(1)}, bf16[2,4,24,1152]{3,2,1,0:T(8,128)(2,1)S(1)}, u32[]{:S(2)}, u32[]{:S(2)}) collective-permute-start(bf16[2,4,24,1152]{3,2,1,0:T(8,128)(2,1)S(1)} %pad_maximum_fusion.9), channel_id=1, source_target_pairs={{0,16},{16,0},{1,17},{17,1},{2,18},{18,2},{3,19},{19,3},{4,20},{20... | collective-permute-start | bytes 1327112 | tf_op jit(solution)/shard_map/ppermute | solution.py:44
  103.2 15.0 %collective-permute-start.9 = (bf16[512,384]{1,0:T(8,128)(2,1)S(1)}, bf16[512,384]{1,0:T(8,128)(2,1)S(1)}, u32[]{:S(2)}, u32[]{:S(2)}) collective-permute-start(bf16[512,384]{1,0:T(8,128)(2,1)S(1)} %bitcast.101), channel_id=1, source_target_pairs={{0,16},{16,0},{1,17},{17,1},{2,18},{18,2},{3,19},{19,3},{4,20},{20... | collective-permute-start | bytes 1179656 | tf_op jit(solution)/shard_map/ppermute | solution.py:44
  104.2 13.9 %all-to-all-start.2 = ((bf16[8,32,384]{2,1,0:T(8,128)(2,1)}), bf16[8,32,384]{2,1,0:T(8,128)(2,1)S(1)}, u32[]{:S(2)}, u32[]{:S(2)}) async-start(bf16[8,32,384]{2,1,0:T(8,128)(2,1)} %get-tuple-element.118), calls=%async_computation.2 | async-start | bytes 393216 | tf_op jit(solution)/shard_map/all_to_all | solution.py:982
  107.6 10.6 %collective-permute-start.10 = (bf16[512,384]{1,0:T(8,128)(2,1)S(1)}, bf16[512,384]{1,0:T(8,128)(2,1)S(1)}, u32[]{:S(2)}, u32[]{:S(2)}) collective-permute-start(bf16[512,384]{1,0:T(8,128)(2,1)S(1)} %bitcast.102), channel_id=1, source_target_pairs={{0,8},{8,0},{1,9},{9,1},{2,10},{10,2},{3,11},{11,3},{4,12},{12,4},... | collective-permute-start | bytes 1179656 | tf_op jit(solution)/shard_map/ppermute | solution.py:44
  129.9 12.1 %all-to-all-start.3 = ((bf16[8,32,384]{2,1,0:T(8,128)(2,1)}), bf16[8,32,384]{2,1,0:T(8,128)(2,1)S(1)}, u32[]{:S(2)}, u32[]{:S(2)}) async-start(bf16[8,32,384]{2,1,0:T(8,128)(2,1)} %get-tuple-element.123), calls=%async_computation.3 | async-start | bytes 393216 | tf_op jit(solution)/shard_map/all_to_all | solution.py:982
  153.4 14.2 %all-to-all-start.4 = ((bf16[8,32,384]{2,1,0:T(8,128)(2,1)}), bf16[8,32,384]{2,1,0:T(8,128)(2,1)S(1)}, u32[]{:S(2)}, u32[]{:S(2)}) async-start(bf16[8,32,384]{2,1,0:T(8,128)(2,1)} %get-tuple-element.131), calls=%async_computation.4 | async-start | bytes 393216 | tf_op jit(solution)/shard_map/all_to_all | solution.py:982
  167.6 15.6 %collective-permute-start.13 = (bf16[2,4,9,24,128]{4,3,2,1,0:T(8,128)(2,1)}, bf16[2,4,9,24,128]{4,3,2,1,0:T(8,128)(2,1)S(1)}, u32[]{:S(2)}, u32[]{:S(2)}) collective-permute-start(bf16[2,4,9,24,128]{4,3,2,1,0:T(8,128)(2,1)} %get-tuple-element.146), channel_id=1, source_target_pairs={{0,1},{1,0},{2,3},{3,2},{4,5},{5,4},{6,7},{7,6},{8,9},{9,8},{10,11... | collective-permute-start | bytes 1327112 | tf_op jit(solution)/shard_map/ppermute | solution.py:44
  168.6 14.6 %collective-permute-start.14 = (bf16[2,4,9,24,128]{4,3,2,1,0:T(8,128)(2,1)}, bf16[2,4,9,24,128]{4,3,2,1,0:T(8,128)(2,1)S(1)}, u32[]{:S(2)}, u32[]{:S(2)}) collective-permute-start(bf16[2,4,9,24,128]{4,3,2,1,0:T(8,128)(2,1)} %get-tuple-element.147), channel_id=1, source_target_pairs={{0,16},{16,0},{1,17},{17,1},{2,18},{18,2},{3,19},{19,3},{4,20},{20... | collective-permute-start | bytes 1327112 | tf_op jit(solution)/shard_map/ppermute | solution.py:44
  183.3 22.1 %collective-permute-start.17 = (bf16[2,4,9,24,256]{4,3,2,1,0:T(8,128)(2,1)S(1)}, bf16[2,4,9,24,256]{4,3,2,1,0:T(8,128)(2,1)S(1)}, u32[]{:S(2)}, u32[]{:S(2)}) collective-permute-start(bf16[2,4,9,24,256]{4,3,2,1,0:T(8,128)(2,1)S(1)} %copy-done.21), channel_id=1, source_target_pairs={{0,1},{1,0},{2,3},{3,2},{4,5},{5,4},{6,7},{7,6},{8,9},{9,8},{10,11... | collective-permute-start | bytes 2654216 | tf_op jit(solution)/shard_map/ppermute | solution.py:44
  185.7 12.0 %collective-permute-start.16 = (bf16[512,384]{1,0:T(8,128)(2,1)S(1)}, bf16[512,384]{1,0:T(8,128)(2,1)S(1)}, u32[]{:S(2)}, u32[]{:S(2)}) collective-permute-start(bf16[512,384]{1,0:T(8,128)(2,1)S(1)} %add_convert_fusion.3), channel_id=1, source_target_pairs={{0,16},{16,0},{1,17},{17,1},{2,18},{18,2},{3,19},{19,3},{4,20},{20... | collective-permute-start | bytes 1179656 | tf_op jit(solution)/shard_map/ppermute | solution.py:44
  186.2 29.8 %collective-permute-start.25 = (bf16[2,4,9,24,256]{4,3,2,1,0:T(8,128)(2,1)}, bf16[2,4,9,24,256]{4,3,2,1,0:T(8,128)(2,1)}, u32[]{:S(2)}, u32[]{:S(2)}) collective-permute-start(bf16[2,4,9,24,256]{4,3,2,1,0:T(8,128)(2,1)} %get-tuple-element.179), channel_id=1, source_target_pairs={{0,16},{16,0},{1,17},{17,1},{2,18},{18,2},{3,19},{19,3},{4,20},{20... | collective-permute-start | bytes 2654216 | tf_op jit(solution)/shard_map/ppermute | solution.py:44
  206.3 19.7 %all-to-all-start.5 = ((bf16[8,96,384]{2,1,0:T(8,128)(2,1)}), bf16[8,96,384]{2,1,0:T(8,128)(2,1)S(1)}, u32[]{:S(2)}, u32[]{:S(2)}) async-start(bf16[8,96,384]{2,1,0:T(8,128)(2,1)} %pad_maximum_fusion.6), calls=%async_computation.5 | async-start | bytes 1179648 | tf_op jit(solution)/shard_map/all_to_all | solution.py:982
  218.4 17.8 %collective-permute-start.26 = (bf16[4,9,24,384]{3,2,1,0:T(8,128)(2,1)}, bf16[4,9,24,384]{3,2,1,0:T(8,128)(2,1)}, u32[]{:S(2)}, u32[]{:S(2)}) collective-permute-start(bf16[4,9,24,384]{3,2,1,0:T(8,128)(2,1)} %pad_maximum_fusion.5), channel_id=1, source_target_pairs={{0,1},{1,0},{2,3},{3,2},{4,5},{5,4},{6,7},{7,6},{8,9},{9,8},{10,11... | collective-permute-start | bytes 1990664 | tf_op jit(solution)/shard_map/ppermute | solution.py:44
  220.7 15.9 %collective-permute-start.24 = (bf16[4,9,24,384]{3,2,1,0:T(8,128)(2,1)S(1)}, bf16[4,9,24,384]{3,2,1,0:T(8,128)(2,1)S(1)}, u32[]{:S(2)}, u32[]{:S(2)}) collective-permute-start(bf16[4,9,24,384]{3,2,1,0:T(8,128)(2,1)S(1)} %pad_maximum_fusion.4), channel_id=1, source_target_pairs={{0,16},{16,0},{1,17},{17,1},{2,18},{18,2},{3,19},{19,3},{4,20},{20... | collective-permute-start | bytes 1990664 | tf_op jit(solution)/shard_map/ppermute | solution.py:44
  233.7 17.0 %collective-permute-start.20 = (bf16[2,4,24,1152]{3,2,1,0:T(8,128)(2,1)}, bf16[2,4,24,1152]{3,2,1,0:T(8,128)(2,1)S(1)}, u32[]{:S(2)}, u32[]{:S(2)}) collective-permute-start(bf16[2,4,24,1152]{3,2,1,0:T(8,128)(2,1)} %get-tuple-element.155), channel_id=1, source_target_pairs={{0,1},{1,0},{2,3},{3,2},{4,5},{5,4},{6,7},{7,6},{8,9},{9,8},{10,11... | collective-permute-start | bytes 1327112 | tf_op jit(solution)/shard_map/ppermute | solution.py:44
  235.2 15.5 %collective-permute-start.21 = (bf16[2,4,24,1152]{3,2,1,0:T(8,128)(2,1)}, bf16[2,4,24,1152]{3,2,1,0:T(8,128)(2,1)S(1)}, u32[]{:S(2)}, u32[]{:S(2)}) collective-permute-start(bf16[2,4,24,1152]{3,2,1,0:T(8,128)(2,1)} %get-tuple-element.157), channel_id=1, source_target_pairs={{0,16},{16,0},{1,17},{17,1},{2,18},{18,2},{3,19},{19,3},{4,20},{20... | collective-permute-start | bytes 1327112 | tf_op jit(solution)/shard_map/ppermute | solution.py:44
  240.6 23.6 %collective-permute-start.29 = (bf16[9,24,768]{2,1,0:T(8,128)(2,1)}, bf16[9,24,768]{2,1,0:T(8,128)(2,1)}, u32[]{:S(2)}, u32[]{:S(2)}) collective-permute-start(bf16[9,24,768]{2,1,0:T(8,128)(2,1)} %get-tuple-element.234), channel_id=1, source_target_pairs={{0,6},{2,0},{4,2},{6,4},{1,7},{3,1},{5,3},{7,5},{8,14},{10,8},{12,... | collective-permute-start | bytes 995336 | tf_op jit(solution)/shard_map/ppermute | solution.py:49
  242.9 42.1 %collective-permute-start.28 = (bf16[9,24,768]{2,1,0:T(8,128)(2,1)}, bf16[9,24,768]{2,1,0:T(8,128)(2,1)}, u32[]{:S(2)}, u32[]{:S(2)}) collective-permute-start(bf16[9,24,768]{2,1,0:T(8,128)(2,1)} %get-tuple-element.235), channel_id=1, source_target_pairs={{0,4},{2,6},{4,0},{6,2},{1,5},{3,7},{5,1},{7,3},{8,12},{10,14},{12... | collective-permute-start | bytes 995336 | tf_op jit(solution)/shard_map/ppermute | solution.py:49
  243.8 41.2 %collective-permute-start.27 = (bf16[9,24,768]{2,1,0:T(8,128)(2,1)}, bf16[9,24,768]{2,1,0:T(8,128)(2,1)}, u32[]{:S(2)}, u32[]{:S(2)}) collective-permute-start(bf16[9,24,768]{2,1,0:T(8,128)(2,1)} %get-tuple-element.236), channel_id=1, source_target_pairs={{0,2},{2,4},{4,6},{6,0},{1,3},{3,5},{5,7},{7,1},{8,10},{10,12},{12... | collective-permute-start | bytes 995336 | tf_op jit(solution)/shard_map/ppermute | solution.py:49
  251.7 6.9 %collective-permute-start.22 = (bf16[4,24,1152]{2,1,0:T(8,128)(2,1)}, bf16[4,24,1152]{2,1,0:T(8,128)(2,1)}, u32[]{:S(2)}, u32[]{:S(2)}) collective-permute-start(bf16[4,24,1152]{2,1,0:T(8,128)(2,1)} %fusion.8), channel_id=1, source_target_pairs={{0,16},{16,0},{1,17},{17,1},{2,18},{18,2},{3,19},{19,3},{4,20},{20... | collective-permute-start | bytes 663560 | tf_op jit(solution)/shard_map/ppermute | solution.py:44
  252.8 27.2 %all-to-all-start.6 = ((f32[32,1,512]{2,1,0:T(1,128)}), f32[32,1,512]{2,1,0:T(1,128)}, u32[]{:S(2)}, u32[]{:S(2)}) async-start(f32[32,1,512]{2,1,0:T(1,128)} %copy.35), calls=%async_computation.6 | async-start | bytes 131072 | tf_op jit(solution)/shard_map/all_to_all | solution.py:1151
  260.7 24.3 %collective-permute-start.32 = (bf16[24,2304]{1,0:T(8,128)(2,1)}, bf16[24,2304]{1,0:T(8,128)(2,1)}, u32[]{:S(2)}, u32[]{:S(2)}) collective-permute-start(bf16[24,2304]{1,0:T(8,128)(2,1)} %get-tuple-element.243), channel_id=1, source_target_pairs={{0,6},{2,0},{4,2},{6,4},{1,7},{3,1},{5,3},{7,5},{8,14},{10,8},{12,... | collective-permute-start | bytes 331784 | tf_op jit(solution)/shard_map/ppermute | solution.py:49
  264.2 20.8 %collective-permute-start.31 = (bf16[24,2304]{1,0:T(8,128)(2,1)}, bf16[24,2304]{1,0:T(8,128)(2,1)}, u32[]{:S(2)}, u32[]{:S(2)}) collective-permute-start(bf16[24,2304]{1,0:T(8,128)(2,1)} %get-tuple-element.244), channel_id=1, source_target_pairs={{0,4},{2,6},{4,0},{6,2},{1,5},{3,7},{5,1},{7,3},{8,12},{10,14},{12... | collective-permute-start | bytes 331784 | tf_op jit(solution)/shard_map/ppermute | solution.py:49
  264.2 20.8 %collective-permute-start.30 = (bf16[24,2304]{1,0:T(8,128)(2,1)}, bf16[24,2304]{1,0:T(8,128)(2,1)}, u32[]{:S(2)}, u32[]{:S(2)}) collective-permute-start(bf16[24,2304]{1,0:T(8,128)(2,1)} %get-tuple-element.245), channel_id=1, source_target_pairs={{0,2},{2,4},{4,6},{6,0},{1,3},{3,5},{5,7},{7,1},{8,10},{10,12},{12... | collective-permute-start | bytes 331784 | tf_op jit(solution)/shard_map/ppermute | solution.py:49
  (30 other events, 126.9 us)
Sparse Core Ops, SparseCore 0:
  12.9 107.6 all-gather.2

commit v7 on v6

--- a/solution.py
+++ b/solution.py
@@ -159,13 +159,6 @@
 
 def third_recvs(total):
     return [turn(total[k].astype(bf16), "sz", -k) for k in (1, 2, 3)]
-
-
-def third_total(total, recvs):
-    result = total[0]
-    for recv in recvs:
-        result = result + recv.astype(f32)
-    return result
 
 
 def enter_kernel(place_ref, x_ref, mod_ref, gains_ref, *refs):
@@ -808,9 +801,9 @@
     for field in fields:
         size = field.shape[1] // devices
         for i in range(devices):
-            small_ref[i : i + 1, pl.ds(begin, size)] = field[:, i * size : (i + 1) * size]
+            small_ref[i, :, pl.ds(begin, size)] = field[:, i * size : (i + 1) * size]
         begin += size
-    small_ref[:, pl.ds(begin, 1)] = jnp.broadcast_to(error, (devices, 1))
+    small_ref[:, :, pl.ds(begin, 1)] = jnp.broadcast_to(error[None], (devices, 1, 1))
 
 
 def leave(home, inputs, grad_hidden, modulation, gains, weight, sums, devices):
@@ -819,7 +812,7 @@
         leave_kernel,
         [
             ((seqs, tokens, width), f32),
-            ((devices, 512), f32, True),
+            ((devices, 1, 512), f32, True),
             ((seqs * tokens, 3 * width), bf16),
         ],
         [home, inputs, grad_hidden, modulation, gains, weight, sums],
@@ -842,9 +835,7 @@
     targets += [(up_ref, 0, size_up), (gains_ref, 2, size_gain)]
     for target, row, size in targets:
         for i in range(devices):
-            target[row : row + 1, pl.ds(i * size, size)] = every_ref[
-                i : i + 1, pl.ds(begin, size)
-            ]
+            target[row : row + 1, pl.ds(i * size, size)] = every_ref[i, :, pl.ds(begin, size)]
         begin += size
     hx, hc, sz, sy, rb = (place_ref[i] for i in range(5))
     second = sz * 2 + sy >= GROUPS
@@ -853,21 +844,19 @@
         for across in range(2):
             for part in range(parts):
                 block = ((hx ^ across) * 2 + (hc ^ core)) * parts + part
-                lines = every_ref[pl.ds(pl.multiple_of(block * 8, 8), 8), pl.ds(begin, 2 * tokens)]
-                lines = jnp.where(second, lines[:, tokens:], lines[:, :tokens])
                 for spot in range(8):
-                    key_docs_ref[row : row + 1, pl.ds(spot * tokens, tokens)] = lines[
-                        spot : spot + 1
-                    ]
+                    line = every_ref[block * 8 + spot, :, pl.ds(begin, 2 * tokens)]
+                    key_docs_ref[row : row + 1, pl.ds(spot * tokens, tokens)] = jnp.where(
+                        second, line[:, tokens:], line[:, :tokens]
+                    )
                 row += 1
-    lines = every_ref[
-        pl.ds(pl.multiple_of(((hx * 2 + hc) * parts + rb) * 8, 8), 8), pl.ds(begin, 2 * tokens)
-    ]
-    lines = jnp.where(second, lines[:, tokens:], lines[:, :tokens])
     for spot in range(8):
-        query_docs_ref[:, pl.ds(spot * tokens, tokens)] = lines[spot : spot + 1]
+        line = every_ref[((hx * 2 + hc) * parts + rb) * 8 + spot, :, pl.ds(begin, 2 * tokens)]
+        query_docs_ref[:, pl.ds(spot * tokens, tokens)] = jnp.where(
+            second, line[:, tokens:], line[:, :tokens]
+        )
     begin += 2 * tokens
-    count = jnp.sum(every_ref[:, pl.ds(begin, 1)], axis=0, keepdims=True)
+    count = jnp.sum(every_ref[:, :, pl.ds(begin, 1)], axis=0)
     gains_ref[3:4, pl.ds(0, 1)] = count
     masks_ref[...] = jnp.zeros(masks_ref.shape, f32)
     for s in range(seqs):
@@ -898,15 +887,15 @@
 def finish_kernel(width, small_ref, embed_ref, gains_ref, *refs):
     ada_ref, bias_ref, *vectors, loss_ref = refs
     seqs = embed_ref.shape[0]
-    columns = ada_ref.shape[1]
-    added = jnp.sum(small_ref[...], axis=0, keepdims=True)
-    turned = embed_ref[...].T
+    columns = ada_ref.shape[0]
+    added = jnp.sum(small_ref[...], axis=0)
     begin = 0
     ada = bias = None
     for s in range(seqs):
         grad = added[:, begin : begin + columns]
         begin += columns
-        term = turned[:, s : s + 1] * grad
+        turned = jnp.broadcast_to(grad, (8, columns)).T[:, 0:1]
+        term = turned * embed_ref[s : s + 1, :]
         ada = term if ada is None else ada + term
         bias = grad if bias is None else bias + grad
     ada_ref[...] = ada
@@ -923,36 +912,75 @@
     sizes = [6 * width // devices] + [size // devices for size in (width, width, units, width)]
     return single(
         partial(finish_kernel, float(width)),
-        [((time_embed.shape[1], sizes[0]), f32)]
+        [((sizes[0], time_embed.shape[1]), f32)]
         + [((1, size), f32, True) for size in sizes]
         + [((1, 1), f32, True)],
         [small, time_embed, gains],
     )
 
 
+def grads_kernel(total_ref, first_ref, second_ref, third_ref, *refs):
+    qkv_total, qkv_first, qkv_second, qkv_third, out_ref, up_ref, down_ref, qkv_ref = refs
+    width = out_ref.shape[1]
+    for j in range(9):
+        value = total_ref[0, j]
+        for ref in (first_ref, second_ref, third_ref):
+            value = value + ref[j].astype(f32)
+        if j == 0:
+            out_ref[...] = value
+        elif j < 5:
+            up_ref[:, pl.ds((j - 1) * width, width)] = value
+        else:
+            down_ref[pl.ds((j - 5) * 24, 24), :] = value
+    value = qkv_total[0]
+    for ref in (qkv_first, qkv_second, qkv_third):
+        value = value + ref[...].astype(f32)
+    qkv_ref[...] = value
+
+
+def weight_grads(total, third, qkv_total, third_qkv):
+    width = total.shape[-1]
+    values = [total, *third, qkv_total, *third_qkv]
+    specs = [
+        pl.BlockSpec((1,) + v.shape[1:], lambda i, n=v.ndim: (0,) * n)
+        if i in (0, 4)
+        else whole_spec(v.shape)
+        for i, v in enumerate(values)
+    ]
+    shapes = ((24, width), (24, 4 * width), (96, width), (24, 3 * width))
+    return pl.pallas_call(
+        grads_kernel,
+        grid=(1,),
+        out_shape=tuple(jax.ShapeDtypeStruct(shape, f32) for shape in shapes),
+        in_specs=specs,
+        out_specs=tuple(whole_spec(shape) for shape in shapes),
+        compiler_params=pltpu.CompilerParams(vmem_limit_bytes=40 << 20),
+    )(*values)
+
+
 def begin_kernel(embed_ref, ada_ref, vectors_ref, segments_ref, valid_ref, *refs):
     *weights, packed_ref = refs[:-1] if len(refs) > 1 else refs
     seqs, tokens = segments_ref.shape
-    modulation = jnp.dot(
-        embed_ref[...], ada_ref[...].astype(f32), precision=precise, preferred_element_type=f32
+    modulation = lax.dot_general(
+        embed_ref[...],
+        ada_ref[...].astype(f32),
+        (((1,), (1,)), ((), ())),
+        precision=precise,
+        preferred_element_type=f32,
     )
     size = modulation.shape[1]
-    modulation = modulation + vectors_ref[:, pl.ds(0, size)]
-    rest = vectors_ref.shape[1] - size
+    vectors = vectors_ref[...].astype(f32)
+    modulation = modulation + vectors[:, :size]
     count = jnp.sum(valid_ref[...].astype(f32), axis=1, keepdims=True)
     count = jnp.sum(count, axis=0, keepdims=True)
     fields = [modulation[s : s + 1] for s in range(seqs)]
-    fields.append(vectors_ref[:, pl.ds(size, rest)])
+    fields.append(vectors[:, size:])
     fields += [segments_ref[s : s + 1, :].astype(f32) for s in range(seqs)]
     fields.append(count)
-    packed_ref[...] = jnp.zeros(packed_ref.shape, f32)
-    begin = 0
-    for field in fields:
-        columns = pl.ds(begin, field.shape[1])
-        packed_ref[:, columns] = jnp.broadcast_to(
-            field, (packed_ref.shape[0], field.shape[1])
-        )
-        begin += field.shape[1]
+    fields.append(jnp.zeros((1, packed_ref.shape[2] - sum(f.shape[1] for f in fields)), f32))
+    packed_ref[...] = jnp.broadcast_to(
+        jnp.concatenate(fields, axis=1)[None], packed_ref.shape
+    )
     if weights:
         out_ref, up_ref, down_ref = weights
         later_ref = refs[-1]
@@ -965,12 +993,12 @@
 
 def begin_with(time_embed, ada_weight, vectors, segments, valid_mask, weights, devices):
     seqs, tokens = segments.shape
-    columns = seqs * ada_weight.shape[1] + vectors.shape[1] - ada_weight.shape[1] + seqs * tokens + 1
-    outs = [((devices, columns + -columns % 128), f32, True)]
+    columns = (seqs - 1) * ada_weight.shape[1] + vectors.shape[1] + seqs * tokens + 1
+    outs = [((devices, 1, columns + -columns % 128), f32, True)]
     if weights:
         outs.append(((9, 24, weights[0].shape[1]), bf16))
     return single(
-        begin_kernel, outs, [time_embed, ada_weight, vectors, segments, valid_mask, *weights]
+        begin_kernel, outs, [time_embed, ada_weight.T, vectors, segments, valid_mask, *weights]
     )
 
 
@@ -1007,8 +1035,8 @@
     queries = 8 * tokens
     here = place()
 
-    vectors = jnp.concatenate([ada_bias, gain_attn, gain_mlp, up_bias, down_bias])
-    vectors = vectors.astype(f32).reshape(1, -1)
+    vectors = [ada_bias, gain_attn, gain_mlp, up_bias, down_bias]
+    vectors = jnp.concatenate([v.astype(f32) for v in vectors]).reshape(1, -1)
     weights = [] if parts > 1 else [out_weight, up_weight, down_weight]
     packed, *later = begin_with(
         time_embed, ada_weight, vectors, segments, valid_mask, weights, devices
@@ -1123,11 +1151,9 @@
         )
         third_qkv = third_recvs(second_qkv)
         third, third_qkv = lax.optimization_barrier((third, third_qkv))
-        owned_later = third_total(second, third)
-        shard_qkv = third_total(second_qkv, third_qkv)
-        shard_out = owned_later[0]
-        shard_up = owned_later[1:5].transpose(1, 0, 2).reshape(24, units)
-        shard_down = owned_later[5:].reshape(96, width)
+        shard_out, shard_up, shard_down, shard_qkv = weight_grads(
+            second, third, second_qkv, third_qkv
+        )
     if parts > 1:
         grad_input, small, flat = leave(
             home, inputs, grad_hidden, modulation, gains, full_qkv, sums, devices
@@ -1157,7 +1183,7 @@
         final,
         loss_value,
         grad_input,
-        grads[0],
+        grads[0].T,
         grads[1].reshape(-1),
         grads[2].reshape(-1),
         shard_qkv,

time: 298 us -> 293 us (0.983)
  local copies, waits for them, and re-layouts: 16.7 us -> 11.2 us
  other arithmetic: 16.7 us -> 13.2 us
  Pallas kernels: 69.5 us -> 72.5 us
  waiting for transfers between devices: 83.9 us -> 86.9 us
    ppermute x24, waiting for transfers between devices: 43 us -> 55.2 us  [swap(): return lax.ppermute(value, axis, [(0, 1), (1, 0)])]
    all_to_all x1, waiting for transfers between devices: 5.59 us -> 0.01 us  [on_device(): every = lax.all_to_all(packed, EVERY, 0, 0, tiled=True)]
    unnamed x48 -> x40, local copies, waits for them, and re-layouts: 9.82 us -> 5.27 us
    add x2 -> x0, other arithmetic: 3.04 us -> none  [third_total(): result = result + recv.astype(f32)]
  transfers between devices with their start and end apart: 40 -> 40, of which waited for: 21 -> 22; matrix products, arithmetic and copies ran while one was open for 7% -> 5% of each run, Pallas kernels for 19% -> 20%
where the time goes in v7:
time: 293 us; the launch traced here: 292 us
  waiting for transfers between devices  86.9 us (30%)
  Pallas kernels  72.5 us (25%)
  starting transfers between devices  65.1 us (22%)
  blocking collectives  28.3 us (10%)
  between operations  14.5 us (5%)
  other arithmetic  13.2 us (5%)
  local copies, waits for them, and re-layouts  11.2 us (4%)
    ppermute x24, waiting for transfers between devices, swap(): return lax.ppermute(value, axis, [(0, 1), (1, 0)])  55.2 us
    pallas_call x8, Pallas kernels, single(): pl.pallas_call(kernel, grid=(1,), out_shape=tuple((result(*o) for o in ou...  39.6 us
    all_to_all x1, blocking collectives, exchange(): return lax.all_to_all(rows, SPOT, 0, 0, tiled=True)  28.3 us
    ppermute x24, starting transfers between devices, swap(): return lax.ppermute(value, axis, [(0, 1), (1, 0)])  20 us
    ppermute x9, starting transfers between devices, turn(): lax.ppermute(value, axis, [(i, (i - step) % size) for i in range(size)])  17.3 us
    all_to_all x4, starting transfers between devices, exchange(): return lax.all_to_all(rows, SPOT, 0, 0, tiled=True)  16.5 us
    all_to_all x4, waiting for transfers between devices, exchange(): return lax.all_to_all(rows, SPOT, 0, 0, tiled=True)  15.4 us
    pallas_call x1, Pallas kernels, attend_back(): pl.pallas_call(partial(backward_kernel, starts), grid=(steps,), out_shape...  13 us
  transfers between devices with their start and end apart: 40, of which 22 were waited for; matrix products, arithmetic and copies ran while one was open for 5% of the time, Pallas kernels for 20%

profile of v7, /device:TPU:0, one launch (start us, length us, event | category | flops | bytes accessed | tf_op | source)
XLA Modules:
  0.0 291.7 jit_solution(8892899665228338735)
XLA Ops:
  7.2 3.4 %concatenate.25 = bf16[312]{0:T(512)(128)(2,1)S(1)} concatenate(bf16[144]{0:T(256)(128)(2,1)} %param.21, bf16[24]{0:T(256)(128)(2,1)} %param.22, bf16[24]{0:T(256)(128)(2,1)} %param.25, bf16[96]{0:T(256)(128)(2,1)} %param.27, bf16[24]{0:T(256)(128)(2,1)} %param.29), dimensions={0} | concatenate | bytes 1248 | tf_op jit(solution)/shard_map/concatenate | solution.py:1039
  13.3 3.1 %collective-permute-start.2 = (bf16[24,2304]{1,0:T(8,128)(2,1)}, bf16[24,2304]{1,0:T(8,128)(2,1)S(1)}, u32[]{:S(2)}, u32[]{:S(2)}) collective-permute-start(bf16[24,2304]{1,0:T(8,128)(2,1)} %param.23), channel_id=1, source_target_pairs={{0,2},{2,4},{4,6},{6,0},{1,3},{3,5},{5,7},{7,1},{8,10},{10,12},{12... | collective-permute-start | bytes 331784 | tf_op jit(solution)/shard_map/ppermute | solution.py:49
  16.4 2.6 collective-permute-start.1
  22.7 3.9 %collective-permute-done.1 = bf16[24,2304]{1,0:T(8,128)(2,1)S(1)} collective-permute-done((bf16[24,2304]{1,0:T(8,128)(2,1)}, bf16[24,2304]{1,0:T(8,128)(2,1)S(1)}, u32[]{:S(2)}, u32[]{:S(2)}) %collective-permute-start.1) | collective-permute-done | bytes 110624 | tf_op jit(solution)/shard_map/ppermute | solution.py:49
  29.2 7.1 %all-to-all-start = ((f32[32,1,640]{2,1,0:T(1,128)}), f32[32,1,640]{2,1,0:T(1,128)S(1)}, u32[]{:S(2)}, u32[]{:S(2)}) async-start(f32[32,1,640]{2,1,0:T(1,128)} %get-tuple-element.106), calls=%async_computation | async-start | bytes 163840 | tf_op jit(solution)/shard_map/all_to_all | solution.py:1044
  38.2 6.6 %collective-permute-done.3 = bf16[4,24,1152]{2,1,0:T(8,128)(2,1)S(1)} collective-permute-done((bf16[4,24,1152]{2,1,0:T(8,128)(2,1)S(1)}, bf16[4,24,1152]{2,1,0:T(8,128)(2,1)S(1)}, u32[]{:S(2)}, u32[]{:S(2)}) %collective-permute-start.3) | collective-permute-done | bytes 221216 | tf_op jit(solution)/shard_map/ppermute | solution.py:44
  47.9 2.5 shard_map.247
  50.4 9.5 %collective-permute-done.5 = bf16[2,4,24,1152]{3,2,1,0:T(8,128)(2,1)S(1)} collective-permute-done((bf16[2,4,24,1152]{3,2,1,0:T(8,128)(2,1)S(1)}, bf16[2,4,24,1152]{3,2,1,0:T(8,128)(2,1)S(1)}, u32[]{:S(2)}, u32[]{:S(2)}) %collective-permute-start.5) | collective-permute-done | bytes 442400 | tf_op jit(solution)/shard_map/ppermute | solution.py:44
  60.0 4.7 %collective-permute-done.6 = bf16[2,4,24,1152]{3,2,1,0:T(8,128)(2,1)S(1)} collective-permute-done((bf16[2,4,24,1152]{3,2,1,0:T(8,128)(2,1)S(1)}, bf16[2,4,24,1152]{3,2,1,0:T(8,128)(2,1)S(1)}, u32[]{:S(2)}, u32[]{:S(2)}) %collective-permute-start.6) | collective-permute-done | bytes 442400 | tf_op jit(solution)/shard_map/ppermute | solution.py:44
  68.5 6.9 %shard_map.248 = (bf16[128,768]{1,0:T(8,128)(2,1)}, bf16[8,64,384]{2,1,0:T(8,128)(2,1)S(1)}, bf16[8,32,384]{2,1,0:T(8,128)(2,1)}, bf16[768,2304]{1,0:T(8,128)(2,1)}) custom-call(s32[5]{0:T(128)S(1)} %stack.71.place_ref, bf16[2,64,768]{2,1,0:T(8,128)(2,1)} %x_ref.5, f32[8,4608]{1,0:T(8,128)} %get-tuple-element.117.mod_ref, ...), custom_call_target="tpu_custom_call" | custom-call | tf_op jit(solution)/shard_map/pallas_call | solution.py:81
  75.4 28.3 %all_to_all.35 = bf16[8,64,384]{2,1,0:T(8,128)(2,1)S(1)} all-to-all(bf16[8,64,384]{2,1,0:T(8,128)(2,1)S(1)} %get-tuple-element.121), channel_id=1, replica_groups=mesh['hx'=2,'hc'=2,'rb'=1,'sz'=4,'sy'=2] {'sz','sy'}, dimensions={0} | all-to-all | bytes 786432 | tf_op jit(solution)/shard_map/all_to_all | solution.py:1010
  104.6 3.4 %all-to-all-start.2 = ((bf16[8,32,384]{2,1,0:T(8,128)(2,1)}), bf16[8,32,384]{2,1,0:T(8,128)(2,1)S(1)}, u32[]{:S(2)}, u32[]{:S(2)}) async-start(bf16[8,32,384]{2,1,0:T(8,128)(2,1)} %get-tuple-element.122), calls=%async_computation.2 | async-start | bytes 393216 | tf_op jit(solution)/shard_map/all_to_all | solution.py:1010
  108.1 10.6 %all-to-all-done.2.came_ref = bf16[8,32,384]{2,1,0:T(8,128)(2,1)S(1)} async-done(((bf16[8,32,384]{2,1,0:T(8,128)(2,1)}), bf16[8,32,384]{2,1,0:T(8,128)(2,1)S(1)}, u32[]{:S(2)}, u32[]{:S(2)}) %all-to-all-start.2) | async-done | bytes 196640 | tf_op jit(solution)/shard_map/all_to_all | solution.py:1010
  121.4 9.2 %shard_map.249 = (bf16[8,32,384]{2,1,0:T(8,128)(2,1)}, f32[192,512]{1,0:T(8,128)}, f32[8,512]{1,0:T(8,128)}) custom-call(bf16[8,32,384]{2,1,0:T(8,128)(2,1)} %copy-done.4, bf16[512,384]{1,0:T(8,128)(2,1)} %bitcast.68, bf16[512,384]{1,0:T(8,128)(2,1)} %copy-done.5, bf16[512,384]{1,0:T(8,128)(2,1)} %copy-done.6, bf16[512,384]{1,0:T(8,128)(2,1)} %copy-done.7, ...), custom_call_target="tpu_custom_call" | custom-call | tf_op jit(solution)/shard_map/pallas_call | solution.py:338
  130.6 3.6 %all-to-all-start.3 = ((bf16[8,32,384]{2,1,0:T(8,128)(2,1)}), bf16[8,32,384]{2,1,0:T(8,128)(2,1)S(1)}, u32[]{:S(2)}, u32[]{:S(2)}) async-start(bf16[8,32,384]{2,1,0:T(8,128)(2,1)} %get-tuple-element.127), calls=%async_computation.3 | async-start | bytes 393216 | tf_op jit(solution)/shard_map/all_to_all | solution.py:1010
  134.2 8.5 %shard_map.250 = (bf16[768,768]{1,0:T(8,128)(2,1)}, bf16[768,3072]{1,0:T(8,128)(2,1)}, bf16[3072,768]{1,0:T(8,128)(2,1)}) custom-call(bf16[32,9,24,768]{3,2,1,0:T(8,128)(2,1)} %bitcast.65), custom_call_target="tpu_custom_call" | custom-call | tf_op jit(solution)/shard_map/pallas_call | solution.py:509
  143.5 10.4 %shard_map.251 = (bf16[2,64,768]{2,1,0:T(8,128)(2,1)}, f32[128,768]{1,0:T(8,128)}, bf16[8,32,384]{2,1,0:T(8,128)(2,1)}, bf16[128,9216]{1,0:T(8,128)(2,1)S(1)}, f32[16,768]{1,0:T(8,128)}) custom-call(bf16[8,32,384]{2,1,0:T(8,128)(2,1)} %copy-done.10, bf16[2,64,768]{2,1,0:T(8,128)(2,1)} %x_ref.5, bf16[2,64,768]{2,1,0:T(8,128)(2,1)} %teacher_ref.1, ...), custom_call_target="tpu_custom_call" | custom-call | tf_op jit(solution)/shard_map/pallas_call | solution.py:81
  154.1 5.6 %all-to-all-start.4 = ((bf16[8,32,384]{2,1,0:T(8,128)(2,1)}), bf16[8,32,384]{2,1,0:T(8,128)(2,1)S(1)}, u32[]{:S(2)}, u32[]{:S(2)}) async-start(bf16[8,32,384]{2,1,0:T(8,128)(2,1)} %get-tuple-element.135), calls=%async_computation.4 | async-start | bytes 393216 | tf_op jit(solution)/shard_map/all_to_all | solution.py:1010
  159.7 6.8 %shard_map.252 = (bf16[2,4,9,24,128]{4,3,2,1,0:T(8,128)(2,1)}, bf16[2,4,9,24,128]{4,3,2,1,0:T(8,128)(2,1)}, bf16[2,4,9,24,256]{4,3,2,1,0:T(8,128)(2,1)}, bf16[2,...) custom-call(s32[5]{0:T(128)S(1)} %stack.71.place_ref, ...), custom_call_target="tpu_custom_call" | custom-call | tf_op jit(solution)/shard_map/pallas_call | solution.py:81
  170.8 13.0 %shard_map.253 = (bf16[8,32,384]{2,1,0:T(8,128)(2,1)S(1)}, f32[512,384]{1,0:T(8,128)S(1)}, f32[512,384]{1,0:T(8,128)S(1)}, bf16[1024,384]{1,0:T(8,128)(2,1)S(1)}) custom-call(bf16[8,32,384]{2,1,0:T(8,128)(2,1)} %copy-done.4, bf16[8,32,384]{2,1,0:T(8,128)(2,1)} %copy-done.9, bf16[512,384]{1,0:T(8,128)(2,1)} %bitcast.69, bf16[512,384]{1,0:T(8,128)(2,1)} %copy-done.5, ...), custom_call_target="tpu_custom_call" | custom-call | tf_op jit(solution)/shard_map/pallas_call | solution.py:435
  188.4 9.8 %collective-permute-done.16 = bf16[512,384]{1,0:T(8,128)(2,1)S(1)} collective-permute-done((bf16[512,384]{1,0:T(8,128)(2,1)S(1)}, bf16[512,384]{1,0:T(8,128)(2,1)S(1)}, u32[]{:S(2)}, u32[]{:S(2)}) %collective-permute-start.16) | collective-permute-done | bytes 393248 | tf_op jit(solution)/shard_map/ppermute | solution.py:44
  199.3 7.0 %collective-permute-done.17 = bf16[2,4,9,24,256]{4,3,2,1,0:T(8,128)(2,1)} collective-permute-done((bf16[2,4,9,24,256]{4,3,2,1,0:T(8,128)(2,1)}, bf16[2,4,9,24,256]{4,3,2,1,0:T(8,128)(2,1)}, u32[]{:S(2)}, u32[]{:S(2)}) %collective-permute-start.17) | collective-permute-done | bytes 884768 | tf_op jit(solution)/shard_map/ppermute | solution.py:44
  206.2 3.9 %all-to-all-start.5 = ((bf16[8,96,384]{2,1,0:T(8,128)(2,1)}), bf16[8,96,384]{2,1,0:T(8,128)(2,1)S(1)}, u32[]{:S(2)}, u32[]{:S(2)}) async-start(bf16[8,96,384]{2,1,0:T(8,128)(2,1)} %pad_maximum_fusion.6), calls=%async_computation.5 | async-start | bytes 1179648 | tf_op jit(solution)/shard_map/all_to_all | solution.py:1010
  210.3 6.2 %collective-permute-done.25 = bf16[2,4,9,24,256]{4,3,2,1,0:T(8,128)(2,1)} collective-permute-done((bf16[2,4,9,24,256]{4,3,2,1,0:T(8,128)(2,1)}, bf16[2,4,9,24,256]{4,3,2,1,0:T(8,128)(2,1)}, u32[]{:S(2)}, u32[]{:S(2)}) %collective-permute-start.25) | collective-permute-done | bytes 884768 | tf_op jit(solution)/shard_map/ppermute | solution.py:44
  222.9 3.0 %all-to-all-done.5.home_ref = bf16[8,96,384]{2,1,0:T(8,128)(2,1)S(1)} async-done(((bf16[8,96,384]{2,1,0:T(8,128)(2,1)}), bf16[8,96,384]{2,1,0:T(8,128)(2,1)S(1)}, u32[]{:S(2)}, u32[]{:S(2)}) %all-to-all-start.5) | async-done | bytes 589856 | tf_op jit(solution)/shard_map/all_to_all | solution.py:1010
  229.5 4.1 %shard_map.254 = (bf16[2,4,24,1152]{3,2,1,0:T(8,128)(2,1)}, bf16[2,4,24,1152]{3,2,1,0:T(8,128)(2,1)}, bf16[2,4,24,1152]{3,2,1,0:T(8,128)(2,1)}, bf16[2,4,24,1152]{3,2,1,0:T(8,128)(2,1)}) custom-call(s32[5]{0:T(128)S(1)} %stack.71.place_ref, bf16[128,768]{1,0:T(8,128)(2,1)} %get-tuple-element.157.entered_ref, bf16[128,768]{1,0:T(8,128)(2,1)} %copy-done.19, ...), custom_call_target="tpu_custom_call" | custom-call | tf_op jit(solution)/shard_map/pallas_call | solution.py:81
  236.4 2.4 collective-permute-done.24
  241.6 3.1 %collective-permute-start.29 = (bf16[9,24,768]{2,1,0:T(8,128)(2,1)}, bf16[9,24,768]{2,1,0:T(8,128)(2,1)S(1)}, u32[]{:S(2)}, u32[]{:S(2)}) collective-permute-start(bf16[9,24,768]{2,1,0:T(8,128)(2,1)} %get-tuple-element.203), channel_id=1, source_target_pairs={{0,6},{2,0},{4,2},{6,4},{1,7},{3,1},{5,3},{7,5},{8,14},{10,8},{12,... | collective-permute-start | bytes 995336 | tf_op jit(solution)/shard_map/ppermute | solution.py:49
  246.6 4.9 %shard_map.255 = (f32[2,64,768]{2,1,0:T(8,128)}, f32[32,1,512]{2,1,0:T(1,128)}, bf16[128,2304]{1,0:T(8,128)(2,1)}) custom-call(bf16[8,96,384]{2,1,0:T(8,128)(2,1)} %copy-done.2, bf16[2,64,768]{2,1,0:T(8,128)(2,1)} %x_ref.5, f32[128,768]{1,0:T(8,128)} %get-tuple-element.163.hidden_ref, f32[8,4608]{1,0:T(8,128)} %get-tuple-element.117.mod_ref, ...), custom_call_target="tpu_custom_call" | custom-call | tf_op jit(solution)/shard_map/pallas_call | solution.py:81
  256.0 4.1 %all-to-all-start.6 = ((f32[32,1,512]{2,1,0:T(1,128)}), f32[32,1,512]{2,1,0:T(1,128)}, u32[]{:S(2)}, u32[]{:S(2)}) async-start(f32[32,1,512]{2,1,0:T(1,128)} %get-tuple-element.169), calls=%async_computation.6 | async-start | bytes 131072 | tf_op jit(solution)/shard_map/all_to_all | solution.py:1177
  263.6 3.2 %collective-permute-start.32 = (bf16[24,2304]{1,0:T(8,128)(2,1)}, bf16[24,2304]{1,0:T(8,128)(2,1)}, u32[]{:S(2)}, u32[]{:S(2)}) collective-permute-start(bf16[24,2304]{1,0:T(8,128)(2,1)} %get-tuple-element.210), channel_id=1, source_target_pairs={{0,6},{2,0},{4,2},{6,4},{1,7},{3,1},{5,3},{7,5},{8,14},{10,8},{12,... | collective-permute-start | bytes 331784 | tf_op jit(solution)/shard_map/ppermute | solution.py:49
  269.8 9.9 %all-to-all-done.6.small_ref = f32[32,1,512]{2,1,0:T(1,128)} async-done(((f32[32,1,512]{2,1,0:T(1,128)}), f32[32,1,512]{2,1,0:T(1,128)}, u32[]{:S(2)}, u32[]{:S(2)}) %all-to-all-start.6) | async-done | bytes 65568 | tf_op jit(solution)/shard_map/all_to_all | solution.py:1177
  (131 shorter events, 65.8 us)
Async XLA Ops:
  7.2 127.0 %all-gather.3.cloned.1.call-start = ((), (), s32[]{:S(2)}) async-start(), calls=%async_computation.7 | async-start | bytes 10948608 | tf_op jit(solution)/shard_map/all_gather | solution.py:1051
  13.3 9.3 %collective-permute-start.2 = (bf16[24,2304]{1,0:T(8,128)(2,1)}, bf16[24,2304]{1,0:T(8,128)(2,1)S(1)}, u32[]{:S(2)}, u32[]{:S(2)}) collective-permute-start(bf16[24,2304]{1,0:T(8,128)(2,1)} %param.23), channel_id=1, source_target_pairs={{0,2},{2,4},{4,6},{6,0},{1,3},{3,5},{5,7},{7,1},{8,10},{10,12},{12... | collective-permute-start | bytes 331784 | tf_op jit(solution)/shard_map/ppermute | solution.py:49
  16.4 10.1 %collective-permute-start.1 = (bf16[24,2304]{1,0:T(8,128)(2,1)}, bf16[24,2304]{1,0:T(8,128)(2,1)S(1)}, u32[]{:S(2)}, u32[]{:S(2)}) collective-permute-start(bf16[24,2304]{1,0:T(8,128)(2,1)} %param.23), channel_id=1, source_target_pairs={{0,4},{2,6},{4,0},{6,2},{1,5},{3,7},{5,1},{7,3},{8,12},{10,14},{12... | collective-permute-start | bytes 331784 | tf_op jit(solution)/shard_map/ppermute | solution.py:49
  19.0 7.5 %collective-permute-start = (bf16[24,2304]{1,0:T(8,128)(2,1)}, bf16[24,2304]{1,0:T(8,128)(2,1)S(1)}, u32[]{:S(2)}, u32[]{:S(2)}) collective-permute-start(bf16[24,2304]{1,0:T(8,128)(2,1)} %param.23), channel_id=1, source_target_pairs={{0,6},{2,0},{4,2},{6,4},{1,7},{3,1},{5,3},{7,5},{8,14},{10,8},{12,... | collective-permute-start | bytes 331784 | tf_op jit(solution)/shard_map/ppermute | solution.py:49
  27.6 10.6 %collective-permute-start.4 = (bf16[4,24,1152]{2,1,0:T(8,128)(2,1)S(1)}, bf16[4,24,1152]{2,1,0:T(8,128)(2,1)S(1)}, u32[]{:S(2)}, u32[]{:S(2)}) collective-permute-start(bf16[4,24,1152]{2,1,0:T(8,128)(2,1)S(1)} %get-tuple-element.215), channel_id=1, source_target_pairs={{0,1},{1,0},{2,3},{3,2},{4,5},{5,4},{6,7},{7,6},{8,9},{9,8},{10,11... | collective-permute-start | bytes 663560 | tf_op jit(solution)/shard_map/ppermute | solution.py:44
  29.2 15.6 %all-to-all-start = ((f32[32,1,640]{2,1,0:T(1,128)}), f32[32,1,640]{2,1,0:T(1,128)S(1)}, u32[]{:S(2)}, u32[]{:S(2)}) async-start(f32[32,1,640]{2,1,0:T(1,128)} %get-tuple-element.106), calls=%async_computation | async-start | bytes 163840 | tf_op jit(solution)/shard_map/all_to_all | solution.py:1044
  36.3 8.5 %collective-permute-start.3 = (bf16[4,24,1152]{2,1,0:T(8,128)(2,1)S(1)}, bf16[4,24,1152]{2,1,0:T(8,128)(2,1)S(1)}, u32[]{:S(2)}, u32[]{:S(2)}) collective-permute-start(bf16[4,24,1152]{2,1,0:T(8,128)(2,1)S(1)} %get-tuple-element.216), channel_id=1, source_target_pairs={{0,16},{16,0},{1,17},{17,1},{2,18},{18,2},{3,19},{19,3},{4,20},{20... | collective-permute-start | bytes 663560 | tf_op jit(solution)/shard_map/ppermute | solution.py:44
  44.9 15.0 %collective-permute-start.5 = (bf16[2,4,24,1152]{3,2,1,0:T(8,128)(2,1)S(1)}, bf16[2,4,24,1152]{3,2,1,0:T(8,128)(2,1)S(1)}, u32[]{:S(2)}, u32[]{:S(2)}) collective-permute-start(bf16[2,4,24,1152]{3,2,1,0:T(8,128)(2,1)S(1)} %pad_maximum_fusion.8), channel_id=1, source_target_pairs={{0,1},{1,0},{2,3},{3,2},{4,5},{5,4},{6,7},{7,6},{8,9},{9,8},{10,11... | collective-permute-start | bytes 1327112 | tf_op jit(solution)/shard_map/ppermute | solution.py:44
  46.5 18.1 %collective-permute-start.6 = (bf16[2,4,24,1152]{3,2,1,0:T(8,128)(2,1)S(1)}, bf16[2,4,24,1152]{3,2,1,0:T(8,128)(2,1)S(1)}, u32[]{:S(2)}, u32[]{:S(2)}) collective-permute-start(bf16[2,4,24,1152]{3,2,1,0:T(8,128)(2,1)S(1)} %pad_maximum_fusion.9), channel_id=1, source_target_pairs={{0,16},{16,0},{1,17},{17,1},{2,18},{18,2},{3,19},{19,3},{4,20},{20... | collective-permute-start | bytes 1327112 | tf_op jit(solution)/shard_map/ppermute | solution.py:44
  103.7 15.0 %collective-permute-start.9 = (bf16[512,384]{1,0:T(8,128)(2,1)S(1)}, bf16[512,384]{1,0:T(8,128)(2,1)S(1)}, u32[]{:S(2)}, u32[]{:S(2)}) collective-permute-start(bf16[512,384]{1,0:T(8,128)(2,1)S(1)} %bitcast.66), channel_id=1, source_target_pairs={{0,16},{16,0},{1,17},{17,1},{2,18},{18,2},{3,19},{19,3},{4,20},{20... | collective-permute-start | bytes 1179656 | tf_op jit(solution)/shard_map/ppermute | solution.py:44
  104.6 14.1 %all-to-all-start.2 = ((bf16[8,32,384]{2,1,0:T(8,128)(2,1)}), bf16[8,32,384]{2,1,0:T(8,128)(2,1)S(1)}, u32[]{:S(2)}, u32[]{:S(2)}) async-start(bf16[8,32,384]{2,1,0:T(8,128)(2,1)} %get-tuple-element.122), calls=%async_computation.2 | async-start | bytes 393216 | tf_op jit(solution)/shard_map/all_to_all | solution.py:1010
  108.0 10.8 %collective-permute-start.10 = (bf16[512,384]{1,0:T(8,128)(2,1)S(1)}, bf16[512,384]{1,0:T(8,128)(2,1)S(1)}, u32[]{:S(2)}, u32[]{:S(2)}) collective-permute-start(bf16[512,384]{1,0:T(8,128)(2,1)S(1)} %bitcast.67), channel_id=1, source_target_pairs={{0,8},{8,0},{1,9},{9,1},{2,10},{10,2},{3,11},{11,3},{4,12},{12,4},... | collective-permute-start | bytes 1179656 | tf_op jit(solution)/shard_map/ppermute | solution.py:44
  130.6 12.2 %all-to-all-start.3 = ((bf16[8,32,384]{2,1,0:T(8,128)(2,1)}), bf16[8,32,384]{2,1,0:T(8,128)(2,1)S(1)}, u32[]{:S(2)}, u32[]{:S(2)}) async-start(bf16[8,32,384]{2,1,0:T(8,128)(2,1)} %get-tuple-element.127), calls=%async_computation.3 | async-start | bytes 393216 | tf_op jit(solution)/shard_map/all_to_all | solution.py:1010
  154.1 14.2 %all-to-all-start.4 = ((bf16[8,32,384]{2,1,0:T(8,128)(2,1)}), bf16[8,32,384]{2,1,0:T(8,128)(2,1)S(1)}, u32[]{:S(2)}, u32[]{:S(2)}) async-start(bf16[8,32,384]{2,1,0:T(8,128)(2,1)} %get-tuple-element.135), calls=%async_computation.4 | async-start | bytes 393216 | tf_op jit(solution)/shard_map/all_to_all | solution.py:1010
  168.3 15.5 %collective-permute-start.13 = (bf16[2,4,9,24,128]{4,3,2,1,0:T(8,128)(2,1)}, bf16[2,4,9,24,128]{4,3,2,1,0:T(8,128)(2,1)S(1)}, u32[]{:S(2)}, u32[]{:S(2)}) collective-permute-start(bf16[2,4,9,24,128]{4,3,2,1,0:T(8,128)(2,1)} %get-tuple-element.150), channel_id=1, source_target_pairs={{0,1},{1,0},{2,3},{3,2},{4,5},{5,4},{6,7},{7,6},{8,9},{9,8},{10,11... | collective-permute-start | bytes 1327112 | tf_op jit(solution)/shard_map/ppermute | solution.py:44
  169.3 14.5 %collective-permute-start.14 = (bf16[2,4,9,24,128]{4,3,2,1,0:T(8,128)(2,1)}, bf16[2,4,9,24,128]{4,3,2,1,0:T(8,128)(2,1)S(1)}, u32[]{:S(2)}, u32[]{:S(2)}) collective-permute-start(bf16[2,4,9,24,128]{4,3,2,1,0:T(8,128)(2,1)} %get-tuple-element.151), channel_id=1, source_target_pairs={{0,16},{16,0},{1,17},{17,1},{2,18},{18,2},{3,19},{19,3},{4,20},{20... | collective-permute-start | bytes 1327112 | tf_op jit(solution)/shard_map/ppermute | solution.py:44
  183.9 22.4 %collective-permute-start.17 = (bf16[2,4,9,24,256]{4,3,2,1,0:T(8,128)(2,1)}, bf16[2,4,9,24,256]{4,3,2,1,0:T(8,128)(2,1)}, u32[]{:S(2)}, u32[]{:S(2)}) collective-permute-start(bf16[2,4,9,24,256]{4,3,2,1,0:T(8,128)(2,1)} %get-tuple-element.155), channel_id=1, source_target_pairs={{0,1},{1,0},{2,3},{3,2},{4,5},{5,4},{6,7},{7,6},{8,9},{9,8},{10,11... | collective-permute-start | bytes 2654216 | tf_op jit(solution)/shard_map/ppermute | solution.py:44
  186.2 12.0 %collective-permute-start.16 = (bf16[512,384]{1,0:T(8,128)(2,1)S(1)}, bf16[512,384]{1,0:T(8,128)(2,1)S(1)}, u32[]{:S(2)}, u32[]{:S(2)}) collective-permute-start(bf16[512,384]{1,0:T(8,128)(2,1)S(1)} %add_convert_fusion.3), channel_id=1, source_target_pairs={{0,16},{16,0},{1,17},{17,1},{2,18},{18,2},{3,19},{19,3},{4,20},{20... | collective-permute-start | bytes 1179656 | tf_op jit(solution)/shard_map/ppermute | solution.py:44
  186.8 29.7 %collective-permute-start.25 = (bf16[2,4,9,24,256]{4,3,2,1,0:T(8,128)(2,1)}, bf16[2,4,9,24,256]{4,3,2,1,0:T(8,128)(2,1)}, u32[]{:S(2)}, u32[]{:S(2)}) collective-permute-start(bf16[2,4,9,24,256]{4,3,2,1,0:T(8,128)(2,1)} %get-tuple-element.183), channel_id=1, source_target_pairs={{0,16},{16,0},{1,17},{17,1},{2,18},{18,2},{3,19},{19,3},{4,20},{20... | collective-permute-start | bytes 2654216 | tf_op jit(solution)/shard_map/ppermute | solution.py:44
  206.2 19.6 %all-to-all-start.5 = ((bf16[8,96,384]{2,1,0:T(8,128)(2,1)}), bf16[8,96,384]{2,1,0:T(8,128)(2,1)S(1)}, u32[]{:S(2)}, u32[]{:S(2)}) async-start(bf16[8,96,384]{2,1,0:T(8,128)(2,1)} %pad_maximum_fusion.6), calls=%async_computation.5 | async-start | bytes 1179648 | tf_op jit(solution)/shard_map/all_to_all | solution.py:1010
  219.0 17.4 %collective-permute-start.26 = (bf16[4,9,24,384]{3,2,1,0:T(8,128)(2,1)}, bf16[4,9,24,384]{3,2,1,0:T(8,128)(2,1)}, u32[]{:S(2)}, u32[]{:S(2)}) collective-permute-start(bf16[4,9,24,384]{3,2,1,0:T(8,128)(2,1)} %pad_maximum_fusion.5), channel_id=1, source_target_pairs={{0,1},{1,0},{2,3},{3,2},{4,5},{5,4},{6,7},{7,6},{8,9},{9,8},{10,11... | collective-permute-start | bytes 1990664 | tf_op jit(solution)/shard_map/ppermute | solution.py:44
  222.4 16.4 %collective-permute-start.24 = (bf16[4,9,24,384]{3,2,1,0:T(8,128)(2,1)}, bf16[4,9,24,384]{3,2,1,0:T(8,128)(2,1)}, u32[]{:S(2)}, u32[]{:S(2)}) collective-permute-start(bf16[4,9,24,384]{3,2,1,0:T(8,128)(2,1)} %pad_maximum_fusion.4), channel_id=1, source_target_pairs={{0,16},{16,0},{1,17},{17,1},{2,18},{18,2},{3,19},{19,3},{4,20},{20... | collective-permute-start | bytes 1990664 | tf_op jit(solution)/shard_map/ppermute | solution.py:44
  233.6 18.1 %collective-permute-start.20 = (bf16[2,4,24,1152]{3,2,1,0:T(8,128)(2,1)}, bf16[2,4,24,1152]{3,2,1,0:T(8,128)(2,1)S(1)}, u32[]{:S(2)}, u32[]{:S(2)}) collective-permute-start(bf16[2,4,24,1152]{3,2,1,0:T(8,128)(2,1)} %get-tuple-element.159), channel_id=1, source_target_pairs={{0,1},{1,0},{2,3},{3,2},{4,5},{5,4},{6,7},{7,6},{8,9},{9,8},{10,11... | collective-permute-start | bytes 1327112 | tf_op jit(solution)/shard_map/ppermute | solution.py:44
  235.1 16.6 %collective-permute-start.21 = (bf16[2,4,24,1152]{3,2,1,0:T(8,128)(2,1)}, bf16[2,4,24,1152]{3,2,1,0:T(8,128)(2,1)S(1)}, u32[]{:S(2)}, u32[]{:S(2)}) collective-permute-start(bf16[2,4,24,1152]{3,2,1,0:T(8,128)(2,1)} %get-tuple-element.161), channel_id=1, source_target_pairs={{0,16},{16,0},{1,17},{17,1},{2,18},{18,2},{3,19},{19,3},{4,20},{20... | collective-permute-start | bytes 1327112 | tf_op jit(solution)/shard_map/ppermute | solution.py:44
  241.6 25.9 %collective-permute-start.29 = (bf16[9,24,768]{2,1,0:T(8,128)(2,1)}, bf16[9,24,768]{2,1,0:T(8,128)(2,1)S(1)}, u32[]{:S(2)}, u32[]{:S(2)}) collective-permute-start(bf16[9,24,768]{2,1,0:T(8,128)(2,1)} %get-tuple-element.203), channel_id=1, source_target_pairs={{0,6},{2,0},{4,2},{6,4},{1,7},{3,1},{5,3},{7,5},{8,14},{10,8},{12,... | collective-permute-start | bytes 995336 | tf_op jit(solution)/shard_map/ppermute | solution.py:49
  244.7 36.8 %collective-permute-start.28 = (bf16[9,24,768]{2,1,0:T(8,128)(2,1)}, bf16[9,24,768]{2,1,0:T(8,128)(2,1)}, u32[]{:S(2)}, u32[]{:S(2)}) collective-permute-start(bf16[9,24,768]{2,1,0:T(8,128)(2,1)} %get-tuple-element.204), channel_id=1, source_target_pairs={{0,4},{2,6},{4,0},{6,2},{1,5},{3,7},{5,1},{7,3},{8,12},{10,14},{12... | collective-permute-start | bytes 995336 | tf_op jit(solution)/shard_map/ppermute | solution.py:49
  244.7 36.8 %collective-permute-start.27 = (bf16[9,24,768]{2,1,0:T(8,128)(2,1)}, bf16[9,24,768]{2,1,0:T(8,128)(2,1)}, u32[]{:S(2)}, u32[]{:S(2)}) collective-permute-start(bf16[9,24,768]{2,1,0:T(8,128)(2,1)} %get-tuple-element.205), channel_id=1, source_target_pairs={{0,2},{2,4},{4,6},{6,0},{1,3},{3,5},{5,7},{7,1},{8,10},{10,12},{12... | collective-permute-start | bytes 995336 | tf_op jit(solution)/shard_map/ppermute | solution.py:49
  253.2 6.9 %collective-permute-start.23 = (bf16[4,24,1152]{2,1,0:T(8,128)(2,1)}, bf16[4,24,1152]{2,1,0:T(8,128)(2,1)}, u32[]{:S(2)}, u32[]{:S(2)}) collective-permute-start(bf16[4,24,1152]{2,1,0:T(8,128)(2,1)} %fusion.3), channel_id=1, source_target_pairs={{0,1},{1,0},{2,3},{3,2},{4,5},{5,4},{6,7},{7,6},{8,9},{9,8},{10,11... | collective-permute-start | bytes 663560 | tf_op jit(solution)/shard_map/ppermute | solution.py:44
  256.0 23.7 %all-to-all-start.6 = ((f32[32,1,512]{2,1,0:T(1,128)}), f32[32,1,512]{2,1,0:T(1,128)}, u32[]{:S(2)}, u32[]{:S(2)}) async-start(f32[32,1,512]{2,1,0:T(1,128)} %get-tuple-element.169), calls=%async_computation.6 | async-start | bytes 131072 | tf_op jit(solution)/shard_map/all_to_all | solution.py:1177
  263.6 17.9 %collective-permute-start.32 = (bf16[24,2304]{1,0:T(8,128)(2,1)}, bf16[24,2304]{1,0:T(8,128)(2,1)}, u32[]{:S(2)}, u32[]{:S(2)}) collective-permute-start(bf16[24,2304]{1,0:T(8,128)(2,1)} %get-tuple-element.210), channel_id=1, source_target_pairs={{0,6},{2,0},{4,2},{6,4},{1,7},{3,1},{5,3},{7,5},{8,14},{10,8},{12,... | collective-permute-start | bytes 331784 | tf_op jit(solution)/shard_map/ppermute | solution.py:49
  266.8 14.9 %collective-permute-start.31 = (bf16[24,2304]{1,0:T(8,128)(2,1)}, bf16[24,2304]{1,0:T(8,128)(2,1)}, u32[]{:S(2)}, u32[]{:S(2)}) collective-permute-start(bf16[24,2304]{1,0:T(8,128)(2,1)} %get-tuple-element.211), channel_id=1, source_target_pairs={{0,4},{2,6},{4,0},{6,2},{1,5},{3,7},{5,1},{7,3},{8,12},{10,14},{12... | collective-permute-start | bytes 331784 | tf_op jit(solution)/shard_map/ppermute | solution.py:49
  268.2 13.5 %collective-permute-start.30 = (bf16[24,2304]{1,0:T(8,128)(2,1)}, bf16[24,2304]{1,0:T(8,128)(2,1)}, u32[]{:S(2)}, u32[]{:S(2)}) collective-permute-start(bf16[24,2304]{1,0:T(8,128)(2,1)} %get-tuple-element.212), channel_id=1, source_target_pairs={{0,2},{2,4},{4,6},{6,0},{1,3},{3,5},{5,7},{7,1},{8,10},{10,12},{12... | collective-permute-start | bytes 331784 | tf_op jit(solution)/shard_map/ppermute | solution.py:49
  (28 other events, 91.0 us)
Sparse Core Ops, SparseCore 0:
  13.5 107.6 all-gather.2

commit v8 on v7

--- a/solution.py
+++ b/solution.py
@@ -118,9 +118,9 @@
     sides = []
     deep = jnp.stack([shard] + [turn(shard, "sz", k) for k in (1, 2, 3)])
     orders = (("hx", "sy"), ("sy", "hx"))
+    deep, every = lax.optimization_barrier((deep, every))
     levels = [deep[:, :, :half], deep[:, :, half:]]
     levels = [jnp.stack([v, swap(v, order[0])]) for v, order in zip(levels, orders)]
-    levels, every = lax.optimization_barrier((levels, every))
     levels = [jnp.stack([v, swap(v, order[1])]) for v, order in zip(levels, orders)]
     used = use(every)
     levels, used = lax.optimization_barrier((levels, used))
@@ -1049,7 +1049,6 @@
         )
     else:
         later = [lax.all_gather(later[0], EVERY, axis=0, tiled=False)]
-        shard, packed = lax.optimization_barrier((qkv_weight, packed))
 
     def use(every):
         return unpack(here, every, valid_mask, width, units, parts, length)
@@ -1058,7 +1057,7 @@
         sides = [sides]
         used = use(every)
     else:
-        sides, used = gather_rows(here, shard, every, use)
+        sides, used = gather_rows(here, qkv_weight, every, use)
     modulation, gains, full_up_bias, key_docs, query_docs, masks = used
 
     entered, pair, query, full_qkv = enter(here, inputs, modulation, gains, sides)
@@ -1100,7 +1099,6 @@
         [grad_pair.astype(bf16).reshape(8, tokens, 2 * WIDTH), grad_query], axis=1
     )
     if parts == 1:
-        home, firsts[1] = lax.optimization_barrier((home, firsts[1]))
         seconds = [
             swap(
                 jnp.concatenate(

time: 293 us -> 286 us (0.976)
  starting transfers between devices: 65.1 us -> 58.6 us
    all_to_all x1, waiting for transfers between devices: 0.01 us -> 4.13 us  [on_device(): every = lax.all_to_all(packed, EVERY, 0, 0, tiled=True)]
    ppermute x24, starting transfers between devices: 20 us -> 16.3 us  [swap(): return lax.ppermute(value, axis, [(0, 1), (1, 0)])]
  transfers between devices with their start and end apart: 40 -> 40, of which waited for: 22 -> 19; matrix products, arithmetic and copies ran while one was open for 5% -> 5% of each run, Pallas kernels for 20% -> 20%
where the time goes in v8:
time: 286 us; the launch traced here: 285 us
  waiting for transfers between devices  87.5 us (31%)
  Pallas kernels  72.7 us (25%)
  starting transfers between devices  58.6 us (20%)
  blocking collectives  27.5 us (10%)
  between operations  14.5 us (5%)
  other arithmetic  13 us (5%)
  local copies, waits for them, and re-layouts  11.4 us (4%)
    ppermute x24, waiting for transfers between devices, swap(): return lax.ppermute(value, axis, [(0, 1), (1, 0)])  54.8 us
    pallas_call x8, Pallas kernels, single(): pl.pallas_call(kernel, grid=(1,), out_shape=tuple((result(*o) for o in ou...  39.6 us
    all_to_all x1, blocking collectives, exchange(): return lax.all_to_all(rows, SPOT, 0, 0, tiled=True)  27.5 us
    all_to_all x4, starting transfers between devices, exchange(): return lax.all_to_all(rows, SPOT, 0, 0, tiled=True)  17 us
    ppermute x24, starting transfers between devices, swap(): return lax.ppermute(value, axis, [(0, 1), (1, 0)])  16.3 us
    all_to_all x4, waiting for transfers between devices, exchange(): return lax.all_to_all(rows, SPOT, 0, 0, tiled=True)  15.4 us
    ppermute x9, starting transfers between devices, turn(): lax.ppermute(value, axis, [(i, (i - step) % size) for i in range(size)])  14.5 us
    pallas_call x1, Pallas kernels, attend_back(): pl.pallas_call(partial(backward_kernel, starts), grid=(steps,), out_shape...  13 us
  transfers between devices with their start and end apart: 40, of which 19 were waited for; matrix products, arithmetic and copies ran while one was open for 5% of the time, Pallas kernels for 20%

profile of v8, /device:TPU:0, one launch (start us, length us, event | category | flops | bytes accessed | tf_op | source)
XLA Modules:
  0.0 285.1 jit_solution(1914912726070678073)
XLA Ops:
  7.2 3.4 %concatenate.25 = bf16[312]{0:T(512)(128)(2,1)S(1)} concatenate(bf16[144]{0:T(256)(128)(2,1)} %param.21, bf16[24]{0:T(256)(128)(2,1)} %param.22, bf16[24]{0:T(256)(128)(2,1)} %param.25, bf16[96]{0:T(256)(128)(2,1)} %param.27, bf16[24]{0:T(256)(128)(2,1)} %param.29), dimensions={0} | concatenate | bytes 1248 | tf_op jit(solution)/shard_map/concatenate | solution.py:1039
  11.2 2.1 shard_map.246
  13.3 5.1 %collective-permute-start = (bf16[24,2304]{1,0:T(8,128)(2,1)}, bf16[24,2304]{1,0:T(8,128)(2,1)S(1)}, u32[]{:S(2)}, u32[]{:S(2)}) collective-permute-start(bf16[24,2304]{1,0:T(8,128)(2,1)} %param.23), channel_id=1, source_target_pairs={{0,6},{2,0},{4,2},{6,4},{1,7},{3,1},{5,3},{7,5},{8,14},{10,8},{12,... | collective-permute-start | bytes 331784 | tf_op jit(solution)/shard_map/ppermute | solution.py:49
  19.4 5.6 %all-to-all-start = ((f32[32,1,640]{2,1,0:T(1,128)}), f32[32,1,640]{2,1,0:T(1,128)S(1)}, u32[]{:S(2)}, u32[]{:S(2)}) async-start(f32[32,1,640]{2,1,0:T(1,128)} %get-tuple-element.102), calls=%async_computation | async-start | bytes 163840 | tf_op jit(solution)/shard_map/all_to_all | solution.py:1044
  26.2 2.8 collective-permute-done.1
  30.0 4.1 %all-to-all-done.every_ref = f32[32,1,640]{2,1,0:T(1,128)S(1)} async-done(((f32[32,1,640]{2,1,0:T(1,128)}), f32[32,1,640]{2,1,0:T(1,128)S(1)}, u32[]{:S(2)}, u32[]{:S(2)}) %all-to-all-start) | async-done | bytes 81952 | tf_op jit(solution)/shard_map/all_to_all | solution.py:1044
  35.6 5.0 %collective-permute-done.5 = bf16[4,24,1152]{2,1,0:T(8,128)(2,1)S(1)} collective-permute-done((bf16[4,24,1152]{2,1,0:T(8,128)(2,1)S(1)}, bf16[4,24,1152]{2,1,0:T(8,128)(2,1)S(1)}, u32[]{:S(2)}, u32[]{:S(2)}) %collective-permute-start.5) | collective-permute-done | bytes 221216 | tf_op jit(solution)/shard_map/ppermute | solution.py:44
  43.2 2.5 shard_map.247
  45.7 13.7 %collective-permute-done.6 = bf16[2,4,24,1152]{3,2,1,0:T(8,128)(2,1)S(1)} collective-permute-done((bf16[2,4,24,1152]{3,2,1,0:T(8,128)(2,1)S(1)}, bf16[2,4,24,1152]{3,2,1,0:T(8,128)(2,1)S(1)}, u32[]{:S(2)}, u32[]{:S(2)}) %collective-permute-start.6) | collective-permute-done | bytes 442400 | tf_op jit(solution)/shard_map/ppermute | solution.py:44
  63.3 6.9 %shard_map.248 = (bf16[128,768]{1,0:T(8,128)(2,1)}, bf16[8,64,384]{2,1,0:T(8,128)(2,1)S(1)}, bf16[8,32,384]{2,1,0:T(8,128)(2,1)}, bf16[768,2304]{1,0:T(8,128)(2,1)}) custom-call(s32[5]{0:T(128)S(1)} %stack.71.place_ref, bf16[2,64,768]{2,1,0:T(8,128)(2,1)} %x_ref.5, f32[8,4608]{1,0:T(8,128)} %get-tuple-element.111.mod_ref, ...), custom_call_target="tpu_custom_call" | custom-call | tf_op jit(solution)/shard_map/pallas_call | solution.py:81
  70.2 27.5 %all_to_all.35 = bf16[8,64,384]{2,1,0:T(8,128)(2,1)S(1)} all-to-all(bf16[8,64,384]{2,1,0:T(8,128)(2,1)S(1)} %get-tuple-element.115), channel_id=1, replica_groups=mesh['hx'=2,'hc'=2,'rb'=1,'sz'=4,'sy'=2] {'sz','sy'}, dimensions={0} | all-to-all | bytes 786432 | tf_op jit(solution)/shard_map/all_to_all | solution.py:1010
  97.7 3.9 %all-to-all-start.2 = ((bf16[8,32,384]{2,1,0:T(8,128)(2,1)}), bf16[8,32,384]{2,1,0:T(8,128)(2,1)S(1)}, u32[]{:S(2)}, u32[]{:S(2)}) async-start(bf16[8,32,384]{2,1,0:T(8,128)(2,1)} %get-tuple-element.116), calls=%async_computation.2 | async-start | bytes 393216 | tf_op jit(solution)/shard_map/all_to_all | solution.py:1010
  101.6 13.7 %all-to-all-done.2.came_ref = bf16[8,32,384]{2,1,0:T(8,128)(2,1)S(1)} async-done(((bf16[8,32,384]{2,1,0:T(8,128)(2,1)}), bf16[8,32,384]{2,1,0:T(8,128)(2,1)S(1)}, u32[]{:S(2)}, u32[]{:S(2)}) %all-to-all-start.2) | async-done | bytes 196640 | tf_op jit(solution)/shard_map/all_to_all | solution.py:1010
  118.1 9.4 %shard_map.249 = (bf16[8,32,384]{2,1,0:T(8,128)(2,1)}, f32[192,512]{1,0:T(8,128)}, f32[8,512]{1,0:T(8,128)}) custom-call(bf16[8,32,384]{2,1,0:T(8,128)(2,1)} %copy-done.4, bf16[512,384]{1,0:T(8,128)(2,1)} %bitcast.70, bf16[512,384]{1,0:T(8,128)(2,1)} %copy-done.5, bf16[512,384]{1,0:T(8,128)(2,1)} %copy-done.6, bf16[512,384]{1,0:T(8,128)(2,1)} %copy-done.7, ...), custom_call_target="tpu_custom_call" | custom-call | tf_op jit(solution)/shard_map/pallas_call | solution.py:338
  127.5 3.6 %all-to-all-start.3 = ((bf16[8,32,384]{2,1,0:T(8,128)(2,1)}), bf16[8,32,384]{2,1,0:T(8,128)(2,1)S(1)}, u32[]{:S(2)}, u32[]{:S(2)}) async-start(bf16[8,32,384]{2,1,0:T(8,128)(2,1)} %get-tuple-element.121), calls=%async_computation.3 | async-start | bytes 393216 | tf_op jit(solution)/shard_map/all_to_all | solution.py:1010
  131.1 8.5 %shard_map.250 = (bf16[768,768]{1,0:T(8,128)(2,1)}, bf16[768,3072]{1,0:T(8,128)(2,1)}, bf16[3072,768]{1,0:T(8,128)(2,1)}) custom-call(bf16[32,9,24,768]{3,2,1,0:T(8,128)(2,1)} %bitcast.67), custom_call_target="tpu_custom_call" | custom-call | tf_op jit(solution)/shard_map/pallas_call | solution.py:509
  140.4 10.4 %shard_map.251 = (bf16[2,64,768]{2,1,0:T(8,128)(2,1)}, f32[128,768]{1,0:T(8,128)}, bf16[8,32,384]{2,1,0:T(8,128)(2,1)}, bf16[128,9216]{1,0:T(8,128)(2,1)S(1)}, f32[16,768]{1,0:T(8,128)}) custom-call(bf16[8,32,384]{2,1,0:T(8,128)(2,1)} %copy-done.11, bf16[2,64,768]{2,1,0:T(8,128)(2,1)} %x_ref.5, bf16[2,64,768]{2,1,0:T(8,128)(2,1)} %teacher_ref.1, ...), custom_call_target="tpu_custom_call" | custom-call | tf_op jit(solution)/shard_map/pallas_call | solution.py:81
  151.0 5.6 %all-to-all-start.4 = ((bf16[8,32,384]{2,1,0:T(8,128)(2,1)}), bf16[8,32,384]{2,1,0:T(8,128)(2,1)S(1)}, u32[]{:S(2)}, u32[]{:S(2)}) async-start(bf16[8,32,384]{2,1,0:T(8,128)(2,1)} %get-tuple-element.129), calls=%async_computation.4 | async-start | bytes 393216 | tf_op jit(solution)/shard_map/all_to_all | solution.py:1010
  156.6 6.9 %shard_map.252 = (bf16[2,4,9,24,128]{4,3,2,1,0:T(8,128)(2,1)}, bf16[2,4,9,24,128]{4,3,2,1,0:T(8,128)(2,1)}, bf16[2,4,9,24,256]{4,3,2,1,0:T(8,128)(2,1)}, bf16[2,...) custom-call(s32[5]{0:T(128)S(1)} %stack.71.place_ref, ...), custom_call_target="tpu_custom_call" | custom-call | tf_op jit(solution)/shard_map/pallas_call | solution.py:81
  167.7 13.0 %shard_map.253 = (bf16[8,32,384]{2,1,0:T(8,128)(2,1)S(1)}, f32[512,384]{1,0:T(8,128)S(1)}, f32[512,384]{1,0:T(8,128)S(1)}, bf16[1024,384]{1,0:T(8,128)(2,1)S(1)}) custom-call(bf16[8,32,384]{2,1,0:T(8,128)(2,1)} %copy-done.4, bf16[8,32,384]{2,1,0:T(8,128)(2,1)} %copy-done.10, bf16[512,384]{1,0:T(8,128)(2,1)} %bitcast.71, bf16[512,384]{1,0:T(8,128)(2,1)} %copy-done.5, ...), custom_call_target="tpu_custom_call" | custom-call | tf_op jit(solution)/shard_map/pallas_call | solution.py:435
  180.8 2.3 collective-permute-done.15
  186.4 8.8 %collective-permute-done.16 = bf16[512,384]{1,0:T(8,128)(2,1)S(1)} collective-permute-done((bf16[512,384]{1,0:T(8,128)(2,1)S(1)}, bf16[512,384]{1,0:T(8,128)(2,1)S(1)}, u32[]{:S(2)}, u32[]{:S(2)}) %collective-permute-start.16) | collective-permute-done | bytes 393248 | tf_op jit(solution)/shard_map/ppermute | solution.py:44
  196.2 3.9 %all-to-all-start.5 = ((bf16[8,96,384]{2,1,0:T(8,128)(2,1)}), bf16[8,96,384]{2,1,0:T(8,128)(2,1)S(1)}, u32[]{:S(2)}, u32[]{:S(2)}) async-start(bf16[8,96,384]{2,1,0:T(8,128)(2,1)} %pad_maximum_fusion.6), calls=%async_computation.5 | async-start | bytes 1179648 | tf_op jit(solution)/shard_map/all_to_all | solution.py:1010
  200.2 9.9 %collective-permute-done.23 = bf16[2,4,9,24,256]{4,3,2,1,0:T(8,128)(2,1)} collective-permute-done((bf16[2,4,9,24,256]{4,3,2,1,0:T(8,128)(2,1)}, bf16[2,4,9,24,256]{4,3,2,1,0:T(8,128)(2,1)}, u32[]{:S(2)}, u32[]{:S(2)}) %collective-permute-start.23) | collective-permute-done | bytes 884768 | tf_op jit(solution)/shard_map/ppermute | solution.py:44
  221.2 4.1 %shard_map.254 = (bf16[2,4,24,1152]{3,2,1,0:T(8,128)(2,1)}, bf16[2,4,24,1152]{3,2,1,0:T(8,128)(2,1)}, bf16[2,4,24,1152]{3,2,1,0:T(8,128)(2,1)}, bf16[2,4,24,1152]{3,2,1,0:T(8,128)(2,1)}) custom-call(s32[5]{0:T(128)S(1)} %stack.71.place_ref, bf16[128,768]{1,0:T(8,128)(2,1)} %get-tuple-element.149.entered_ref, bf16[128,768]{1,0:T(8,128)(2,1)} %copy-done.21, ...), custom_call_target="tpu_custom_call" | custom-call | tf_op jit(solution)/shard_map/pallas_call | solution.py:81
  227.6 7.0 %collective-permute-done.26 = bf16[4,9,24,384]{3,2,1,0:T(8,128)(2,1)} collective-permute-done((bf16[4,9,24,384]{3,2,1,0:T(8,128)(2,1)}, bf16[4,9,24,384]{3,2,1,0:T(8,128)(2,1)}, u32[]{:S(2)}, u32[]{:S(2)}) %collective-permute-start.26) | collective-permute-done | bytes 663584 | tf_op jit(solution)/shard_map/ppermute | solution.py:44
  237.5 3.2 %collective-permute-start.29 = (bf16[9,24,768]{2,1,0:T(8,128)(2,1)}, bf16[9,24,768]{2,1,0:T(8,128)(2,1)S(1)}, u32[]{:S(2)}, u32[]{:S(2)}) collective-permute-start(bf16[9,24,768]{2,1,0:T(8,128)(2,1)} %get-tuple-element.195), channel_id=1, source_target_pairs={{0,6},{2,0},{4,2},{6,4},{1,7},{3,1},{5,3},{7,5},{8,14},{10,8},{12,... | collective-permute-start | bytes 995336 | tf_op jit(solution)/shard_map/ppermute | solution.py:49
  241.3 4.9 %shard_map.255 = (f32[2,64,768]{2,1,0:T(8,128)}, f32[32,1,512]{2,1,0:T(1,128)}, bf16[128,2304]{1,0:T(8,128)(2,1)}) custom-call(bf16[8,96,384]{2,1,0:T(8,128)(2,1)} %copy-done.2, bf16[2,64,768]{2,1,0:T(8,128)(2,1)} %x_ref.5, f32[128,768]{1,0:T(8,128)} %get-tuple-element.155.hidden_ref, f32[8,4608]{1,0:T(8,128)} %get-tuple-element.111.mod_ref, ...), custom_call_target="tpu_custom_call" | custom-call | tf_op jit(solution)/shard_map/pallas_call | solution.py:81
  250.4 5.0 %all-to-all-start.6 = ((f32[32,1,512]{2,1,0:T(1,128)}), f32[32,1,512]{2,1,0:T(1,128)}, u32[]{:S(2)}, u32[]{:S(2)}) async-start(f32[32,1,512]{2,1,0:T(1,128)} %get-tuple-element.161), calls=%async_computation.6 | async-start | bytes 131072 | tf_op jit(solution)/shard_map/all_to_all | solution.py:1175
  258.6 3.5 %collective-permute-start.32 = (bf16[24,2304]{1,0:T(8,128)(2,1)}, bf16[24,2304]{1,0:T(8,128)(2,1)}, u32[]{:S(2)}, u32[]{:S(2)}) collective-permute-start(bf16[24,2304]{1,0:T(8,128)(2,1)} %get-tuple-element.202), channel_id=1, source_target_pairs={{0,6},{2,0},{4,2},{6,4},{1,7},{3,1},{5,3},{7,5},{8,14},{10,8},{12,... | collective-permute-start | bytes 331784 | tf_op jit(solution)/shard_map/ppermute | solution.py:49
  264.0 8.6 %all-to-all-done.6.small_ref = f32[32,1,512]{2,1,0:T(1,128)} async-done(((f32[32,1,512]{2,1,0:T(1,128)}), f32[32,1,512]{2,1,0:T(1,128)}, u32[]{:S(2)}, u32[]{:S(2)}) %all-to-all-start.6) | async-done | bytes 65568 | tf_op jit(solution)/shard_map/all_to_all | solution.py:1175
  276.1 2.2 shard_map.257
  (135 shorter events, 53.5 us)
Async XLA Ops:
  7.2 123.9 %all-gather.3.cloned.1.call-start = ((), (), s32[]{:S(2)}) async-start(), calls=%async_computation.7 | async-start | bytes 10948608 | tf_op jit(solution)/shard_map/all_gather | solution.py:1051
  13.3 11.7 %collective-permute-start = (bf16[24,2304]{1,0:T(8,128)(2,1)}, bf16[24,2304]{1,0:T(8,128)(2,1)S(1)}, u32[]{:S(2)}, u32[]{:S(2)}) collective-permute-start(bf16[24,2304]{1,0:T(8,128)(2,1)} %param.23), channel_id=1, source_target_pairs={{0,6},{2,0},{4,2},{6,4},{1,7},{3,1},{5,3},{7,5},{8,14},{10,8},{12,... | collective-permute-start | bytes 331784 | tf_op jit(solution)/shard_map/ppermute | solution.py:49
  18.4 7.8 %collective-permute-start.2 = (bf16[24,2304]{1,0:T(8,128)(2,1)}, bf16[24,2304]{1,0:T(8,128)(2,1)S(1)}, u32[]{:S(2)}, u32[]{:S(2)}) collective-permute-start(bf16[24,2304]{1,0:T(8,128)(2,1)} %param.23), channel_id=1, source_target_pairs={{0,2},{2,4},{4,6},{6,0},{1,3},{3,5},{5,7},{7,1},{8,10},{10,12},{12... | collective-permute-start | bytes 331784 | tf_op jit(solution)/shard_map/ppermute | solution.py:49
  18.4 10.6 %collective-permute-start.1 = (bf16[24,2304]{1,0:T(8,128)(2,1)}, bf16[24,2304]{1,0:T(8,128)(2,1)S(1)}, u32[]{:S(2)}, u32[]{:S(2)}) collective-permute-start(bf16[24,2304]{1,0:T(8,128)(2,1)} %param.23), channel_id=1, source_target_pairs={{0,4},{2,6},{4,0},{6,2},{1,5},{3,7},{5,1},{7,3},{8,12},{10,14},{12... | collective-permute-start | bytes 331784 | tf_op jit(solution)/shard_map/ppermute | solution.py:49
  19.4 14.7 %all-to-all-start = ((f32[32,1,640]{2,1,0:T(1,128)}), f32[32,1,640]{2,1,0:T(1,128)S(1)}, u32[]{:S(2)}, u32[]{:S(2)}) async-start(f32[32,1,640]{2,1,0:T(1,128)} %get-tuple-element.102), calls=%async_computation | async-start | bytes 163840 | tf_op jit(solution)/shard_map/all_to_all | solution.py:1044
  34.8 7.5 %collective-permute-start.3 = (bf16[4,24,1152]{2,1,0:T(8,128)(2,1)S(1)}, bf16[4,24,1152]{2,1,0:T(8,128)(2,1)S(1)}, u32[]{:S(2)}, u32[]{:S(2)}) collective-permute-start(bf16[4,24,1152]{2,1,0:T(8,128)(2,1)S(1)} %get-tuple-element.210), channel_id=1, source_target_pairs={{0,16},{16,0},{1,17},{17,1},{2,18},{18,2},{3,19},{19,3},{4,20},{20... | collective-permute-start | bytes 663560 | tf_op jit(solution)/shard_map/ppermute | solution.py:44
  40.6 18.7 %collective-permute-start.6 = (bf16[2,4,24,1152]{3,2,1,0:T(8,128)(2,1)S(1)}, bf16[2,4,24,1152]{3,2,1,0:T(8,128)(2,1)S(1)}, u32[]{:S(2)}, u32[]{:S(2)}) collective-permute-start(bf16[2,4,24,1152]{3,2,1,0:T(8,128)(2,1)S(1)} %get-tuple-element.206), channel_id=1, source_target_pairs={{0,16},{16,0},{1,17},{17,1},{2,18},{18,2},{3,19},{19,3},{4,20},{20... | collective-permute-start | bytes 1327112 | tf_op jit(solution)/shard_map/ppermute | solution.py:44
  42.4 17.0 %collective-permute-start.4 = (bf16[2,4,24,1152]{3,2,1,0:T(8,128)(2,1)S(1)}, bf16[2,4,24,1152]{3,2,1,0:T(8,128)(2,1)S(1)}, u32[]{:S(2)}, u32[]{:S(2)}) collective-permute-start(bf16[2,4,24,1152]{3,2,1,0:T(8,128)(2,1)S(1)} %get-tuple-element.212), channel_id=1, source_target_pairs={{0,1},{1,0},{2,3},{3,2},{4,5},{5,4},{6,7},{7,6},{8,9},{9,8},{10,11... | collective-permute-start | bytes 1327112 | tf_op jit(solution)/shard_map/ppermute | solution.py:44
  97.7 17.5 %collective-permute-start.9 = (bf16[512,384]{1,0:T(8,128)(2,1)S(1)}, bf16[512,384]{1,0:T(8,128)(2,1)S(1)}, u32[]{:S(2)}, u32[]{:S(2)}) collective-permute-start(bf16[512,384]{1,0:T(8,128)(2,1)S(1)} %bitcast.68), channel_id=1, source_target_pairs={{0,16},{16,0},{1,17},{17,1},{2,18},{18,2},{3,19},{19,3},{4,20},{20... | collective-permute-start | bytes 1179656 | tf_op jit(solution)/shard_map/ppermute | solution.py:44
  97.7 17.5 %all-to-all-start.2 = ((bf16[8,32,384]{2,1,0:T(8,128)(2,1)}), bf16[8,32,384]{2,1,0:T(8,128)(2,1)S(1)}, u32[]{:S(2)}, u32[]{:S(2)}) async-start(bf16[8,32,384]{2,1,0:T(8,128)(2,1)} %get-tuple-element.116), calls=%async_computation.2 | async-start | bytes 393216 | tf_op jit(solution)/shard_map/all_to_all | solution.py:1010
  101.6 13.8 %collective-permute-start.10 = (bf16[512,384]{1,0:T(8,128)(2,1)S(1)}, bf16[512,384]{1,0:T(8,128)(2,1)S(1)}, u32[]{:S(2)}, u32[]{:S(2)}) collective-permute-start(bf16[512,384]{1,0:T(8,128)(2,1)S(1)} %bitcast.69), channel_id=1, source_target_pairs={{0,8},{8,0},{1,9},{9,1},{2,10},{10,2},{3,11},{11,3},{4,12},{12,4},... | collective-permute-start | bytes 1179656 | tf_op jit(solution)/shard_map/ppermute | solution.py:44
  127.5 12.2 %all-to-all-start.3 = ((bf16[8,32,384]{2,1,0:T(8,128)(2,1)}), bf16[8,32,384]{2,1,0:T(8,128)(2,1)S(1)}, u32[]{:S(2)}, u32[]{:S(2)}) async-start(bf16[8,32,384]{2,1,0:T(8,128)(2,1)} %get-tuple-element.121), calls=%async_computation.3 | async-start | bytes 393216 | tf_op jit(solution)/shard_map/all_to_all | solution.py:1010
  151.0 14.2 %all-to-all-start.4 = ((bf16[8,32,384]{2,1,0:T(8,128)(2,1)}), bf16[8,32,384]{2,1,0:T(8,128)(2,1)S(1)}, u32[]{:S(2)}, u32[]{:S(2)}) async-start(bf16[8,32,384]{2,1,0:T(8,128)(2,1)} %get-tuple-element.129), calls=%async_computation.4 | async-start | bytes 393216 | tf_op jit(solution)/shard_map/all_to_all | solution.py:1010
  165.2 15.5 %collective-permute-start.13 = (bf16[2,4,9,24,128]{4,3,2,1,0:T(8,128)(2,1)}, bf16[2,4,9,24,128]{4,3,2,1,0:T(8,128)(2,1)S(1)}, u32[]{:S(2)}, u32[]{:S(2)}) collective-permute-start(bf16[2,4,9,24,128]{4,3,2,1,0:T(8,128)(2,1)} %get-tuple-element.144), channel_id=1, source_target_pairs={{0,1},{1,0},{2,3},{3,2},{4,5},{5,4},{6,7},{7,6},{8,9},{9,8},{10,11... | collective-permute-start | bytes 1327112 | tf_op jit(solution)/shard_map/ppermute | solution.py:44
  166.2 14.5 %collective-permute-start.14 = (bf16[2,4,9,24,128]{4,3,2,1,0:T(8,128)(2,1)}, bf16[2,4,9,24,128]{4,3,2,1,0:T(8,128)(2,1)S(1)}, u32[]{:S(2)}, u32[]{:S(2)}) collective-permute-start(bf16[2,4,9,24,128]{4,3,2,1,0:T(8,128)(2,1)} %get-tuple-element.145), channel_id=1, source_target_pairs={{0,16},{16,0},{1,17},{17,1},{2,18},{18,2},{3,19},{19,3},{4,20},{20... | collective-permute-start | bytes 1327112 | tf_op jit(solution)/shard_map/ppermute | solution.py:44
  183.1 12.0 %collective-permute-start.16 = (bf16[512,384]{1,0:T(8,128)(2,1)S(1)}, bf16[512,384]{1,0:T(8,128)(2,1)S(1)}, u32[]{:S(2)}, u32[]{:S(2)}) collective-permute-start(bf16[512,384]{1,0:T(8,128)(2,1)S(1)} %add_convert_fusion.3), channel_id=1, source_target_pairs={{0,16},{16,0},{1,17},{17,1},{2,18},{18,2},{3,19},{19,3},{4,20},{20... | collective-permute-start | bytes 1179656 | tf_op jit(solution)/shard_map/ppermute | solution.py:44
  183.7 26.4 %collective-permute-start.23 = (bf16[2,4,9,24,256]{4,3,2,1,0:T(8,128)(2,1)}, bf16[2,4,9,24,256]{4,3,2,1,0:T(8,128)(2,1)}, u32[]{:S(2)}, u32[]{:S(2)}) collective-permute-start(bf16[2,4,9,24,256]{4,3,2,1,0:T(8,128)(2,1)} %get-tuple-element.171), channel_id=1, source_target_pairs={{0,1},{1,0},{2,3},{3,2},{4,5},{5,4},{6,7},{7,6},{8,9},{9,8},{10,11... | collective-permute-start | bytes 2654216 | tf_op jit(solution)/shard_map/ppermute | solution.py:44
  184.8 29.4 %collective-permute-start.25 = (bf16[2,4,9,24,256]{4,3,2,1,0:T(8,128)(2,1)}, bf16[2,4,9,24,256]{4,3,2,1,0:T(8,128)(2,1)}, u32[]{:S(2)}, u32[]{:S(2)}) collective-permute-start(bf16[2,4,9,24,256]{4,3,2,1,0:T(8,128)(2,1)} %get-tuple-element.175), channel_id=1, source_target_pairs={{0,16},{16,0},{1,17},{17,1},{2,18},{18,2},{3,19},{19,3},{4,20},{20... | collective-permute-start | bytes 2654216 | tf_op jit(solution)/shard_map/ppermute | solution.py:44
  196.2 21.2 %all-to-all-start.5 = ((bf16[8,96,384]{2,1,0:T(8,128)(2,1)}), bf16[8,96,384]{2,1,0:T(8,128)(2,1)S(1)}, u32[]{:S(2)}, u32[]{:S(2)}) async-start(bf16[8,96,384]{2,1,0:T(8,128)(2,1)} %pad_maximum_fusion.6), calls=%async_computation.5 | async-start | bytes 1179648 | tf_op jit(solution)/shard_map/all_to_all | solution.py:1010
  212.4 15.2 %collective-permute-start.24 = (bf16[4,9,24,384]{3,2,1,0:T(8,128)(2,1)}, bf16[4,9,24,384]{3,2,1,0:T(8,128)(2,1)}, u32[]{:S(2)}, u32[]{:S(2)}) collective-permute-start(bf16[4,9,24,384]{3,2,1,0:T(8,128)(2,1)} %pad_maximum_fusion.4), channel_id=1, source_target_pairs={{0,16},{16,0},{1,17},{17,1},{2,18},{18,2},{3,19},{19,3},{4,20},{20... | collective-permute-start | bytes 1990664 | tf_op jit(solution)/shard_map/ppermute | solution.py:44
  216.5 18.2 %collective-permute-start.26 = (bf16[4,9,24,384]{3,2,1,0:T(8,128)(2,1)}, bf16[4,9,24,384]{3,2,1,0:T(8,128)(2,1)}, u32[]{:S(2)}, u32[]{:S(2)}) collective-permute-start(bf16[4,9,24,384]{3,2,1,0:T(8,128)(2,1)} %pad_maximum_fusion.5), channel_id=1, source_target_pairs={{0,1},{1,0},{2,3},{3,2},{4,5},{5,4},{6,7},{7,6},{8,9},{9,8},{10,11... | collective-permute-start | bytes 1990664 | tf_op jit(solution)/shard_map/ppermute | solution.py:44
  225.2 21.2 %collective-permute-start.19 = (bf16[2,4,24,1152]{3,2,1,0:T(8,128)(2,1)}, bf16[2,4,24,1152]{3,2,1,0:T(8,128)(2,1)S(1)}, u32[]{:S(2)}, u32[]{:S(2)}) collective-permute-start(bf16[2,4,24,1152]{3,2,1,0:T(8,128)(2,1)} %get-tuple-element.151), channel_id=1, source_target_pairs={{0,1},{1,0},{2,3},{3,2},{4,5},{5,4},{6,7},{7,6},{8,9},{9,8},{10,11... | collective-permute-start | bytes 1327112 | tf_op jit(solution)/shard_map/ppermute | solution.py:44
  226.5 20.0 %collective-permute-start.20 = (bf16[2,4,24,1152]{3,2,1,0:T(8,128)(2,1)}, bf16[2,4,24,1152]{3,2,1,0:T(8,128)(2,1)S(1)}, u32[]{:S(2)}, u32[]{:S(2)}) collective-permute-start(bf16[2,4,24,1152]{3,2,1,0:T(8,128)(2,1)} %get-tuple-element.153), channel_id=1, source_target_pairs={{0,16},{16,0},{1,17},{17,1},{2,18},{18,2},{3,19},{19,3},{4,20},{20... | collective-permute-start | bytes 1327112 | tf_op jit(solution)/shard_map/ppermute | solution.py:44
  237.5 24.6 %collective-permute-start.29 = (bf16[9,24,768]{2,1,0:T(8,128)(2,1)}, bf16[9,24,768]{2,1,0:T(8,128)(2,1)S(1)}, u32[]{:S(2)}, u32[]{:S(2)}) collective-permute-start(bf16[9,24,768]{2,1,0:T(8,128)(2,1)} %get-tuple-element.195), channel_id=1, source_target_pairs={{0,6},{2,0},{4,2},{6,4},{1,7},{3,1},{5,3},{7,5},{8,14},{10,8},{12,... | collective-permute-start | bytes 995336 | tf_op jit(solution)/shard_map/ppermute | solution.py:49
  240.7 33.7 %collective-permute-start.28 = (bf16[9,24,768]{2,1,0:T(8,128)(2,1)}, bf16[9,24,768]{2,1,0:T(8,128)(2,1)}, u32[]{:S(2)}, u32[]{:S(2)}) collective-permute-start(bf16[9,24,768]{2,1,0:T(8,128)(2,1)} %get-tuple-element.196), channel_id=1, source_target_pairs={{0,4},{2,6},{4,0},{6,2},{1,5},{3,7},{5,1},{7,3},{8,12},{10,14},{12... | collective-permute-start | bytes 995336 | tf_op jit(solution)/shard_map/ppermute | solution.py:49
  240.7 33.7 %collective-permute-start.27 = (bf16[9,24,768]{2,1,0:T(8,128)(2,1)}, bf16[9,24,768]{2,1,0:T(8,128)(2,1)}, u32[]{:S(2)}, u32[]{:S(2)}) collective-permute-start(bf16[9,24,768]{2,1,0:T(8,128)(2,1)} %get-tuple-element.197), channel_id=1, source_target_pairs={{0,2},{2,4},{4,6},{6,0},{1,3},{3,5},{5,7},{7,1},{8,10},{10,12},{12... | collective-permute-start | bytes 995336 | tf_op jit(solution)/shard_map/ppermute | solution.py:49
  248.0 7.4 %collective-permute-start.22 = (bf16[4,24,1152]{2,1,0:T(8,128)(2,1)}, bf16[4,24,1152]{2,1,0:T(8,128)(2,1)}, u32[]{:S(2)}, u32[]{:S(2)}) collective-permute-start(bf16[4,24,1152]{2,1,0:T(8,128)(2,1)} %fusion.3), channel_id=1, source_target_pairs={{0,1},{1,0},{2,3},{3,2},{4,5},{5,4},{6,7},{7,6},{8,9},{9,8},{10,11... | collective-permute-start | bytes 663560 | tf_op jit(solution)/shard_map/ppermute | solution.py:44
  249.8 6.8 %collective-permute-start.21 = (bf16[4,24,1152]{2,1,0:T(8,128)(2,1)}, bf16[4,24,1152]{2,1,0:T(8,128)(2,1)}, u32[]{:S(2)}, u32[]{:S(2)}) collective-permute-start(bf16[4,24,1152]{2,1,0:T(8,128)(2,1)} %fusion.2), channel_id=1, source_target_pairs={{0,16},{16,0},{1,17},{17,1},{2,18},{18,2},{3,19},{19,3},{4,20},{20... | collective-permute-start | bytes 663560 | tf_op jit(solution)/shard_map/ppermute | solution.py:44
  250.4 22.2 %all-to-all-start.6 = ((f32[32,1,512]{2,1,0:T(1,128)}), f32[32,1,512]{2,1,0:T(1,128)}, u32[]{:S(2)}, u32[]{:S(2)}) async-start(f32[32,1,512]{2,1,0:T(1,128)} %get-tuple-element.161), calls=%async_computation.6 | async-start | bytes 131072 | tf_op jit(solution)/shard_map/all_to_all | solution.py:1175
  258.6 15.9 %collective-permute-start.32 = (bf16[24,2304]{1,0:T(8,128)(2,1)}, bf16[24,2304]{1,0:T(8,128)(2,1)}, u32[]{:S(2)}, u32[]{:S(2)}) collective-permute-start(bf16[24,2304]{1,0:T(8,128)(2,1)} %get-tuple-element.202), channel_id=1, source_target_pairs={{0,6},{2,0},{4,2},{6,4},{1,7},{3,1},{5,3},{7,5},{8,14},{10,8},{12,... | collective-permute-start | bytes 331784 | tf_op jit(solution)/shard_map/ppermute | solution.py:49
  262.1 13.0 %collective-permute-start.31 = (bf16[24,2304]{1,0:T(8,128)(2,1)}, bf16[24,2304]{1,0:T(8,128)(2,1)}, u32[]{:S(2)}, u32[]{:S(2)}) collective-permute-start(bf16[24,2304]{1,0:T(8,128)(2,1)} %get-tuple-element.203), channel_id=1, source_target_pairs={{0,4},{2,6},{4,0},{6,2},{1,5},{3,7},{5,1},{7,3},{8,12},{10,14},{12... | collective-permute-start | bytes 331784 | tf_op jit(solution)/shard_map/ppermute | solution.py:49
  262.9 12.3 %collective-permute-start.30 = (bf16[24,2304]{1,0:T(8,128)(2,1)}, bf16[24,2304]{1,0:T(8,128)(2,1)}, u32[]{:S(2)}, u32[]{:S(2)}) collective-permute-start(bf16[24,2304]{1,0:T(8,128)(2,1)} %get-tuple-element.204), channel_id=1, source_target_pairs={{0,2},{2,4},{4,6},{6,0},{1,3},{3,5},{5,7},{7,1},{8,10},{10,12},{12... | collective-permute-start | bytes 331784 | tf_op jit(solution)/shard_map/ppermute | solution.py:49
  (30 other events, 103.9 us)
Sparse Core Ops, SparseCore 0:
  13.5 106.6 all-gather.2

commit v9 on v8

--- a/solution.py
+++ b/solution.py
@@ -958,7 +958,8 @@
     )(*values)
 
 
-def begin_kernel(embed_ref, ada_ref, vectors_ref, segments_ref, valid_ref, *refs):
+def begin_kernel(embed_ref, ada_ref, segments_ref, valid_ref, *refs):
+    vectors, refs = [ref[...].astype(f32) for ref in refs[:5]], refs[5:]
     *weights, packed_ref = refs[:-1] if len(refs) > 1 else refs
     seqs, tokens = segments_ref.shape
     modulation = lax.dot_general(
@@ -968,13 +969,11 @@
         precision=precise,
         preferred_element_type=f32,
     )
-    size = modulation.shape[1]
-    vectors = vectors_ref[...].astype(f32)
-    modulation = modulation + vectors[:, :size]
+    modulation = modulation + vectors[0]
     count = jnp.sum(valid_ref[...].astype(f32), axis=1, keepdims=True)
     count = jnp.sum(count, axis=0, keepdims=True)
     fields = [modulation[s : s + 1] for s in range(seqs)]
-    fields.append(vectors[:, size:])
+    fields += vectors[1:]
     fields += [segments_ref[s : s + 1, :].astype(f32) for s in range(seqs)]
     fields.append(count)
     fields.append(jnp.zeros((1, packed_ref.shape[2] - sum(f.shape[1] for f in fields)), f32))
@@ -993,12 +992,12 @@
 
 def begin_with(time_embed, ada_weight, vectors, segments, valid_mask, weights, devices):
     seqs, tokens = segments.shape
-    columns = (seqs - 1) * ada_weight.shape[1] + vectors.shape[1] + seqs * tokens + 1
+    columns = (seqs - 1) * ada_weight.shape[1] + sum(v.shape[1] for v in vectors) + seqs * tokens + 1
     outs = [((devices, 1, columns + -columns % 128), f32, True)]
     if weights:
         outs.append(((9, 24, weights[0].shape[1]), bf16))
     return single(
-        begin_kernel, outs, [time_embed, ada_weight.T, vectors, segments, valid_mask, *weights]
+        begin_kernel, outs, [time_embed, ada_weight.T, segments, valid_mask, *vectors, *weights]
     )
 
 
@@ -1035,8 +1034,7 @@
     queries = 8 * tokens
     here = place()
 
-    vectors = [ada_bias, gain_attn, gain_mlp, up_bias, down_bias]
-    vectors = jnp.concatenate([v.astype(f32) for v in vectors]).reshape(1, -1)
+    vectors = [v.reshape(1, -1) for v in (ada_bias, gain_attn, gain_mlp, up_bias, down_bias)]
     weights = [] if parts > 1 else [out_weight, up_weight, down_weight]
     packed, *later = begin_with(
         time_embed, ada_weight, vectors, segments, valid_mask, weights, devices

time: 286 us -> 283 us (0.990)
    concatenate x1 -> x0, local copies, waits for them, and re-layouts: 3.43 us -> none  [on_device(): vectors = jnp.concatenate([v.astype(f32) for v in vectors]).reshape(1, -1)]
  transfers between devices with their start and end apart: 40 -> 40, of which waited for: 19 -> 19; matrix products, arithmetic and copies ran while one was open for 5% -> 5% of each run, Pallas kernels for 20% -> 21%
where the time goes in v9:
time: 283 us; the launch traced here: 282 us
  waiting for transfers between devices  86.2 us (30%)
  Pallas kernels  72.7 us (26%)
  starting transfers between devices  58.8 us (21%)
  blocking collectives  28.3 us (10%)
  between operations  14.5 us (5%)
  other arithmetic  13 us (5%)
  local copies, waits for them, and re-layouts  8.59 us (3%)
    ppermute x24, waiting for transfers between devices, swap(): return lax.ppermute(value, axis, [(0, 1), (1, 0)])  53.8 us
    pallas_call x8, Pallas kernels, single(): pl.pallas_call(kernel, grid=(1,), out_shape=tuple((result(*o) for o in ou...  39.7 us
    all_to_all x1, blocking collectives, exchange(): return lax.all_to_all(rows, SPOT, 0, 0, tiled=True)  28.3 us
    all_to_all x4, starting transfers between devices, exchange(): return lax.all_to_all(rows, SPOT, 0, 0, tiled=True)  17.2 us
    ppermute x24, starting transfers between devices, swap(): return lax.ppermute(value, axis, [(0, 1), (1, 0)])  16.7 us
    all_to_all x4, waiting for transfers between devices, exchange(): return lax.all_to_all(rows, SPOT, 0, 0, tiled=True)  15.4 us
    ppermute x9, starting transfers between devices, turn(): lax.ppermute(value, axis, [(i, (i - step) % size) for i in range(size)])  14.5 us
    pallas_call x1, Pallas kernels, attend_back(): pl.pallas_call(partial(backward_kernel, starts), grid=(steps,), out_shape...  13 us
  transfers between devices with their start and end apart: 40, of which 19 were waited for; matrix products, arithmetic and copies ran while one was open for 5% of the time, Pallas kernels for 21%

profile of v9, /device:TPU:0, one launch (start us, length us, event | category | flops | bytes accessed | tf_op | source)
XLA Modules:
  0.0 282.1 jit_solution(10035631280571613115)
XLA Ops:
  8.4 2.1 shard_map.246
  10.6 5.1 %collective-permute-start = (bf16[24,2304]{1,0:T(8,128)(2,1)}, bf16[24,2304]{1,0:T(8,128)(2,1)S(1)}, u32[]{:S(2)}, u32[]{:S(2)}) collective-permute-start(bf16[24,2304]{1,0:T(8,128)(2,1)} %param.23), channel_id=1, source_target_pairs={{0,6},{2,0},{4,2},{6,4},{1,7},{3,1},{5,3},{7,5},{8,14},{10,8},{12,... | collective-permute-start | bytes 331784 | tf_op jit(solution)/shard_map/ppermute | solution.py:49
  16.7 5.6 %all-to-all-start = ((f32[32,1,640]{2,1,0:T(1,128)}), f32[32,1,640]{2,1,0:T(1,128)S(1)}, u32[]{:S(2)}, u32[]{:S(2)}) async-start(f32[32,1,640]{2,1,0:T(1,128)} %get-tuple-element.102), calls=%async_computation | async-start | bytes 163840 | tf_op jit(solution)/shard_map/all_to_all | solution.py:1042
  23.5 2.7 collective-permute-done.1
  27.1 3.9 %all-to-all-done.every_ref = f32[32,1,640]{2,1,0:T(1,128)S(1)} async-done(((f32[32,1,640]{2,1,0:T(1,128)}), f32[32,1,640]{2,1,0:T(1,128)S(1)}, u32[]{:S(2)}, u32[]{:S(2)}) %all-to-all-start) | async-done | bytes 81952 | tf_op jit(solution)/shard_map/all_to_all | solution.py:1042
  32.6 4.8 %collective-permute-done.5 = bf16[4,24,1152]{2,1,0:T(8,128)(2,1)S(1)} collective-permute-done((bf16[4,24,1152]{2,1,0:T(8,128)(2,1)S(1)}, bf16[4,24,1152]{2,1,0:T(8,128)(2,1)S(1)}, u32[]{:S(2)}, u32[]{:S(2)}) %collective-permute-start.5) | collective-permute-done | bytes 221216 | tf_op jit(solution)/shard_map/ppermute | solution.py:44
  40.5 2.5 shard_map.247
  42.9 12.9 %collective-permute-done.6 = bf16[2,4,24,1152]{3,2,1,0:T(8,128)(2,1)S(1)} collective-permute-done((bf16[2,4,24,1152]{3,2,1,0:T(8,128)(2,1)S(1)}, bf16[2,4,24,1152]{3,2,1,0:T(8,128)(2,1)S(1)}, u32[]{:S(2)}, u32[]{:S(2)}) %collective-permute-start.6) | collective-permute-done | bytes 442400 | tf_op jit(solution)/shard_map/ppermute | solution.py:44
  56.6 1.9 collective-permute-done.7.refs_1_
  59.8 6.9 %shard_map.248 = (bf16[128,768]{1,0:T(8,128)(2,1)}, bf16[8,64,384]{2,1,0:T(8,128)(2,1)S(1)}, bf16[8,32,384]{2,1,0:T(8,128)(2,1)}, bf16[768,2304]{1,0:T(8,128)(2,1)}) custom-call(s32[5]{0:T(128)S(1)} %stack.71.place_ref, bf16[2,64,768]{2,1,0:T(8,128)(2,1)} %x_ref.5, f32[8,4608]{1,0:T(8,128)} %get-tuple-element.111.mod_ref, ...), custom_call_target="tpu_custom_call" | custom-call | tf_op jit(solution)/shard_map/pallas_call | solution.py:81
  66.7 28.3 %all_to_all.35 = bf16[8,64,384]{2,1,0:T(8,128)(2,1)S(1)} all-to-all(bf16[8,64,384]{2,1,0:T(8,128)(2,1)S(1)} %get-tuple-element.115), channel_id=1, replica_groups=mesh['hx'=2,'hc'=2,'rb'=1,'sz'=4,'sy'=2] {'sz','sy'}, dimensions={0} | all-to-all | bytes 786432 | tf_op jit(solution)/shard_map/all_to_all | solution.py:1009
  94.9 4.0 %all-to-all-start.2 = ((bf16[8,32,384]{2,1,0:T(8,128)(2,1)}), bf16[8,32,384]{2,1,0:T(8,128)(2,1)S(1)}, u32[]{:S(2)}, u32[]{:S(2)}) async-start(bf16[8,32,384]{2,1,0:T(8,128)(2,1)} %get-tuple-element.116), calls=%async_computation.2 | async-start | bytes 393216 | tf_op jit(solution)/shard_map/all_to_all | solution.py:1009
  98.9 13.7 %all-to-all-done.2.came_ref = bf16[8,32,384]{2,1,0:T(8,128)(2,1)S(1)} async-done(((bf16[8,32,384]{2,1,0:T(8,128)(2,1)}), bf16[8,32,384]{2,1,0:T(8,128)(2,1)S(1)}, u32[]{:S(2)}, u32[]{:S(2)}) %all-to-all-start.2) | async-done | bytes 196640 | tf_op jit(solution)/shard_map/all_to_all | solution.py:1009
  115.4 9.4 %shard_map.249 = (bf16[8,32,384]{2,1,0:T(8,128)(2,1)}, f32[192,512]{1,0:T(8,128)}, f32[8,512]{1,0:T(8,128)}) custom-call(bf16[8,32,384]{2,1,0:T(8,128)(2,1)} %copy-done.4, bf16[512,384]{1,0:T(8,128)(2,1)} %bitcast.74, bf16[512,384]{1,0:T(8,128)(2,1)} %copy-done.5, bf16[512,384]{1,0:T(8,128)(2,1)} %copy-done.6, bf16[512,384]{1,0:T(8,128)(2,1)} %copy-done.7, ...), custom_call_target="tpu_custom_call" | custom-call | tf_op jit(solution)/shard_map/pallas_call | solution.py:338
  124.8 3.6 %all-to-all-start.3 = ((bf16[8,32,384]{2,1,0:T(8,128)(2,1)}), bf16[8,32,384]{2,1,0:T(8,128)(2,1)S(1)}, u32[]{:S(2)}, u32[]{:S(2)}) async-start(bf16[8,32,384]{2,1,0:T(8,128)(2,1)} %get-tuple-element.121), calls=%async_computation.3 | async-start | bytes 393216 | tf_op jit(solution)/shard_map/all_to_all | solution.py:1009
  128.4 8.5 %shard_map.250 = (bf16[768,768]{1,0:T(8,128)(2,1)}, bf16[768,3072]{1,0:T(8,128)(2,1)}, bf16[3072,768]{1,0:T(8,128)(2,1)}) custom-call(bf16[32,9,24,768]{3,2,1,0:T(8,128)(2,1)} %bitcast.71), custom_call_target="tpu_custom_call" | custom-call | tf_op jit(solution)/shard_map/pallas_call | solution.py:509
  137.6 10.4 %shard_map.251 = (bf16[2,64,768]{2,1,0:T(8,128)(2,1)}, f32[128,768]{1,0:T(8,128)}, bf16[8,32,384]{2,1,0:T(8,128)(2,1)}, bf16[128,9216]{1,0:T(8,128)(2,1)S(1)}, f32[16,768]{1,0:T(8,128)}) custom-call(bf16[8,32,384]{2,1,0:T(8,128)(2,1)} %copy-done.11, bf16[2,64,768]{2,1,0:T(8,128)(2,1)} %x_ref.5, bf16[2,64,768]{2,1,0:T(8,128)(2,1)} %teacher_ref.1, ...), custom_call_target="tpu_custom_call" | custom-call | tf_op jit(solution)/shard_map/pallas_call | solution.py:81
  148.2 5.7 %all-to-all-start.4 = ((bf16[8,32,384]{2,1,0:T(8,128)(2,1)}), bf16[8,32,384]{2,1,0:T(8,128)(2,1)S(1)}, u32[]{:S(2)}, u32[]{:S(2)}) async-start(bf16[8,32,384]{2,1,0:T(8,128)(2,1)} %get-tuple-element.129), calls=%async_computation.4 | async-start | bytes 393216 | tf_op jit(solution)/shard_map/all_to_all | solution.py:1009
  153.9 6.9 %shard_map.252 = (bf16[2,4,9,24,128]{4,3,2,1,0:T(8,128)(2,1)}, bf16[2,4,9,24,128]{4,3,2,1,0:T(8,128)(2,1)}, bf16[2,4,9,24,256]{4,3,2,1,0:T(8,128)(2,1)}, bf16[2,...) custom-call(s32[5]{0:T(128)S(1)} %stack.71.place_ref, ...), custom_call_target="tpu_custom_call" | custom-call | tf_op jit(solution)/shard_map/pallas_call | solution.py:81
  164.7 13.0 %shard_map.253 = (bf16[8,32,384]{2,1,0:T(8,128)(2,1)S(1)}, f32[512,384]{1,0:T(8,128)S(1)}, f32[512,384]{1,0:T(8,128)S(1)}, bf16[1024,384]{1,0:T(8,128)(2,1)S(1)}) custom-call(bf16[8,32,384]{2,1,0:T(8,128)(2,1)} %copy-done.4, bf16[8,32,384]{2,1,0:T(8,128)(2,1)} %copy-done.10, bf16[512,384]{1,0:T(8,128)(2,1)} %bitcast.75, bf16[512,384]{1,0:T(8,128)(2,1)} %copy-done.5, ...), custom_call_target="tpu_custom_call" | custom-call | tf_op jit(solution)/shard_map/pallas_call | solution.py:435
  177.8 2.3 collective-permute-done.15
  183.4 8.8 %collective-permute-done.16 = bf16[512,384]{1,0:T(8,128)(2,1)S(1)} collective-permute-done((bf16[512,384]{1,0:T(8,128)(2,1)S(1)}, bf16[512,384]{1,0:T(8,128)(2,1)S(1)}, u32[]{:S(2)}, u32[]{:S(2)}) %collective-permute-start.16) | collective-permute-done | bytes 393248 | tf_op jit(solution)/shard_map/ppermute | solution.py:44
  193.1 3.9 %all-to-all-start.5 = ((bf16[8,96,384]{2,1,0:T(8,128)(2,1)}), bf16[8,96,384]{2,1,0:T(8,128)(2,1)S(1)}, u32[]{:S(2)}, u32[]{:S(2)}) async-start(bf16[8,96,384]{2,1,0:T(8,128)(2,1)} %pad_maximum_fusion.6), calls=%async_computation.5 | async-start | bytes 1179648 | tf_op jit(solution)/shard_map/all_to_all | solution.py:1009
  197.2 10.2 %collective-permute-done.23 = bf16[2,4,9,24,256]{4,3,2,1,0:T(8,128)(2,1)} collective-permute-done((bf16[2,4,9,24,256]{4,3,2,1,0:T(8,128)(2,1)}, bf16[2,4,9,24,256]{4,3,2,1,0:T(8,128)(2,1)}, u32[]{:S(2)}, u32[]{:S(2)}) %collective-permute-start.23) | collective-permute-done | bytes 884768 | tf_op jit(solution)/shard_map/ppermute | solution.py:44
  218.1 4.1 %shard_map.254 = (bf16[2,4,24,1152]{3,2,1,0:T(8,128)(2,1)}, bf16[2,4,24,1152]{3,2,1,0:T(8,128)(2,1)}, bf16[2,4,24,1152]{3,2,1,0:T(8,128)(2,1)}, bf16[2,4,24,1152]{3,2,1,0:T(8,128)(2,1)}) custom-call(s32[5]{0:T(128)S(1)} %stack.71.place_ref, bf16[128,768]{1,0:T(8,128)(2,1)} %get-tuple-element.149.entered_ref, bf16[128,768]{1,0:T(8,128)(2,1)} %copy-done.21, ...), custom_call_target="tpu_custom_call" | custom-call | tf_op jit(solution)/shard_map/pallas_call | solution.py:81
  224.6 7.0 %collective-permute-done.26 = bf16[4,9,24,384]{3,2,1,0:T(8,128)(2,1)} collective-permute-done((bf16[4,9,24,384]{3,2,1,0:T(8,128)(2,1)}, bf16[4,9,24,384]{3,2,1,0:T(8,128)(2,1)}, u32[]{:S(2)}, u32[]{:S(2)}) %collective-permute-start.26) | collective-permute-done | bytes 663584 | tf_op jit(solution)/shard_map/ppermute | solution.py:44
  234.4 3.2 %collective-permute-start.29 = (bf16[9,24,768]{2,1,0:T(8,128)(2,1)}, bf16[9,24,768]{2,1,0:T(8,128)(2,1)S(1)}, u32[]{:S(2)}, u32[]{:S(2)}) collective-permute-start(bf16[9,24,768]{2,1,0:T(8,128)(2,1)} %get-tuple-element.195), channel_id=1, source_target_pairs={{0,6},{2,0},{4,2},{6,4},{1,7},{3,1},{5,3},{7,5},{8,14},{10,8},{12,... | collective-permute-start | bytes 995336 | tf_op jit(solution)/shard_map/ppermute | solution.py:49
  238.3 4.9 %shard_map.255 = (f32[2,64,768]{2,1,0:T(8,128)}, f32[32,1,512]{2,1,0:T(1,128)}, bf16[128,2304]{1,0:T(8,128)(2,1)}) custom-call(bf16[8,96,384]{2,1,0:T(8,128)(2,1)} %copy-done.2, bf16[2,64,768]{2,1,0:T(8,128)(2,1)} %x_ref.5, f32[128,768]{1,0:T(8,128)} %get-tuple-element.155.hidden_ref, f32[8,4608]{1,0:T(8,128)} %get-tuple-element.111.mod_ref, ...), custom_call_target="tpu_custom_call" | custom-call | tf_op jit(solution)/shard_map/pallas_call | solution.py:81
  247.6 4.7 %all-to-all-start.6 = ((f32[32,1,512]{2,1,0:T(1,128)}), f32[32,1,512]{2,1,0:T(1,128)}, u32[]{:S(2)}, u32[]{:S(2)}) async-start(f32[32,1,512]{2,1,0:T(1,128)} %get-tuple-element.161), calls=%async_computation.6 | async-start | bytes 131072 | tf_op jit(solution)/shard_map/all_to_all | solution.py:1173
  255.5 3.5 %collective-permute-start.32 = (bf16[24,2304]{1,0:T(8,128)(2,1)}, bf16[24,2304]{1,0:T(8,128)(2,1)}, u32[]{:S(2)}, u32[]{:S(2)}) collective-permute-start(bf16[24,2304]{1,0:T(8,128)(2,1)} %get-tuple-element.202), channel_id=1, source_target_pairs={{0,6},{2,0},{4,2},{6,4},{1,7},{3,1},{5,3},{7,5},{8,14},{10,8},{12,... | collective-permute-start | bytes 331784 | tf_op jit(solution)/shard_map/ppermute | solution.py:49
  261.0 9.1 %all-to-all-done.6.small_ref = f32[32,1,512]{2,1,0:T(1,128)} async-done(((f32[32,1,512]{2,1,0:T(1,128)}), f32[32,1,512]{2,1,0:T(1,128)}, u32[]{:S(2)}, u32[]{:S(2)}) %all-to-all-start.6) | async-done | bytes 65568 | tf_op jit(solution)/shard_map/all_to_all | solution.py:1173
  273.1 2.2 shard_map.257
  (134 shorter events, 51.7 us)
Async XLA Ops:
  7.2 121.2 %all-gather.3.cloned.1.call-start = ((), (), s32[]{:S(2)}) async-start(), calls=%async_computation.7 | async-start | bytes 10948608 | tf_op jit(solution)/shard_map/all_gather | solution.py:1049
  10.6 11.7 %collective-permute-start = (bf16[24,2304]{1,0:T(8,128)(2,1)}, bf16[24,2304]{1,0:T(8,128)(2,1)S(1)}, u32[]{:S(2)}, u32[]{:S(2)}) collective-permute-start(bf16[24,2304]{1,0:T(8,128)(2,1)} %param.23), channel_id=1, source_target_pairs={{0,6},{2,0},{4,2},{6,4},{1,7},{3,1},{5,3},{7,5},{8,14},{10,8},{12,... | collective-permute-start | bytes 331784 | tf_op jit(solution)/shard_map/ppermute | solution.py:49
  15.7 7.8 %collective-permute-start.2 = (bf16[24,2304]{1,0:T(8,128)(2,1)}, bf16[24,2304]{1,0:T(8,128)(2,1)S(1)}, u32[]{:S(2)}, u32[]{:S(2)}) collective-permute-start(bf16[24,2304]{1,0:T(8,128)(2,1)} %param.23), channel_id=1, source_target_pairs={{0,2},{2,4},{4,6},{6,0},{1,3},{3,5},{5,7},{7,1},{8,10},{10,12},{12... | collective-permute-start | bytes 331784 | tf_op jit(solution)/shard_map/ppermute | solution.py:49
  15.7 10.5 %collective-permute-start.1 = (bf16[24,2304]{1,0:T(8,128)(2,1)}, bf16[24,2304]{1,0:T(8,128)(2,1)S(1)}, u32[]{:S(2)}, u32[]{:S(2)}) collective-permute-start(bf16[24,2304]{1,0:T(8,128)(2,1)} %param.23), channel_id=1, source_target_pairs={{0,4},{2,6},{4,0},{6,2},{1,5},{3,7},{5,1},{7,3},{8,12},{10,14},{12... | collective-permute-start | bytes 331784 | tf_op jit(solution)/shard_map/ppermute | solution.py:49
  16.7 14.3 %all-to-all-start = ((f32[32,1,640]{2,1,0:T(1,128)}), f32[32,1,640]{2,1,0:T(1,128)S(1)}, u32[]{:S(2)}, u32[]{:S(2)}) async-start(f32[32,1,640]{2,1,0:T(1,128)} %get-tuple-element.102), calls=%async_computation | async-start | bytes 163840 | tf_op jit(solution)/shard_map/all_to_all | solution.py:1042
  32.1 7.2 %collective-permute-start.3 = (bf16[4,24,1152]{2,1,0:T(8,128)(2,1)S(1)}, bf16[4,24,1152]{2,1,0:T(8,128)(2,1)S(1)}, u32[]{:S(2)}, u32[]{:S(2)}) collective-permute-start(bf16[4,24,1152]{2,1,0:T(8,128)(2,1)S(1)} %get-tuple-element.210), channel_id=1, source_target_pairs={{0,16},{16,0},{1,17},{17,1},{2,18},{18,2},{3,19},{19,3},{4,20},{20... | collective-permute-start | bytes 663560 | tf_op jit(solution)/shard_map/ppermute | solution.py:44
  37.6 18.2 %collective-permute-start.6 = (bf16[2,4,24,1152]{3,2,1,0:T(8,128)(2,1)S(1)}, bf16[2,4,24,1152]{3,2,1,0:T(8,128)(2,1)S(1)}, u32[]{:S(2)}, u32[]{:S(2)}) collective-permute-start(bf16[2,4,24,1152]{3,2,1,0:T(8,128)(2,1)S(1)} %get-tuple-element.206), channel_id=1, source_target_pairs={{0,16},{16,0},{1,17},{17,1},{2,18},{18,2},{3,19},{19,3},{4,20},{20... | collective-permute-start | bytes 1327112 | tf_op jit(solution)/shard_map/ppermute | solution.py:44
  39.3 16.6 %collective-permute-start.4 = (bf16[2,4,24,1152]{3,2,1,0:T(8,128)(2,1)S(1)}, bf16[2,4,24,1152]{3,2,1,0:T(8,128)(2,1)S(1)}, u32[]{:S(2)}, u32[]{:S(2)}) collective-permute-start(bf16[2,4,24,1152]{3,2,1,0:T(8,128)(2,1)S(1)} %get-tuple-element.212), channel_id=1, source_target_pairs={{0,1},{1,0},{2,3},{3,2},{4,5},{5,4},{6,7},{7,6},{8,9},{9,8},{10,11... | collective-permute-start | bytes 1327112 | tf_op jit(solution)/shard_map/ppermute | solution.py:44
  94.9 17.7 %collective-permute-start.9 = (bf16[512,384]{1,0:T(8,128)(2,1)S(1)}, bf16[512,384]{1,0:T(8,128)(2,1)S(1)}, u32[]{:S(2)}, u32[]{:S(2)}) collective-permute-start(bf16[512,384]{1,0:T(8,128)(2,1)S(1)} %bitcast.72), channel_id=1, source_target_pairs={{0,16},{16,0},{1,17},{17,1},{2,18},{18,2},{3,19},{19,3},{4,20},{20... | collective-permute-start | bytes 1179656 | tf_op jit(solution)/shard_map/ppermute | solution.py:44
  94.9 17.7 %all-to-all-start.2 = ((bf16[8,32,384]{2,1,0:T(8,128)(2,1)}), bf16[8,32,384]{2,1,0:T(8,128)(2,1)S(1)}, u32[]{:S(2)}, u32[]{:S(2)}) async-start(bf16[8,32,384]{2,1,0:T(8,128)(2,1)} %get-tuple-element.116), calls=%async_computation.2 | async-start | bytes 393216 | tf_op jit(solution)/shard_map/all_to_all | solution.py:1009
  98.9 13.8 %collective-permute-start.10 = (bf16[512,384]{1,0:T(8,128)(2,1)S(1)}, bf16[512,384]{1,0:T(8,128)(2,1)S(1)}, u32[]{:S(2)}, u32[]{:S(2)}) collective-permute-start(bf16[512,384]{1,0:T(8,128)(2,1)S(1)} %bitcast.73), channel_id=1, source_target_pairs={{0,8},{8,0},{1,9},{9,1},{2,10},{10,2},{3,11},{11,3},{4,12},{12,4},... | collective-permute-start | bytes 1179656 | tf_op jit(solution)/shard_map/ppermute | solution.py:44
  124.8 12.2 %all-to-all-start.3 = ((bf16[8,32,384]{2,1,0:T(8,128)(2,1)}), bf16[8,32,384]{2,1,0:T(8,128)(2,1)S(1)}, u32[]{:S(2)}, u32[]{:S(2)}) async-start(bf16[8,32,384]{2,1,0:T(8,128)(2,1)} %get-tuple-element.121), calls=%async_computation.3 | async-start | bytes 393216 | tf_op jit(solution)/shard_map/all_to_all | solution.py:1009
  148.2 14.3 %all-to-all-start.4 = ((bf16[8,32,384]{2,1,0:T(8,128)(2,1)}), bf16[8,32,384]{2,1,0:T(8,128)(2,1)S(1)}, u32[]{:S(2)}, u32[]{:S(2)}) async-start(bf16[8,32,384]{2,1,0:T(8,128)(2,1)} %get-tuple-element.129), calls=%async_computation.4 | async-start | bytes 393216 | tf_op jit(solution)/shard_map/all_to_all | solution.py:1009
  162.5 15.2 %collective-permute-start.13 = (bf16[2,4,9,24,128]{4,3,2,1,0:T(8,128)(2,1)}, bf16[2,4,9,24,128]{4,3,2,1,0:T(8,128)(2,1)S(1)}, u32[]{:S(2)}, u32[]{:S(2)}) collective-permute-start(bf16[2,4,9,24,128]{4,3,2,1,0:T(8,128)(2,1)} %get-tuple-element.144), channel_id=1, source_target_pairs={{0,1},{1,0},{2,3},{3,2},{4,5},{5,4},{6,7},{7,6},{8,9},{9,8},{10,11... | collective-permute-start | bytes 1327112 | tf_op jit(solution)/shard_map/ppermute | solution.py:44
  163.5 14.2 %collective-permute-start.14 = (bf16[2,4,9,24,128]{4,3,2,1,0:T(8,128)(2,1)}, bf16[2,4,9,24,128]{4,3,2,1,0:T(8,128)(2,1)S(1)}, u32[]{:S(2)}, u32[]{:S(2)}) collective-permute-start(bf16[2,4,9,24,128]{4,3,2,1,0:T(8,128)(2,1)} %get-tuple-element.145), channel_id=1, source_target_pairs={{0,16},{16,0},{1,17},{17,1},{2,18},{18,2},{3,19},{19,3},{4,20},{20... | collective-permute-start | bytes 1327112 | tf_op jit(solution)/shard_map/ppermute | solution.py:44
  180.1 12.0 %collective-permute-start.16 = (bf16[512,384]{1,0:T(8,128)(2,1)S(1)}, bf16[512,384]{1,0:T(8,128)(2,1)S(1)}, u32[]{:S(2)}, u32[]{:S(2)}) collective-permute-start(bf16[512,384]{1,0:T(8,128)(2,1)S(1)} %add_convert_fusion.3), channel_id=1, source_target_pairs={{0,16},{16,0},{1,17},{17,1},{2,18},{18,2},{3,19},{19,3},{4,20},{20... | collective-permute-start | bytes 1179656 | tf_op jit(solution)/shard_map/ppermute | solution.py:44
  181.0 26.4 %collective-permute-start.23 = (bf16[2,4,9,24,256]{4,3,2,1,0:T(8,128)(2,1)}, bf16[2,4,9,24,256]{4,3,2,1,0:T(8,128)(2,1)}, u32[]{:S(2)}, u32[]{:S(2)}) collective-permute-start(bf16[2,4,9,24,256]{4,3,2,1,0:T(8,128)(2,1)} %get-tuple-element.171), channel_id=1, source_target_pairs={{0,1},{1,0},{2,3},{3,2},{4,5},{5,4},{6,7},{7,6},{8,9},{9,8},{10,11... | collective-permute-start | bytes 2654216 | tf_op jit(solution)/shard_map/ppermute | solution.py:44
  182.1 29.1 %collective-permute-start.25 = (bf16[2,4,9,24,256]{4,3,2,1,0:T(8,128)(2,1)}, bf16[2,4,9,24,256]{4,3,2,1,0:T(8,128)(2,1)}, u32[]{:S(2)}, u32[]{:S(2)}) collective-permute-start(bf16[2,4,9,24,256]{4,3,2,1,0:T(8,128)(2,1)} %get-tuple-element.175), channel_id=1, source_target_pairs={{0,16},{16,0},{1,17},{17,1},{2,18},{18,2},{3,19},{19,3},{4,20},{20... | collective-permute-start | bytes 2654216 | tf_op jit(solution)/shard_map/ppermute | solution.py:44
  193.1 21.2 %all-to-all-start.5 = ((bf16[8,96,384]{2,1,0:T(8,128)(2,1)}), bf16[8,96,384]{2,1,0:T(8,128)(2,1)S(1)}, u32[]{:S(2)}, u32[]{:S(2)}) async-start(bf16[8,96,384]{2,1,0:T(8,128)(2,1)} %pad_maximum_fusion.6), calls=%async_computation.5 | async-start | bytes 1179648 | tf_op jit(solution)/shard_map/all_to_all | solution.py:1009
  209.7 14.9 %collective-permute-start.24 = (bf16[4,9,24,384]{3,2,1,0:T(8,128)(2,1)}, bf16[4,9,24,384]{3,2,1,0:T(8,128)(2,1)}, u32[]{:S(2)}, u32[]{:S(2)}) collective-permute-start(bf16[4,9,24,384]{3,2,1,0:T(8,128)(2,1)} %pad_maximum_fusion.4), channel_id=1, source_target_pairs={{0,16},{16,0},{1,17},{17,1},{2,18},{18,2},{3,19},{19,3},{4,20},{20... | collective-permute-start | bytes 1990664 | tf_op jit(solution)/shard_map/ppermute | solution.py:44
  213.5 18.2 %collective-permute-start.26 = (bf16[4,9,24,384]{3,2,1,0:T(8,128)(2,1)}, bf16[4,9,24,384]{3,2,1,0:T(8,128)(2,1)}, u32[]{:S(2)}, u32[]{:S(2)}) collective-permute-start(bf16[4,9,24,384]{3,2,1,0:T(8,128)(2,1)} %pad_maximum_fusion.5), channel_id=1, source_target_pairs={{0,1},{1,0},{2,3},{3,2},{4,5},{5,4},{6,7},{7,6},{8,9},{9,8},{10,11... | collective-permute-start | bytes 1990664 | tf_op jit(solution)/shard_map/ppermute | solution.py:44
  222.2 21.2 %collective-permute-start.19 = (bf16[2,4,24,1152]{3,2,1,0:T(8,128)(2,1)}, bf16[2,4,24,1152]{3,2,1,0:T(8,128)(2,1)S(1)}, u32[]{:S(2)}, u32[]{:S(2)}) collective-permute-start(bf16[2,4,24,1152]{3,2,1,0:T(8,128)(2,1)} %get-tuple-element.151), channel_id=1, source_target_pairs={{0,1},{1,0},{2,3},{3,2},{4,5},{5,4},{6,7},{7,6},{8,9},{9,8},{10,11... | collective-permute-start | bytes 1327112 | tf_op jit(solution)/shard_map/ppermute | solution.py:44
  223.5 20.0 %collective-permute-start.20 = (bf16[2,4,24,1152]{3,2,1,0:T(8,128)(2,1)}, bf16[2,4,24,1152]{3,2,1,0:T(8,128)(2,1)S(1)}, u32[]{:S(2)}, u32[]{:S(2)}) collective-permute-start(bf16[2,4,24,1152]{3,2,1,0:T(8,128)(2,1)} %get-tuple-element.153), channel_id=1, source_target_pairs={{0,16},{16,0},{1,17},{17,1},{2,18},{18,2},{3,19},{19,3},{4,20},{20... | collective-permute-start | bytes 1327112 | tf_op jit(solution)/shard_map/ppermute | solution.py:44
  234.4 24.6 %collective-permute-start.29 = (bf16[9,24,768]{2,1,0:T(8,128)(2,1)}, bf16[9,24,768]{2,1,0:T(8,128)(2,1)S(1)}, u32[]{:S(2)}, u32[]{:S(2)}) collective-permute-start(bf16[9,24,768]{2,1,0:T(8,128)(2,1)} %get-tuple-element.195), channel_id=1, source_target_pairs={{0,6},{2,0},{4,2},{6,4},{1,7},{3,1},{5,3},{7,5},{8,14},{10,8},{12,... | collective-permute-start | bytes 995336 | tf_op jit(solution)/shard_map/ppermute | solution.py:49
  237.7 34.3 %collective-permute-start.28 = (bf16[9,24,768]{2,1,0:T(8,128)(2,1)}, bf16[9,24,768]{2,1,0:T(8,128)(2,1)}, u32[]{:S(2)}, u32[]{:S(2)}) collective-permute-start(bf16[9,24,768]{2,1,0:T(8,128)(2,1)} %get-tuple-element.196), channel_id=1, source_target_pairs={{0,4},{2,6},{4,0},{6,2},{1,5},{3,7},{5,1},{7,3},{8,12},{10,14},{12... | collective-permute-start | bytes 995336 | tf_op jit(solution)/shard_map/ppermute | solution.py:49
  237.7 34.3 %collective-permute-start.27 = (bf16[9,24,768]{2,1,0:T(8,128)(2,1)}, bf16[9,24,768]{2,1,0:T(8,128)(2,1)}, u32[]{:S(2)}, u32[]{:S(2)}) collective-permute-start(bf16[9,24,768]{2,1,0:T(8,128)(2,1)} %get-tuple-element.197), channel_id=1, source_target_pairs={{0,2},{2,4},{4,6},{6,0},{1,3},{3,5},{5,7},{7,1},{8,10},{10,12},{12... | collective-permute-start | bytes 995336 | tf_op jit(solution)/shard_map/ppermute | solution.py:49
  244.9 7.4 %collective-permute-start.22 = (bf16[4,24,1152]{2,1,0:T(8,128)(2,1)}, bf16[4,24,1152]{2,1,0:T(8,128)(2,1)}, u32[]{:S(2)}, u32[]{:S(2)}) collective-permute-start(bf16[4,24,1152]{2,1,0:T(8,128)(2,1)} %fusion.3), channel_id=1, source_target_pairs={{0,1},{1,0},{2,3},{3,2},{4,5},{5,4},{6,7},{7,6},{8,9},{9,8},{10,11... | collective-permute-start | bytes 663560 | tf_op jit(solution)/shard_map/ppermute | solution.py:44
  246.8 6.8 %collective-permute-start.21 = (bf16[4,24,1152]{2,1,0:T(8,128)(2,1)}, bf16[4,24,1152]{2,1,0:T(8,128)(2,1)}, u32[]{:S(2)}, u32[]{:S(2)}) collective-permute-start(bf16[4,24,1152]{2,1,0:T(8,128)(2,1)} %fusion.2), channel_id=1, source_target_pairs={{0,16},{16,0},{1,17},{17,1},{2,18},{18,2},{3,19},{19,3},{4,20},{20... | collective-permute-start | bytes 663560 | tf_op jit(solution)/shard_map/ppermute | solution.py:44
  247.6 22.4 %all-to-all-start.6 = ((f32[32,1,512]{2,1,0:T(1,128)}), f32[32,1,512]{2,1,0:T(1,128)}, u32[]{:S(2)}, u32[]{:S(2)}) async-start(f32[32,1,512]{2,1,0:T(1,128)} %get-tuple-element.161), calls=%async_computation.6 | async-start | bytes 131072 | tf_op jit(solution)/shard_map/all_to_all | solution.py:1173
  255.5 16.4 %collective-permute-start.32 = (bf16[24,2304]{1,0:T(8,128)(2,1)}, bf16[24,2304]{1,0:T(8,128)(2,1)}, u32[]{:S(2)}, u32[]{:S(2)}) collective-permute-start(bf16[24,2304]{1,0:T(8,128)(2,1)} %get-tuple-element.202), channel_id=1, source_target_pairs={{0,6},{2,0},{4,2},{6,4},{1,7},{3,1},{5,3},{7,5},{8,14},{10,8},{12,... | collective-permute-start | bytes 331784 | tf_op jit(solution)/shard_map/ppermute | solution.py:49
  259.1 13.0 %collective-permute-start.31 = (bf16[24,2304]{1,0:T(8,128)(2,1)}, bf16[24,2304]{1,0:T(8,128)(2,1)}, u32[]{:S(2)}, u32[]{:S(2)}) collective-permute-start(bf16[24,2304]{1,0:T(8,128)(2,1)} %get-tuple-element.203), channel_id=1, source_target_pairs={{0,4},{2,6},{4,0},{6,2},{1,5},{3,7},{5,1},{7,3},{8,12},{10,14},{12... | collective-permute-start | bytes 331784 | tf_op jit(solution)/shard_map/ppermute | solution.py:49
  259.8 12.3 %collective-permute-start.30 = (bf16[24,2304]{1,0:T(8,128)(2,1)}, bf16[24,2304]{1,0:T(8,128)(2,1)}, u32[]{:S(2)}, u32[]{:S(2)}) collective-permute-start(bf16[24,2304]{1,0:T(8,128)(2,1)} %get-tuple-element.204), channel_id=1, source_target_pairs={{0,2},{2,4},{4,6},{6,0},{1,3},{3,5},{5,7},{7,1},{8,10},{10,12},{12... | collective-permute-start | bytes 331784 | tf_op jit(solution)/shard_map/ppermute | solution.py:49
  (30 other events, 103.4 us)
Sparse Core Ops, SparseCore 0:
  10.9 106.4 all-gather.2

commit v10 on v9

--- a/solution.py
+++ b/solution.py
@@ -355,7 +355,7 @@
             pltpu.VMEM((WIDTH, queries), f32),
         ],
         compiler_params=pltpu.CompilerParams(vmem_limit_bytes=48 << 20),
-    )(*map(hbm, (came, *pairs, key_docs, query_docs)))
+    )(*map(hbm, (came, *pairs[:-1])), pairs[-1], *map(hbm, (key_docs, query_docs)))
 
 
 def backward_kernel(

time: 283 us -> 283 us (level)
  no operation moved by 1% of the time
where the time goes in v10:
time: 283 us; the launch traced here: 281 us
  waiting for transfers between devices  86.2 us (30%)
  Pallas kernels  72.7 us (26%)
  starting transfers between devices  58.9 us (21%)
  blocking collectives  28.3 us (10%)
  between operations  14.5 us (5%)
  other arithmetic  13 us (5%)
  local copies, waits for them, and re-layouts  7.84 us (3%)
    ppermute x24, waiting for transfers between devices, swap(): return lax.ppermute(value, axis, [(0, 1), (1, 0)])  53.8 us
    pallas_call x8, Pallas kernels, single(): pl.pallas_call(kernel, grid=(1,), out_shape=tuple((result(*o) for o in ou...  39.7 us
    all_to_all x1, blocking collectives, exchange(): return lax.all_to_all(rows, SPOT, 0, 0, tiled=True)  28.3 us
    all_to_all x4, starting transfers between devices, exchange(): return lax.all_to_all(rows, SPOT, 0, 0, tiled=True)  17.3 us
    ppermute x24, starting transfers between devices, swap(): return lax.ppermute(value, axis, [(0, 1), (1, 0)])  16.6 us
    all_to_all x4, waiting for transfers between devices, exchange(): return lax.all_to_all(rows, SPOT, 0, 0, tiled=True)  15.4 us
    ppermute x9, starting transfers between devices, turn(): lax.ppermute(value, axis, [(i, (i - step) % size) for i in range(size)])  14.5 us
    pallas_call x1, Pallas kernels, attend_back(): pl.pallas_call(partial(backward_kernel, starts), grid=(steps,), out_shape...  13 us
  transfers between devices with their start and end apart: 40, of which 19 were waited for; matrix products, arithmetic and copies ran while one was open for 5% of the time, Pallas kernels for 21%

profile of v10, /device:TPU:0, one launch (start us, length us, event | category | flops | bytes accessed | tf_op | source)
XLA Modules:
  0.0 281.4 jit_solution(16695694889404491858)
XLA Ops:
  8.4 2.1 shard_map.246
  10.6 5.1 %collective-permute-start = (bf16[24,2304]{1,0:T(8,128)(2,1)}, bf16[24,2304]{1,0:T(8,128)(2,1)S(1)}, u32[]{:S(2)}, u32[]{:S(2)}) collective-permute-start(bf16[24,2304]{1,0:T(8,128)(2,1)} %param.23), channel_id=1, source_target_pairs={{0,6},{2,0},{4,2},{6,4},{1,7},{3,1},{5,3},{7,5},{8,14},{10,8},{12,... | collective-permute-start | bytes 331784 | tf_op jit(solution)/shard_map/ppermute | solution.py:49
  16.7 5.6 %all-to-all-start = ((f32[32,1,640]{2,1,0:T(1,128)}), f32[32,1,640]{2,1,0:T(1,128)S(1)}, u32[]{:S(2)}, u32[]{:S(2)}) async-start(f32[32,1,640]{2,1,0:T(1,128)} %get-tuple-element.102), calls=%async_computation | async-start | bytes 163840 | tf_op jit(solution)/shard_map/all_to_all | solution.py:1042
  23.5 2.7 collective-permute-done.1
  27.1 3.9 %all-to-all-done.every_ref = f32[32,1,640]{2,1,0:T(1,128)S(1)} async-done(((f32[32,1,640]{2,1,0:T(1,128)}), f32[32,1,640]{2,1,0:T(1,128)S(1)}, u32[]{:S(2)}, u32[]{:S(2)}) %all-to-all-start) | async-done | bytes 81952 | tf_op jit(solution)/shard_map/all_to_all | solution.py:1042
  32.6 4.8 %collective-permute-done.5 = bf16[4,24,1152]{2,1,0:T(8,128)(2,1)S(1)} collective-permute-done((bf16[4,24,1152]{2,1,0:T(8,128)(2,1)S(1)}, bf16[4,24,1152]{2,1,0:T(8,128)(2,1)S(1)}, u32[]{:S(2)}, u32[]{:S(2)}) %collective-permute-start.5) | collective-permute-done | bytes 221216 | tf_op jit(solution)/shard_map/ppermute | solution.py:44
  40.5 2.5 shard_map.247
  42.9 12.9 %collective-permute-done.6 = bf16[2,4,24,1152]{3,2,1,0:T(8,128)(2,1)S(1)} collective-permute-done((bf16[2,4,24,1152]{3,2,1,0:T(8,128)(2,1)S(1)}, bf16[2,4,24,1152]{3,2,1,0:T(8,128)(2,1)S(1)}, u32[]{:S(2)}, u32[]{:S(2)}) %collective-permute-start.6) | collective-permute-done | bytes 442400 | tf_op jit(solution)/shard_map/ppermute | solution.py:44
  56.6 1.9 collective-permute-done.7.refs_1_
  59.8 6.9 %shard_map.248 = (bf16[128,768]{1,0:T(8,128)(2,1)}, bf16[8,64,384]{2,1,0:T(8,128)(2,1)S(1)}, bf16[8,32,384]{2,1,0:T(8,128)(2,1)}, bf16[768,2304]{1,0:T(8,128)(2,1)}) custom-call(s32[5]{0:T(128)S(1)} %stack.71.place_ref, bf16[2,64,768]{2,1,0:T(8,128)(2,1)} %x_ref.5, f32[8,4608]{1,0:T(8,128)} %get-tuple-element.111.mod_ref, ...), custom_call_target="tpu_custom_call" | custom-call | tf_op jit(solution)/shard_map/pallas_call | solution.py:81
  66.7 28.3 %all_to_all.35 = bf16[8,64,384]{2,1,0:T(8,128)(2,1)S(1)} all-to-all(bf16[8,64,384]{2,1,0:T(8,128)(2,1)S(1)} %get-tuple-element.115), channel_id=1, replica_groups=mesh['hx'=2,'hc'=2,'rb'=1,'sz'=4,'sy'=2] {'sz','sy'}, dimensions={0} | all-to-all | bytes 786432 | tf_op jit(solution)/shard_map/all_to_all | solution.py:1009
  94.9 4.0 %all-to-all-start.2 = ((bf16[8,32,384]{2,1,0:T(8,128)(2,1)}), bf16[8,32,384]{2,1,0:T(8,128)(2,1)S(1)}, u32[]{:S(2)}, u32[]{:S(2)}) async-start(bf16[8,32,384]{2,1,0:T(8,128)(2,1)} %get-tuple-element.116), calls=%async_computation.2 | async-start | bytes 393216 | tf_op jit(solution)/shard_map/all_to_all | solution.py:1009
  98.9 13.7 %all-to-all-done.2.came_ref = bf16[8,32,384]{2,1,0:T(8,128)(2,1)S(1)} async-done(((bf16[8,32,384]{2,1,0:T(8,128)(2,1)}), bf16[8,32,384]{2,1,0:T(8,128)(2,1)S(1)}, u32[]{:S(2)}, u32[]{:S(2)}) %all-to-all-start.2) | async-done | bytes 196640 | tf_op jit(solution)/shard_map/all_to_all | solution.py:1009
  114.6 9.4 %shard_map.249 = (bf16[8,32,384]{2,1,0:T(8,128)(2,1)}, f32[192,512]{1,0:T(8,128)}, f32[8,512]{1,0:T(8,128)}) custom-call(bf16[8,32,384]{2,1,0:T(8,128)(2,1)} %copy-done.5, bf16[512,384]{1,0:T(8,128)(2,1)} %bitcast.74, bf16[512,384]{1,0:T(8,128)(2,1)} %copy-done.6, bf16[512,384]{1,0:T(8,128)(2,1)} %copy-done.7, ...), custom_call_target="tpu_custom_call" | custom-call | tf_op jit(solution)/shard_map/pallas_call | solution.py:338
  124.0 3.6 %all-to-all-start.3 = ((bf16[8,32,384]{2,1,0:T(8,128)(2,1)}), bf16[8,32,384]{2,1,0:T(8,128)(2,1)S(1)}, u32[]{:S(2)}, u32[]{:S(2)}) async-start(bf16[8,32,384]{2,1,0:T(8,128)(2,1)} %get-tuple-element.121), calls=%async_computation.3 | async-start | bytes 393216 | tf_op jit(solution)/shard_map/all_to_all | solution.py:1009
  127.6 8.5 %shard_map.250 = (bf16[768,768]{1,0:T(8,128)(2,1)}, bf16[768,3072]{1,0:T(8,128)(2,1)}, bf16[3072,768]{1,0:T(8,128)(2,1)}) custom-call(bf16[32,9,24,768]{3,2,1,0:T(8,128)(2,1)} %bitcast.71), custom_call_target="tpu_custom_call" | custom-call | tf_op jit(solution)/shard_map/pallas_call | solution.py:509
  136.9 10.4 %shard_map.251 = (bf16[2,64,768]{2,1,0:T(8,128)(2,1)}, f32[128,768]{1,0:T(8,128)}, bf16[8,32,384]{2,1,0:T(8,128)(2,1)}, bf16[128,9216]{1,0:T(8,128)(2,1)S(1)}, f32[16,768]{1,0:T(8,128)}) custom-call(bf16[8,32,384]{2,1,0:T(8,128)(2,1)} %copy-done.11, bf16[2,64,768]{2,1,0:T(8,128)(2,1)} %x_ref.5, bf16[2,64,768]{2,1,0:T(8,128)(2,1)} %teacher_ref.1, ...), custom_call_target="tpu_custom_call" | custom-call | tf_op jit(solution)/shard_map/pallas_call | solution.py:81
  147.4 5.7 %all-to-all-start.4 = ((bf16[8,32,384]{2,1,0:T(8,128)(2,1)}), bf16[8,32,384]{2,1,0:T(8,128)(2,1)S(1)}, u32[]{:S(2)}, u32[]{:S(2)}) async-start(bf16[8,32,384]{2,1,0:T(8,128)(2,1)} %get-tuple-element.129), calls=%async_computation.4 | async-start | bytes 393216 | tf_op jit(solution)/shard_map/all_to_all | solution.py:1009
  153.1 6.9 %shard_map.252 = (bf16[2,4,9,24,128]{4,3,2,1,0:T(8,128)(2,1)}, bf16[2,4,9,24,128]{4,3,2,1,0:T(8,128)(2,1)}, bf16[2,4,9,24,256]{4,3,2,1,0:T(8,128)(2,1)}, bf16[2,...) custom-call(s32[5]{0:T(128)S(1)} %stack.71.place_ref, ...), custom_call_target="tpu_custom_call" | custom-call | tf_op jit(solution)/shard_map/pallas_call | solution.py:81
  164.0 13.0 %shard_map.253 = (bf16[8,32,384]{2,1,0:T(8,128)(2,1)S(1)}, f32[512,384]{1,0:T(8,128)S(1)}, f32[512,384]{1,0:T(8,128)S(1)}, bf16[1024,384]{1,0:T(8,128)(2,1)S(1)}) custom-call(bf16[8,32,384]{2,1,0:T(8,128)(2,1)} %copy-done.5, bf16[8,32,384]{2,1,0:T(8,128)(2,1)} %copy-done.10, bf16[512,384]{1,0:T(8,128)(2,1)} %bitcast.75, bf16[512,384]{1,0:T(8,128)(2,1)} %copy-done.6, ...), custom_call_target="tpu_custom_call" | custom-call | tf_op jit(solution)/shard_map/pallas_call | solution.py:435
  177.1 2.3 collective-permute-done.15
  182.7 8.8 %collective-permute-done.16 = bf16[512,384]{1,0:T(8,128)(2,1)S(1)} collective-permute-done((bf16[512,384]{1,0:T(8,128)(2,1)S(1)}, bf16[512,384]{1,0:T(8,128)(2,1)S(1)}, u32[]{:S(2)}, u32[]{:S(2)}) %collective-permute-start.16) | collective-permute-done | bytes 393248 | tf_op jit(solution)/shard_map/ppermute | solution.py:44
  192.5 3.9 %all-to-all-start.5 = ((bf16[8,96,384]{2,1,0:T(8,128)(2,1)}), bf16[8,96,384]{2,1,0:T(8,128)(2,1)S(1)}, u32[]{:S(2)}, u32[]{:S(2)}) async-start(bf16[8,96,384]{2,1,0:T(8,128)(2,1)} %pad_maximum_fusion.6), calls=%async_computation.5 | async-start | bytes 1179648 | tf_op jit(solution)/shard_map/all_to_all | solution.py:1009
  196.5 10.1 %collective-permute-done.23 = bf16[2,4,9,24,256]{4,3,2,1,0:T(8,128)(2,1)} collective-permute-done((bf16[2,4,9,24,256]{4,3,2,1,0:T(8,128)(2,1)}, bf16[2,4,9,24,256]{4,3,2,1,0:T(8,128)(2,1)}, u32[]{:S(2)}, u32[]{:S(2)}) %collective-permute-start.23) | collective-permute-done | bytes 884768 | tf_op jit(solution)/shard_map/ppermute | solution.py:44
  217.5 4.1 %shard_map.254 = (bf16[2,4,24,1152]{3,2,1,0:T(8,128)(2,1)}, bf16[2,4,24,1152]{3,2,1,0:T(8,128)(2,1)}, bf16[2,4,24,1152]{3,2,1,0:T(8,128)(2,1)}, bf16[2,4,24,1152]{3,2,1,0:T(8,128)(2,1)}) custom-call(s32[5]{0:T(128)S(1)} %stack.71.place_ref, bf16[128,768]{1,0:T(8,128)(2,1)} %get-tuple-element.149.entered_ref, bf16[128,768]{1,0:T(8,128)(2,1)} %copy-done.21, ...), custom_call_target="tpu_custom_call" | custom-call | tf_op jit(solution)/shard_map/pallas_call | solution.py:81
  224.0 7.0 %collective-permute-done.26 = bf16[4,9,24,384]{3,2,1,0:T(8,128)(2,1)} collective-permute-done((bf16[4,9,24,384]{3,2,1,0:T(8,128)(2,1)}, bf16[4,9,24,384]{3,2,1,0:T(8,128)(2,1)}, u32[]{:S(2)}, u32[]{:S(2)}) %collective-permute-start.26) | collective-permute-done | bytes 663584 | tf_op jit(solution)/shard_map/ppermute | solution.py:44
  233.8 3.2 %collective-permute-start.29 = (bf16[9,24,768]{2,1,0:T(8,128)(2,1)}, bf16[9,24,768]{2,1,0:T(8,128)(2,1)S(1)}, u32[]{:S(2)}, u32[]{:S(2)}) collective-permute-start(bf16[9,24,768]{2,1,0:T(8,128)(2,1)} %get-tuple-element.195), channel_id=1, source_target_pairs={{0,6},{2,0},{4,2},{6,4},{1,7},{3,1},{5,3},{7,5},{8,14},{10,8},{12,... | collective-permute-start | bytes 995336 | tf_op jit(solution)/shard_map/ppermute | solution.py:49
  237.6 4.9 %shard_map.255 = (f32[2,64,768]{2,1,0:T(8,128)}, f32[32,1,512]{2,1,0:T(1,128)}, bf16[128,2304]{1,0:T(8,128)(2,1)}) custom-call(bf16[8,96,384]{2,1,0:T(8,128)(2,1)} %copy-done.3, bf16[2,64,768]{2,1,0:T(8,128)(2,1)} %x_ref.5, f32[128,768]{1,0:T(8,128)} %get-tuple-element.155.hidden_ref, f32[8,4608]{1,0:T(8,128)} %get-tuple-element.111.mod_ref, ...), custom_call_target="tpu_custom_call" | custom-call | tf_op jit(solution)/shard_map/pallas_call | solution.py:81
  246.9 4.8 %all-to-all-start.6 = ((f32[32,1,512]{2,1,0:T(1,128)}), f32[32,1,512]{2,1,0:T(1,128)}, u32[]{:S(2)}, u32[]{:S(2)}) async-start(f32[32,1,512]{2,1,0:T(1,128)} %get-tuple-element.161), calls=%async_computation.6 | async-start | bytes 131072 | tf_op jit(solution)/shard_map/all_to_all | solution.py:1173
  254.9 3.5 %collective-permute-start.32 = (bf16[24,2304]{1,0:T(8,128)(2,1)}, bf16[24,2304]{1,0:T(8,128)(2,1)}, u32[]{:S(2)}, u32[]{:S(2)}) collective-permute-start(bf16[24,2304]{1,0:T(8,128)(2,1)} %get-tuple-element.202), channel_id=1, source_target_pairs={{0,6},{2,0},{4,2},{6,4},{1,7},{3,1},{5,3},{7,5},{8,14},{10,8},{12,... | collective-permute-start | bytes 331784 | tf_op jit(solution)/shard_map/ppermute | solution.py:49
  260.3 8.6 %all-to-all-done.6.small_ref = f32[32,1,512]{2,1,0:T(1,128)} async-done(((f32[32,1,512]{2,1,0:T(1,128)}), f32[32,1,512]{2,1,0:T(1,128)}, u32[]{:S(2)}, u32[]{:S(2)}) %all-to-all-start.6) | async-done | bytes 65568 | tf_op jit(solution)/shard_map/all_to_all | solution.py:1173
  272.4 2.2 shard_map.257
  (134 shorter events, 51.5 us)
Async XLA Ops:
  7.2 120.4 %all-gather.3.cloned.1.call-start = ((), (), s32[]{:S(2)}) async-start(), calls=%async_computation.7 | async-start | bytes 10948608 | tf_op jit(solution)/shard_map/all_gather | solution.py:1049
  10.6 11.7 %collective-permute-start = (bf16[24,2304]{1,0:T(8,128)(2,1)}, bf16[24,2304]{1,0:T(8,128)(2,1)S(1)}, u32[]{:S(2)}, u32[]{:S(2)}) collective-permute-start(bf16[24,2304]{1,0:T(8,128)(2,1)} %param.23), channel_id=1, source_target_pairs={{0,6},{2,0},{4,2},{6,4},{1,7},{3,1},{5,3},{7,5},{8,14},{10,8},{12,... | collective-permute-start | bytes 331784 | tf_op jit(solution)/shard_map/ppermute | solution.py:49
  15.7 7.8 %collective-permute-start.2 = (bf16[24,2304]{1,0:T(8,128)(2,1)}, bf16[24,2304]{1,0:T(8,128)(2,1)S(1)}, u32[]{:S(2)}, u32[]{:S(2)}) collective-permute-start(bf16[24,2304]{1,0:T(8,128)(2,1)} %param.23), channel_id=1, source_target_pairs={{0,2},{2,4},{4,6},{6,0},{1,3},{3,5},{5,7},{7,1},{8,10},{10,12},{12... | collective-permute-start | bytes 331784 | tf_op jit(solution)/shard_map/ppermute | solution.py:49
  15.7 10.5 %collective-permute-start.1 = (bf16[24,2304]{1,0:T(8,128)(2,1)}, bf16[24,2304]{1,0:T(8,128)(2,1)S(1)}, u32[]{:S(2)}, u32[]{:S(2)}) collective-permute-start(bf16[24,2304]{1,0:T(8,128)(2,1)} %param.23), channel_id=1, source_target_pairs={{0,4},{2,6},{4,0},{6,2},{1,5},{3,7},{5,1},{7,3},{8,12},{10,14},{12... | collective-permute-start | bytes 331784 | tf_op jit(solution)/shard_map/ppermute | solution.py:49
  16.7 14.3 %all-to-all-start = ((f32[32,1,640]{2,1,0:T(1,128)}), f32[32,1,640]{2,1,0:T(1,128)S(1)}, u32[]{:S(2)}, u32[]{:S(2)}) async-start(f32[32,1,640]{2,1,0:T(1,128)} %get-tuple-element.102), calls=%async_computation | async-start | bytes 163840 | tf_op jit(solution)/shard_map/all_to_all | solution.py:1042
  32.1 7.2 %collective-permute-start.3 = (bf16[4,24,1152]{2,1,0:T(8,128)(2,1)S(1)}, bf16[4,24,1152]{2,1,0:T(8,128)(2,1)S(1)}, u32[]{:S(2)}, u32[]{:S(2)}) collective-permute-start(bf16[4,24,1152]{2,1,0:T(8,128)(2,1)S(1)} %get-tuple-element.210), channel_id=1, source_target_pairs={{0,16},{16,0},{1,17},{17,1},{2,18},{18,2},{3,19},{19,3},{4,20},{20... | collective-permute-start | bytes 663560 | tf_op jit(solution)/shard_map/ppermute | solution.py:44
  37.6 18.2 %collective-permute-start.6 = (bf16[2,4,24,1152]{3,2,1,0:T(8,128)(2,1)S(1)}, bf16[2,4,24,1152]{3,2,1,0:T(8,128)(2,1)S(1)}, u32[]{:S(2)}, u32[]{:S(2)}) collective-permute-start(bf16[2,4,24,1152]{3,2,1,0:T(8,128)(2,1)S(1)} %get-tuple-element.206), channel_id=1, source_target_pairs={{0,16},{16,0},{1,17},{17,1},{2,18},{18,2},{3,19},{19,3},{4,20},{20... | collective-permute-start | bytes 1327112 | tf_op jit(solution)/shard_map/ppermute | solution.py:44
  39.3 16.6 %collective-permute-start.4 = (bf16[2,4,24,1152]{3,2,1,0:T(8,128)(2,1)S(1)}, bf16[2,4,24,1152]{3,2,1,0:T(8,128)(2,1)S(1)}, u32[]{:S(2)}, u32[]{:S(2)}) collective-permute-start(bf16[2,4,24,1152]{3,2,1,0:T(8,128)(2,1)S(1)} %get-tuple-element.212), channel_id=1, source_target_pairs={{0,1},{1,0},{2,3},{3,2},{4,5},{5,4},{6,7},{7,6},{8,9},{9,8},{10,11... | collective-permute-start | bytes 1327112 | tf_op jit(solution)/shard_map/ppermute | solution.py:44
  94.9 17.7 %collective-permute-start.9 = (bf16[512,384]{1,0:T(8,128)(2,1)S(1)}, bf16[512,384]{1,0:T(8,128)(2,1)S(1)}, u32[]{:S(2)}, u32[]{:S(2)}) collective-permute-start(bf16[512,384]{1,0:T(8,128)(2,1)S(1)} %bitcast.72), channel_id=1, source_target_pairs={{0,16},{16,0},{1,17},{17,1},{2,18},{18,2},{3,19},{19,3},{4,20},{20... | collective-permute-start | bytes 1179656 | tf_op jit(solution)/shard_map/ppermute | solution.py:44
  94.9 17.7 %all-to-all-start.2 = ((bf16[8,32,384]{2,1,0:T(8,128)(2,1)}), bf16[8,32,384]{2,1,0:T(8,128)(2,1)S(1)}, u32[]{:S(2)}, u32[]{:S(2)}) async-start(bf16[8,32,384]{2,1,0:T(8,128)(2,1)} %get-tuple-element.116), calls=%async_computation.2 | async-start | bytes 393216 | tf_op jit(solution)/shard_map/all_to_all | solution.py:1009
  98.9 13.8 %collective-permute-start.10 = (bf16[512,384]{1,0:T(8,128)(2,1)S(1)}, bf16[512,384]{1,0:T(8,128)(2,1)S(1)}, u32[]{:S(2)}, u32[]{:S(2)}) collective-permute-start(bf16[512,384]{1,0:T(8,128)(2,1)S(1)} %bitcast.73), channel_id=1, source_target_pairs={{0,8},{8,0},{1,9},{9,1},{2,10},{10,2},{3,11},{11,3},{4,12},{12,4},... | collective-permute-start | bytes 1179656 | tf_op jit(solution)/shard_map/ppermute | solution.py:44
  124.0 12.2 %all-to-all-start.3 = ((bf16[8,32,384]{2,1,0:T(8,128)(2,1)}), bf16[8,32,384]{2,1,0:T(8,128)(2,1)S(1)}, u32[]{:S(2)}, u32[]{:S(2)}) async-start(bf16[8,32,384]{2,1,0:T(8,128)(2,1)} %get-tuple-element.121), calls=%async_computation.3 | async-start | bytes 393216 | tf_op jit(solution)/shard_map/all_to_all | solution.py:1009
  147.4 14.3 %all-to-all-start.4 = ((bf16[8,32,384]{2,1,0:T(8,128)(2,1)}), bf16[8,32,384]{2,1,0:T(8,128)(2,1)S(1)}, u32[]{:S(2)}, u32[]{:S(2)}) async-start(bf16[8,32,384]{2,1,0:T(8,128)(2,1)} %get-tuple-element.129), calls=%async_computation.4 | async-start | bytes 393216 | tf_op jit(solution)/shard_map/all_to_all | solution.py:1009
  161.7 15.3 %collective-permute-start.13 = (bf16[2,4,9,24,128]{4,3,2,1,0:T(8,128)(2,1)}, bf16[2,4,9,24,128]{4,3,2,1,0:T(8,128)(2,1)S(1)}, u32[]{:S(2)}, u32[]{:S(2)}) collective-permute-start(bf16[2,4,9,24,128]{4,3,2,1,0:T(8,128)(2,1)} %get-tuple-element.144), channel_id=1, source_target_pairs={{0,1},{1,0},{2,3},{3,2},{4,5},{5,4},{6,7},{7,6},{8,9},{9,8},{10,11... | collective-permute-start | bytes 1327112 | tf_op jit(solution)/shard_map/ppermute | solution.py:44
  162.7 14.3 %collective-permute-start.14 = (bf16[2,4,9,24,128]{4,3,2,1,0:T(8,128)(2,1)}, bf16[2,4,9,24,128]{4,3,2,1,0:T(8,128)(2,1)S(1)}, u32[]{:S(2)}, u32[]{:S(2)}) collective-permute-start(bf16[2,4,9,24,128]{4,3,2,1,0:T(8,128)(2,1)} %get-tuple-element.145), channel_id=1, source_target_pairs={{0,16},{16,0},{1,17},{17,1},{2,18},{18,2},{3,19},{19,3},{4,20},{20... | collective-permute-start | bytes 1327112 | tf_op jit(solution)/shard_map/ppermute | solution.py:44
  179.5 12.0 %collective-permute-start.16 = (bf16[512,384]{1,0:T(8,128)(2,1)S(1)}, bf16[512,384]{1,0:T(8,128)(2,1)S(1)}, u32[]{:S(2)}, u32[]{:S(2)}) collective-permute-start(bf16[512,384]{1,0:T(8,128)(2,1)S(1)} %add_convert_fusion.3), channel_id=1, source_target_pairs={{0,16},{16,0},{1,17},{17,1},{2,18},{18,2},{3,19},{19,3},{4,20},{20... | collective-permute-start | bytes 1179656 | tf_op jit(solution)/shard_map/ppermute | solution.py:44
  180.2 26.4 %collective-permute-start.23 = (bf16[2,4,9,24,256]{4,3,2,1,0:T(8,128)(2,1)}, bf16[2,4,9,24,256]{4,3,2,1,0:T(8,128)(2,1)}, u32[]{:S(2)}, u32[]{:S(2)}) collective-permute-start(bf16[2,4,9,24,256]{4,3,2,1,0:T(8,128)(2,1)} %get-tuple-element.171), channel_id=1, source_target_pairs={{0,1},{1,0},{2,3},{3,2},{4,5},{5,4},{6,7},{7,6},{8,9},{9,8},{10,11... | collective-permute-start | bytes 2654216 | tf_op jit(solution)/shard_map/ppermute | solution.py:44
  181.3 29.3 %collective-permute-start.25 = (bf16[2,4,9,24,256]{4,3,2,1,0:T(8,128)(2,1)}, bf16[2,4,9,24,256]{4,3,2,1,0:T(8,128)(2,1)}, u32[]{:S(2)}, u32[]{:S(2)}) collective-permute-start(bf16[2,4,9,24,256]{4,3,2,1,0:T(8,128)(2,1)} %get-tuple-element.175), channel_id=1, source_target_pairs={{0,16},{16,0},{1,17},{17,1},{2,18},{18,2},{3,19},{19,3},{4,20},{20... | collective-permute-start | bytes 2654216 | tf_op jit(solution)/shard_map/ppermute | solution.py:44
  192.5 21.2 %all-to-all-start.5 = ((bf16[8,96,384]{2,1,0:T(8,128)(2,1)}), bf16[8,96,384]{2,1,0:T(8,128)(2,1)S(1)}, u32[]{:S(2)}, u32[]{:S(2)}) async-start(bf16[8,96,384]{2,1,0:T(8,128)(2,1)} %pad_maximum_fusion.6), calls=%async_computation.5 | async-start | bytes 1179648 | tf_op jit(solution)/shard_map/all_to_all | solution.py:1009
  208.9 15.0 %collective-permute-start.24 = (bf16[4,9,24,384]{3,2,1,0:T(8,128)(2,1)}, bf16[4,9,24,384]{3,2,1,0:T(8,128)(2,1)}, u32[]{:S(2)}, u32[]{:S(2)}) collective-permute-start(bf16[4,9,24,384]{3,2,1,0:T(8,128)(2,1)} %pad_maximum_fusion.4), channel_id=1, source_target_pairs={{0,16},{16,0},{1,17},{17,1},{2,18},{18,2},{3,19},{19,3},{4,20},{20... | collective-permute-start | bytes 1990664 | tf_op jit(solution)/shard_map/ppermute | solution.py:44
  212.9 18.2 %collective-permute-start.26 = (bf16[4,9,24,384]{3,2,1,0:T(8,128)(2,1)}, bf16[4,9,24,384]{3,2,1,0:T(8,128)(2,1)}, u32[]{:S(2)}, u32[]{:S(2)}) collective-permute-start(bf16[4,9,24,384]{3,2,1,0:T(8,128)(2,1)} %pad_maximum_fusion.5), channel_id=1, source_target_pairs={{0,1},{1,0},{2,3},{3,2},{4,5},{5,4},{6,7},{7,6},{8,9},{9,8},{10,11... | collective-permute-start | bytes 1990664 | tf_op jit(solution)/shard_map/ppermute | solution.py:44
  221.6 21.2 %collective-permute-start.19 = (bf16[2,4,24,1152]{3,2,1,0:T(8,128)(2,1)}, bf16[2,4,24,1152]{3,2,1,0:T(8,128)(2,1)S(1)}, u32[]{:S(2)}, u32[]{:S(2)}) collective-permute-start(bf16[2,4,24,1152]{3,2,1,0:T(8,128)(2,1)} %get-tuple-element.151), channel_id=1, source_target_pairs={{0,1},{1,0},{2,3},{3,2},{4,5},{5,4},{6,7},{7,6},{8,9},{9,8},{10,11... | collective-permute-start | bytes 1327112 | tf_op jit(solution)/shard_map/ppermute | solution.py:44
  222.8 20.0 %collective-permute-start.20 = (bf16[2,4,24,1152]{3,2,1,0:T(8,128)(2,1)}, bf16[2,4,24,1152]{3,2,1,0:T(8,128)(2,1)S(1)}, u32[]{:S(2)}, u32[]{:S(2)}) collective-permute-start(bf16[2,4,24,1152]{3,2,1,0:T(8,128)(2,1)} %get-tuple-element.153), channel_id=1, source_target_pairs={{0,16},{16,0},{1,17},{17,1},{2,18},{18,2},{3,19},{19,3},{4,20},{20... | collective-permute-start | bytes 1327112 | tf_op jit(solution)/shard_map/ppermute | solution.py:44
  233.8 24.6 %collective-permute-start.29 = (bf16[9,24,768]{2,1,0:T(8,128)(2,1)}, bf16[9,24,768]{2,1,0:T(8,128)(2,1)S(1)}, u32[]{:S(2)}, u32[]{:S(2)}) collective-permute-start(bf16[9,24,768]{2,1,0:T(8,128)(2,1)} %get-tuple-element.195), channel_id=1, source_target_pairs={{0,6},{2,0},{4,2},{6,4},{1,7},{3,1},{5,3},{7,5},{8,14},{10,8},{12,... | collective-permute-start | bytes 995336 | tf_op jit(solution)/shard_map/ppermute | solution.py:49
  237.0 33.8 %collective-permute-start.28 = (bf16[9,24,768]{2,1,0:T(8,128)(2,1)}, bf16[9,24,768]{2,1,0:T(8,128)(2,1)}, u32[]{:S(2)}, u32[]{:S(2)}) collective-permute-start(bf16[9,24,768]{2,1,0:T(8,128)(2,1)} %get-tuple-element.196), channel_id=1, source_target_pairs={{0,4},{2,6},{4,0},{6,2},{1,5},{3,7},{5,1},{7,3},{8,12},{10,14},{12... | collective-permute-start | bytes 995336 | tf_op jit(solution)/shard_map/ppermute | solution.py:49
  237.0 33.8 %collective-permute-start.27 = (bf16[9,24,768]{2,1,0:T(8,128)(2,1)}, bf16[9,24,768]{2,1,0:T(8,128)(2,1)}, u32[]{:S(2)}, u32[]{:S(2)}) collective-permute-start(bf16[9,24,768]{2,1,0:T(8,128)(2,1)} %get-tuple-element.197), channel_id=1, source_target_pairs={{0,2},{2,4},{4,6},{6,0},{1,3},{3,5},{5,7},{7,1},{8,10},{10,12},{12... | collective-permute-start | bytes 995336 | tf_op jit(solution)/shard_map/ppermute | solution.py:49
  244.3 7.4 %collective-permute-start.22 = (bf16[4,24,1152]{2,1,0:T(8,128)(2,1)}, bf16[4,24,1152]{2,1,0:T(8,128)(2,1)}, u32[]{:S(2)}, u32[]{:S(2)}) collective-permute-start(bf16[4,24,1152]{2,1,0:T(8,128)(2,1)} %fusion.3), channel_id=1, source_target_pairs={{0,1},{1,0},{2,3},{3,2},{4,5},{5,4},{6,7},{7,6},{8,9},{9,8},{10,11... | collective-permute-start | bytes 663560 | tf_op jit(solution)/shard_map/ppermute | solution.py:44
  246.2 6.8 %collective-permute-start.21 = (bf16[4,24,1152]{2,1,0:T(8,128)(2,1)}, bf16[4,24,1152]{2,1,0:T(8,128)(2,1)}, u32[]{:S(2)}, u32[]{:S(2)}) collective-permute-start(bf16[4,24,1152]{2,1,0:T(8,128)(2,1)} %fusion.2), channel_id=1, source_target_pairs={{0,16},{16,0},{1,17},{17,1},{2,18},{18,2},{3,19},{19,3},{4,20},{20... | collective-permute-start | bytes 663560 | tf_op jit(solution)/shard_map/ppermute | solution.py:44
  246.9 22.1 %all-to-all-start.6 = ((f32[32,1,512]{2,1,0:T(1,128)}), f32[32,1,512]{2,1,0:T(1,128)}, u32[]{:S(2)}, u32[]{:S(2)}) async-start(f32[32,1,512]{2,1,0:T(1,128)} %get-tuple-element.161), calls=%async_computation.6 | async-start | bytes 131072 | tf_op jit(solution)/shard_map/all_to_all | solution.py:1173
  254.9 15.9 %collective-permute-start.32 = (bf16[24,2304]{1,0:T(8,128)(2,1)}, bf16[24,2304]{1,0:T(8,128)(2,1)}, u32[]{:S(2)}, u32[]{:S(2)}) collective-permute-start(bf16[24,2304]{1,0:T(8,128)(2,1)} %get-tuple-element.202), channel_id=1, source_target_pairs={{0,6},{2,0},{4,2},{6,4},{1,7},{3,1},{5,3},{7,5},{8,14},{10,8},{12,... | collective-permute-start | bytes 331784 | tf_op jit(solution)/shard_map/ppermute | solution.py:49
  258.4 13.0 %collective-permute-start.31 = (bf16[24,2304]{1,0:T(8,128)(2,1)}, bf16[24,2304]{1,0:T(8,128)(2,1)}, u32[]{:S(2)}, u32[]{:S(2)}) collective-permute-start(bf16[24,2304]{1,0:T(8,128)(2,1)} %get-tuple-element.203), channel_id=1, source_target_pairs={{0,4},{2,6},{4,0},{6,2},{1,5},{3,7},{5,1},{7,3},{8,12},{10,14},{12... | collective-permute-start | bytes 331784 | tf_op jit(solution)/shard_map/ppermute | solution.py:49
  259.2 12.3 %collective-permute-start.30 = (bf16[24,2304]{1,0:T(8,128)(2,1)}, bf16[24,2304]{1,0:T(8,128)(2,1)}, u32[]{:S(2)}, u32[]{:S(2)}) collective-permute-start(bf16[24,2304]{1,0:T(8,128)(2,1)} %get-tuple-element.204), channel_id=1, source_target_pairs={{0,2},{2,4},{4,6},{6,0},{1,3},{3,5},{5,7},{7,1},{8,10},{10,12},{12... | collective-permute-start | bytes 331784 | tf_op jit(solution)/shard_map/ppermute | solution.py:49
  (30 other events, 124.3 us)
Sparse Core Ops, SparseCore 0:
  10.9 106.4 all-gather.2
